TPU v7x, 32 devices: a whole 2x2x4 slice. The times are simulated.
32 devices in a mesh: seg: 4 (over x, core), wide: 8 (over z, y).
Axes of the slice: x: 2, y: 2, z: 4, core: 2. Of those that a mesh axis runs over, the one named last changes fastest.
Arguments:
- encoded: bfloat16 [4, 4096, 384], P('seg', 'wide'), may hold values from -6 to 6
- targets: float32 [4, 2048, 128], P('seg'), may hold values from -60 to 60
- present: int32 [4, 4], P('seg'), may hold values 0 or 1
- wide_master: float32 [768, 3200], P('wide'), may hold values from -2 to 2
- down_master: float32 [3072, 384], P('wide'), may hold values from -0.15625 to 0.15625
- gain_master: float32 [6144], P('wide'), may hold values from -2 to 2
- wide_first: float32 [768, 3200], P('wide'), may hold values from -3.5762787e-07 to 3.5762787e-07
- down_first: float32 [3072, 384], P('wide'), may hold values from -3.5762787e-07 to 3.5762787e-07
- gain_first: float32 [6144], P('wide'), may hold values from -1.4305115e-06 to 1.4305115e-06
- wide_second: float32 [768, 3200], P('wide'), may hold values from 2.744695e-16 to 1.097878e-15
- down_second: float32 [3072, 384], P('wide'), may hold values from 2.744695e-16 to 1.097878e-15
- gain_second: float32 [6144], P('wide'), may hold values from 4.391512e-15 to 1.7566049e-14
Outputs:
- loss: float32 [], replicated
- grad_norm: float32 [], replicated
- wide_new: float32 [768, 3200], P('wide')
- down_new: float32 [3072, 384], P('wide')
- gain_new: float32 [6144], P('wide')
- wide_first_new: float32 [768, 3200], P('wide')
- down_first_new: float32 [3072, 384], P('wide')
- gain_first_new: float32 [6144], P('wide')
- wide_second_new: float32 [768, 3200], P('wide')
- down_second_new: float32 [3072, 384], P('wide')
- gain_second_new: float32 [6144], P('wide')
- wide_copy: bfloat16 [768, 3200], P('wide')
- down_copy: bfloat16 [3072, 384], P('wide')
- gain_copy: bfloat16 [6144], P('wide')
All inputs are finite; a program needn't handle non-finite values. No bound on the sum of `present` on one device may be relied on, other than what follows from the above.
Results may differ from a plain program's by a relative error of at most 0.015.
Values may be sent and summed in bfloat16 or wider, within the bound.
No kernel may reach another device: no remote copies, remote signals or barrier semaphores. Data moves between devices by JAX's collectives and lax.ppermute only.
A program may use at most 192 MiB of HBM per device.

v0:
```python
import math

import jax
import jax.numpy as jnp
from jax import lax
from jax.sharding import PartitionSpec as P

D = 384
HEADS = 8
FF = 1536
STEMS = 4
SAMPLES = 32
ADAM_STEP = 10


NORM_EPS = 1e-05
ENERGY_EPS = 1e-05
BETA_ONE = 0.9
BETA_TWO = 0.999
ADAM_EPS = 1e-08
LEARN_RATE = 0.1
GAIN_RATE = 0.5
WEIGHT_DECAY = 0.01
CLIP_LIMIT = 0.001


def from_partner(x, axis, stride):
    return lax.ppermute(x, axis, [(i, i ^ 1 << stride) for i in range(lax.axis_size(axis))])


def layer_norm(values, gain, shift):
    centred = values - jnp.mean(values, axis=-1, keepdims=True)
    spread = jnp.mean(centred * centred, axis=-1, keepdims=True)
    return centred * lax.rsqrt(spread + NORM_EPS) * gain + shift


def norm_grad(values, gain, shift, grad):
    _, pull = jax.vjp(layer_norm, values, gain, shift)
    return pull(grad)


def gelu_exact(values):
    return jax.nn.gelu(values, approximate=False)


def dense(left, right):
    return jnp.dot(left, right, preferred_element_type=jnp.float32)


def dense_tn(left, right):
    return lax.dot_general(
        left, right, (((0,), (0,)), ((), ())), preferred_element_type=jnp.float32
    )


def dense_nt(left, right):
    return lax.dot_general(
        left, right, (((1,), (1,)), ((), ())), preferred_element_type=jnp.float32
    )


def key_blocks(shard_rows):
    row_count = shard_rows.shape[0]
    key_block = math.gcd(row_count, 512)
    firsts = key_block * jnp.arange(row_count // key_block, dtype=jnp.int32)
    return (
        shard_rows.reshape(row_count // key_block, key_block, shard_rows.shape[1]),
        firsts,
        key_block,
    )


def adam_update(weight, grad, moment, second, rate):
    moment = BETA_ONE * moment + (1 - BETA_ONE) * grad
    second = BETA_TWO * second + (1 - BETA_TWO) * grad * grad
    fixed_one = moment / (1 - BETA_ONE**ADAM_STEP)
    fixed_two = second / (1 - BETA_TWO**ADAM_STEP)
    weight = weight - rate * (fixed_one / (jnp.sqrt(fixed_two) + ADAM_EPS) + WEIGHT_DECAY * weight)
    return (weight, moment, second)


def layer_forward(inputs, own_wide, far_wide, own_down, own_gain, far_gain, partner, half_rows):
    tokens = inputs.shape[0]
    head_size = D // HEADS
    score_scale = 1.0 / math.sqrt(head_size)
    normed = layer_norm(inputs, own_gain[0], own_gain[1]).astype(jnp.bfloat16)
    crossed = layer_norm(inputs, far_gain[2], far_gain[3]).astype(jnp.bfloat16)
    queries = dense(normed, own_wide[:, :D]).astype(jnp.bfloat16)
    key_vals = dense(crossed, far_wide[:, D : 3 * D]).astype(jnp.bfloat16)
    query_heads = queries.reshape(tokens, HEADS, head_size)
    start_state = (
        jnp.full((HEADS, tokens), -1e30, jnp.float32),
        jnp.zeros((HEADS, tokens), jnp.float32),
        jnp.zeros((tokens, HEADS, head_size), jnp.float32),
    )
    carry = start_state
    blocks, firsts, key_block = key_blocks(lax.all_gather(key_vals, "wide", axis=0, tiled=True))

    def fold_visit(state_now, item):
        block_rows, first_row = item
        usable = ((first_row + jnp.arange(key_block)) // half_rows == partner).astype(jnp.float32)

        def fold_compute(state_in):
            running, totals, accum = state_in
            keys = block_rows[:, :D].reshape(key_block, HEADS, head_size)
            values = block_rows[:, D:].reshape(key_block, HEADS, head_size)
            scores = (
                jnp.einsum("qhd,khd->hqk", query_heads, keys, preferred_element_type=jnp.float32)
                * score_scale
            )
            scores = jnp.where(usable[None, None, :] > 0, scores, -1e30)
            newest = jnp.maximum(running, jnp.max(scores, axis=-1))
            factor = jnp.exp(running - newest)
            weights = jnp.exp(scores - newest[:, :, None]) * usable[None, None, :]
            totals = totals * factor + jnp.sum(weights, axis=-1)
            accum = accum * factor.T[:, :, None] + jnp.einsum(
                "hqk,khd->qhd",
                weights.astype(jnp.bfloat16),
                values,
                preferred_element_type=jnp.float32,
            )
            return (newest, totals, accum)

        return (
            lax.cond(jnp.sum(usable) > 0, fold_compute, lambda unchanged: unchanged, state_now),
            None,
        )

    carry, _ = lax.scan(fold_visit, carry, (blocks, firsts))
    running, totals, accum = carry
    log_total = running + jnp.log(totals)
    attended_full = (accum / totals.T[:, :, None]).reshape(tokens, D)
    attended = attended_full.astype(jnp.bfloat16)
    branch_out = dense(attended, own_wide[:, 3 * D : 4 * D])
    mid_rows = inputs + own_gain[6] * branch_out
    normed_two = layer_norm(mid_rows, own_gain[4], own_gain[5]).astype(jnp.bfloat16)
    pre_act = dense(normed_two, own_wide[:, 4 * D : 4 * D + FF])
    hidden = gelu_exact(pre_act).astype(jnp.bfloat16)
    ffn_out = dense(hidden, own_down)
    out_rows = (mid_rows + own_gain[7] * ffn_out).astype(jnp.bfloat16)
    kept = (
        normed,
        crossed,
        queries,
        key_vals,
        log_total,
        attended_full,
        attended,
        branch_out,
        mid_rows,
        normed_two,
        pre_act,
        hidden,
        ffn_out,
        out_rows,
    )
    return (dense(out_rows, own_wide[:, 4 * D + FF :]), kept)


def layer_backward(
    inputs, grad_est, kept, own_wide, far_wide, own_down, own_gain, far_gain, partner, half_rows
):
    (
        normed,
        crossed,
        queries,
        key_vals,
        log_total,
        attended_full,
        attended,
        branch_out,
        mid_rows,
        normed_two,
        pre_act,
        hidden,
        ffn_out,
        out_rows,
    ) = kept
    tokens = inputs.shape[0]
    head_size = D // HEADS
    score_scale = 1.0 / math.sqrt(head_size)
    grad_low = grad_est.astype(jnp.bfloat16)
    grad_head = dense_tn(out_rows, grad_low)
    grad_out = dense_nt(grad_low, own_wide[:, 4 * D + FF :])
    grad_scale_two = jnp.sum(grad_out * ffn_out, axis=0)
    grad_ffn = (grad_out * own_gain[7]).astype(jnp.bfloat16)
    grad_down = dense_tn(hidden, grad_ffn)
    grad_hidden = dense_nt(grad_ffn, own_down).astype(jnp.bfloat16)
    _, gelu_pull = jax.vjp(gelu_exact, pre_act)
    grad_pre = gelu_pull(grad_hidden.astype(jnp.float32))[0].astype(jnp.bfloat16)
    grad_up = dense_tn(normed_two, grad_pre)
    grad_normed_two = dense_nt(grad_pre, own_wide[:, 4 * D : 4 * D + FF])
    grad_mid_norm, grad_gain_three, grad_shift_three = norm_grad(
        mid_rows, own_gain[4], own_gain[5], grad_normed_two
    )
    grad_mid = grad_out + grad_mid_norm
    grad_scale_one = jnp.sum(grad_mid * branch_out, axis=0)
    grad_branch = (grad_mid * own_gain[6]).astype(jnp.bfloat16)
    grad_wo = dense_tn(attended, grad_branch)
    grad_attended = dense_nt(grad_branch, own_wide[:, 3 * D : 4 * D]).astype(jnp.bfloat16)
    grad_heads = grad_attended.reshape(tokens, HEADS, head_size)
    query_heads = queries.reshape(tokens, HEADS, head_size)
    delta = jnp.sum(
        grad_heads.astype(jnp.float32) * attended_full.reshape(tokens, HEADS, head_size), axis=-1
    ).T
    query_start = jnp.zeros((tokens, HEADS, head_size), jnp.float32)
    start_state = (query_start, jnp.zeros((lax.axis_size("wide") * tokens, 2 * D), jnp.float32))
    carry = start_state
    blocks, firsts, key_block = key_blocks(lax.all_gather(key_vals, "wide", axis=0, tiled=True))

    def make_visit(state_now, item):
        block_rows, first_row = item
        usable = ((first_row + jnp.arange(key_block)) // half_rows == partner).astype(jnp.float32)

        def make_compute(state_in):
            keys = block_rows[:, :D].reshape(key_block, HEADS, head_size)
            values = block_rows[:, D:].reshape(key_block, HEADS, head_size)
            scores = (
                jnp.einsum("qhd,khd->hqk", query_heads, keys, preferred_element_type=jnp.float32)
                * score_scale
            )
            probs = (
                jnp.exp(jnp.minimum(scores - log_total[:, :, None], 0.0)) * usable[None, None, :]
            )
            grad_probs = jnp.einsum(
                "qhd,khd->hqk", grad_heads, values, preferred_element_type=jnp.float32
            )
            grad_scores = (probs * (grad_probs - delta[:, :, None])).astype(jnp.bfloat16)
            grad_query = (
                state_in[0]
                + jnp.einsum("hqk,khd->qhd", grad_scores, keys, preferred_element_type=jnp.float32)
                * score_scale
            )
            grad_keys = (
                jnp.einsum(
                    "hqk,qhd->khd", grad_scores, query_heads, preferred_element_type=jnp.float32
                )
                * score_scale
            )
            grad_values = jnp.einsum(
                "hqk,qhd->khd",
                probs.astype(jnp.bfloat16),
                grad_heads,
                preferred_element_type=jnp.float32,
            )
            rows_new = jnp.concatenate(
                [grad_keys.reshape(key_block, D), grad_values.reshape(key_block, D)], axis=1
            )
            return (
                grad_query,
                lax.dynamic_update_slice_in_dim(state_in[1], rows_new, first_row, 0),
            )

        return (
            lax.cond(jnp.sum(usable) > 0, make_compute, lambda unchanged: unchanged, state_now),
            None,
        )

    carry, _ = lax.scan(make_visit, carry, (blocks, firsts))
    grad_query = carry[0]
    own_kv_grad = lax.psum_scatter(
        carry[1].astype(jnp.bfloat16), "wide", scatter_dimension=0, tiled=True
    )
    grad_query = grad_query.reshape(tokens, D).astype(jnp.bfloat16)
    grad_wq = dense_tn(normed, grad_query)
    grad_normed = dense_nt(grad_query, own_wide[:, :D])
    _, grad_gain_one, grad_shift_one = norm_grad(inputs, own_gain[0], own_gain[1], grad_normed)
    grad_wkv = dense_tn(crossed, own_kv_grad)
    grad_crossed = dense_nt(own_kv_grad, far_wide[:, D : 3 * D])
    _, grad_gain_two, grad_shift_two = norm_grad(inputs, far_gain[2], far_gain[3], grad_crossed)
    own_rows = jnp.concatenate(
        [grad_wq, jnp.zeros((D, 2 * D), jnp.float32), grad_wo, grad_up, grad_head], axis=1
    )
    far_rows = jnp.concatenate(
        [
            jnp.zeros((D, D), jnp.float32),
            grad_wkv,
            jnp.zeros((D, D + FF + grad_head.shape[1]), jnp.float32),
        ],
        axis=1,
    )
    zero_vec = jnp.zeros((D,), jnp.float32)
    own_gains = jnp.stack(
        [
            grad_gain_one,
            grad_shift_one,
            zero_vec,
            zero_vec,
            grad_gain_three,
            grad_shift_three,
            grad_scale_one,
            grad_scale_two,
        ]
    )
    far_gains = jnp.stack(
        [zero_vec, zero_vec, grad_gain_two, grad_shift_two, zero_vec, zero_vec, zero_vec, zero_vec]
    )
    return (own_rows, far_rows, grad_down, own_gains, far_gains)


def body(
    encoded,
    targets,
    present,
    wide_master,
    down_master,
    gain_master,
    wide_first,
    down_first,
    gain_first,
    wide_second,
    down_second,
    gain_second,
):
    half_size = lax.axis_size("wide") // 2
    wide_place = lax.axis_index("wide")
    branch = wide_place // half_size
    partner = 1 - branch
    position = wide_place % half_size
    tokens = encoded.shape[1]
    half_rows = half_size * tokens
    wide_all, down_all, gain_all = (
        lax.all_gather(wide_master.astype(jnp.bfloat16), "wide", axis=0, tiled=True),
        lax.all_gather(down_master.astype(jnp.bfloat16), "wide", axis=0, tiled=True),
        lax.all_gather(gain_master.astype(jnp.bfloat16), "wide", axis=0, tiled=True),
    )
    wide_all = wide_all.reshape(2, D, -1)
    down_all = down_all.reshape(2, FF, D)
    gain_all = gain_all.astype(jnp.float32).reshape(2, 8, D)
    own_wide = lax.dynamic_index_in_dim(wide_all, branch, 0, keepdims=False)
    far_wide = lax.dynamic_index_in_dim(wide_all, partner, 0, keepdims=False)
    own_down = lax.dynamic_index_in_dim(down_all, branch, 0, keepdims=False)
    own_gain = lax.dynamic_index_in_dim(gain_all, branch, 0, keepdims=False)
    far_gain = lax.dynamic_index_in_dim(gain_all, partner, 0, keepdims=False)
    inputs = encoded[0].astype(jnp.float32)
    est_own, kept = layer_forward(
        inputs, own_wide, far_wide, own_down, own_gain, far_gain, partner, half_rows
    )
    estimate = est_own + from_partner(
        est_own.astype(jnp.bfloat16), "wide", half_size.bit_length() - 1
    ).astype(est_own.dtype)
    seg_target = targets[0]
    mine = lax.dynamic_slice_in_dim(seg_target, position * tokens, tokens, 0)
    errors = (mine - estimate).reshape(tokens, STEMS, SAMPLES)
    counted = jnp.where((branch == 0) == (position < half_size // 2), 1.0, 0.0).astype(jnp.float32)
    err_energy = lax.psum(counted * jnp.sum(errors * errors, axis=(0, 2)), "wide")
    clean = seg_target.reshape(-1, STEMS, SAMPLES)
    tgt_energy = jnp.sum(clean * clean, axis=(0, 2))
    seg_count = present.shape[0] * lax.axis_size("seg")
    weight_stem = present[0].astype(jnp.float32)
    coeff = 10.0 / math.log(10.0)
    loss_here = -jnp.sum(
        weight_stem * coeff * (jnp.log(tgt_energy + ENERGY_EPS) - jnp.log(err_energy + ENERGY_EPS))
    ) / (seg_count * STEMS)
    per_stem = -coeff * weight_stem / (seg_count * STEMS) / (err_energy + ENERGY_EPS)
    grad_est = (2.0 * per_stem[None, :, None] * errors).reshape(tokens, STEMS * SAMPLES)
    own_rows, far_rows, grad_down, own_gains, far_gains = layer_backward(
        inputs, grad_est, kept, own_wide, far_wide, own_down, own_gain, far_gain, partner, half_rows
    )
    first_time = branch == 0
    wide_term = jnp.where(
        first_time,
        jnp.concatenate([own_rows, far_rows], 0),
        jnp.concatenate([far_rows, own_rows], 0),
    )
    down_zero = jnp.zeros_like(grad_down)
    down_term = jnp.where(
        first_time,
        jnp.concatenate([grad_down, down_zero], 0),
        jnp.concatenate([down_zero, grad_down], 0),
    )
    gain_term = jnp.where(
        first_time,
        jnp.concatenate([own_gains, far_gains], 0),
        jnp.concatenate([far_gains, own_gains], 0),
    ).reshape(-1)
    masters = (wide_master, down_master, gain_master)
    firsts = (wide_first, down_first, gain_first)
    seconds = (wide_second, down_second, gain_second)
    rates = (LEARN_RATE, LEARN_RATE, GAIN_RATE)
    wide_part, down_part, gain_part = (
        lax.psum_scatter(
            wide_term.astype(jnp.bfloat16), "wide", scatter_dimension=0, tiled=True
        ).astype(jnp.float32),
        lax.psum_scatter(
            down_term.astype(jnp.bfloat16), "wide", scatter_dimension=0, tiled=True
        ).astype(jnp.float32),
        lax.psum_scatter(
            gain_term.astype(jnp.bfloat16), "wide", scatter_dimension=0, tiled=True
        ).astype(jnp.float32),
    )
    wide_grad, down_grad, gain_grad, loss = (
        lax.psum(wide_part.astype(jnp.bfloat16), "seg").astype(jnp.float32),
        lax.psum(down_part.astype(jnp.bfloat16), "seg").astype(jnp.float32),
        lax.psum(gain_part.astype(jnp.bfloat16), "seg").astype(jnp.float32),
        lax.psum(loss_here.astype(jnp.bfloat16), "seg").astype(jnp.float32),
    )
    grads = (wide_grad, down_grad, gain_grad)
    squares = (
        jnp.sum(wide_grad * wide_grad)
        + jnp.sum(down_grad * down_grad)
        + jnp.sum(gain_grad * gain_grad)
    )
    grad_norm = jnp.sqrt(lax.psum(squares, "wide"))
    factor = jnp.minimum(1.0, CLIP_LIMIT / (grad_norm + 1e-06))
    updated = [
        adam_update(
            masters[index], grads[index] * factor, firsts[index], seconds[index], rates[index]
        )
        for index in range(3)
    ]
    return (
        loss,
        grad_norm,
        updated[0][0],
        updated[1][0],
        updated[2][0],
        updated[0][1],
        updated[1][1],
        updated[2][1],
        updated[0][2],
        updated[1][2],
        updated[2][2],
        updated[0][0].astype(jnp.bfloat16),
        updated[1][0].astype(jnp.bfloat16),
        updated[2][0].astype(jnp.bfloat16),
    )


def solution(mesh):
    placed = (
        P("seg", "wide", None),
        P("seg", None, None),
        P("seg", None),
        P("wide", None),
        P("wide", None),
        P("wide"),
        P("wide", None),
        P("wide", None),
        P("wide"),
        P("wide", None),
        P("wide", None),
        P("wide"),
    )
    return jax.shard_map(
        body,
        mesh=mesh,
        in_specs=placed,
        out_specs=(
            P(),
            P(),
            P("wide", None),
            P("wide", None),
            P("wide"),
            P("wide", None),
            P("wide", None),
            P("wide"),
            P("wide", None),
            P("wide", None),
            P("wide"),
            P("wide", None),
            P("wide", None),
            P("wide"),
        ),
        check_vma=False,
    )
```

profile of v0, /device:TPU:0, one launch (start us, length us, event | category | flops | bytes accessed | tf_op | source)
XLA Modules:
  0.0 861.6 jit_solution(9315602684295313473)
XLA Ops:
  10.2 32.4 %all-gather = bf16[8,1,768]{2,1,0:T(2,128)(2,1)S(1)} all-gather(bf16[1,1,768]{2,1,0:T(2,128)(2,1)S(1)} %reshape.233), channel_id=1, replica_groups=mesh['seg'=4,'wide'=8] {'wide'}, dimensions={0}, use_global_device_ids=true | all-gather | bytes 13824 | tf_op jit(solution)/shard_map/all_gather | solution.py:325
  44.3 51.7 %all-gather.5.cloned.1.call-done = bf16[768,3200]{1,0:T(8,128)(2,1)} async-done(((bf16[96,3200]{1,0:T(8,128)(2,1)}), bf16[768,3200]{1,0:T(8,128)(2,1)}) %all-gather.5.cloned.1.call-update) | async-done | bytes 4915216 | tf_op jit(solution)/shard_map/all_gather | solution.py:323
  105.4 93.8 %all-gather.7.cloned.1.call-done = bf16[4096,768]{1,0:T(8,128)(2,1)} async-done(((bf16[512,768]{1,0:T(8,128)(2,1)}), bf16[4096,768]{1,0:T(8,128)(2,1)}) %all-gather.7.cloned.1.call-update) | async-done | bytes 6291472 | tf_op jit(solution)/shard_map/all_gather | solution.py:97
  199.2 8.7 %copy.42 = bf16[8,512,768]{1,2,0:T(8,128)(2,1)} copy(bf16[8,512,768]{2,1,0:T(8,128)(2,1)} %bitcast.149) | data formatting | bytes 12582912 | tf_op jit(solution)/shard_map/while | solution.py:129
  208.0 63.7 %while.30 = (s32[]{:T(128)}, f32[8,512]{1,0:T(8,128)S(1)}, f32[8,512]{1,0:T(8,128)S(1)}, f32[512,8,48]{0,2,1:T(8,128)S(1)}, s32[8]{0:T(128)}, /*index=5*/s32[]{:...) while((s32[]{:T(128)}, f32[8,512]{1,0:T(8,128)S(1)}, ...), condition=%wide.region_10.11_spmd, body=%wide.region_4.10_spmd.sunk | while | flops 430341120 | bytes 31336712 | solution.py:129
  227.0 8.4 conditional.4
  239.2 8.3 conditional.4
  251.3 8.3 conditional.4
  263.4 8.3 conditional.4
  274.9 10.9 %multiply_convert_fusion.1 = (bf16[512,1536]{1,0:T(8,128)(2,1)}, f32[512,1536]{1,0:T(8,128)}, f32[512,1536]{1,0:T(8,128)}) fusion(bf16[384,3200]{1,0:T(8,128)(2,1)} %copy-done.3, f32[512,384]{0,1:T(8,128)S(1)} %get-tuple-element.475, f32[384]{0:T(512)S(1)} %get-tuple-element.413, f32[384]{0:T(512)S(1)} %get-tuple-element.407, f32[512]{0:T(512)S(1)} %fusion.115, ...), kind=kOutput, calls=%fused_computation.68 | convolution fusion | flops 656080896 | bytes 9837568 | tf_op jit(solution)/shard_map/dot_general | solution.py:47
  304.2 19.8 %psum.42 = f32[4]{0:T(128)S(1)} all-reduce(f32[4]{0:T(128)S(1)} %broadcast_multiply_fusion.2), channel_id=1, replica_groups=mesh['seg'=4,'wide'=8] {'wide'}, use_global_device_ids=true, to_apply=%region_15.16 | all-reduce | flops 4 | bytes 32 | tf_op jit(solution)/shard_map/psum | solution.py:346
  352.6 135.7 %while.31 = (s32[]{:T(128)}, f32[512,8,48]{0,2,1:T(8,128)S(1)}, bf16[4096,768]{0,1:T(8,128)(2,1)}, s32[8]{0:T(128)}, s32[]{:T(128)}, /*index=5*/bf16[8,512,768]{...) while((s32[]{:T(128)}, f32[512,8,48]{0,2,1:T(8,128)S(1)}, ...), condition=%wide.region_25.26_spmd, body=%wide.region_21.25_spmd.sunk | while | flops 1034177024 | bytes 65984864 | solution.py:259
  371.6 26.5 %conditional.5 = ((f32[512,8,48]{0,2,1:T(8,128)S(1)}, bf16[4096,768]{0,1:T(8,128)(2,1)})) conditional(s32[]{:T(128)} %convert_element_type.396, (f32[512,8,48]{0,2,1:T(8,128)S(1)}, bf16[4096,768]{0,1:T(8,128)(2,1)}) %tuple.115, (bf16[8,512,768]{1,2,0:T(8,128)(2,1)}, s32[]{:T(128)}, bf16[512,8,48]{0,2,1:T(8,128)(2,1)S(1)}, f32[8,512]{1,0:T(8,128)}, ...), branch_computations={%region_23.23_spmd, %region_24.24_spmd} | conditional | flops 1034158080 | bytes 65982556 | solution.py:255
  401.9 26.5 %conditional.5 = ((f32[512,8,48]{0,2,1:T(8,128)S(1)}, bf16[4096,768]{0,1:T(8,128)(2,1)})) conditional(s32[]{:T(128)} %convert_element_type.396, (f32[512,8,48]{0,2,1:T(8,128)S(1)}, bf16[4096,768]{0,1:T(8,128)(2,1)}) %tuple.115, (bf16[8,512,768]{1,2,0:T(8,128)(2,1)}, s32[]{:T(128)}, bf16[512,8,48]{0,2,1:T(8,128)(2,1)S(1)}, f32[8,512]{1,0:T(8,128)}, ...), branch_computations={%region_23.23_spmd, %region_24.24_spmd} | conditional | flops 1034158080 | bytes 65982556 | solution.py:255
  417.6 7.8 dynamic_update_slice.3
  432.2 26.5 %conditional.5 = ((f32[512,8,48]{0,2,1:T(8,128)S(1)}, bf16[4096,768]{0,1:T(8,128)(2,1)})) conditional(s32[]{:T(128)} %convert_element_type.396, (f32[512,8,48]{0,2,1:T(8,128)S(1)}, bf16[4096,768]{0,1:T(8,128)(2,1)}) %tuple.115, (bf16[8,512,768]{1,2,0:T(8,128)(2,1)}, s32[]{:T(128)}, bf16[512,8,48]{0,2,1:T(8,128)(2,1)S(1)}, f32[8,512]{1,0:T(8,128)}, ...), branch_computations={%region_23.23_spmd, %region_24.24_spmd} | conditional | flops 1034158080 | bytes 65982556 | solution.py:255
  447.9 7.8 dynamic_update_slice.3
  462.5 25.7 %conditional.5 = ((f32[512,8,48]{0,2,1:T(8,128)S(1)}, bf16[4096,768]{0,1:T(8,128)(2,1)})) conditional(s32[]{:T(128)} %convert_element_type.396, (f32[512,8,48]{0,2,1:T(8,128)S(1)}, bf16[4096,768]{0,1:T(8,128)(2,1)}) %tuple.115, (bf16[8,512,768]{1,2,0:T(8,128)(2,1)}, s32[]{:T(128)}, bf16[512,8,48]{0,2,1:T(8,128)(2,1)S(1)}, f32[8,512]{1,0:T(8,128)}, ...), branch_computations={%region_23.23_spmd, %region_24.24_spmd} | conditional | flops 1034158080 | bytes 65982556 | solution.py:255
  500.1 104.0 %reduce-scatter.4.cloned.1.call-done = bf16[512,768]{0,1:T(8,128)(2,1)} async-done(((bf16[4096,768]{0,1:T(8,128)(2,1)}), bf16[512,768]{0,1:T(8,128)(2,1)}) %reduce-scatter.4.cloned.1.call-update) | async-done | bytes 786448 | tf_op jit(solution)/shard_map/reduce_scatter | solution.py:261
  606.1 20.5 %fusion.34 = bf16[768,3200]{1,0:T(8,128)(2,1)} fusion(bf16[384,2048]{1,0:T(8,128)(2,1)S(1)} %broadcast_in_dim.44, bf16[384,768]{1,0:T(8,128)(2,1)S(1)} %fusion.127, bf16[384,384]{1,0:T(8,128)(2,1)S(1)} %broadcast_in_dim.43, bf16[384,3200]{1,0:T(8,128)(2,1)} %convolution_dynamic-update-slice_fusion.3, pred[]{:T(512)S(6)} %eq.33), kind=kLoop, calls=%fused_computation.54 | loop fusion | flops 41779200 | bytes 9830401 | tf_op jit(solution)/shard_map/convert_element_type | solution.py:383
  633.1 42.5 %reduce-scatter.8.cloned.1.call-done = bf16[384,384]{1,0:T(8,128)(2,1)} async-done(((bf16[3072,384]{1,0:T(8,128)(2,1)}), bf16[384,384]{1,0:T(8,128)(2,1)}) %reduce-scatter.8.cloned.1.call-update) | async-done | bytes 294928 | tf_op jit(solution)/shard_map/reduce_scatter | solution.py:385
  675.6 101.7 %reduce-scatter.6.cloned.1.call-done = bf16[96,3200]{1,0:T(8,128)(2,1)} async-done(((bf16[768,3200]{1,0:T(8,128)(2,1)}), bf16[96,3200]{1,0:T(8,128)(2,1)}) %reduce-scatter.6.cloned.1.call-update) | async-done | bytes 614416 | tf_op jit(solution)/shard_map/reduce_scatter | solution.py:382
  777.9 36.0 %all-reduce.2 = bf16[6144]{0:T(1024)(128)(2,1)S(1)} all-reduce(bf16[6144]{0:T(1024)(128)(2,1)S(1)} %convert_element_type.208), channel_id=5, replica_groups=mesh['seg'=4,'wide'=8] {'wide'}, use_global_device_ids=true, to_apply=%region_41.42.clone | all-reduce | flops 6144 | bytes 24576
  827.2 17.8 %psum.47 = f32[]{:T(128)} all-reduce(f32[]{:T(128)S(6)} %add.263), channel_id=1, replica_groups=mesh['seg'=4,'wide'=8] {'wide'}, use_global_device_ids=true, to_apply=%region_44.45 | all-reduce | flops 1 | bytes 8 | tf_op jit(solution)/shard_map/psum | solution.py:404
  (342 shorter events, 265.2 us)
Async XLA Ops:
  7.2 88.8 %all-gather.5.cloned.1.call-start = ((), (), s32[]{:S(2)}) async-start(), calls=%async_computation.3 | async-start | bytes 5529600 | tf_op jit(solution)/shard_map/all_gather | solution.py:323
  9.4 189.8 %all-gather.7.cloned.1.call-start = ((), (), s32[]{:S(2)}) async-start(), calls=%async_computation.4 | async-start | bytes 7077888 | tf_op jit(solution)/shard_map/all_gather | solution.py:97
  43.9 54.8 %copy-start.39 = (f32[384]{0:T(512)}, f32[384]{0:T(512)S(1)}, u32[]{:S(2)}) copy-start(f32[384]{0:T(512)S(1)} %get-tuple-element.410) | copy-start | bytes 4612
  43.9 54.8 %copy-start.41 = (f32[384]{0:T(512)}, f32[384]{0:T(512)S(1)}, u32[]{:S(2)}) copy-start(f32[384]{0:T(512)S(1)} %get-tuple-element.412) | copy-start | bytes 4612
  44.0 60.9 %copy-start.43 = (f32[384]{0:T(512)}, f32[384]{0:T(512)S(1)}, u32[]{:S(2)}) copy-start(f32[384]{0:T(512)S(1)} %get-tuple-element.408) | copy-start | bytes 4612
  44.0 60.9 %copy-start.45 = (f32[384]{0:T(512)}, f32[384]{0:T(512)S(1)}, u32[]{:S(2)}) copy-start(f32[384]{0:T(512)S(1)} %get-tuple-element.409) | copy-start | bytes 4612
  44.0 230.9 %copy-start.28 = (f32[384]{0:T(512)}, f32[384]{0:T(512)S(1)}, u32[]{:S(2)}) copy-start(f32[384]{0:T(512)S(1)} %get-tuple-element.413) | copy-start | bytes 4612
  44.0 284.9 %copy-start.23 = (f32[384]{0:T(512)}, f32[384]{0:T(512)S(1)}, u32[]{:S(2)}) copy-start(f32[384]{0:T(512)S(1)} %get-tuple-element.406) | copy-start | bytes 4612
  44.1 60.7 %copy-start.25 = (f32[512]{0:T(512)}, f32[512]{0:T(512)S(1)}, u32[]{:S(2)}) copy-start(f32[512]{0:T(512)S(1)} %broadcast_multiply_fusion.1) | copy-start | bytes 6148
  44.3 60.6 %copy-start.30 = (f32[512]{0:T(512)}, f32[512]{0:T(512)S(1)}, u32[]{:S(2)}) copy-start(f32[512]{0:T(512)S(1)} %add_rsqrt_fusion) | copy-start | bytes 6148
  101.8 184.0 %all-gather.9.cloned.1.call-start = ((), (), s32[]{:S(2)}) async-start(), calls=%async_computation.5 | async-start | bytes 2654208 | tf_op jit(solution)/shard_map/all_gather | solution.py:324
  103.7 500.5 %reduce-scatter.4.cloned.1.call-start = ((), (), s32[]{:S(2)}) async-start(), calls=%async_computation.6 | async-start | bytes 7077888 | tf_op jit(solution)/shard_map/reduce_scatter | solution.py:261
  289.5 34.6 %copy-start.48 = (s32[1,4]{1,0:T(1,128)S(1)}, s32[1,4]{1,0:T(1,128)}, u32[]{:S(2)}) copy-start(s32[1,4]{1,0:T(1,128)} %param.22) | copy-start | bytes 52
  293.8 7.8 collective-permute-start
  488.3 187.3 %reduce-scatter.8.cloned.1.call-start = ((), (), s32[]{:S(2)}) async-start(), calls=%async_computation.8 | async-start | bytes 2654208 | tf_op jit(solution)/shard_map/reduce_scatter | solution.py:385
  493.9 283.5 %reduce-scatter.6.cloned.1.call-start = ((), (), s32[]{:S(2)}) async-start(), calls=%async_computation.7 | async-start | bytes 5529600 | tf_op jit(solution)/shard_map/reduce_scatter | solution.py:382
  496.1 108.0 %copy-start.40 = (f32[384]{0:T(512)S(1)}, f32[384]{0:T(512)}, u32[]{:S(2)}) copy-start(f32[384]{0:T(512)} %copy-done.39) | copy-start | bytes 4612
  496.2 108.0 %copy-start.42 = (f32[384]{0:T(512)S(1)}, f32[384]{0:T(512)}, u32[]{:S(2)}) copy-start(f32[384]{0:T(512)} %copy-done.41) | copy-start | bytes 4612
  626.6 194.2 %all-reduce.7.cloned.1.call-start = ((), (), s32[]{:S(2)}) async-start(), calls=%async_computation.9 | async-start | bytes 1818624 | tf_op jit(solution)/shard_map/psum | solution.py:393
  632.8 212.9 %copy-start.27 = (f32[768]{0:T(1024)S(1)}, f32[768]{0:T(1024)}, u32[]{:S(2)}) copy-start(f32[768]{0:T(1024)} %param.25) | copy-start | bytes 9220
  632.8 212.9 %copy-start.36 = (f32[768]{0:T(1024)S(1)}, f32[768]{0:T(1024)}, u32[]{:S(2)}) copy-start(f32[768]{0:T(1024)} %param.28) | copy-start | bytes 9220
  632.8 212.9 %copy-start.37 = (f32[768]{0:T(1024)S(1)}, f32[768]{0:T(1024)}, u32[]{:S(2)}) copy-start(f32[768]{0:T(1024)} %param.31) | copy-start | bytes 9220
  777.4 72.1 %copy-start.4 = (f32[96,3200]{1,0:T(8,128)S(1)}, f32[96,3200]{1,0:T(8,128)}, u32[]{:S(2)}) copy-start(f32[96,3200]{1,0:T(8,128)} %param.23) | copy-start | bytes 3686404
  777.7 71.8 %copy-start.20 = (f32[96,3200]{1,0:T(8,128)S(1)}, f32[96,3200]{1,0:T(8,128)}, u32[]{:S(2)}) copy-start(f32[96,3200]{1,0:T(8,128)} %param.26) | copy-start | bytes 3686404
  (37 other events, 201.6 us)
Sparse Core Ops, SparseCore 0:
  10.8 85.1 all-gather.4
  101.9 97.1 all-gather.6
  201.9 50.2 all-gather.8
  488.4 115.6 reduce-scatter.3
  607.5 68.0 reduce-scatter.7
  679.2 98.1 reduce-scatter.5
  779.9 35.0 all-reduce.6
where the time goes:
time: 867 us; the launch traced here: 862 us
  waiting for transfers between devices  400 us (46%)
  matrix products  120 us (14%)
  blocking collectives  112 us (13%)
  local copies, waits for them, and re-layouts  97 us (11%)
  other arithmetic  88.9 us (10%)
  between operations  22 us (3%)
  loops' own time  19 us (2%)
    reduce_scatter x1, waiting for transfers between devices, layer_backward(): lax.psum_scatter(carry[1].astype(jnp.bfloat16), 'wide', scatter_dimension...  104 us
    reduce_scatter x1, waiting for transfers between devices, body(): lax.psum_scatter(wide_term.astype(jnp.bfloat16), 'wide', scatter_dimensio...  102 us
    all_gather x1, waiting for transfers between devices, layer_forward(): lax.all_gather(key_vals, 'wide', axis=0, tiled=True)  93.8 us
    all_gather x1, waiting for transfers between devices, body(): lax.all_gather(wide_master.astype(jnp.bfloat16), 'wide', axis=0, tiled=True)  51.7 us
    reduce_scatter x1, waiting for transfers between devices, body(): lax.psum_scatter(down_term.astype(jnp.bfloat16), 'wide', scatter_dimensio...  42.5 us
    unnamed x1, blocking collectives  36 us
    all_gather x1, blocking collectives, body(): lax.all_gather(gain_master.astype(jnp.bfloat16), 'wide', axis=0, tiled=True)  32.4 us
    dynamic_update_slice x4, local copies, waits for them, and re-layouts, make_compute(): lax.dynamic_update_slice_in_dim(state_in[1], rows_new, first_row, 0)  30.5 us
  transfers between devices with their start and end apart: 8, of which 6 were waited for; matrix products, arithmetic and copies ran while one was open for 14% of the time, Pallas kernels for 0%

commit v1 on v0

v1 whole, which is shorter than its diff:
```python
import math

import jax
import jax.numpy as jnp
from jax import lax
from jax.experimental import pallas as pl
from jax.experimental.pallas import tpu as pltpu
from jax.sharding import PartitionSpec as P

D = 384
HEADS = 8
HEAD = D // HEADS
FF = 1536
STEMS = 4
SAMPLES = 32
OUT = STEMS * SAMPLES
QKV = 3 * D
REST = D + FF + OUT
ADAM_STEP = 10
LANES = 128

NORM_EPS = 1e-05
ENERGY_EPS = 1e-05
BETA_ONE = 0.9
BETA_TWO = 0.999
ADAM_EPS = 1e-08
LEARN_RATE = 0.1
GAIN_RATE = 0.5
WEIGHT_DECAY = 0.01
CLIP_LIMIT = 0.001

BF = jnp.bfloat16
F32 = jnp.float32
SCALE = 1.0 / math.sqrt(HEAD)
LOG_TWO = math.log(2.0)
VMEM_LIMIT = 60 * 2**20


def swap(x, axis, mask):
    return lax.ppermute(x, axis, [(i, i ^ mask) for i in range(lax.axis_size(axis))])


def dot(left, right, left_dim=1, right_dim=0):
    return lax.dot_general(
        left,
        right,
        (((left_dim,), (right_dim,)), ((), ())),
        preferred_element_type=F32,
    )


def unit_rows(values):
    centred = values - jnp.mean(values, axis=-1, keepdims=True)
    spread = jnp.mean(centred * centred, axis=-1, keepdims=True)
    inverse = lax.rsqrt(spread + NORM_EPS)
    return centred * inverse, inverse


def call(kernel, out_shape, flops, moved, **more):
    return pl.pallas_call(
        kernel,
        out_shape=out_shape,
        compiler_params=pltpu.CompilerParams(vmem_limit_bytes=VMEM_LIMIT),
        cost_estimate=pl.CostEstimate(flops=flops, bytes_accessed=moved, transcendentals=0),
        **more,
    )


def sds(shape, dtype):
    return jax.ShapeDtypeStruct(shape, dtype)


def attend_kernel(own, blocks, weights, gains, probs, keys_t, values_t, unit, tops,
                  queries_t, own_unit, weights_t, attended_t, final_top, inverse_total,
                  accum, top):
    step = pl.program_id(0)
    last = pl.num_programs(0) - 1

    @pl.when(step == 0)
    def _():
        weights_t[...] = weights[:, :QKV].T
        hat, _ = unit_rows(own[...].astype(F32))
        own_unit[...] = hat.astype(BF)
        normed = (hat * gains[0:1] + gains[1:2]).astype(BF)
        found = dot(weights_t[:D], normed, 1, 1)
        queries_t[...] = (found * (SCALE / LOG_TWO)).astype(BF)
        accum[...] = jnp.zeros_like(accum)
        top[...] = jnp.full_like(top, -1e30)

    hat, _ = unit_rows(blocks[0].astype(F32))
    unit[0] = hat.astype(BF)
    crossed = (hat * gains[2:3] + gains[3:4]).astype(BF)
    keys_t[0] = dot(weights_t[D : 2 * D], crossed, 1, 1).astype(BF)
    values_t[0] = dot(weights_t[2 * D :], crossed, 1, 1).astype(BF)
    rows = crossed.shape[0]
    ones = jnp.ones((16, rows), BF)
    for h in range(HEADS):
        at = slice(HEAD * h, HEAD * (h + 1))
        wide = slice(64 * h, 64 * (h + 1))
        scores = dot(keys_t[0, at], queries_t[at], 0, 0)
        before = top[h : h + 1]
        newest = jnp.maximum(before, jnp.max(scores, axis=0, keepdims=True))
        top[h : h + 1] = newest
        weight = jnp.exp2(scores - newest).astype(BF)
        probs[0, h] = weight
        values = jnp.concatenate([values_t[0, at], ones], axis=0)
        accum[wide] = accum[wide] * jnp.exp2(before - newest) + dot(values, weight)
    tops[0] = top[...]

    @pl.when(step == last)
    def _():
        final_top[...] = top[...]
        for h in range(HEADS):
            total = accum[64 * h + HEAD : 64 * h + HEAD + 1]
            inverse = 1.0 / total
            inverse_total[h : h + 1] = inverse
            attended_t[HEAD * h : HEAD * (h + 1)] = accum[64 * h : 64 * h + HEAD] * inverse


def attend(own, blocks, weights, gains):
    count, rows, _ = blocks.shape
    whole = lambda *shape: pl.BlockSpec(shape, lambda j: (0,) * len(shape))
    each = lambda *shape: pl.BlockSpec((1,) + shape, lambda j: (j,) + (0,) * len(shape))
    return call(
        attend_kernel,
        (
            sds((count, HEADS, rows, rows), BF),
            sds((count, D, rows), BF),
            sds((count, D, rows), BF),
            sds((count, rows, D), BF),
            sds((count, HEADS, rows), F32),
            sds((D, rows), BF),
            sds((rows, D), BF),
            sds((QKV, D), BF),
            sds((D, rows), F32),
            sds((HEADS, rows), F32),
            sds((HEADS, rows), F32),
        ),
        count * (4 * rows * rows * D * 5 + 4 * rows * D * D),
        count * (HEADS * rows * rows * 2),
        grid=(count,),
        in_specs=[whole(rows, D), each(rows, D), whole(*weights.shape), whole(8, D)],
        out_specs=(
            each(HEADS, rows, rows),
            each(D, rows),
            each(D, rows),
            each(rows, D),
            each(HEADS, rows),
            whole(D, rows),
            whole(rows, D),
            whole(QKV, D),
            whole(D, rows),
            whole(HEADS, rows),
            whole(HEADS, rows),
        ),
        scratch_shapes=[pltpu.VMEM((64 * HEADS, rows), F32), pltpu.VMEM((HEADS, rows), F32)],
    )(own, blocks, weights, gains)


def dense_kernel(inputs, attended_t, rest, down, gains, estimate, branch_out, third,
                 third_inverse, normed_two, slope, hidden, ffn_out, out_rows):
    branch = dot(attended_t[...].astype(BF), rest[:, :D], 0, 0)
    branch_out[...] = branch
    mid = inputs[...].astype(F32) + gains[6:7] * branch
    hat, inverse = unit_rows(mid)
    third[...] = hat
    third_inverse[...] = inverse
    normed = (hat * gains[4:5] + gains[5:6]).astype(BF)
    normed_two[...] = normed
    pre = dot(normed, rest[:, D : D + FF])
    gate = 0.5 * (1.0 + lax.erf(pre * math.sqrt(0.5)))
    hid = (pre * gate).astype(BF)
    hidden[...] = hid
    bell = jnp.exp(-0.5 * pre * pre) * (1.0 / math.sqrt(2.0 * math.pi))
    slope[...] = gate + pre * bell
    ffn = dot(hid, down[...])
    ffn_out[...] = ffn
    out = (mid + gains[7:8] * ffn).astype(BF)
    out_rows[...] = out
    estimate[...] = dot(out, rest[:, D + FF :]).astype(BF)


def dense_forward(inputs, attended_t, rest, down, gains):
    rows = inputs.shape[0]
    return call(
        dense_kernel,
        (
            sds((rows, OUT), BF),
            sds((rows, D), F32),
            sds((rows, D), F32),
            sds((rows, 1), F32),
            sds((rows, D), BF),
            sds((rows, FF), F32),
            sds((rows, FF), BF),
            sds((rows, D), F32),
            sds((rows, D), BF),
        ),
        2 * rows * D * (D + 2 * FF + OUT),
        rows * FF * 8,
    )(inputs, attended_t, rest, down, gains)


def dense_back_kernel(grad_est, rest, down, gains, branch_out, third, third_inverse,
                      slope, ffn_out, grad_ffn, grad_pre, grad_branch, grad_attended_t,
                      grad_gains):
    low = grad_est[...]
    grad_out = dot(low, rest[:, D + FF :], 1, 1)
    grad_gains[3:4] = jnp.sum(grad_out * ffn_out[...], axis=0, keepdims=True)
    ffn = (grad_out * gains[7:8]).astype(BF)
    grad_ffn[...] = ffn
    hidden = dot(ffn, down[...], 1, 1).astype(BF)
    pre = (hidden.astype(F32) * slope[...]).astype(BF)
    grad_pre[...] = pre
    normed = dot(pre, rest[:, D : D + FF], 1, 1)
    hat = third[...]
    grad_gains[0:1] = jnp.sum(normed * hat, axis=0, keepdims=True)
    grad_gains[1:2] = jnp.sum(normed, axis=0, keepdims=True)
    scaled = normed * gains[4:5]
    grad_mid = grad_out + third_inverse[...] * (
        scaled
        - jnp.mean(scaled, axis=-1, keepdims=True)
        - hat * jnp.mean(scaled * hat, axis=-1, keepdims=True)
    )
    grad_gains[2:3] = jnp.sum(grad_mid * branch_out[...], axis=0, keepdims=True)
    branch = (grad_mid * gains[6:7]).astype(BF)
    grad_branch[...] = branch
    grad_attended_t[...] = dot(rest[:, :D], branch, 1, 1).astype(BF)


def dense_back(grad_est, rest, down, gains, branch_out, third, third_inverse, slope, ffn_out):
    rows = grad_est.shape[0]
    return call(
        dense_back_kernel,
        (
            sds((rows, D), BF),
            sds((rows, FF), BF),
            sds((rows, D), BF),
            sds((D, rows), BF),
            sds((4, D), F32),
        ),
        2 * rows * D * (D + 2 * FF + OUT),
        rows * FF * 8,
    )(grad_est, rest, down, gains, branch_out, third, third_inverse, slope, ffn_out)


def dense_weights_kernel(grad_est, grad_ffn, grad_pre, grad_branch, attended_t, normed_two,
                         hidden, out_rows, grad_rest, grad_down):
    grad_rest[:, D + FF :] = dot(out_rows[...], grad_est[...], 0, 0).astype(BF)
    grad_rest[:, D : D + FF] = dot(normed_two[...], grad_pre[...], 0, 0).astype(BF)
    grad_rest[:, :D] = dot(attended_t[...].astype(BF), grad_branch[...]).astype(BF)
    grad_down[...] = dot(hidden[...], grad_ffn[...], 0, 0).astype(BF)


def dense_weights(grad_est, grad_ffn, grad_pre, grad_branch, attended_t, normed_two, hidden,
                  out_rows):
    rows = grad_est.shape[0]
    return call(
        dense_weights_kernel,
        (sds((D, REST), BF), sds((FF, D), BF)),
        2 * rows * D * (D + 2 * FF + OUT),
        rows * FF * 8,
    )(grad_est, grad_ffn, grad_pre, grad_branch, attended_t, normed_two, hidden, out_rows)


def attend_back_kernel(probs, keys_t, values_t, unit, tops, queries_t, own_unit, weights_t,
                       attended_t, final_top, inverse_total, grad_attended_t, gains,
                       grad_weights, grad_gains, delta, grad_queries, grad_kv, moments):
    step = pl.program_id(0)
    last = pl.num_programs(0) - 1
    rows = unit.shape[1]

    @pl.when(step == 0)
    def _():
        for h in range(HEADS):
            at = slice(HEAD * h, HEAD * (h + 1))
            product = grad_attended_t[at].astype(F32) * attended_t[at]
            delta[h : h + 1] = jnp.sum(product, axis=0, keepdims=True)
        grad_queries[...] = jnp.zeros_like(grad_queries)
        moments[...] = jnp.zeros_like(moments)

    factor = jnp.exp2(tops[0] - final_top[...]) * inverse_total[...]
    shift = delta[...] * factor
    for h in range(HEADS):
        at = slice(HEAD * h, HEAD * (h + 1))
        low = slice(D + HEAD * h, D + HEAD * (h + 1))
        grad = (grad_attended_t[at].astype(F32) * factor[h : h + 1]).astype(BF)
        weight = probs[0, h]
        grad_probs = dot(values_t[0, at], grad, 0, 0)
        scores = (weight.astype(F32) * (grad_probs - shift[h : h + 1])).astype(BF)
        grad_queries[at] += dot(keys_t[0, at], scores)
        grad_kv[at] = (dot(queries_t[at], scores, 1, 1) * LOG_TWO).astype(BF)
        grad_kv[low] = dot(grad, weight, 1, 1).astype(BF)
    ones = jnp.ones((rows, LANES), BF)
    moments[D:] += dot(grad_kv[...], jnp.concatenate([unit[0], ones], axis=1))

    @pl.when(step == last)
    def _():
        query = (grad_queries[...] * SCALE).astype(BF)
        moments[:D] = dot(query, jnp.concatenate([own_unit[...], ones], axis=1))
        for first, size, row in ((0, D, 0), (D, 2 * D, 2)):
            at = slice(first, first + size)
            moment = moments[at, :D]
            column = moments[at, D : D + 1]
            weight = weights_t[at].astype(F32)
            grad_gains[row : row + 1] = jnp.sum(weight * moment, axis=0, keepdims=True)
            grad_gains[row + 1 : row + 2] = jnp.sum(weight * column, axis=0, keepdims=True)
            full = moment * gains[row : row + 1] + column * gains[row + 1 : row + 2]
            grad_weights[:, at] = full.T.astype(BF)


def attend_back(saved, grad_attended_t, gains):
    (probs, keys_t, values_t, unit, tops, queries_t, own_unit, weights_t, attended_t,
     final_top, inverse_total) = saved
    count, rows, _ = unit.shape
    whole = lambda *shape: pl.BlockSpec(shape, lambda j: (0,) * len(shape))
    each = lambda *shape: pl.BlockSpec((1,) + shape, lambda j: (j,) + (0,) * len(shape))
    return call(
        attend_back_kernel,
        (sds((D, QKV), BF), sds((4, D), F32)),
        count * (8 * rows * rows * D * 5),
        count * (HEADS * rows * rows * 2),
        grid=(count,),
        in_specs=[
            each(HEADS, rows, rows),
            each(D, rows),
            each(D, rows),
            each(rows, D),
            each(HEADS, rows),
            whole(D, rows),
            whole(rows, D),
            whole(QKV, D),
            whole(D, rows),
            whole(HEADS, rows),
            whole(HEADS, rows),
            whole(D, rows),
            whole(8, D),
        ],
        out_specs=(whole(D, QKV), whole(4, D)),
        scratch_shapes=[
            pltpu.VMEM((HEADS, rows), F32),
            pltpu.VMEM((D, rows), F32),
            pltpu.VMEM((2 * D, rows), BF),
            pltpu.VMEM((QKV, D + LANES), F32),
        ],
    )(probs, keys_t, values_t, unit, tops, queries_t, own_unit, weights_t, attended_t,
      final_top, inverse_total, grad_attended_t, gains)


def bits(size):
    return [1 << k for k in range(size.bit_length() - 1)]


def gather_group(x, position, size):
    stack = x[None]
    for mask in bits(size):
        other = swap(stack, "wide", mask)
        upper = (position & mask) > 0
        stack = jnp.where(
            upper, jnp.concatenate([other, stack], 0), jnp.concatenate([stack, other], 0)
        )
    return stack


def gather_rows(x, position, size, core):
    half = x.shape[0] // 2
    mine = gather_group(lax.dynamic_slice_in_dim(x, core * half, half, 0), position, size)
    other = swap(mine, "seg", 1)
    both = jnp.where(
        core == 0, jnp.stack([mine, other], axis=1), jnp.stack([other, mine], axis=1)
    )
    return both.reshape(size * x.shape[0], x.shape[1])


def reduce_rows(grads, position, size, core):
    rows = grads.shape[0] // size
    pieces = grads.reshape(size, 2, rows // 2, grads.shape[1])
    keep = lax.dynamic_index_in_dim(pieces, core, 1, keepdims=False)
    send = lax.dynamic_index_in_dim(pieces, 1 - core, 1, keepdims=False)
    total = keep.astype(F32) + swap(send, "seg", 1).astype(F32)
    for mask in reversed(bits(size)):
        total = total.astype(BF).reshape((2, mask) + total.shape[1:])
        bit = (position & mask) // mask
        keep = lax.dynamic_index_in_dim(total, bit, 0, keepdims=False)
        send = lax.dynamic_index_in_dim(total, 1 - bit, 0, keepdims=False)
        total = keep.astype(F32) + swap(send, "wide", mask).astype(F32)
    total = total[0]
    for mask in bits(lax.axis_size("seg"))[1:]:
        low = total.astype(BF)
        total = low.astype(F32) + swap(low, "seg", mask).astype(F32)
    mine = total.astype(BF)
    other = swap(mine, "seg", 1)
    both = jnp.where(core == 0, jnp.concatenate([mine, other]), jnp.concatenate([other, mine]))
    return both.astype(F32)


def gain_shape(size):
    count = 8 * D // size
    width = math.gcd(count, LANES)
    return count // width, width


def pack_gains(gains, rows, size):
    tall, across = gain_shape(size)
    block = gains.reshape(-1, tall, across)
    return jnp.pad(block, ((0, 0), (0, rows - tall), (0, LANES - across)))


def unpack_gains(block, size):
    tall, across = gain_shape(size)
    return block[:, :tall, :across].reshape(-1)


def pack_down(down):
    rows = down.shape[-2] // 4
    split = down.reshape(-1, 4, rows, D)
    return jnp.moveaxis(split, 1, 2).reshape(-1, rows, 4 * D)


def unpack_down(block):
    rows = block.shape[-2]
    split = block.reshape(-1, rows, 4, D)
    return jnp.moveaxis(split, 2, 1).reshape(-1, D)


def adam_update(weight, grad, moment, second, rate):
    moment = BETA_ONE * moment + (1 - BETA_ONE) * grad
    second = BETA_TWO * second + (1 - BETA_TWO) * grad * grad
    fixed_one = moment / (1 - BETA_ONE**ADAM_STEP)
    fixed_two = second / (1 - BETA_TWO**ADAM_STEP)
    weight = weight - rate * (fixed_one / (jnp.sqrt(fixed_two) + ADAM_EPS) + WEIGHT_DECAY * weight)
    return (weight, moment, second)


def body(
    encoded,
    targets,
    present,
    wide_master,
    down_master,
    gain_master,
    wide_first,
    down_first,
    gain_first,
    wide_second,
    down_second,
    gain_second,
):
    size = lax.axis_size("wide") // 2
    position = lax.axis_index("wide") % size
    core = lax.axis_index("seg") % 2
    own = encoded[0]
    tokens = own.shape[0]
    rows = wide_master.shape[0]

    far = swap(own, "wide", size)[None]
    for mask in bits(size):
        far = jnp.concatenate([far, swap(far, "wide", mask)], 0)

    first_pack = jnp.concatenate(
        [
            wide_master[:, :QKV].astype(BF),
            pack_gains(gain_master.astype(BF), rows, size)[0],
        ],
        axis=1,
    )
    rest_pack = jnp.concatenate(
        [wide_master[:, QKV:].astype(BF), pack_down(down_master.astype(BF))[0]], axis=1
    )
    first_all = gather_rows(first_pack, position, size, core)
    gains = unpack_gains(first_all[:, QKV:].reshape(size, rows, LANES), size)
    gains = gains.astype(F32).reshape(8, D)
    rest_all = gather_rows(rest_pack, position, size, core)
    rest = rest_all[:, :REST]
    down = unpack_down(rest_all[:, REST:].reshape(size, rows, 4 * D))

    saved = attend(own, far, first_all, gains)
    attended_t = saved[8]
    (est_own, branch_out, third, third_inverse, normed_two, slope, hidden, ffn_out,
     out_rows) = dense_forward(own, attended_t, rest, down, gains)

    estimate = est_own.astype(F32) + swap(est_own, "wide", size).astype(F32)
    mine = lax.dynamic_slice_in_dim(targets[0], position * tokens, tokens, 0)
    errors = mine - estimate
    energy = jnp.stack([jnp.sum(errors * errors, axis=0), jnp.sum(mine * mine, axis=0)])
    energy = jnp.sum(energy.reshape(2, STEMS, SAMPLES), axis=-1)
    for mask in bits(size):
        energy = energy + swap(energy, "wide", mask)
    err_energy, tgt_energy = energy[0], energy[1]
    seg_count = lax.axis_size("seg")
    weight_stem = present[0].astype(F32)
    coeff = 10.0 / math.log(10.0)
    loss = -jnp.sum(
        weight_stem * coeff * (jnp.log(tgt_energy + ENERGY_EPS) - jnp.log(err_energy + ENERGY_EPS))
    ) / (seg_count * STEMS)
    for mask in bits(seg_count):
        loss = loss + swap(loss, "seg", mask)
    per_stem = -coeff * weight_stem / (seg_count * STEMS) / (err_energy + ENERGY_EPS)
    grad_est = (errors * jnp.repeat(2.0 * per_stem, SAMPLES)[None, :]).astype(BF)

    grad_ffn, grad_pre, grad_branch, grad_attended_t, late_gains = dense_back(
        grad_est, rest, down, gains, branch_out, third, third_inverse, slope, ffn_out
    )
    grad_rest, grad_down = dense_weights(
        grad_est, grad_ffn, grad_pre, grad_branch, attended_t, normed_two, hidden, out_rows
    )
    grad_early = jnp.concatenate(
        [grad_rest, pack_down(grad_down.reshape(size, 4 * rows, D)).reshape(-1, 4 * D)], axis=1
    )
    early = reduce_rows(grad_early, position, size, core)

    grad_first, early_gains = attend_back(saved, grad_attended_t, gains)
    grad_gains = jnp.concatenate([early_gains, late_gains], 0).astype(BF).reshape(-1)
    grad_late = jnp.concatenate(
        [grad_first, pack_gains(grad_gains, rows, size).reshape(-1, LANES)], axis=1
    )
    late = reduce_rows(grad_late, position, size, core)

    squares = jnp.sum(early * early) + jnp.sum(late * late)
    for mask in bits(2 * size):
        squares = squares + swap(squares, "wide", mask)
    grad_norm = jnp.sqrt(squares)
    factor = jnp.minimum(1.0, CLIP_LIMIT / (grad_norm + 1e-06))
    grads = (
        jnp.concatenate([late[:, :QKV], early[:, :REST]], axis=1),
        unpack_down(early[None, :, REST:]),
        unpack_gains(late[None, :, QKV:], size),
    )
    masters = (wide_master, down_master, gain_master)
    firsts = (wide_first, down_first, gain_first)
    seconds = (wide_second, down_second, gain_second)
    rates = (LEARN_RATE, LEARN_RATE, GAIN_RATE)
    updated = [
        adam_update(
            masters[index], grads[index] * factor, firsts[index], seconds[index], rates[index]
        )
        for index in range(3)
    ]
    return (
        loss,
        grad_norm,
        *(updated[index][kind] for kind in range(3) for index in range(3)),
        *(updated[index][0].astype(BF) for index in range(3)),
    )


def solution(mesh):
    split, line = P("wide", None), P("wide")
    states = (split, split, line)
    return jax.shard_map(
        body,
        mesh=mesh,
        in_specs=(P("seg", "wide", None), P("seg", None, None), P("seg", None)) + states * 3,
        out_specs=(P(), P()) + states * 4,
        check_vma=False,
    )
```

time: 867 us -> 238 us (0.27)
  waiting for transfers between devices: 400 us -> 76.1 us
  matrix products: 120 us -> 0 us
  blocking collectives: 112 us -> 0 us
  local copies, waits for them, and re-layouts: 97 us -> 11.9 us
  Pallas kernels: 0 us -> 71.8 us
  other arithmetic: 88.9 us -> 28 us
  starting transfers between devices: 2.68 us -> 41.1 us
  loops' own time: 19 us -> 0 us
  between operations: 22 us -> 8.62 us
    reduce_scatter x3 -> x0, waiting for transfers between devices: 248 us -> none  [the longest x1 104 us: layer_backward(): lax.psum_scatter(carry[1].astype(jnp.bfloat16), 'wide', scatter_dimension...]
    all_gather x3 -> x0, waiting for transfers between devices: 145 us -> none  [the longest x1 93.8 us: layer_forward(): lax.all_gather(key_vals, 'wide', axis=0, tiled=True)]
    dot_general x46 -> x0, matrix products: 120 us -> none  [the longest x6 20.9 us: dense(): return jnp.dot(left, right, preferred_element_type=jnp.float32)]
    pallas_call x0 -> x5, Pallas kernels: none -> 71.8 us  [the longest x1 27.5 us: attend_back(): call(attend_back_kernel, (sds((D, QKV), BF), sds((4, D), F32)), count * (...]
    ppermute x1 -> x27, waiting for transfers between devices: 5.93 us -> 76.1 us  [swap(): lax.ppermute(x, axis, [(i, i ^ mask) for i in range(lax.axis_size(axis))])]
    psum x3 -> x0, blocking collectives: 43.7 us -> none  [the longest x1 19.8 us: body(): lax.psum(counted * jnp.sum(errors * errors, axis=(0, 2)), 'wide')]
    reduce_sum x35 -> x4, other arithmetic: 42.5 us -> 2.76 us  [the longest x2 1.68 us: body(): squares = jnp.sum(early * early) + jnp.sum(late * late)]
    ppermute x1 -> x27, starting transfers between devices: 1.4 us -> 41.1 us  [swap(): lax.ppermute(x, axis, [(i, i ^ mask) for i in range(lax.axis_size(axis))])]
  transfers between devices with their start and end apart: 8 -> 27, of which waited for: 6 -> 19; matrix products, arithmetic and copies ran while one was open for 14% -> 5% of each run, Pallas kernels for 0% -> 10%
where the time goes in v1:
time: 238 us
  waiting for transfers between devices  76.1 us (32%)
  Pallas kernels  71.8 us (30%)
  starting transfers between devices  41.1 us (17%)
  other arithmetic  28 us (12%)
  local copies, waits for them, and re-layouts  11.9 us (5%)
  between operations  8.62 us (4%)
    ppermute x27, waiting for transfers between devices, swap(): lax.ppermute(x, axis, [(i, i ^ mask) for i in range(lax.axis_size(axis))])  76.1 us
    ppermute x27, starting transfers between devices, swap(): lax.ppermute(x, axis, [(i, i ^ mask) for i in range(lax.axis_size(axis))])  41.1 us
    pallas_call x1, Pallas kernels, attend_back(): call(attend_back_kernel, (sds((D, QKV), BF), sds((4, D), F32)), count * (...  27.5 us
    pallas_call x1, Pallas kernels, attend(): call(attend_kernel, (sds((count, HEADS, rows, rows), BF), sds((count, D,...  24.7 us
    pallas_call x1, Pallas kernels, dense_forward(): call(dense_kernel, (sds((rows, OUT), BF), sds((rows, D), F32), sds((rows,...  7.31 us
    pallas_call x1, Pallas kernels, dense_back(): call(dense_back_kernel, (sds((rows, D), BF), sds((rows, FF), BF), sds((ro...  6.77 us
    convert_element_type x3, other arithmetic, body(): updated[index][0].astype(BF)  6.31 us
    pallas_call x1, Pallas kernels, dense_weights(): call(dense_weights_kernel, (sds((D, REST), BF), sds((FF, D), BF)), 2 * ro...  5.53 us
  transfers between devices with their start and end apart: 27, of which 19 were waited for; matrix products, arithmetic and copies ran while one was open for 5% of the time, Pallas kernels for 10%

profile of v1, /device:TPU:0, one launch (start us, length us, event | category | flops | bytes accessed | tf_op | source)
XLA Modules:
  0.0 237.5 jit_solution(1136094105633525789)
XLA Ops:
  2.2 3.0 %collective-permute-start.3 = (bf16[1,48,1280]{2,1,0:T(8,128)(2,1)S(1)}, bf16[1,48,1280]{2,1,0:T(8,128)(2,1)S(1)}, u32[]{:S(2)}, u32[]{:S(2)}) collective-permute-start(bf16[1,48,1280]{2,1,0:T(8,128)(2,1)S(1)} %fusion.25), channel_id=1, source_target_pairs={{0,1},{1,0},{2,3},{3,2},{4,5},{5,4},{6,7},{7,6},{8,9},{9,8},{10,11... | collective-permute-start | bytes 368648 | tf_op jit(solution)/shard_map/ppermute | solution.py:40
  5.6 3.1 %collective-permute-start = (bf16[512,384]{1,0:T(8,128)(2,1)}, bf16[512,384]{1,0:T(8,128)(2,1)S(1)}, u32[]{:S(2)}, u32[]{:S(2)}) collective-permute-start(bf16[512,384]{1,0:T(8,128)(2,1)} %bitcast.1.own.inputs), channel_id=1, source_target_pairs={{0,4},{1,5},{2,6},{3,7},{4,0},{5,1},{6,2},{7,3},{8,12},{9,13},{10,... | collective-permute-start | bytes 1179656 | tf_op jit(solution)/shard_map/ppermute | solution.py:40
  11.5 4.5 %collective-permute-done.6 = bf16[1,48,3584]{2,1,0:T(8,128)(2,1)S(1)} collective-permute-done((bf16[1,48,3584]{2,1,0:T(8,128)(2,1)S(1)}, bf16[1,48,3584]{2,1,0:T(8,128)(2,1)S(1)}, u32[]{:S(2)}, u32[]{:S(2)}) %collective-permute-start.6) | collective-permute-done | bytes 344096 | tf_op jit(solution)/shard_map/ppermute | solution.py:40
  17.9 5.9 %collective-permute-done.4 = bf16[2,48,1280]{2,1,0:T(8,128)(2,1)S(1)} collective-permute-done((bf16[2,48,1280]{2,1,0:T(8,128)(2,1)S(1)}, bf16[2,48,1280]{2,1,0:T(8,128)(2,1)S(1)}, u32[]{:S(2)}, u32[]{:S(2)}) %collective-permute-start.4) | collective-permute-done | bytes 245792 | tf_op jit(solution)/shard_map/ppermute | solution.py:40
  28.9 7.0 %collective-permute-done.1 = bf16[1,512,384]{2,1,0:T(8,128)(2,1)S(1)} collective-permute-done((bf16[1,512,384]{2,1,0:T(8,128)(2,1)S(1)}, bf16[1,512,384]{2,1,0:T(8,128)(2,1)S(1)}, u32[]{:S(2)}, u32[]{:S(2)}) %collective-permute-start.1) | collective-permute-done | bytes 393248 | tf_op jit(solution)/shard_map/ppermute | solution.py:40
  42.3 14.2 %collective-permute-done.2 = bf16[2,512,384]{2,1,0:T(8,128)(2,1)} collective-permute-done((bf16[2,512,384]{2,1,0:T(8,128)(2,1)}, bf16[2,512,384]{2,1,0:T(8,128)(2,1)}, u32[]{:S(2)}, u32[]{:S(2)}) %collective-permute-start.2) | collective-permute-done | bytes 786464 | tf_op jit(solution)/shard_map/ppermute | solution.py:40
  59.0 24.7 %shard_map.227 = (bf16[4,8,512,512]{3,2,1,0:T(8,128)(2,1)}, bf16[4,384,512]{2,1,0:T(8,128)(2,1)}, bf16[4,384,512]{2,1,0:T(8,128)(2,1)}, bf16[4,512,384]{2,1,0:T(...) custom-call(bf16[512,384]{1,0:T(8,128)(2,1)} %bitcast.1.own.inputs, ...), custom_call_target="tpu_custom_call" | custom-call | flops 9261023232 | bytes 16777216 | tf_op jit(solution)/shard_map/pallas_call | solution.py:124
  88.9 7.3 %shard_map.228 = (bf16[512,128]{1,0:T(8,128)(2,1)}, f32[512,384]{1,0:T(8,128)}, f32[512,384]{1,0:T(8,128)}, f32[512,1]{1,0:T(8,128)}, bf16[512,384]{1,0:T(8,128)...) custom-call(bf16[512,384]{1,0:T(8,128)(2,1)} %bitcast.1.own.inputs, ...), custom_call_target="tpu_custom_call" | custom-call | flops 1409286144 | bytes 6291456 | tf_op jit(solution)/shard_map/pallas_call | solution.py:185
  96.2 2.8 %collective-permute-start.9 = (bf16[512,128]{1,0:T(8,128)(2,1)}, bf16[512,128]{1,0:T(8,128)(2,1)S(1)}, u32[]{:S(2)}, u32[]{:S(2)}) collective-permute-start(bf16[512,128]{1,0:T(8,128)(2,1)} %get-tuple-element.44), channel_id=1, source_target_pairs={{0,4},{1,5},{2,6},{3,7},{4,0},{5,1},{6,2},{7,3},{8,12},{9,13},{10,... | collective-permute-start | bytes 393224 | tf_op jit(solution)/shard_map/ppermute | solution.py:40
  99.0 5.4 %collective-permute-done.9 = bf16[512,128]{1,0:T(8,128)(2,1)S(1)} collective-permute-done((bf16[512,128]{1,0:T(8,128)(2,1)}, bf16[512,128]{1,0:T(8,128)(2,1)S(1)}, u32[]{:S(2)}, u32[]{:S(2)}) %collective-permute-start.9) | collective-permute-done | bytes 131104 | tf_op jit(solution)/shard_map/ppermute | solution.py:40
  109.8 3.0 %collective-permute-done.11 = f32[2,4]{1,0:T(2,128)S(1)} collective-permute-done((f32[2,4]{1,0:T(2,128)S(1)}, f32[2,4]{1,0:T(2,128)S(1)}, u32[]{:S(2)}, u32[]{:S(2)}) %collective-permute-start.11) | collective-permute-done | bytes 64 | tf_op jit(solution)/shard_map/ppermute | solution.py:40
  115.2 6.8 %shard_map.229 = (bf16[512,384]{1,0:T(8,128)(2,1)}, bf16[512,1536]{1,0:T(8,128)(2,1)}, bf16[512,384]{1,0:T(8,128)(2,1)}, bf16[384,512]{1,0:T(8,128)(2,1)}, f32[4,384]{1,0:T(4,128)}) custom-call(bf16[512,128]{1,0:T(8,128)(2,1)} %multiply_convert_fusion.grad_est, bf16[384,2048]{1,0:T(8,128)(2,1)} %slice.58.rest, bf16[1536,384]{1,0:T(8,128)(2,1)} %bitcast.120, ...), custom_call_target="tpu_custom_call" | custom-call | flops 1409286144 | bytes 6291456 | tf_op jit(solution)/shard_map/pallas_call | solution.py:232
  122.0 27.5 %shard_map.231 = (bf16[384,1152]{1,0:T(8,128)(2,1)}, f32[4,384]{1,0:T(4,128)}) custom-call(bf16[4,8,512,512]{3,2,1,0:T(8,128)(2,1)} %get-tuple-element.58.probs, bf16[4,384,512]{2,1,0:T(8,128)(2,1)} %get-tuple-element.59.keys_t, bf16[4,384,512]{2,1,0:T(8,128)(2,1)} %get-tuple-element.60.values_t, bf16[4,512,384]{2,1,0:T(8,128)(2,1)} %get-tuple-element.61.unit, ...), custom_call_target="tpu_custom_call" | custom-call | flops 16106127360 | bytes 16777216 | tf_op jit(solution)/shard_map/pallas_call | solution.py:317
  150.2 5.5 %shard_map.230 = (bf16[384,2048]{1,0:T(8,128)(2,1)}, bf16[1536,384]{1,0:T(8,128)(2,1)}) custom-call(bf16[512,128]{1,0:T(8,128)(2,1)} %multiply_convert_fusion.grad_est, bf16[512,384]{1,0:T(8,128)(2,1)} %get-tuple-element.50.grad_ffn, bf16[512,1536]{1,0:T(8,128)(2,1)} %get-tuple-element.51.grad_pre, bf16[512,384]{1,0:T(8,128)(2,1)} %get-tuple-element.52.grad_branch, ...), custom_call_target="tpu_custom_call" | custom-call | flops 1409286144 | bytes 6291456 | tf_op jit(solution)/shard_map/pallas_call | solution.py:257
  155.7 2.9 %copy.43 = bf16[4,4,96,384]{3,1,2,0:T(4,128)(2,1)} copy(bf16[4,4,96,384]{3,2,1,0:T(8,128)(2,1)} %bitcast.134) | data formatting | bytes 2359296 | tf_op jit(solution)/shard_map/reshape;reshape | solution.py:415
  158.6 2.8 %concatenate.174 = bf16[4,2,48,1536]{3,2,1,0:T(8,128)(2,1)S(1)} reshape(bf16[4,96,4,384]{3,2,1,0:T(4,128)(2,1)} %bitcast.121) | data formatting | bytes 2359296 | tf_op jit(solution)/shard_map/concatenate | solution.py:506
  167.3 3.0 %collective-permute-start.13 = (f32[]{:T(128)}, f32[]{:T(128)}, u32[]{:S(2)}, u32[]{:S(2)}) collective-permute-start(f32[]{:T(128)} %add.170), channel_id=1, source_target_pairs={{0,16},{8,24},{16,0},{24,8},{1,17},{9,25},{17,1},{25,9},{2,18},{10... | collective-permute-start | bytes 20 | tf_op jit(solution)/shard_map/ppermute | solution.py:40
  176.8 5.1 %collective-permute-done.20 = bf16[2,48,1280]{2,1,0:T(8,128)(2,1)S(1)} collective-permute-done((bf16[2,48,1280]{2,1,0:T(8,128)(2,1)S(1)}, bf16[2,48,1280]{2,1,0:T(8,128)(2,1)S(1)}, u32[]{:S(2)}, u32[]{:S(2)}) %collective-permute-start.20) | collective-permute-done | bytes 245792 | tf_op jit(solution)/shard_map/ppermute | solution.py:40
  183.6 10.9 %collective-permute-done.15 = bf16[2,48,3584]{2,1,0:T(8,128)(2,1)S(1)} collective-permute-done((bf16[2,48,3584]{2,1,0:T(8,128)(2,1)S(1)}, bf16[2,48,3584]{2,1,0:T(8,128)(2,1)S(1)}, u32[]{:S(2)}, u32[]{:S(2)}) %collective-permute-start.15) | collective-permute-done | bytes 688160 | tf_op jit(solution)/shard_map/ppermute | solution.py:40
  197.9 4.8 %collective-permute-done.16 = bf16[1,48,3584]{2,1,0:T(8,128)(2,1)S(1)} collective-permute-done((bf16[1,48,3584]{2,1,0:T(8,128)(2,1)S(1)}, bf16[1,48,3584]{2,1,0:T(8,128)(2,1)S(1)}, u32[]{:S(2)}, u32[]{:S(2)}) %collective-permute-start.16) | collective-permute-done | bytes 344096 | tf_op jit(solution)/shard_map/ppermute | solution.py:40
  204.6 5.5 %collective-permute-done.17 = bf16[48,3584]{1,0:T(8,128)(2,1)S(1)} collective-permute-done((bf16[48,3584]{1,0:T(8,128)(2,1)S(1)}, bf16[48,3584]{1,0:T(8,128)(2,1)S(1)}, u32[]{:S(2)}, u32[]{:S(2)}) %collective-permute-start.17) | collective-permute-done | bytes 344096 | tf_op jit(solution)/shard_map/ppermute | solution.py:40
  214.2 2.9 %collective-permute-start.24 = (f32[]{:T(128)}, f32[]{:T(128)}, u32[]{:S(2)}, u32[]{:S(2)}) collective-permute-start(f32[]{:T(128)} %add.186), channel_id=1, source_target_pairs={{0,1},{1,0},{2,3},{3,2},{4,5},{5,4},{6,7},{7,6},{8,9},{9,8},{10,11... | collective-permute-start | bytes 20 | tf_op jit(solution)/shard_map/ppermute | solution.py:40
  222.8 3.8 %collective-permute-start.26 = (f32[]{:T(128)}, f32[]{:T(128)}, u32[]{:S(2)}, u32[]{:S(2)}) collective-permute-start(f32[]{:T(128)} %add.188), channel_id=1, source_target_pairs={{0,4},{1,5},{2,6},{3,7},{4,0},{5,1},{6,2},{7,3},{8,12},{9,13},{10,... | collective-permute-start | bytes 20 | tf_op jit(solution)/shard_map/ppermute | solution.py:40
  229.6 3.0 %fusion.30 = (bf16[384,384]{1,0:T(8,128)(2,1)}, f32[384,384]{1,0:T(8,128)}, f32[384,384]{1,0:T(8,128)}, f32[384,384]{1,0:T(8,128)}) fusion(f32[384,384]{1,0:T(8,128)S(1)} %copy-done.4, f32[1,96,4,384]{3,1,2,0:T(8,128)S(1)} %copy.40, f32[384,384]{1,0:T(8,128)} %param.19, f32[384,384]{1,0:T(8,128)} %param.22), kind=kLoop, calls=%fused_computation.96 | loop fusion | flops 2359296 | bytes 4423680 | tf_op jit(solution)/shard_map/convert_element_type | solution.py:542
  (150 shorter events, 63.6 us)
Async XLA Ops:
  2.2 7.1 %collective-permute-start.3 = (bf16[1,48,1280]{2,1,0:T(8,128)(2,1)S(1)}, bf16[1,48,1280]{2,1,0:T(8,128)(2,1)S(1)}, u32[]{:S(2)}, u32[]{:S(2)}) collective-permute-start(bf16[1,48,1280]{2,1,0:T(8,128)(2,1)S(1)} %fusion.25), channel_id=1, source_target_pairs={{0,1},{1,0},{2,3},{3,2},{4,5},{5,4},{6,7},{7,6},{8,9},{9,8},{10,11... | collective-permute-start | bytes 368648 | tf_op jit(solution)/shard_map/ppermute | solution.py:40
  5.6 10.4 %collective-permute-start.6 = (bf16[1,48,3584]{2,1,0:T(8,128)(2,1)S(1)}, bf16[1,48,3584]{2,1,0:T(8,128)(2,1)S(1)}, u32[]{:S(2)}, u32[]{:S(2)}) collective-permute-start(bf16[1,48,3584]{2,1,0:T(8,128)(2,1)S(1)} %fusion.20), channel_id=1, source_target_pairs={{0,1},{1,0},{2,3},{3,2},{4,5},{5,4},{6,7},{7,6},{8,9},{9,8},{10,11... | collective-permute-start | bytes 1032200 | tf_op jit(solution)/shard_map/ppermute | solution.py:40
  5.6 20.4 %collective-permute-start = (bf16[512,384]{1,0:T(8,128)(2,1)}, bf16[512,384]{1,0:T(8,128)(2,1)S(1)}, u32[]{:S(2)}, u32[]{:S(2)}) collective-permute-start(bf16[512,384]{1,0:T(8,128)(2,1)} %bitcast.1.own.inputs), channel_id=1, source_target_pairs={{0,4},{1,5},{2,6},{3,7},{4,0},{5,1},{6,2},{7,3},{8,12},{9,13},{10,... | collective-permute-start | bytes 1179656 | tf_op jit(solution)/shard_map/ppermute | solution.py:40
  9.4 14.5 %collective-permute-start.4 = (bf16[2,48,1280]{2,1,0:T(8,128)(2,1)S(1)}, bf16[2,48,1280]{2,1,0:T(8,128)(2,1)S(1)}, u32[]{:S(2)}, u32[]{:S(2)}) collective-permute-start(bf16[2,48,1280]{2,1,0:T(8,128)(2,1)S(1)} %maximum_select_fusion.6), channel_id=1, source_target_pairs={{0,2},{1,3},{2,0},{3,1},{4,6},{5,7},{6,4},{7,5},{8,10},{9,11},{10,... | collective-permute-start | bytes 737288 | tf_op jit(solution)/shard_map/ppermute | solution.py:40
  16.0 24.7 %collective-permute-start.7 = (bf16[2,48,3584]{2,1,0:T(8,128)(2,1)S(1)}, bf16[2,48,3584]{2,1,0:T(8,128)(2,1)S(1)}, u32[]{:S(2)}, u32[]{:S(2)}) collective-permute-start(bf16[2,48,3584]{2,1,0:T(8,128)(2,1)S(1)} %maximum_select_fusion.3), channel_id=1, source_target_pairs={{0,2},{1,3},{2,0},{3,1},{4,6},{5,7},{6,4},{7,5},{8,10},{9,11},{10,... | collective-permute-start | bytes 2064392 | tf_op jit(solution)/shard_map/ppermute | solution.py:40
  23.9 15.2 %collective-permute-start.5 = (bf16[4,48,1280]{2,1,0:T(8,128)(2,1)S(1)}, bf16[4,48,1280]{2,1,0:T(8,128)(2,1)S(1)}, u32[]{:S(2)}, u32[]{:S(2)}) collective-permute-start(bf16[4,48,1280]{2,1,0:T(8,128)(2,1)S(1)} %maximum_select_fusion.5), channel_id=1, source_target_pairs={{0,8},{8,0},{16,24},{24,16},{1,9},{9,1},{17,25},{25,17},{2,10},{10... | collective-permute-start | bytes 1474568 | tf_op jit(solution)/shard_map/ppermute | solution.py:40
  26.0 9.9 %collective-permute-start.1 = (bf16[1,512,384]{2,1,0:T(8,128)(2,1)S(1)}, bf16[1,512,384]{2,1,0:T(8,128)(2,1)S(1)}, u32[]{:S(2)}, u32[]{:S(2)}) collective-permute-start(bf16[1,512,384]{2,1,0:T(8,128)(2,1)S(1)} %bitcast.127), channel_id=1, source_target_pairs={{0,1},{1,0},{2,3},{3,2},{4,5},{5,4},{6,7},{7,6},{8,9},{9,8},{10,11... | collective-permute-start | bytes 1179656 | tf_op jit(solution)/shard_map/ppermute | solution.py:40
  36.9 19.6 %collective-permute-start.2 = (bf16[2,512,384]{2,1,0:T(8,128)(2,1)}, bf16[2,512,384]{2,1,0:T(8,128)(2,1)}, u32[]{:S(2)}, u32[]{:S(2)}) collective-permute-start(bf16[2,512,384]{2,1,0:T(8,128)(2,1)} %pad_maximum_fusion.1), channel_id=1, source_target_pairs={{0,2},{1,3},{2,0},{3,1},{4,6},{5,7},{6,4},{7,5},{8,10},{9,11},{10,... | collective-permute-start | bytes 2359304 | tf_op jit(solution)/shard_map/ppermute | solution.py:40
  42.0 41.7 %collective-permute-start.8 = (bf16[4,48,3584]{2,1,0:T(8,128)(2,1)}, bf16[4,48,3584]{2,1,0:T(8,128)(2,1)}, u32[]{:S(2)}, u32[]{:S(2)}) collective-permute-start(bf16[4,48,3584]{2,1,0:T(8,128)(2,1)} %maximum_select_fusion.1), channel_id=1, source_target_pairs={{0,8},{8,0},{16,24},{24,16},{1,9},{9,1},{17,25},{25,17},{2,10},{10... | collective-permute-start | bytes 4128776 | tf_op jit(solution)/shard_map/ppermute | solution.py:40
  96.2 8.2 %collective-permute-start.9 = (bf16[512,128]{1,0:T(8,128)(2,1)}, bf16[512,128]{1,0:T(8,128)(2,1)S(1)}, u32[]{:S(2)}, u32[]{:S(2)}) collective-permute-start(bf16[512,128]{1,0:T(8,128)(2,1)} %get-tuple-element.44), channel_id=1, source_target_pairs={{0,4},{1,5},{2,6},{3,7},{4,0},{5,1},{6,2},{7,3},{8,12},{9,13},{10,... | collective-permute-start | bytes 393224 | tf_op jit(solution)/shard_map/ppermute | solution.py:40
  105.7 3.6 %collective-permute-start.10 = (f32[2,4]{1,0:T(2,128)S(1)}, f32[2,4]{1,0:T(2,128)S(1)}, u32[]{:S(2)}, u32[]{:S(2)}) collective-permute-start(f32[2,4]{1,0:T(2,128)S(1)} %maximum_reduce_fusion), channel_id=1, source_target_pairs={{0,1},{1,0},{2,3},{3,2},{4,5},{5,4},{6,7},{7,6},{8,9},{9,8},{10,11... | collective-permute-start | bytes 104 | tf_op jit(solution)/shard_map/ppermute | solution.py:40
  162.7 10.9 %collective-permute-start.14 = (bf16[4,48,3584]{2,1,0:T(8,128)(2,1)}, bf16[4,48,3584]{2,1,0:T(8,128)(2,1)}, u32[]{:S(2)}, u32[]{:S(2)}) collective-permute-start(bf16[4,48,3584]{2,1,0:T(8,128)(2,1)} %fusion.2), channel_id=1, source_target_pairs={{0,8},{8,0},{16,24},{24,16},{1,9},{9,1},{17,25},{25,17},{2,10},{10... | collective-permute-start | bytes 4128776 | tf_op jit(solution)/shard_map/ppermute | solution.py:40
  163.8 7.9 %collective-permute-start.19 = (bf16[4,48,1280]{2,1,0:T(8,128)(2,1)}, bf16[4,48,1280]{2,1,0:T(8,128)(2,1)}, u32[]{:S(2)}, u32[]{:S(2)}) collective-permute-start(bf16[4,48,1280]{2,1,0:T(8,128)(2,1)} %fusion.13), channel_id=1, source_target_pairs={{0,8},{8,0},{16,24},{24,16},{1,9},{9,1},{17,25},{25,17},{2,10},{10... | collective-permute-start | bytes 1474568 | tf_op jit(solution)/shard_map/ppermute | solution.py:40
  167.3 3.7 %collective-permute-start.13 = (f32[]{:T(128)}, f32[]{:T(128)}, u32[]{:S(2)}, u32[]{:S(2)}) collective-permute-start(f32[]{:T(128)} %add.170), channel_id=1, source_target_pairs={{0,16},{8,24},{16,0},{24,8},{1,17},{9,25},{17,1},{25,9},{2,18},{10... | collective-permute-start | bytes 20 | tf_op jit(solution)/shard_map/ppermute | solution.py:40
  172.9 9.0 %collective-permute-start.20 = (bf16[2,48,1280]{2,1,0:T(8,128)(2,1)S(1)}, bf16[2,48,1280]{2,1,0:T(8,128)(2,1)S(1)}, u32[]{:S(2)}, u32[]{:S(2)}) collective-permute-start(bf16[2,48,1280]{2,1,0:T(8,128)(2,1)S(1)} %dynamic-slice_bitcast_fusion.1), channel_id=1, source_target_pairs={{0,2},{1,3},{2,0},{3,1},{4,6},{5,7},{6,4},{7,5},{8,10},{9,11},{10,... | collective-permute-start | bytes 737288 | tf_op jit(solution)/shard_map/ppermute | solution.py:40
  175.3 19.1 %collective-permute-start.15 = (bf16[2,48,3584]{2,1,0:T(8,128)(2,1)S(1)}, bf16[2,48,3584]{2,1,0:T(8,128)(2,1)S(1)}, u32[]{:S(2)}, u32[]{:S(2)}) collective-permute-start(bf16[2,48,3584]{2,1,0:T(8,128)(2,1)S(1)} %dynamic-slice_bitcast_fusion), channel_id=1, source_target_pairs={{0,2},{1,3},{2,0},{3,1},{4,6},{5,7},{6,4},{7,5},{8,10},{9,11},{10,... | collective-permute-start | bytes 2064392 | tf_op jit(solution)/shard_map/ppermute | solution.py:40
  182.0 14.3 %collective-permute-start.21 = (bf16[1,48,1280]{2,1,0:T(8,128)(2,1)S(1)}, bf16[1,48,1280]{2,1,0:T(8,128)(2,1)S(1)}, u32[]{:S(2)}, u32[]{:S(2)}) collective-permute-start(bf16[1,48,1280]{2,1,0:T(8,128)(2,1)S(1)} %constant_dynamic-slice_fusion), channel_id=1, source_target_pairs={{0,1},{1,0},{2,3},{3,2},{4,5},{5,4},{6,7},{7,6},{8,9},{9,8},{10,11... | collective-permute-start | bytes 368648 | tf_op jit(solution)/shard_map/ppermute | solution.py:40
  194.7 8.0 %collective-permute-start.16 = (bf16[1,48,3584]{2,1,0:T(8,128)(2,1)S(1)}, bf16[1,48,3584]{2,1,0:T(8,128)(2,1)S(1)}, u32[]{:S(2)}, u32[]{:S(2)}) collective-permute-start(bf16[1,48,3584]{2,1,0:T(8,128)(2,1)S(1)} %constant_dynamic-slice_fusion.1), channel_id=1, source_target_pairs={{0,1},{1,0},{2,3},{3,2},{4,5},{5,4},{6,7},{7,6},{8,9},{9,8},{10,11... | collective-permute-start | bytes 1032200 | tf_op jit(solution)/shard_map/ppermute | solution.py:40
  196.3 8.1 %collective-permute-start.22 = (bf16[48,1280]{1,0:T(8,128)(2,1)S(1)}, bf16[48,1280]{1,0:T(8,128)(2,1)S(1)}, u32[]{:S(2)}, u32[]{:S(2)}) collective-permute-start(bf16[48,1280]{1,0:T(8,128)(2,1)S(1)} %fusion.23), channel_id=1, source_target_pairs={{0,16},{8,24},{16,0},{24,8},{1,17},{9,25},{17,1},{25,9},{2,18},{10... | collective-permute-start | bytes 368648 | tf_op jit(solution)/shard_map/ppermute | solution.py:40
  202.8 7.3 %collective-permute-start.17 = (bf16[48,3584]{1,0:T(8,128)(2,1)S(1)}, bf16[48,3584]{1,0:T(8,128)(2,1)S(1)}, u32[]{:S(2)}, u32[]{:S(2)}) collective-permute-start(bf16[48,3584]{1,0:T(8,128)(2,1)S(1)} %fusion.18), channel_id=1, source_target_pairs={{0,16},{8,24},{16,0},{24,8},{1,17},{9,25},{17,1},{25,9},{2,18},{10... | collective-permute-start | bytes 1032200 | tf_op jit(solution)/shard_map/ppermute | solution.py:40
  204.5 5.8 %collective-permute-start.23 = (bf16[48,1280]{1,0:T(8,128)(2,1)S(1)}, bf16[48,1280]{1,0:T(8,128)(2,1)S(1)}, u32[]{:S(2)}, u32[]{:S(2)}) collective-permute-start(bf16[48,1280]{1,0:T(8,128)(2,1)S(1)} %add_convert_fusion.2), channel_id=1, source_target_pairs={{0,8},{8,0},{16,24},{24,16},{1,9},{9,1},{17,25},{25,17},{2,10},{10... | collective-permute-start | bytes 368648 | tf_op jit(solution)/shard_map/ppermute | solution.py:40
  214.2 3.7 %collective-permute-start.24 = (f32[]{:T(128)}, f32[]{:T(128)}, u32[]{:S(2)}, u32[]{:S(2)}) collective-permute-start(f32[]{:T(128)} %add.186), channel_id=1, source_target_pairs={{0,1},{1,0},{2,3},{3,2},{4,5},{5,4},{6,7},{7,6},{8,9},{9,8},{10,11... | collective-permute-start | bytes 20 | tf_op jit(solution)/shard_map/ppermute | solution.py:40
  218.5 3.7 %collective-permute-start.25 = (f32[]{:T(128)}, f32[]{:T(128)}, u32[]{:S(2)}, u32[]{:S(2)}) collective-permute-start(f32[]{:T(128)} %add.187), channel_id=1, source_target_pairs={{0,2},{1,3},{2,0},{3,1},{4,6},{5,7},{6,4},{7,5},{8,10},{9,11},{10,... | collective-permute-start | bytes 20 | tf_op jit(solution)/shard_map/ppermute | solution.py:40
  222.8 4.6 %collective-permute-start.26 = (f32[]{:T(128)}, f32[]{:T(128)}, u32[]{:S(2)}, u32[]{:S(2)}) collective-permute-start(f32[]{:T(128)} %add.188), channel_id=1, source_target_pairs={{0,4},{1,5},{2,6},{3,7},{4,0},{5,1},{6,2},{7,3},{8,12},{9,13},{10,... | collective-permute-start | bytes 20 | tf_op jit(solution)/shard_map/ppermute | solution.py:40
  (25 other events, 174.7 us)

commit v2 on v1

v2 whole, which is shorter than its diff:
```python
import functools
import math

import jax
import jax.numpy as jnp
from jax import lax
from jax.experimental import pallas as pl
from jax.experimental.pallas import tpu as pltpu
from jax.sharding import PartitionSpec as P

D = 384
HEADS = 8
HEAD = D // HEADS
FF = 1536
STEMS = 4
SAMPLES = 32
OUT = STEMS * SAMPLES
QKV = 3 * D
REST = D + FF + OUT
ADAM_STEP = 10
LANES = 128

NORM_EPS = 1e-05
ENERGY_EPS = 1e-05
BETA_ONE = 0.9
BETA_TWO = 0.999
ADAM_EPS = 1e-08
LEARN_RATE = 0.1
GAIN_RATE = 0.5
WEIGHT_DECAY = 0.01
CLIP_LIMIT = 0.001

BF = jnp.bfloat16
F32 = jnp.float32
SCALE = 1.0 / math.sqrt(HEAD)
LOG_TWO = math.log(2.0)
VMEM_LIMIT = 14 * 2**20


def swap(x, axis, mask):
    return lax.ppermute(x, axis, [(i, i ^ mask) for i in range(lax.axis_size(axis))])


def dot(left, right, left_dim=1, right_dim=0):
    return lax.dot_general(
        left,
        right,
        (((left_dim,), (right_dim,)), ((), ())),
        preferred_element_type=F32,
    )


def unit_rows(values):
    centred = values - jnp.mean(values, axis=-1, keepdims=True)
    spread = jnp.mean(centred * centred, axis=-1, keepdims=True)
    inverse = lax.rsqrt(spread + NORM_EPS)
    return centred * inverse, inverse


def call(kernel, operands, out_shape, flops, moved, place=(), scratch=()):
    here = pl.BlockSpec(memory_space=pltpu.VMEM)
    small = pl.BlockSpec(memory_space=pltpu.SMEM)
    return pl.pallas_call(
        kernel,
        out_shape=out_shape,
        in_specs=[small] * len(place) + [here] * len(operands),
        out_specs=jax.tree.map(lambda _: here, out_shape),
        scratch_shapes=scratch,
        compiler_params=pltpu.CompilerParams(vmem_limit_bytes=VMEM_LIMIT),
        cost_estimate=pl.CostEstimate(flops=flops, bytes_accessed=moved, transcendentals=0),
    )(*place, *operands)


def sds(shape, dtype):
    return jax.ShapeDtypeStruct(shape, dtype)


def gain_shape(size):
    count = 8 * D // size
    width = math.gcd(count, LANES)
    return count // width, width


def gain_places(size):
    tall, across = gain_shape(size)
    for owner in range(size):
        for row in range(tall):
            flat = (owner * tall + row) * across
            yield owner, row, flat // D, flat % D, across


def pack_kernel(size, place, wide, down, gains, first, rest):
    half = first.shape[0]
    same = place[0] == 0
    picked = jnp.where(same, wide[:half], wide[half:]).astype(BF)
    first[:, :QKV] = picked[:, :QKV]
    rest[:, :REST] = picked[:, QKV:]
    for part in range(4):
        row, other = half * part, half * (4 + part)
        piece = jnp.where(same, down[row : row + half], down[other : other + half])
        rest[:, REST + D * part : REST + D * (part + 1)] = piece.astype(BF)
    first[:, QKV:] = jnp.zeros((half, LANES), BF)
    tall, across = gain_shape(size)
    first[:tall, QKV : QKV + across] = jnp.where(same, gains[...], 0.0).astype(BF)


def pack(place, wide, down, gains, size):
    half = wide.shape[0] // 2
    return call(
        functools.partial(pack_kernel, size),
        (wide, down, gains.reshape(gain_shape(size))),
        (sds((half, QKV + LANES), BF), sds((half, REST + 4 * D), BF)),
        1000,
        4 * (wide.size + down.size),
        place=(place,),
    )


def start_kernel(size, place, own, mine, other, queries_t, own_unit, weights_t, gains, joined):
    core, position = place[0], place[1]
    half = mine.shape[1]
    for owner in range(size):
        slot = owner ^ position
        near, far = mine[slot], other[slot]
        row = 2 * owner * half
        joined[row : row + half] = jnp.where(core == 0, near, far)
        joined[row + half : row + 2 * half] = jnp.where(core == 0, far, near)
    for owner, row, vector, lane, across in gain_places(size):
        at = 2 * owner * half + row
        gains[vector : vector + 1, lane : lane + across] = joined[
            at : at + 1, QKV : QKV + across
        ].astype(F32)
    weights_t[...] = joined[:, :QKV].T
    hat, _ = unit_rows(own[...].astype(F32))
    own_unit[...] = hat.astype(BF)
    normed = (hat * gains[0:1] + gains[1:2]).astype(BF)
    found = dot(weights_t[:D], normed, 1, 1)
    queries_t[...] = (found * (SCALE / LOG_TWO)).astype(BF)


def start(place, own, mine, other, size):
    rows = own.shape[0]
    return call(
        functools.partial(start_kernel, size),
        (own, mine, other),
        (sds((D, rows), BF), sds((rows, D), BF), sds((QKV, D), BF), sds((8, D), F32)),
        2 * rows * D * D,
        rows * D * 8,
        place=(place,),
        scratch=[pltpu.VMEM((D, QKV + LANES), BF)],
    )


def heads_in_step(first, second, third):
    ahead, behind = first(0), None
    for h in range(HEADS):
        found = ahead
        if h + 1 < HEADS:
            ahead = first(h + 1)
        found = second(h, found)
        if behind is not None:
            third(h - 1, behind)
        behind = found
    third(HEADS - 1, behind)


def head_rows(h, offset=0, height=HEAD):
    return slice(offset + height * h, offset + height * (h + 1))


def over_blocks(count, visit):
    if count == 1:
        visit(0)
    else:
        lax.fori_loop(0, count, lambda block, carry: (visit(block), carry)[1], 0)


def attend_kernel(count, carried, *refs):
    queries_t, weights_t, gains = refs[:3]
    blocks = refs[3 : 3 + count]
    refs = refs[3 + count :]
    if carried:
        accum_in, top_in = refs[:2]
        refs = refs[2:]
    probs, keys_t, values_t, unit, tops, accum, top, joined = refs
    if carried:
        accum[...] = accum_in[...]
        top[...] = top_in[...]
    else:
        accum[...] = jnp.zeros_like(accum)
        top[...] = jnp.full_like(top, -1e30)
    for block in range(count):
        joined[block] = blocks[block][...]

    def visit(block):
        hat, _ = unit_rows(joined[block].astype(F32))
        unit[block] = hat.astype(BF)
        crossed = (hat * gains[2:3] + gains[3:4]).astype(BF)
        keys_t[block] = dot(weights_t[D : 2 * D], crossed, 1, 1).astype(BF)
        values_t[block] = dot(weights_t[2 * D :], crossed, 1, 1).astype(BF)
        ones = jnp.ones((16, crossed.shape[0]), BF)

        def score(h):
            return dot(keys_t[block, head_rows(h)], queries_t[head_rows(h)], 0, 0)

        def soften(h, scores):
            before = top[h : h + 1]
            newest = jnp.maximum(before, jnp.max(scores, axis=0, keepdims=True))
            top[h : h + 1] = newest
            weight = jnp.exp2(scores - newest).astype(BF)
            probs[block, h] = weight
            return weight, jnp.exp2(before - newest)

        def gather(h, found):
            weight, fade = found
            tall = head_rows(h, 0, 64)
            values = jnp.concatenate([values_t[block, head_rows(h)], ones], axis=0)
            accum[tall] = accum[tall] * fade + dot(values, weight)

        heads_in_step(score, soften, gather)
        tops[block] = top[...]

    over_blocks(count, visit)


def attend(blocks, queries_t, weights_t, gains, carry):
    count, rows = len(blocks), blocks[0].shape[0]
    tokens = queries_t.shape[1]
    return call(
        functools.partial(attend_kernel, count, carry is not None),
        (queries_t, weights_t, gains, *blocks, *(carry or ())),
        (
            sds((count, HEADS, rows, tokens), BF),
            sds((count, D, rows), BF),
            sds((count, D, rows), BF),
            sds((count, rows, D), BF),
            sds((count, HEADS, tokens), F32),
            sds((64 * HEADS, tokens), F32),
            sds((HEADS, tokens), F32),
        ),
        count * (4 * rows * tokens * D * 5 + 4 * rows * D * D),
        count * (HEADS * rows * tokens * 2),
        scratch=[pltpu.VMEM((count, rows, D), BF)],
    )


def unpack_kernel(size, place, *refs):
    pieces, (rest, down) = refs[: 2 * size], refs[2 * size : 2 * size + 2]
    joined = refs[2 * size + 2]
    core, position = place[0], place[1]
    half = joined.shape[1]
    for side in range(2):
        for other in range(size):
            slot = 2 * (other ^ position) + (side ^ core)
            joined[slot] = pieces[side * size + other][...]
    for owner in range(size):
        for side in range(2):
            slot = 2 * owner + side
            rest[slot * half : (slot + 1) * half] = joined[slot, :, :REST]
            for part in range(4):
                row = (4 * slot + part) * half
                down[row : row + half] = joined[
                    slot, :, REST + D * part : REST + D * (part + 1)
                ]


def unpack(place, pieces, size):
    half, across = pieces[0].shape
    return call(
        functools.partial(unpack_kernel, size),
        tuple(pieces),
        (sds((D, REST), BF), sds((FF, D), BF)),
        1000,
        4 * D * across,
        place=(place,),
        scratch=[pltpu.VMEM((2 * size, half, across), BF)],
    )


def dense_kernel(inputs, accum, rest, down, gains, estimate, attended_t, inverse_total,
                 branch_out, third, third_inverse, normed_two, slope, hidden, ffn_out,
                 out_rows):
    for h in range(HEADS):
        inverse = 1.0 / accum[64 * h + HEAD : 64 * h + HEAD + 1]
        inverse_total[h : h + 1] = inverse
        attended_t[HEAD * h : HEAD * (h + 1)] = accum[64 * h : 64 * h + HEAD] * inverse
    branch = dot(attended_t[...].astype(BF), rest[:, :D], 0, 0)
    branch_out[...] = branch
    mid = inputs[...].astype(F32) + gains[6:7] * branch
    hat, inverse = unit_rows(mid)
    third[...] = hat
    third_inverse[...] = inverse
    normed = (hat * gains[4:5] + gains[5:6]).astype(BF)
    normed_two[...] = normed
    pre = dot(normed, rest[:, D : D + FF])
    gate = 0.5 * (1.0 + lax.erf(pre * math.sqrt(0.5)))
    hid = (pre * gate).astype(BF)
    hidden[...] = hid
    bell = jnp.exp(-0.5 * pre * pre) * (1.0 / math.sqrt(2.0 * math.pi))
    slope[...] = gate + pre * bell
    ffn = dot(hid, down[...])
    ffn_out[...] = ffn
    out = (mid + gains[7:8] * ffn).astype(BF)
    out_rows[...] = out
    estimate[...] = dot(out, rest[:, D + FF :]).astype(BF)


def dense_forward(inputs, accum, rest, down, gains):
    rows = inputs.shape[0]
    return call(
        dense_kernel,
        (inputs, accum, rest, down, gains),
        (
            sds((rows, OUT), BF),
            sds((D, rows), F32),
            sds((HEADS, rows), F32),
            sds((rows, D), F32),
            sds((rows, D), F32),
            sds((rows, 1), F32),
            sds((rows, D), BF),
            sds((rows, FF), F32),
            sds((rows, FF), BF),
            sds((rows, D), F32),
            sds((rows, D), BF),
        ),
        2 * rows * D * (D + 2 * FF + OUT),
        rows * FF * 8,
    )


def error_kernel(place, own, far, targets, errors, energy):
    rows = own.shape[0]
    wanted = targets[pl.ds(pl.multiple_of(place[1] * rows, 8), rows)]
    error = wanted - (own[...].astype(F32) + far[...].astype(F32))
    errors[...] = error
    row = lax.broadcasted_iota(jnp.int32, (8, OUT), 0)
    found = jnp.sum(error * error, axis=0, keepdims=True)
    clean = jnp.sum(wanted * wanted, axis=0, keepdims=True)
    energy[...] = jnp.where(row == 0, found, jnp.where(row == 1, clean, 0.0))


def error_energy(place, own, far, targets):
    rows = own.shape[0]
    return call(
        error_kernel,
        (own, far, targets),
        (sds((rows, OUT), F32), sds((8, OUT), F32)),
        rows * OUT * 8,
        rows * OUT * 12,
        place=(place,),
    )


def stem_sums(values):
    stem = lax.broadcasted_iota(jnp.int32, values.shape, 1) // SAMPLES
    total = jnp.zeros_like(values)
    for k in range(STEMS):
        part = jnp.sum(jnp.where(stem == k, values, 0.0), axis=1, keepdims=True)
        total = jnp.where(stem == k, part, total)
    return total


def dense_back_kernel(segments, present, energy, errors, rest, down, gains, attended_t, branch_out,
                      third, third_inverse, slope, ffn_out, grad_est, grad_ffn, grad_pre,
                      grad_branch, grad_attended_t, delta, grad_gains, loss):
    lane = lax.broadcasted_iota(jnp.int32, (1, OUT), 1)
    counted = jnp.zeros((1, OUT), F32)
    for k in range(STEMS):
        counted = jnp.where(lane // SAMPLES == k, present[0, k].astype(F32), counted)
    counted = counted * (10.0 / math.log(10.0) / (segments * STEMS))
    found = stem_sums(energy[0:1]) + ENERGY_EPS
    clean = stem_sums(energy[1:2]) + ENERGY_EPS
    terms = counted * (jnp.log(found) - jnp.log(clean))
    terms = jnp.where(lane % SAMPLES == 0, terms, 0.0)
    loss[...] = jnp.broadcast_to(jnp.sum(terms, axis=1, keepdims=True), loss.shape)
    low = (errors[...] * (-2.0 * counted / found)).astype(BF)
    grad_est[...] = low
    grad_out = dot(low, rest[:, D + FF :], 1, 1)
    grad_gains[3:4] = jnp.sum(grad_out * ffn_out[...], axis=0, keepdims=True)
    ffn = (grad_out * gains[7:8]).astype(BF)
    grad_ffn[...] = ffn
    hidden = dot(ffn, down[...], 1, 1).astype(BF)
    pre = (hidden.astype(F32) * slope[...]).astype(BF)
    grad_pre[...] = pre
    normed = dot(pre, rest[:, D : D + FF], 1, 1)
    hat = third[...]
    grad_gains[0:1] = jnp.sum(normed * hat, axis=0, keepdims=True)
    grad_gains[1:2] = jnp.sum(normed, axis=0, keepdims=True)
    scaled = normed * gains[4:5]
    grad_mid = grad_out + third_inverse[...] * (
        scaled
        - jnp.mean(scaled, axis=-1, keepdims=True)
        - hat * jnp.mean(scaled * hat, axis=-1, keepdims=True)
    )
    grad_gains[2:3] = jnp.sum(grad_mid * branch_out[...], axis=0, keepdims=True)
    branch = (grad_mid * gains[6:7]).astype(BF)
    grad_branch[...] = branch
    attended = dot(rest[:, :D], branch, 1, 1).astype(BF)
    grad_attended_t[...] = attended
    product = attended.astype(F32) * attended_t[...]
    for h in range(HEADS):
        delta[h : h + 1] = jnp.sum(product[head_rows(h)], axis=0, keepdims=True)


def dense_back(segments, present, energy, errors, rest, down, gains, attended_t, branch_out, third,
               third_inverse, slope, ffn_out):
    rows = errors.shape[0]
    return call(
        functools.partial(dense_back_kernel, segments),
        (energy, errors, rest, down, gains, attended_t, branch_out, third,
         third_inverse, slope, ffn_out),
        (
            sds((rows, OUT), BF),
            sds((rows, D), BF),
            sds((rows, FF), BF),
            sds((rows, D), BF),
            sds((D, rows), BF),
            sds((HEADS, rows), F32),
            sds((4, D), F32),
            sds((8, LANES), F32),
        ),
        2 * rows * D * (D + 2 * FF + OUT),
        rows * FF * 8,
        place=(present,),
    )


def deal(size, place, first, second, keep, send, owner, at):
    slot = owner ^ place[1]
    same = place[0] == 0
    keep[slot, :, at] = jnp.where(same, first, second).astype(BF)
    send[slot, :, at] = jnp.where(same, second, first).astype(BF)


def dense_weights_kernel(size, place, grad_est, grad_ffn, grad_pre, grad_branch, attended_t,
                         normed_two, hidden, out_rows, keep, send, wide, tall):
    half = keep.shape[1]
    wide[:, D + FF :] = dot(out_rows[...], grad_est[...], 0, 0)
    wide[:, D : D + FF] = dot(normed_two[...], grad_pre[...], 0, 0)
    wide[:, :D] = dot(attended_t[...].astype(BF), grad_branch[...])
    tall[...] = dot(hidden[...], grad_ffn[...], 0, 0)
    for owner in range(size):
        row = 2 * owner * half
        deal(
            size, place, wide[row : row + half], wide[row + half : row + 2 * half],
            keep, send, owner, slice(0, REST),
        )
        for part in range(4):
            first = (8 * owner + part) * half
            second = (8 * owner + 4 + part) * half
            deal(
                size, place, tall[first : first + half], tall[second : second + half],
                keep, send, owner, slice(REST + D * part, REST + D * (part + 1)),
            )


def dense_weights(place, grad_est, grad_ffn, grad_pre, grad_branch, attended_t, normed_two,
                  hidden, out_rows, size):
    rows = grad_est.shape[0]
    piece = (size, D // size // 2, REST + 4 * D)
    return call(
        functools.partial(dense_weights_kernel, size),
        (grad_est, grad_ffn, grad_pre, grad_branch, attended_t, normed_two, hidden, out_rows),
        (sds(piece, BF), sds(piece, BF)),
        2 * rows * D * (D + 2 * FF + OUT),
        rows * FF * 8,
        place=(place,),
        scratch=[pltpu.VMEM((D, REST), F32), pltpu.VMEM((FF, D), F32)],
    )


def attend_back_kernel(carried, probs, keys_t, values_t, tops, queries_t, delta, top,
                       inverse_total, grad_attended_t, *refs):
    if carried:
        refs[1][...] = refs[0][...]
    else:
        refs[0][...] = jnp.zeros_like(refs[0])
    grad_queries, grad_kv = refs[-2:]

    def visit(block):
        factor = jnp.exp2(tops[block] - top[...]) * inverse_total[...]
        shift = delta[...] * factor

        def begin(h):
            grad = grad_attended_t[head_rows(h)].astype(F32) * factor[h : h + 1]
            grad = grad.astype(BF)
            return grad, dot(values_t[block, head_rows(h)], grad, 0, 0)

        def turn(h, found):
            grad, grad_probs = found
            scores = probs[block, h].astype(F32) * (grad_probs - shift[h : h + 1])
            return grad, scores.astype(BF)

        def end(h, found):
            grad, scores = found
            at = head_rows(h)
            grad_queries[at] += dot(keys_t[block, at], scores)
            grad_kv[block, at] = (dot(queries_t[at], scores, 1, 1) * LOG_TWO).astype(BF)
            grad_kv[block, head_rows(h, D)] = dot(grad, probs[block, h], 1, 1).astype(BF)

        heads_in_step(begin, turn, end)

    over_blocks(probs.shape[0], visit)


def attend_back(saved, queries_t, delta, top, inverse_total, grad_attended_t, carry):
    probs, keys_t, values_t, tops = saved
    count, _, rows, tokens = probs.shape
    carry = () if carry is None else (carry,)
    return call(
        functools.partial(attend_back_kernel, len(carry)),
        (probs, keys_t, values_t, tops, queries_t, delta, top, inverse_total,
         grad_attended_t, *carry),
        (sds((D, tokens), F32), sds((count, 2 * D, rows), BF)),
        count * (8 * rows * tokens * D * 5),
        count * (HEADS * rows * tokens * 2),
    )


def finish_kernel(size, groups, place, grad_queries, own_unit, weights_t, gains, late,
                  *refs):
    grads, units = refs[:groups], refs[groups : 2 * groups]
    keep, send, moments, full, grad_gains = refs[2 * groups :]
    rows = own_unit.shape[0]
    ones = jnp.ones((rows, LANES), BF)
    query = (grad_queries[...] * SCALE).astype(BF)
    moments[:D] = dot(query, jnp.concatenate([own_unit[...], ones], axis=1))
    total = None
    for grad, unit in zip(grads, units):
        for block in range(grad.shape[0]):
            term = dot(grad[block], jnp.concatenate([unit[block], ones], axis=1))
            total = term if total is None else total + term
    moments[D:] = total
    for first, size_out, row in ((0, D, 0), (D, 2 * D, 2)):
        at = slice(first, first + size_out)
        moment = moments[at, :D]
        column = moments[at, D : D + 1]
        weight = weights_t[at].astype(F32)
        grad_gains[row : row + 1] = jnp.sum(weight * moment, axis=0, keepdims=True)
        grad_gains[row + 1 : row + 2] = jnp.sum(weight * column, axis=0, keepdims=True)
        product = moment * gains[row : row + 1] + column * gains[row + 1 : row + 2]
        full[:, at] = product.T
    grad_gains[4:8] = late[...]
    half = keep.shape[1]
    for owner in range(size):
        row = 2 * owner * half
        deal(
            size, place, full[row : row + half], full[row + half : row + 2 * half],
            keep, send, owner, slice(0, QKV),
        )
        slot = owner ^ place[1]
        keep[slot, :, QKV:] = jnp.zeros((half, LANES), BF)
        send[slot, :, QKV:] = jnp.zeros((half, LANES), BF)
    same = place[0] == 0
    for owner, row, vector, lane, across in gain_places(size):
        slot = owner ^ place[1]
        value = grad_gains[vector : vector + 1, lane : lane + across]
        at = slice(QKV, QKV + across)
        keep[slot, row : row + 1, at] = jnp.where(same, value, 0.0).astype(BF)
        send[slot, row : row + 1, at] = jnp.where(same, 0.0, value).astype(BF)


def finish(place, grad_queries, own_unit, weights_t, gains, late, grads, units, size):
    rows = own_unit.shape[0]
    piece = (size, D // size // 2, QKV + LANES)
    return call(
        functools.partial(finish_kernel, size, len(grads)),
        (grad_queries, own_unit, weights_t, gains, late, *grads, *units),
        (sds(piece, BF), sds(piece, BF)),
        2 * rows * D * QKV * size,
        rows * D * 2 * size,
        place=(place,),
        scratch=[
            pltpu.VMEM((QKV, D + LANES), F32),
            pltpu.VMEM((D, QKV), F32),
            pltpu.VMEM((8, D), F32),
        ],
    )


def square_kernel(*refs):
    total = jnp.zeros((1, 1), F32)
    for ref in refs[:-1]:
        values = ref[...].astype(F32)
        rows = jnp.sum(values * values, axis=0, keepdims=True)
        total = total + jnp.sum(rows, axis=1, keepdims=True)
    refs[-1][...] = jnp.broadcast_to(total, refs[-1].shape)


def square_sum(*parts):
    size = sum(x.size for x in parts)
    return call(square_kernel, parts, sds((8, LANES), F32), 2 * size, 2 * size)


def bits(size):
    return [1 << k for k in range(size.bit_length() - 1)]


def masks(size):
    return sorted(range(1, size), key=lambda mask: (mask.bit_count(), mask))


def tie(*values):
    return lax.optimization_barrier(values)


def add_low(left, right):
    return (left.astype(F32) + right.astype(F32)).astype(BF)


def core_step(keep, send):
    return add_low(keep, swap(send, "seg", 1))


def scatter_step(total, size):
    received = [swap(total[mask], "wide", mask) for mask in range(1, size)]
    return functools.reduce(jnp.add, [x.astype(F32) for x in [total[0]] + received]).astype(BF)


def segment_step(total):
    for mask in bits(lax.axis_size("seg"))[1:]:
        total = add_low(total, swap(total, "seg", mask))
    return total


def adam_update(weight, grad, moment, second, rate):
    moment = BETA_ONE * moment + (1 - BETA_ONE) * grad
    second = BETA_TWO * second + (1 - BETA_TWO) * grad * grad
    fixed_one = moment / (1 - BETA_ONE**ADAM_STEP)
    fixed_two = second / (1 - BETA_TWO**ADAM_STEP)
    weight = weight - rate * (fixed_one / (jnp.sqrt(fixed_two) + ADAM_EPS) + WEIGHT_DECAY * weight)
    return (weight, moment, second)


def adam_kernel(size, place, squares, early, early_other, late, late_other, *refs):
    masters, firsts, seconds = refs[0:3], refs[3:6], refs[6:9]
    news, new_firsts, new_seconds = refs[9:12], refs[12:15], refs[15:18]
    copies, norm = refs[18:21], refs[21]
    half = early.shape[0]
    same = place[0] == 0
    grad_norm = jnp.sqrt(squares[0:1, 0:1])
    norm[...] = jnp.broadcast_to(grad_norm, norm.shape)
    factor = jnp.minimum(1.0, CLIP_LIMIT / (grad_norm + 1e-06))

    def update(index, rows, lanes, grad, rate):
        at = (rows, lanes)
        found = adam_update(
            masters[index][at], grad * factor, firsts[index][at], seconds[index][at], rate
        )
        news[index][at], new_firsts[index][at], new_seconds[index][at] = found
        copies[index][at] = found[0].astype(BF)

    for side in range(2):
        use_own = same if side == 0 else jnp.logical_not(same)

        def pick(own, other, lanes):
            return jnp.where(use_own, own[:, lanes], other[:, lanes]).astype(F32)

        rows = slice(side * half, (side + 1) * half)
        update(0, rows, slice(0, QKV), pick(late, late_other, slice(0, QKV)), LEARN_RATE)
        update(0, rows, slice(QKV, QKV + REST), pick(early, early_other, slice(0, REST)),
               LEARN_RATE)
        for part in range(4):
            first = (4 * side + part) * half
            lanes = slice(REST + D * part, REST + D * (part + 1))
            update(1, slice(first, first + half), slice(0, D),
                   pick(early, early_other, lanes), LEARN_RATE)
    tall, across = gain_shape(size)
    lanes = slice(QKV, QKV + across)
    grad = jnp.where(same, late[:tall, lanes], late_other[:tall, lanes]).astype(F32)
    update(2, slice(0, tall), slice(0, across), grad, GAIN_RATE)


def adam(place, squares, grads, states, size):
    flat = gain_shape(size)
    states = [x.reshape(flat) if x.ndim == 1 else x for x in states]
    shapes = [x.shape for x in states[:3]]
    count = sum(x.size for x in states[:3])
    return call(
        functools.partial(adam_kernel, size),
        (squares, *grads, *states),
        tuple(sds(x, F32) for x in shapes) * 3
        + tuple(sds(x, BF) for x in shapes)
        + (sds((8, LANES), F32),),
        20 * count,
        28 * count,
        place=(place,),
    )


def adam_update(weight, grad, moment, second, rate):
    moment = BETA_ONE * moment + (1 - BETA_ONE) * grad
    second = BETA_TWO * second + (1 - BETA_TWO) * grad * grad
    fixed_one = moment / (1 - BETA_ONE**ADAM_STEP)
    fixed_two = second / (1 - BETA_TWO**ADAM_STEP)
    weight = weight - rate * (fixed_one / (jnp.sqrt(fixed_two) + ADAM_EPS) + WEIGHT_DECAY * weight)
    return (weight, moment, second)


def body(
    encoded,
    targets,
    present,
    wide_master,
    down_master,
    gain_master,
    wide_first,
    down_first,
    gain_first,
    wide_second,
    down_second,
    gain_second,
):
    size = lax.axis_size("wide") // 2
    position = lax.axis_index("wide") % size
    core = lax.axis_index("seg") % 2
    place = jnp.stack([core, position]).astype(jnp.int32)
    own = encoded[0]
    far = {0: swap(own, "wide", size)}
    first, rest = pack(place, wide_master, down_master, gain_master, size)

    first_mine = jnp.stack([first] + [swap(first, "wide", mask) for mask in range(1, size)])
    first_other = swap(first_mine, "seg", 1)
    queries_t, own_unit, weights_t, gains = start(place, own, first_mine, first_other, size)

    far[0], rest = tie(far[0], rest)
    order = [0] + masks(size)
    for mask in order[1:]:
        far[mask] = swap(far[0], "wide", mask)
    groups = [order[:1]] + [order[k : k + 2] for k in range(1, size, 2)]

    rest_mine = [rest] + [swap(rest, "wide", mask) for mask in range(1, size)]
    rest_other = [swap(x, "seg", 1) for x in rest_mine]

    carry = None
    saved, units = [], []
    for group in groups:
        probs, keys_t, values_t, unit, tops, *carry = attend(
            [far[mask] for mask in group], queries_t, weights_t, gains, carry
        )
        saved.append((probs, keys_t, values_t, tops))
        units.append(unit)
    accum, top = carry

    rest_all, down_all = unpack(place, rest_mine + rest_other, size)
    (est_own, attended_t, inverse_total, branch_out, third, third_inverse, normed_two, slope,
     hidden, ffn_out, out_rows) = dense_forward(own, accum, rest_all, down_all, gains)

    errors, energy = error_energy(place, est_own, swap(est_own, "wide", size), targets[0])
    for mask in bits(size):
        energy = energy + swap(energy, "wide", mask)
    seg_count = lax.axis_size("seg")
    (grad_est, grad_ffn, grad_pre, grad_branch, grad_attended_t, delta, late_gains,
     loss) = dense_back(
        seg_count, present, energy, errors, rest_all, down_all, gains, attended_t, branch_out,
        third, third_inverse, slope, ffn_out,
    )
    keep, send = dense_weights(
        place, grad_est, grad_ffn, grad_pre, grad_branch, attended_t, normed_two, hidden,
        out_rows, size,
    )
    grad_attended_t, keep, send = tie(grad_attended_t, keep, send)

    early = core_step(keep, send)
    grad_queries, grads = None, []
    for k, item in enumerate(saved):
        grad_queries, grad_kv = attend_back(
            item, queries_t, delta, top, inverse_total, grad_attended_t, grad_queries
        )
        grads.append(grad_kv)
        if k == 0:
            grad_queries, early = tie(grad_queries, early)
            early = scatter_step(early, size)
    grad_queries, early = tie(grad_queries, early)
    early = segment_step(early)
    keep, send = finish(
        place, grad_queries, own_unit, weights_t, gains, late_gains, grads, units, size
    )
    keep, send, early = tie(keep, send, early)
    early_other = swap(early, "seg", 1)
    late = core_step(keep, send)
    late, loss = tie(late, loss)
    for mask in bits(seg_count):
        loss = loss + swap(loss, "seg", mask)
    late = scatter_step(late, size)
    late, loss = tie(late, loss)
    late = segment_step(late)
    late_other = swap(late, "seg", 1)

    squares = square_sum(early, early_other, late, late_other)
    for mask in bits(2 * size):
        squares = squares + swap(squares, "wide", mask)
    *updated, grad_norm = adam(
        place,
        squares,
        (early, early_other, late, late_other),
        (wide_master, down_master, gain_master, wide_first, down_first, gain_first,
         wide_second, down_second, gain_second),
        size,
    )
    return (
        loss[0, 0],
        grad_norm[0, 0],
        *(x.reshape(-1) if k % 3 == 2 else x for k, x in enumerate(updated)),
    )


def solution(mesh):
    split, line = P("wide", None), P("wide")
    states = (split, split, line)
    return jax.shard_map(
        body,
        mesh=mesh,
        in_specs=(P("seg", "wide", None), P("seg", None, None), P("seg", None)) + states * 3,
        out_specs=(P(), P()) + states * 4,
        check_vma=False,
    )
```

time: 238 us -> 172 us (0.72)
  other arithmetic: 28 us -> 0.96 us
  Pallas kernels: 71.8 us -> 52.9 us
  local copies, waits for them, and re-layouts: 11.9 us -> 4.22 us
  between operations: 8.62 us -> 1.05 us
  starting transfers between devices: 41.1 us -> 34.1 us
  waiting for transfers between devices: 76.1 us -> 78.5 us
    pallas_call x5 -> x16, Pallas kernels: 71.8 us -> 52.9 us  [call(): pl.pallas_call(kernel, out_shape=out_shape, in_specs=[small] * len(place)...]
    convert_element_type x16 -> x6, other arithmetic: 11.5 us -> 0.8 us  [the longest x4 0.56 us: add_low(): return (left.astype(F32) + right.astype(F32)).astype(BF)]
    ppermute x27 -> x35, starting transfers between devices: 41.1 us -> 34.1 us  [swap(): lax.ppermute(x, axis, [(i, i ^ mask) for i in range(lax.axis_size(axis))])]
    concatenate x5 -> x0, other arithmetic: 4.73 us -> none  [the longest x2 3.5 us: body(): far = jnp.concatenate([far, swap(far, 'wide', mask)], 0)]
    another operation x5 -> x0, local copies, waits for them, and re-layouts: 4.52 us -> none  [the longest x1 2.89 us: pack_down(): split = down.reshape(-1, 4, rows, D)]
    select_n x8 -> x0, other arithmetic: 4.09 us -> none  [the longest x2 2.27 us: gather_rows(): jnp.where(core == 0, jnp.stack([mine, other], axis=1), jnp.stack([other,...]
    concatenate x1 -> x0, local copies, waits for them, and re-layouts: 2.81 us -> none  [body(): jnp.concatenate([grad_rest, pack_down(grad_down.reshape(size, 4 * rows, D...]
    reduce_sum x4 -> x0, other arithmetic: 2.76 us -> none  [the longest x2 1.68 us: body(): squares = jnp.sum(early * early) + jnp.sum(late * late)]
  transfers between devices with their start and end apart: 27 -> 35, of which waited for: 19 -> 21; matrix products, arithmetic and copies ran while one was open for 5% -> 0% of each run, Pallas kernels for 10% -> 22%
where the time goes in v2:
time: 172 us
  waiting for transfers between devices  78.5 us (46%)
  Pallas kernels  52.9 us (31%)
  starting transfers between devices  34.1 us (20%)
  local copies, waits for them, and re-layouts  4.22 us (2%)
    ppermute x35, waiting for transfers between devices, swap(): lax.ppermute(x, axis, [(i, i ^ mask) for i in range(lax.axis_size(axis))])  78.5 us
    pallas_call x16, Pallas kernels, call(): pl.pallas_call(kernel, out_shape=out_shape, in_specs=[small] * len(place)...  52.9 us
    ppermute x35, starting transfers between devices, swap(): lax.ppermute(x, axis, [(i, i ^ mask) for i in range(lax.axis_size(axis))])  34.1 us
  transfers between devices with their start and end apart: 35, of which 21 were waited for; matrix products, arithmetic and copies ran while one was open for 0% of the time, Pallas kernels for 22%

profile of v2, /device:TPU:0, one launch (start us, length us, event | category | flops | bytes accessed | tf_op | source)
XLA Modules:
  0.0 171.7 jit_solution(7033700835597988327)
XLA Ops:
  4.4 4.0 %collective-permute-start.2 = (bf16[48,1280]{1,0:T(8,128)(2,1)S(1)}, bf16[48,1280]{1,0:T(8,128)(2,1)S(1)}, u32[]{:S(2)}, u32[]{:S(2)}) collective-permute-start(bf16[48,1280]{1,0:T(8,128)(2,1)S(1)} %get-tuple-element.103), channel_id=1, source_target_pairs={{0,3},{1,2},{2,1},{3,0},{4,7},{5,6},{6,5},{7,4},{8,11},{9,10},{10,... | collective-permute-start | bytes 368648 | tf_op jit(solution)/shard_map/ppermute | solution.py:41
  9.1 3.5 %collective-permute-done.2 = bf16[48,1280]{1,0:T(8,128)(2,1)S(1)} collective-permute-done((bf16[48,1280]{1,0:T(8,128)(2,1)S(1)}, bf16[48,1280]{1,0:T(8,128)(2,1)S(1)}, u32[]{:S(2)}, u32[]{:S(2)}) %collective-permute-start.2) | collective-permute-done | bytes 122912 | tf_op jit(solution)/shard_map/ppermute | solution.py:41
  17.4 18.2 %collective-permute-done.4.refs_3_ = bf16[512,384]{1,0:T(8,128)(2,1)S(1)} collective-permute-done((bf16[512,384]{1,0:T(8,128)(2,1)S(1)}, bf16[512,384]{1,0:T(8,128)(2,1)S(1)}, u32[]{:S(2)}, u32[]{:S(2)}) %collective-permute-start.4) | collective-permute-done | bytes 393248 | tf_op jit(solution)/shard_map/ppermute | solution.py:41
  42.5 3.6 %shard_map.229 = (bf16[1,8,512,512]{3,2,1,0:T(8,128)(2,1)S(1)}, bf16[1,384,512]{2,1,0:T(8,128)(2,1)S(1)}, bf16[1,384,512]{2,1,0:T(8,128)(2,1)S(1)}, bf16[1,512,3...) custom-call(bf16[384,512]{1,0:T(8,128)(2,1)S(1)} %get-tuple-element.104.refs_0_., ...), custom_call_target="tpu_custom_call" | custom-call | flops 2315255808 | bytes 4194304 | tf_op jit(solution)/shard_map/pallas_call | solution.py:63
  46.1 9.8 %collective-permute-done.10.refs_3_ = bf16[48,3584]{1,0:T(8,128)(2,1)S(1)} collective-permute-done((bf16[48,3584]{1,0:T(8,128)(2,1)S(1)}, bf16[48,3584]{1,0:T(8,128)(2,1)S(1)}, u32[]{:S(2)}, u32[]{:S(2)}) %collective-permute-start.10) | collective-permute-done | bytes 344096 | tf_op jit(solution)/shard_map/ppermute | solution.py:41
  55.9 5.1 %collective-permute-done.9.refs_2_ = bf16[48,3584]{1,0:T(8,128)(2,1)S(1)} collective-permute-done((bf16[48,3584]{1,0:T(8,128)(2,1)S(1)}, bf16[48,3584]{1,0:T(8,128)(2,1)S(1)}, u32[]{:S(2)}, u32[]{:S(2)}) %collective-permute-start.9) | collective-permute-done | bytes 344096 | tf_op jit(solution)/shard_map/ppermute | solution.py:41
  63.6 7.7 %shard_map.230 = (bf16[2,8,512,512]{3,2,1,0:T(8,128)(2,1)S(1)}, bf16[2,384,512]{2,1,0:T(8,128)(2,1)S(1)}, bf16[2,384,512]{2,1,0:T(8,128)(2,1)S(1)}, bf16[2,512,3...) custom-call(bf16[384,512]{1,0:T(8,128)(2,1)S(1)} %get-tuple-element.104.refs_0_., ...), custom_call_target="tpu_custom_call" | custom-call | flops 4630511616 | bytes 8388608 | tf_op jit(solution)/shard_map/pallas_call | solution.py:63
  71.7 3.7 %shard_map.231 = (bf16[1,8,512,512]{3,2,1,0:T(8,128)(2,1)S(1)}, bf16[1,384,512]{2,1,0:T(8,128)(2,1)S(1)}, bf16[1,384,512]{2,1,0:T(8,128)(2,1)S(1)}, bf16[1,512,3...) custom-call(bf16[384,512]{1,0:T(8,128)(2,1)S(1)} %get-tuple-element.104.refs_0_., ...), custom_call_target="tpu_custom_call" | custom-call | flops 2315255808 | bytes 4194304 | tf_op jit(solution)/shard_map/pallas_call | solution.py:63
  76.4 2.8 %shard_map.233 = (bf16[512,128]{1,0:T(8,128)(2,1)S(1)}, f32[384,512]{1,0:T(8,128)S(1)}, f32[8,512]{1,0:T(8,128)S(1)}, f32[512,384]{1,0:T(8,128)S(1)}, f32[512,38...) custom-call(bf16[512,384]{1,0:T(8,128)(2,1)S(1)} %bitcast.38, ...), custom_call_target="tpu_custom_call" | custom-call | flops 1409286144 | bytes 6291456 | tf_op jit(solution)/shard_map/pallas_call | solution.py:63
  79.3 3.6 %collective-permute-start.15 = (bf16[512,128]{1,0:T(8,128)(2,1)S(1)}, bf16[512,128]{1,0:T(8,128)(2,1)S(1)}, u32[]{:S(2)}, u32[]{:S(2)}) collective-permute-start(bf16[512,128]{1,0:T(8,128)(2,1)S(1)} %get-tuple-element.121.own), channel_id=1, source_target_pairs={{0,4},{1,5},{2,6},{3,7},{4,0},{5,1},{6,2},{7,3},{8,12},{9,13},{10,... | collective-permute-start | bytes 393224 | tf_op jit(solution)/shard_map/ppermute | solution.py:41
  82.9 6.1 %collective-permute-done.15.far = bf16[512,128]{1,0:T(8,128)(2,1)S(1)} collective-permute-done((bf16[512,128]{1,0:T(8,128)(2,1)S(1)}, bf16[512,128]{1,0:T(8,128)(2,1)S(1)}, u32[]{:S(2)}, u32[]{:S(2)}) %collective-permute-start.15) | collective-permute-done | bytes 131104 | tf_op jit(solution)/shard_map/ppermute | solution.py:41
  90.5 2.8 %collective-permute-done.16 = f32[8,128]{1,0:T(8,128)S(1)} collective-permute-done((f32[8,128]{1,0:T(8,128)S(1)}, f32[8,128]{1,0:T(8,128)S(1)}, u32[]{:S(2)}, u32[]{:S(2)}) %collective-permute-start.16) | collective-permute-done | bytes 4128 | tf_op jit(solution)/shard_map/ppermute | solution.py:41
  93.3 3.6 %collective-permute-done.17 = f32[8,128]{1,0:T(8,128)S(1)} collective-permute-done((f32[8,128]{1,0:T(8,128)S(1)}, f32[8,128]{1,0:T(8,128)S(1)}, u32[]{:S(2)}, u32[]{:S(2)}) %collective-permute-start.17) | collective-permute-done | bytes 4128 | tf_op jit(solution)/shard_map/ppermute | solution.py:41
  96.9 3.3 %shard_map.235 = (bf16[512,128]{1,0:T(8,128)(2,1)S(1)}, bf16[512,384]{1,0:T(8,128)(2,1)S(1)}, bf16[512,1536]{1,0:T(8,128)(2,1)S(1)}, bf16[512,384]{1,0:T(8,128)(...) custom-call(s32[1,4]{1,0:T(1,128)S(1)} %copy-done.14, ...), custom_call_target="tpu_custom_call" | custom-call | flops 1409286144 | bytes 6291456 | tf_op jit(solution)/shard_map/pallas_call | solution.py:63
  102.8 4.6 %shard_map.237 = (f32[384,512]{1,0:T(8,128)S(1)}, bf16[1,768,512]{2,1,0:T(8,128)(2,1)S(1)}) custom-call(bf16[1,8,512,512]{3,2,1,0:T(8,128)(2,1)S(1)} %get-tuple-element.148.probs, bf16[1,384,512]{2,1,0:T(8,128)(2,1)S(1)} %get-tuple-element.149.keys_t, bf16[1,384,512]{2,1,0:T(8,128)(2,1)S(1)} %get-tuple-element.150.values_t, ...), custom_call_target="tpu_custom_call" | custom-call | flops 4026531840 | bytes 4194304 | tf_op jit(solution)/shard_map/pallas_call | solution.py:63
  111.4 8.9 %shard_map.238 = (f32[384,512]{1,0:T(8,128)S(1)}, bf16[2,768,512]{2,1,0:T(8,128)(2,1)S(1)}) custom-call(bf16[2,8,512,512]{3,2,1,0:T(8,128)(2,1)S(1)} %get-tuple-element.144.probs, bf16[2,384,512]{2,1,0:T(8,128)(2,1)S(1)} %get-tuple-element.145.keys_t, bf16[2,384,512]{2,1,0:T(8,128)(2,1)S(1)} %get-tuple-element.146.values_t, ...), custom_call_target="tpu_custom_call" | custom-call | flops 8053063680 | bytes 8388608 | tf_op jit(solution)/shard_map/pallas_call | solution.py:63
  120.3 4.4 %shard_map.239 = (f32[384,512]{1,0:T(8,128)S(1)}, bf16[1,768,512]{2,1,0:T(8,128)(2,1)S(1)}) custom-call(bf16[1,8,512,512]{3,2,1,0:T(8,128)(2,1)S(1)} %get-tuple-element.113.probs, bf16[1,384,512]{2,1,0:T(8,128)(2,1)S(1)} %get-tuple-element.114.keys_t, bf16[1,384,512]{2,1,0:T(8,128)(2,1)S(1)} %get-tuple-element.115.values_t, ...), custom_call_target="tpu_custom_call" | custom-call | flops 4026531840 | bytes 4194304 | tf_op jit(solution)/shard_map/pallas_call | solution.py:63
  128.7 3.1 %shard_map.240 = (bf16[4,48,1280]{2,1,0:T(8,128)(2,1)S(1)}, bf16[4,48,1280]{2,1,0:T(8,128)(2,1)S(1)}) custom-call(s32[2]{0:T(128)S(1)} %pad_add_fusion.place, f32[384,512]{1,0:T(8,128)S(1)} %get-tuple-element.159.grad_queries, bf16[512,384]{1,0:T(8,128)(2,1)S(1)} %get-tuple-element.160.own_unit, bf16[1152,384]{1,0:T(8,128)(2,1)S(1)} %get-tuple-element.105.refs_1_.weights_t, ...), custom_call_target="tpu_custom_call" | custom-call | flops 1811939328 | bytes 1572864 | tf_op jit(solution)/shard_map/pallas_call | solution.py:63
  131.8 4.8 %collective-permute-done.22 = bf16[48,3584]{1,0:T(8,128)(2,1)S(1)} collective-permute-done((bf16[48,3584]{1,0:T(8,128)(2,1)S(1)}, bf16[48,3584]{1,0:T(8,128)(2,1)S(1)}, u32[]{:S(2)}, u32[]{:S(2)}) %collective-permute-start.22) | collective-permute-done | bytes 344096 | tf_op jit(solution)/shard_map/ppermute | solution.py:41
  149.8 3.4 %collective-permute-done.30 = bf16[48,1280]{1,0:T(8,128)(2,1)S(1)} collective-permute-done((bf16[48,1280]{1,0:T(8,128)(2,1)S(1)}, bf16[48,1280]{1,0:T(8,128)(2,1)S(1)}, u32[]{:S(2)}, u32[]{:S(2)}) %collective-permute-start.30) | collective-permute-done | bytes 122912 | tf_op jit(solution)/shard_map/ppermute | solution.py:41
  155.7 2.8 %collective-permute-done.32 = f32[8,128]{1,0:T(8,128)S(1)} collective-permute-done((f32[8,128]{1,0:T(8,128)S(1)}, f32[8,128]{1,0:T(8,128)S(1)}, u32[]{:S(2)}, u32[]{:S(2)}) %collective-permute-start.32) | collective-permute-done | bytes 4128 | tf_op jit(solution)/shard_map/ppermute | solution.py:41
  158.4 3.6 %collective-permute-done.33 = f32[8,128]{1,0:T(8,128)S(1)} collective-permute-done((f32[8,128]{1,0:T(8,128)S(1)}, f32[8,128]{1,0:T(8,128)S(1)}, u32[]{:S(2)}, u32[]{:S(2)}) %collective-permute-start.33) | collective-permute-done | bytes 4128 | tf_op jit(solution)/shard_map/ppermute | solution.py:41
  163.7 2.8 %collective-permute-done.34 = f32[8,128]{1,0:T(8,128)S(1)} collective-permute-done((f32[8,128]{1,0:T(8,128)S(1)}, f32[8,128]{1,0:T(8,128)S(1)}, u32[]{:S(2)}, u32[]{:S(2)}) %collective-permute-start.34) | collective-permute-done | bytes 4128 | tf_op jit(solution)/shard_map/ppermute | solution.py:41
  166.6 4.6 %shard_map.242 = (f32[96,3200]{1,0:T(8,128)}, f32[384,384]{1,0:T(8,128)}, f32[6,128]{1,0:T(8,128)}, f32[96,3200]{1,0:T(8,128)}, f32[384,384]{1,0:T(8,128)}, /*in...) custom-call(s32[2]{0:T(128)S(1)} %pad_add_fusion.place, ...), custom_call_target="tpu_custom_call" | custom-call | flops 9108480 | bytes 12751872 | tf_op jit(solution)/shard_map/pallas_call | solution.py:63
  (111 shorter events, 49.8 us)
Async XLA Ops:
  4.4 8.2 %collective-permute-start.2 = (bf16[48,1280]{1,0:T(8,128)(2,1)S(1)}, bf16[48,1280]{1,0:T(8,128)(2,1)S(1)}, u32[]{:S(2)}, u32[]{:S(2)}) collective-permute-start(bf16[48,1280]{1,0:T(8,128)(2,1)S(1)} %get-tuple-element.103), channel_id=1, source_target_pairs={{0,3},{1,2},{2,1},{3,0},{4,7},{5,6},{6,5},{7,4},{8,11},{9,10},{10,... | collective-permute-start | bytes 368648 | tf_op jit(solution)/shard_map/ppermute | solution.py:41
  8.5 6.1 %collective-permute-start.1 = (bf16[48,1280]{1,0:T(8,128)(2,1)S(1)}, bf16[48,1280]{1,0:T(8,128)(2,1)S(1)}, u32[]{:S(2)}, u32[]{:S(2)}) collective-permute-start(bf16[48,1280]{1,0:T(8,128)(2,1)S(1)} %get-tuple-element.103), channel_id=1, source_target_pairs={{0,2},{1,3},{2,0},{3,1},{4,6},{5,7},{6,4},{7,5},{8,10},{9,11},{10,... | collective-permute-start | bytes 368648 | tf_op jit(solution)/shard_map/ppermute | solution.py:41
  8.9 5.7 %collective-permute-start = (bf16[48,1280]{1,0:T(8,128)(2,1)S(1)}, bf16[48,1280]{1,0:T(8,128)(2,1)S(1)}, u32[]{:S(2)}, u32[]{:S(2)}) collective-permute-start(bf16[48,1280]{1,0:T(8,128)(2,1)S(1)} %get-tuple-element.103), channel_id=1, source_target_pairs={{0,1},{1,0},{2,3},{3,2},{4,5},{5,4},{6,7},{7,6},{8,9},{9,8},{10,11... | collective-permute-start | bytes 368648 | tf_op jit(solution)/shard_map/ppermute | solution.py:41
  14.6 25.1 %collective-permute-start.3 = (bf16[4,48,1280]{2,1,0:T(8,128)(2,1)S(1)}, bf16[4,48,1280]{2,1,0:T(8,128)(2,1)S(1)}, u32[]{:S(2)}, u32[]{:S(2)}) collective-permute-start(bf16[4,48,1280]{2,1,0:T(8,128)(2,1)S(1)} %pad_maximum_fusion.mine), channel_id=1, source_target_pairs={{0,8},{8,0},{16,24},{24,16},{1,9},{9,1},{17,25},{25,17},{2,10},{10... | collective-permute-start | bytes 1474568 | tf_op jit(solution)/shard_map/ppermute | solution.py:41
  14.7 20.8 %collective-permute-start.4 = (bf16[512,384]{1,0:T(8,128)(2,1)S(1)}, bf16[512,384]{1,0:T(8,128)(2,1)S(1)}, u32[]{:S(2)}, u32[]{:S(2)}) collective-permute-start(bf16[512,384]{1,0:T(8,128)(2,1)S(1)} %bitcast.36), channel_id=1, source_target_pairs={{0,4},{1,5},{2,6},{3,7},{4,0},{5,1},{6,2},{7,3},{8,12},{9,13},{10,... | collective-permute-start | bytes 1179656 | tf_op jit(solution)/shard_map/ppermute | solution.py:41
  35.6 27.5 %collective-permute-start.7 = (bf16[512,384]{1,0:T(8,128)(2,1)S(1)}, bf16[512,384]{1,0:T(8,128)(2,1)S(1)}, u32[]{:S(2)}, u32[]{:S(2)}) collective-permute-start(bf16[512,384]{1,0:T(8,128)(2,1)S(1)} %collective-permute-done.4.refs_3_), channel_id=1, source_target_pairs={{0,2},{1,3},{2,0},{3,1},{4,6},{5,7},{6,4},{7,5},{8,10},{9,11},{10,... | collective-permute-start | bytes 1179656 | tf_op jit(solution)/shard_map/ppermute | solution.py:41
  36.3 27.3 %collective-permute-start.6 = (bf16[512,384]{1,0:T(8,128)(2,1)S(1)}, bf16[512,384]{1,0:T(8,128)(2,1)S(1)}, u32[]{:S(2)}, u32[]{:S(2)}) collective-permute-start(bf16[512,384]{1,0:T(8,128)(2,1)S(1)} %collective-permute-done.4.refs_3_), channel_id=1, source_target_pairs={{0,1},{1,0},{2,3},{3,2},{4,5},{5,4},{6,7},{7,6},{8,9},{9,8},{10,11... | collective-permute-start | bytes 1179656 | tf_op jit(solution)/shard_map/ppermute | solution.py:41
  37.7 18.2 %collective-permute-start.10 = (bf16[48,3584]{1,0:T(8,128)(2,1)S(1)}, bf16[48,3584]{1,0:T(8,128)(2,1)S(1)}, u32[]{:S(2)}, u32[]{:S(2)}) collective-permute-start(bf16[48,3584]{1,0:T(8,128)(2,1)S(1)} %get-tuple-element.118.refs_0_), channel_id=1, source_target_pairs={{0,3},{1,2},{2,1},{3,0},{4,7},{5,6},{6,5},{7,4},{8,11},{9,10},{10,... | collective-permute-start | bytes 1032200 | tf_op jit(solution)/shard_map/ppermute | solution.py:41
  39.1 22.0 %collective-permute-start.9 = (bf16[48,3584]{1,0:T(8,128)(2,1)S(1)}, bf16[48,3584]{1,0:T(8,128)(2,1)S(1)}, u32[]{:S(2)}, u32[]{:S(2)}) collective-permute-start(bf16[48,3584]{1,0:T(8,128)(2,1)S(1)} %get-tuple-element.118.refs_0_), channel_id=1, source_target_pairs={{0,2},{1,3},{2,0},{3,1},{4,6},{5,7},{6,4},{7,5},{8,10},{9,11},{10,... | collective-permute-start | bytes 1032200 | tf_op jit(solution)/shard_map/ppermute | solution.py:41
  39.8 23.3 %collective-permute-start.8 = (bf16[48,3584]{1,0:T(8,128)(2,1)S(1)}, bf16[48,3584]{1,0:T(8,128)(2,1)S(1)}, u32[]{:S(2)}, u32[]{:S(2)}) collective-permute-start(bf16[48,3584]{1,0:T(8,128)(2,1)S(1)} %get-tuple-element.118.refs_0_), channel_id=1, source_target_pairs={{0,1},{1,0},{2,3},{3,2},{4,5},{5,4},{6,7},{7,6},{8,9},{9,8},{10,11... | collective-permute-start | bytes 1032200 | tf_op jit(solution)/shard_map/ppermute | solution.py:41
  55.9 19.5 %collective-permute-start.11 = (bf16[48,3584]{1,0:T(8,128)(2,1)S(1)}, bf16[48,3584]{1,0:T(8,128)(2,1)S(1)}, u32[]{:S(2)}, u32[]{:S(2)}) collective-permute-start(bf16[48,3584]{1,0:T(8,128)(2,1)S(1)} %get-tuple-element.118.refs_0_), channel_id=1, source_target_pairs={{0,8},{8,0},{16,24},{24,16},{1,9},{9,1},{17,25},{25,17},{2,10},{10... | collective-permute-start | bytes 1032200 | tf_op jit(solution)/shard_map/ppermute | solution.py:41
  61.0 10.7 %collective-permute-start.5 = (bf16[512,384]{1,0:T(8,128)(2,1)S(1)}, bf16[512,384]{1,0:T(8,128)(2,1)S(1)}, u32[]{:S(2)}, u32[]{:S(2)}) collective-permute-start(bf16[512,384]{1,0:T(8,128)(2,1)S(1)} %collective-permute-done.4.refs_3_), channel_id=1, source_target_pairs={{0,3},{1,2},{2,1},{3,0},{4,7},{5,6},{6,5},{7,4},{8,11},{9,10},{10,... | collective-permute-start | bytes 1179656 | tf_op jit(solution)/shard_map/ppermute | solution.py:41
  63.0 12.4 %collective-permute-start.14 = (bf16[48,3584]{1,0:T(8,128)(2,1)S(1)}, bf16[48,3584]{1,0:T(8,128)(2,1)S(1)}, u32[]{:S(2)}, u32[]{:S(2)}) collective-permute-start(bf16[48,3584]{1,0:T(8,128)(2,1)S(1)} %collective-permute-done.10.refs_3_), channel_id=1, source_target_pairs={{0,8},{8,0},{16,24},{24,16},{1,9},{9,1},{17,25},{25,17},{2,10},{10... | collective-permute-start | bytes 1032200 | tf_op jit(solution)/shard_map/ppermute | solution.py:41
  63.0 12.4 %collective-permute-start.13 = (bf16[48,3584]{1,0:T(8,128)(2,1)S(1)}, bf16[48,3584]{1,0:T(8,128)(2,1)S(1)}, u32[]{:S(2)}, u32[]{:S(2)}) collective-permute-start(bf16[48,3584]{1,0:T(8,128)(2,1)S(1)} %collective-permute-done.9.refs_2_), channel_id=1, source_target_pairs={{0,8},{8,0},{16,24},{24,16},{1,9},{9,1},{17,25},{25,17},{2,10},{10... | collective-permute-start | bytes 1032200 | tf_op jit(solution)/shard_map/ppermute | solution.py:41
  63.6 11.9 %collective-permute-start.12 = (bf16[48,3584]{1,0:T(8,128)(2,1)S(1)}, bf16[48,3584]{1,0:T(8,128)(2,1)S(1)}, u32[]{:S(2)}, u32[]{:S(2)}) collective-permute-start(bf16[48,3584]{1,0:T(8,128)(2,1)S(1)} %collective-permute-done.8.refs_1_), channel_id=1, source_target_pairs={{0,8},{8,0},{16,24},{24,16},{1,9},{9,1},{17,25},{25,17},{2,10},{10... | collective-permute-start | bytes 1032200 | tf_op jit(solution)/shard_map/ppermute | solution.py:41
  79.3 9.7 %collective-permute-start.15 = (bf16[512,128]{1,0:T(8,128)(2,1)S(1)}, bf16[512,128]{1,0:T(8,128)(2,1)S(1)}, u32[]{:S(2)}, u32[]{:S(2)}) collective-permute-start(bf16[512,128]{1,0:T(8,128)(2,1)S(1)} %get-tuple-element.121.own), channel_id=1, source_target_pairs={{0,4},{1,5},{2,6},{3,7},{4,0},{5,1},{6,2},{7,3},{8,12},{9,13},{10,... | collective-permute-start | bytes 393224 | tf_op jit(solution)/shard_map/ppermute | solution.py:41
  107.9 17.9 %collective-permute-start.19 = (bf16[48,3584]{1,0:T(8,128)(2,1)S(1)}, bf16[48,3584]{1,0:T(8,128)(2,1)S(1)}, u32[]{:S(2)}, u32[]{:S(2)}) collective-permute-start(bf16[48,3584]{1,0:T(8,128)(2,1)S(1)} %get-tuple-element.192), channel_id=1, source_target_pairs={{0,1},{1,0},{2,3},{3,2},{4,5},{5,4},{6,7},{7,6},{8,9},{9,8},{10,11... | collective-permute-start | bytes 1032200 | tf_op jit(solution)/shard_map/ppermute | solution.py:41
  108.8 17.0 %collective-permute-start.21 = (bf16[48,3584]{1,0:T(8,128)(2,1)S(1)}, bf16[48,3584]{1,0:T(8,128)(2,1)S(1)}, u32[]{:S(2)}, u32[]{:S(2)}) collective-permute-start(bf16[48,3584]{1,0:T(8,128)(2,1)S(1)} %get-tuple-element.193), channel_id=1, source_target_pairs={{0,3},{1,2},{2,1},{3,0},{4,7},{5,6},{6,5},{7,4},{8,11},{9,10},{10,... | collective-permute-start | bytes 1032200 | tf_op jit(solution)/shard_map/ppermute | solution.py:41
  109.4 17.6 %collective-permute-start.20 = (bf16[48,3584]{1,0:T(8,128)(2,1)S(1)}, bf16[48,3584]{1,0:T(8,128)(2,1)S(1)}, u32[]{:S(2)}, u32[]{:S(2)}) collective-permute-start(bf16[48,3584]{1,0:T(8,128)(2,1)S(1)} %get-tuple-element.194), channel_id=1, source_target_pairs={{0,2},{1,3},{2,0},{3,1},{4,6},{5,7},{6,4},{7,5},{8,10},{9,11},{10,... | collective-permute-start | bytes 1032200 | tf_op jit(solution)/shard_map/ppermute | solution.py:41
  127.2 9.4 %collective-permute-start.22 = (bf16[48,3584]{1,0:T(8,128)(2,1)S(1)}, bf16[48,3584]{1,0:T(8,128)(2,1)S(1)}, u32[]{:S(2)}, u32[]{:S(2)}) collective-permute-start(bf16[48,3584]{1,0:T(8,128)(2,1)S(1)} %fusion.2), channel_id=1, source_target_pairs={{0,16},{8,24},{16,0},{24,8},{1,17},{9,25},{17,1},{25,9},{2,18},{10... | collective-permute-start | bytes 1032200 | tf_op jit(solution)/shard_map/ppermute | solution.py:41
  138.9 8.3 %collective-permute-start.24 = (bf16[48,1280]{1,0:T(8,128)(2,1)S(1)}, bf16[48,1280]{1,0:T(8,128)(2,1)S(1)}, u32[]{:S(2)}, u32[]{:S(2)}) collective-permute-start(bf16[48,1280]{1,0:T(8,128)(2,1)S(1)} %get-tuple-element.195), channel_id=1, source_target_pairs={{0,1},{1,0},{2,3},{3,2},{4,5},{5,4},{6,7},{7,6},{8,9},{9,8},{10,11... | collective-permute-start | bytes 368648 | tf_op jit(solution)/shard_map/ppermute | solution.py:41
  139.8 7.4 %collective-permute-start.26 = (bf16[48,1280]{1,0:T(8,128)(2,1)S(1)}, bf16[48,1280]{1,0:T(8,128)(2,1)S(1)}, u32[]{:S(2)}, u32[]{:S(2)}) collective-permute-start(bf16[48,1280]{1,0:T(8,128)(2,1)S(1)} %get-tuple-element.196), channel_id=1, source_target_pairs={{0,3},{1,2},{2,1},{3,0},{4,7},{5,6},{6,5},{7,4},{8,11},{9,10},{10,... | collective-permute-start | bytes 368648 | tf_op jit(solution)/shard_map/ppermute | solution.py:41
  140.4 7.8 %collective-permute-start.25 = (bf16[48,1280]{1,0:T(8,128)(2,1)S(1)}, bf16[48,1280]{1,0:T(8,128)(2,1)S(1)}, u32[]{:S(2)}, u32[]{:S(2)}) collective-permute-start(bf16[48,1280]{1,0:T(8,128)(2,1)S(1)} %get-tuple-element.197), channel_id=1, source_target_pairs={{0,2},{1,3},{2,0},{3,1},{4,6},{5,7},{6,4},{7,5},{8,10},{9,11},{10,... | collective-permute-start | bytes 368648 | tf_op jit(solution)/shard_map/ppermute | solution.py:41
  148.2 4.9 %collective-permute-start.30 = (bf16[48,1280]{1,0:T(8,128)(2,1)S(1)}, bf16[48,1280]{1,0:T(8,128)(2,1)S(1)}, u32[]{:S(2)}, u32[]{:S(2)}) collective-permute-start(bf16[48,1280]{1,0:T(8,128)(2,1)S(1)} %fusion.5), channel_id=1, source_target_pairs={{0,16},{8,24},{16,0},{24,8},{1,17},{9,25},{17,1},{25,9},{2,18},{10... | collective-permute-start | bytes 368648 | tf_op jit(solution)/shard_map/ppermute | solution.py:41
  (26 other events, 345.0 us)

commit v3 on v2

--- a/solution.py
+++ b/solution.py
@@ -351,6 +351,16 @@
     )
 
 
+def ordered_sum(place, values, joined):
+    size = joined.shape[0]
+    for slot in range(size):
+        joined[slot ^ place[1]] = values[slot]
+    total = joined[0]
+    for slot in range(1, size):
+        total = total + joined[slot]
+    return total
+
+
 def stem_sums(values):
     stem = lax.broadcasted_iota(jnp.int32, values.shape, 1) // SAMPLES
     total = jnp.zeros_like(values)
@@ -360,9 +370,10 @@
     return total
 
 
-def dense_back_kernel(segments, present, energy, errors, rest, down, gains, attended_t, branch_out,
+def dense_back_kernel(segments, place, present, energies, errors, rest, down, gains, attended_t, branch_out,
                       third, third_inverse, slope, ffn_out, grad_est, grad_ffn, grad_pre,
-                      grad_branch, grad_attended_t, delta, grad_gains, loss):
+                      grad_branch, grad_attended_t, delta, grad_gains, loss, joined):
+    energy = ordered_sum(place, energies, joined)
     lane = lax.broadcasted_iota(jnp.int32, (1, OUT), 1)
     counted = jnp.zeros((1, OUT), F32)
     for k in range(STEMS):
@@ -402,12 +413,12 @@
         delta[h : h + 1] = jnp.sum(product[head_rows(h)], axis=0, keepdims=True)
 
 
-def dense_back(segments, present, energy, errors, rest, down, gains, attended_t, branch_out, third,
+def dense_back(segments, place, present, energies, errors, rest, down, gains, attended_t, branch_out, third,
                third_inverse, slope, ffn_out):
     rows = errors.shape[0]
     return call(
         functools.partial(dense_back_kernel, segments),
-        (energy, errors, rest, down, gains, attended_t, branch_out, third,
+        (energies, errors, rest, down, gains, attended_t, branch_out, third,
          third_inverse, slope, ffn_out),
         (
             sds((rows, OUT), BF),
@@ -421,7 +432,8 @@
         ),
         2 * rows * D * (D + 2 * FF + OUT),
         rows * FF * 8,
-        place=(present,),
+        place=(place, present),
+        scratch=[pltpu.VMEM(energies.shape, F32)],
     )
 
 
@@ -592,6 +604,22 @@
     return call(square_kernel, parts, sds((8, LANES), F32), 2 * size, 2 * size)
 
 
+def group_sum_kernel(place, values, total, joined):
+    total[...] = ordered_sum(place, values, joined)
+
+
+def group_sum(place, values):
+    return call(
+        group_sum_kernel,
+        (values,),
+        sds(values.shape[1:], F32),
+        values.size,
+        4 * values.size,
+        place=(place,),
+        scratch=[pltpu.VMEM(values.shape, F32)],
+    )
+
+
 def bits(size):
     return [1 << k for k in range(size.bit_length() - 1)]
 
@@ -615,6 +643,10 @@
 def scatter_step(total, size):
     received = [swap(total[mask], "wide", mask) for mask in range(1, size)]
     return functools.reduce(jnp.add, [x.astype(F32) for x in [total[0]] + received]).astype(BF)
+
+
+def exchange(values, size):
+    return jnp.stack([values] + [swap(values, "wide", mask) for mask in range(1, size)])
 
 
 def segment_step(total):
@@ -719,18 +751,21 @@
     far = {0: swap(own, "wide", size)}
     first, rest = pack(place, wide_master, down_master, gain_master, size)
 
+    high = size // 2
     first_mine = jnp.stack([first] + [swap(first, "wide", mask) for mask in range(1, size)])
+    low_mine = [rest] + [swap(rest, "wide", mask) for mask in range(1, high)]
+    far[0], first_mine, *low_mine = tie(far[0], first_mine, *low_mine)
     first_other = swap(first_mine, "seg", 1)
     queries_t, own_unit, weights_t, gains = start(place, own, first_mine, first_other, size)
 
-    far[0], rest = tie(far[0], rest)
-    order = [0] + masks(size)
-    for mask in order[1:]:
+    for mask in [high, *range(1, high)]:
         far[mask] = swap(far[0], "wide", mask)
-    groups = [order[:1]] + [order[k : k + 2] for k in range(1, size, 2)]
-
-    rest_mine = [rest] + [swap(rest, "wide", mask) for mask in range(1, size)]
-    rest_other = [swap(x, "seg", 1) for x in rest_mine]
+    high_mine = [swap(x, "wide", high) for x in low_mine]
+    low_other = [swap(x, "seg", 1) for x in low_mine]
+    for mask in range(1, high):
+        far[high + mask] = swap(far[high], "wide", mask)
+    order = [high, *range(1, high), *range(high + 1, size)]
+    groups = [[0]] + [order[k : k + 2] for k in range(0, size - 1, 2)]
 
     carry = None
     saved, units = [], []
@@ -741,18 +776,20 @@
         saved.append((probs, keys_t, values_t, tops))
         units.append(unit)
     accum, top = carry
+    accum, *high_mine = tie(accum, *high_mine)
+    high_other = [swap(x, "seg", 1) for x in high_mine]
+    rest_mine, rest_other = low_mine + high_mine, low_other + high_other
 
     rest_all, down_all = unpack(place, rest_mine + rest_other, size)
     (est_own, attended_t, inverse_total, branch_out, third, third_inverse, normed_two, slope,
      hidden, ffn_out, out_rows) = dense_forward(own, accum, rest_all, down_all, gains)
 
     errors, energy = error_energy(place, est_own, swap(est_own, "wide", size), targets[0])
-    for mask in bits(size):
-        energy = energy + swap(energy, "wide", mask)
+    energy = exchange(energy, size)
     seg_count = lax.axis_size("seg")
     (grad_est, grad_ffn, grad_pre, grad_branch, grad_attended_t, delta, late_gains,
      loss) = dense_back(
-        seg_count, present, energy, errors, rest_all, down_all, gains, attended_t, branch_out,
+        seg_count, place, present, energy, errors, rest_all, down_all, gains, attended_t, branch_out,
         third, third_inverse, slope, ffn_out,
     )
     keep, send = dense_weights(
@@ -776,20 +813,19 @@
     keep, send = finish(
         place, grad_queries, own_unit, weights_t, gains, late_gains, grads, units, size
     )
-    keep, send, early = tie(keep, send, early)
-    early_other = swap(early, "seg", 1)
     late = core_step(keep, send)
     late, loss = tie(late, loss)
     for mask in bits(seg_count):
         loss = loss + swap(loss, "seg", mask)
     late = scatter_step(late, size)
-    late, loss = tie(late, loss)
+    late, loss, early = tie(late, loss, early)
+    early_other = swap(early, "seg", 1)
     late = segment_step(late)
     late_other = swap(late, "seg", 1)
 
     squares = square_sum(early, early_other, late, late_other)
-    for mask in bits(2 * size):
-        squares = squares + swap(squares, "wide", mask)
+    squares = group_sum(place, exchange(squares, size))
+    squares = squares + swap(squares, "wide", size)
     *updated, grad_norm = adam(
         place,
         squares,

time: 172 us -> 144 us (0.84)
  waiting for transfers between devices: 78.5 us -> 47.3 us
  starting transfers between devices: 34.1 us -> 36.4 us
    ppermute x35 -> x37, waiting for transfers between devices: 78.5 us -> 47.3 us  [swap(): lax.ppermute(x, axis, [(i, i ^ mask) for i in range(lax.axis_size(axis))])]
    ppermute x35 -> x37, starting transfers between devices: 34.1 us -> 36.4 us  [swap(): lax.ppermute(x, axis, [(i, i ^ mask) for i in range(lax.axis_size(axis))])]
    pallas_call x16 -> x17, Pallas kernels: 52.9 us -> 53.5 us  [call(): pl.pallas_call(kernel, out_shape=out_shape, in_specs=[small] * len(place)...]
  transfers between devices with their start and end apart: 35 -> 37, of which waited for: 21 -> 22; matrix products, arithmetic and copies ran while one was open for 0% -> 1% of each run, Pallas kernels for 22% -> 24%
where the time goes in v3:
time: 144 us; the launch traced here: 143 us
  Pallas kernels  53.5 us (37%)
  waiting for transfers between devices  47.3 us (33%)
  starting transfers between devices  36.4 us (25%)
  local copies, waits for them, and re-layouts  4.22 us (3%)
    pallas_call x17, Pallas kernels, call(): pl.pallas_call(kernel, out_shape=out_shape, in_specs=[small] * len(place)...  53.5 us
    ppermute x37, waiting for transfers between devices, swap(): lax.ppermute(x, axis, [(i, i ^ mask) for i in range(lax.axis_size(axis))])  47.3 us
    ppermute x37, starting transfers between devices, swap(): lax.ppermute(x, axis, [(i, i ^ mask) for i in range(lax.axis_size(axis))])  36.4 us
    unnamed x30, local copies, waits for them, and re-layouts  3.1 us
  transfers between devices with their start and end apart: 37, of which 22 were waited for; matrix products, arithmetic and copies ran while one was open for 1% of the time, Pallas kernels for 24%

profile of v3, /device:TPU:0, one launch (start us, length us, event | category | flops | bytes accessed | tf_op | source)
XLA Modules:
  0.0 143.5 jit_solution(69306174812626212)
XLA Ops:
  0.6 4.1 %collective-permute-start = (bf16[512,384]{1,0:T(8,128)(2,1)}, bf16[512,384]{1,0:T(8,128)(2,1)S(1)}, u32[]{:S(2)}, u32[]{:S(2)}) collective-permute-start(bf16[512,384]{1,0:T(8,128)(2,1)} %bitcast.44), channel_id=1, source_target_pairs={{0,4},{1,5},{2,6},{3,7},{4,0},{5,1},{6,2},{7,3},{8,12},{9,13},{10,... | collective-permute-start | bytes 1179656 | tf_op jit(solution)/shard_map/ppermute | solution.py:41
  8.5 2.6 %collective-permute-start.3 = (bf16[48,1280]{1,0:T(8,128)(2,1)S(1)}, bf16[48,1280]{1,0:T(8,128)(2,1)S(1)}, u32[]{:S(2)}, u32[]{:S(2)}) collective-permute-start(bf16[48,1280]{1,0:T(8,128)(2,1)S(1)} %get-tuple-element.106), channel_id=1, source_target_pairs={{0,3},{1,2},{2,1},{3,0},{4,7},{5,6},{6,5},{7,4},{8,11},{9,10},{10,... | collective-permute-start | bytes 368648 | tf_op jit(solution)/shard_map/ppermute | solution.py:41
  13.6 3.6 %collective-permute-done.3 = bf16[48,1280]{1,0:T(8,128)(2,1)S(1)} collective-permute-done((bf16[48,1280]{1,0:T(8,128)(2,1)S(1)}, bf16[48,1280]{1,0:T(8,128)(2,1)S(1)}, u32[]{:S(2)}, u32[]{:S(2)}) %collective-permute-start.3) | collective-permute-done | bytes 122912 | tf_op jit(solution)/shard_map/ppermute | solution.py:41
  17.2 7.0 %collective-permute-done.2 = bf16[48,1280]{1,0:T(8,128)(2,1)S(1)} collective-permute-done((bf16[48,1280]{1,0:T(8,128)(2,1)S(1)}, bf16[48,1280]{1,0:T(8,128)(2,1)S(1)}, u32[]{:S(2)}, u32[]{:S(2)}) %collective-permute-start.2) | collective-permute-done | bytes 122912 | tf_op jit(solution)/shard_map/ppermute | solution.py:41
  25.8 2.1 %collective-permute-start.6 = (bf16[512,384]{1,0:T(8,128)(2,1)S(1)}, bf16[512,384]{1,0:T(8,128)(2,1)S(1)}, u32[]{:S(2)}, u32[]{:S(2)}) collective-permute-start(bf16[512,384]{1,0:T(8,128)(2,1)S(1)} %collective-permute-done.refs_3_), channel_id=1, source_target_pairs={{0,2},{1,3},{2,0},{3,1},{4,6},{5,7},{6,4},{7,5},{8,10},{9,11},{10,... | collective-permute-start | bytes 1179656 | tf_op jit(solution)/shard_map/ppermute | solution.py:41
  29.6 3.6 %shard_map.229 = (bf16[1,8,512,512]{3,2,1,0:T(8,128)(2,1)S(1)}, bf16[1,384,512]{2,1,0:T(8,128)(2,1)S(1)}, bf16[1,384,512]{2,1,0:T(8,128)(2,1)S(1)}, bf16[1,512,3...) custom-call(bf16[384,512]{1,0:T(8,128)(2,1)S(1)} %get-tuple-element.109.refs_0_., ...), custom_call_target="tpu_custom_call" | custom-call | flops 2315255808 | bytes 4194304 | tf_op jit(solution)/shard_map/pallas_call | solution.py:63
  33.2 2.7 %collective-permute-done.8.refs_4_ = bf16[512,384]{1,0:T(8,128)(2,1)S(1)} collective-permute-done((bf16[512,384]{1,0:T(8,128)(2,1)S(1)}, bf16[512,384]{1,0:T(8,128)(2,1)S(1)}, u32[]{:S(2)}, u32[]{:S(2)}) %collective-permute-start.8) | collective-permute-done | bytes 393248 | tf_op jit(solution)/shard_map/ppermute | solution.py:41
  36.0 2.9 %collective-permute-start.10 = (bf16[48,3584]{1,0:T(8,128)(2,1)S(1)}, bf16[48,3584]{1,0:T(8,128)(2,1)S(1)}, u32[]{:S(2)}, u32[]{:S(2)}) collective-permute-start(bf16[48,3584]{1,0:T(8,128)(2,1)S(1)} %collective-permute-done.4.refs_1_), channel_id=1, source_target_pairs={{0,2},{1,3},{2,0},{3,1},{4,6},{5,7},{6,4},{7,5},{8,10},{9,11},{10,... | collective-permute-start | bytes 1032200 | tf_op jit(solution)/shard_map/ppermute | solution.py:41
  39.4 7.7 %shard_map.230 = (bf16[2,8,512,512]{3,2,1,0:T(8,128)(2,1)S(1)}, bf16[2,384,512]{2,1,0:T(8,128)(2,1)S(1)}, bf16[2,384,512]{2,1,0:T(8,128)(2,1)S(1)}, bf16[2,512,3...) custom-call(bf16[384,512]{1,0:T(8,128)(2,1)S(1)} %get-tuple-element.109.refs_0_., ...), custom_call_target="tpu_custom_call" | custom-call | flops 4630511616 | bytes 8388608 | tf_op jit(solution)/shard_map/pallas_call | solution.py:63
  47.1 2.2 %collective-permute-done.7.refs_3_ = bf16[512,384]{1,0:T(8,128)(2,1)S(1)} collective-permute-done((bf16[512,384]{1,0:T(8,128)(2,1)S(1)}, bf16[512,384]{1,0:T(8,128)(2,1)S(1)}, u32[]{:S(2)}, u32[]{:S(2)}) %collective-permute-start.7) | collective-permute-done | bytes 393248 | tf_op jit(solution)/shard_map/ppermute | solution.py:41
  49.4 3.7 %shard_map.231 = (bf16[1,8,512,512]{3,2,1,0:T(8,128)(2,1)S(1)}, bf16[1,384,512]{2,1,0:T(8,128)(2,1)S(1)}, bf16[1,384,512]{2,1,0:T(8,128)(2,1)S(1)}, bf16[1,512,3...) custom-call(bf16[384,512]{1,0:T(8,128)(2,1)S(1)} %get-tuple-element.109.refs_0_., ...), custom_call_target="tpu_custom_call" | custom-call | flops 2315255808 | bytes 4194304 | tf_op jit(solution)/shard_map/pallas_call | solution.py:63
  56.3 2.8 %shard_map.233 = (bf16[512,128]{1,0:T(8,128)(2,1)S(1)}, f32[384,512]{1,0:T(8,128)S(1)}, f32[8,512]{1,0:T(8,128)S(1)}, f32[512,384]{1,0:T(8,128)S(1)}, f32[512,38...) custom-call(bf16[512,384]{1,0:T(8,128)(2,1)S(1)} %bitcast.46, ...), custom_call_target="tpu_custom_call" | custom-call | flops 1409286144 | bytes 6291456 | tf_op jit(solution)/shard_map/pallas_call | solution.py:63
  59.2 9.2 %collective-permute-done.15.far = bf16[512,128]{1,0:T(8,128)(2,1)S(1)} collective-permute-done((bf16[512,128]{1,0:T(8,128)(2,1)S(1)}, bf16[512,128]{1,0:T(8,128)(2,1)S(1)}, u32[]{:S(2)}, u32[]{:S(2)}) %collective-permute-start.15) | collective-permute-done | bytes 131104 | tf_op jit(solution)/shard_map/ppermute | solution.py:41
  74.7 3.3 %shard_map.235 = (bf16[512,128]{1,0:T(8,128)(2,1)S(1)}, bf16[512,384]{1,0:T(8,128)(2,1)S(1)}, bf16[512,1536]{1,0:T(8,128)(2,1)S(1)}, bf16[512,384]{1,0:T(8,128)(...) custom-call(s32[2]{0:T(128)S(1)} %pad_add_fusion.place, ...), custom_call_target="tpu_custom_call" | custom-call | flops 1409286144 | bytes 6291456 | tf_op jit(solution)/shard_map/pallas_call | solution.py:63
  78.0 2.5 %shard_map.236 = (bf16[4,48,3584]{2,1,0:T(8,128)(2,1)S(1)}, bf16[4,48,3584]{2,1,0:T(8,128)(2,1)S(1)}) custom-call(s32[2]{0:T(128)S(1)} %pad_add_fusion.place, bf16[512,128]{1,0:T(8,128)(2,1)S(1)} %get-tuple-element.142.grad_est, bf16[512,384]{1,0:T(8,128)(2,1)S(1)} %get-tuple-element.143.grad_ffn, bf16[512,1536]{1,0:T(8,128)(2,1)S(1)} %get-tuple-element.144.grad_pre, ...), custom_call_target="tpu_custom_call" | custom-call | flops 1409286144 | bytes 6291456 | tf_op jit(solution)/shard_map/pallas_call | solution.py:63
  80.6 4.7 %shard_map.237 = (f32[384,512]{1,0:T(8,128)S(1)}, bf16[1,768,512]{2,1,0:T(8,128)(2,1)S(1)}) custom-call(bf16[1,8,512,512]{3,2,1,0:T(8,128)(2,1)S(1)} %get-tuple-element.156.probs, bf16[1,384,512]{2,1,0:T(8,128)(2,1)S(1)} %get-tuple-element.157.keys_t, bf16[1,384,512]{2,1,0:T(8,128)(2,1)S(1)} %get-tuple-element.158.values_t, ...), custom_call_target="tpu_custom_call" | custom-call | flops 4026531840 | bytes 4194304 | tf_op jit(solution)/shard_map/pallas_call | solution.py:63
  89.2 8.9 %shard_map.238 = (f32[384,512]{1,0:T(8,128)S(1)}, bf16[2,768,512]{2,1,0:T(8,128)(2,1)S(1)}) custom-call(bf16[2,8,512,512]{3,2,1,0:T(8,128)(2,1)S(1)} %get-tuple-element.152.probs, bf16[2,384,512]{2,1,0:T(8,128)(2,1)S(1)} %get-tuple-element.153.keys_t, bf16[2,384,512]{2,1,0:T(8,128)(2,1)S(1)} %get-tuple-element.154.values_t, ...), custom_call_target="tpu_custom_call" | custom-call | flops 8053063680 | bytes 8388608 | tf_op jit(solution)/shard_map/pallas_call | solution.py:63
  98.2 4.4 %shard_map.239 = (f32[384,512]{1,0:T(8,128)S(1)}, bf16[1,768,512]{2,1,0:T(8,128)(2,1)S(1)}) custom-call(bf16[1,8,512,512]{3,2,1,0:T(8,128)(2,1)S(1)} %get-tuple-element.117.probs, bf16[1,384,512]{2,1,0:T(8,128)(2,1)S(1)} %get-tuple-element.118.keys_t, bf16[1,384,512]{2,1,0:T(8,128)(2,1)S(1)} %get-tuple-element.119.values_t, ...), custom_call_target="tpu_custom_call" | custom-call | flops 4026531840 | bytes 4194304 | tf_op jit(solution)/shard_map/pallas_call | solution.py:63
  105.0 3.1 %shard_map.240 = (bf16[4,48,1280]{2,1,0:T(8,128)(2,1)S(1)}, bf16[4,48,1280]{2,1,0:T(8,128)(2,1)S(1)}) custom-call(s32[2]{0:T(128)S(1)} %pad_add_fusion.place, f32[384,512]{1,0:T(8,128)S(1)} %get-tuple-element.167.grad_queries, bf16[512,384]{1,0:T(8,128)(2,1)S(1)} %get-tuple-element.168.own_unit, bf16[1152,384]{1,0:T(8,128)(2,1)S(1)} %get-tuple-element.110.refs_1_.weights_t, ...), custom_call_target="tpu_custom_call" | custom-call | flops 1811939328 | bytes 1572864 | tf_op jit(solution)/shard_map/pallas_call | solution.py:63
  115.5 3.2 %collective-permute-done.29 = bf16[48,3584]{1,0:T(8,128)(2,1)S(1)} collective-permute-done((bf16[48,3584]{1,0:T(8,128)(2,1)S(1)}, bf16[48,3584]{1,0:T(8,128)(2,1)S(1)}, u32[]{:S(2)}, u32[]{:S(2)}) %collective-permute-start.29) | collective-permute-done | bytes 344096 | tf_op jit(solution)/shard_map/ppermute | solution.py:41
  121.5 3.4 %collective-permute-done.31 = bf16[48,1280]{1,0:T(8,128)(2,1)S(1)} collective-permute-done((bf16[48,1280]{1,0:T(8,128)(2,1)S(1)}, bf16[48,1280]{1,0:T(8,128)(2,1)S(1)}, u32[]{:S(2)}, u32[]{:S(2)}) %collective-permute-start.31) | collective-permute-done | bytes 122912 | tf_op jit(solution)/shard_map/ppermute | solution.py:41
  127.6 2.0 %collective-permute-start.34 = (f32[8,128]{1,0:T(8,128)S(1)}, f32[8,128]{1,0:T(8,128)S(1)}, u32[]{:S(2)}, u32[]{:S(2)}) collective-permute-start(f32[8,128]{1,0:T(8,128)S(1)} %shard_map.241), channel_id=1, source_target_pairs={{0,2},{1,3},{2,0},{3,1},{4,6},{5,7},{6,4},{7,5},{8,10},{9,11},{10,... | collective-permute-start | bytes 12296 | tf_op jit(solution)/shard_map/ppermute | solution.py:41
  134.3 4.0 %collective-permute-done.36 = f32[8,128]{1,0:T(8,128)S(1)} collective-permute-done((f32[8,128]{1,0:T(8,128)S(1)}, f32[8,128]{1,0:T(8,128)S(1)}, u32[]{:S(2)}, u32[]{:S(2)}) %collective-permute-start.36) | collective-permute-done | bytes 4128 | tf_op jit(solution)/shard_map/ppermute | solution.py:41
  138.4 4.6 %shard_map.243 = (f32[96,3200]{1,0:T(8,128)}, f32[384,384]{1,0:T(8,128)}, f32[6,128]{1,0:T(8,128)}, f32[96,3200]{1,0:T(8,128)}, f32[384,384]{1,0:T(8,128)}, /*in...) custom-call(s32[2]{0:T(128)S(1)} %pad_add_fusion.place, ...), custom_call_target="tpu_custom_call" | custom-call | flops 9108480 | bytes 12751872 | tf_op jit(solution)/shard_map/pallas_call | solution.py:63
  (114 shorter events, 44.0 us)
Async XLA Ops:
  0.6 23.8 %collective-permute-start = (bf16[512,384]{1,0:T(8,128)(2,1)}, bf16[512,384]{1,0:T(8,128)(2,1)S(1)}, u32[]{:S(2)}, u32[]{:S(2)}) collective-permute-start(bf16[512,384]{1,0:T(8,128)(2,1)} %bitcast.44), channel_id=1, source_target_pairs={{0,4},{1,5},{2,6},{3,7},{4,0},{5,1},{6,2},{7,3},{8,12},{9,13},{10,... | collective-permute-start | bytes 1179656 | tf_op jit(solution)/shard_map/ppermute | solution.py:41
  8.5 8.7 %collective-permute-start.3 = (bf16[48,1280]{1,0:T(8,128)(2,1)S(1)}, bf16[48,1280]{1,0:T(8,128)(2,1)S(1)}, u32[]{:S(2)}, u32[]{:S(2)}) collective-permute-start(bf16[48,1280]{1,0:T(8,128)(2,1)S(1)} %get-tuple-element.106), channel_id=1, source_target_pairs={{0,3},{1,2},{2,1},{3,0},{4,7},{5,6},{6,5},{7,4},{8,11},{9,10},{10,... | collective-permute-start | bytes 368648 | tf_op jit(solution)/shard_map/ppermute | solution.py:41
  11.1 13.1 %collective-permute-start.2 = (bf16[48,1280]{1,0:T(8,128)(2,1)S(1)}, bf16[48,1280]{1,0:T(8,128)(2,1)S(1)}, u32[]{:S(2)}, u32[]{:S(2)}) collective-permute-start(bf16[48,1280]{1,0:T(8,128)(2,1)S(1)} %get-tuple-element.106), channel_id=1, source_target_pairs={{0,2},{1,3},{2,0},{3,1},{4,6},{5,7},{6,4},{7,5},{8,10},{9,11},{10,... | collective-permute-start | bytes 368648 | tf_op jit(solution)/shard_map/ppermute | solution.py:41
  11.5 12.7 %collective-permute-start.1 = (bf16[48,1280]{1,0:T(8,128)(2,1)S(1)}, bf16[48,1280]{1,0:T(8,128)(2,1)S(1)}, u32[]{:S(2)}, u32[]{:S(2)}) collective-permute-start(bf16[48,1280]{1,0:T(8,128)(2,1)S(1)} %get-tuple-element.106), channel_id=1, source_target_pairs={{0,1},{1,0},{2,3},{3,2},{4,5},{5,4},{6,7},{7,6},{8,9},{9,8},{10,11... | collective-permute-start | bytes 368648 | tf_op jit(solution)/shard_map/ppermute | solution.py:41
  12.0 12.4 %collective-permute-start.4 = (bf16[48,3584]{1,0:T(8,128)(2,1)S(1)}, bf16[48,3584]{1,0:T(8,128)(2,1)S(1)}, u32[]{:S(2)}, u32[]{:S(2)}) collective-permute-start(bf16[48,3584]{1,0:T(8,128)(2,1)S(1)} %get-tuple-element.122.refs_0_), channel_id=1, source_target_pairs={{0,1},{1,0},{2,3},{3,2},{4,5},{5,4},{6,7},{7,6},{8,9},{9,8},{10,11... | collective-permute-start | bytes 1032200 | tf_op jit(solution)/shard_map/ppermute | solution.py:41
  24.4 11.5 %collective-permute-start.8 = (bf16[512,384]{1,0:T(8,128)(2,1)S(1)}, bf16[512,384]{1,0:T(8,128)(2,1)S(1)}, u32[]{:S(2)}, u32[]{:S(2)}) collective-permute-start(bf16[512,384]{1,0:T(8,128)(2,1)S(1)} %collective-permute-done.refs_3_), channel_id=1, source_target_pairs={{0,1},{1,0},{2,3},{3,2},{4,5},{5,4},{6,7},{7,6},{8,9},{9,8},{10,11... | collective-permute-start | bytes 1179656 | tf_op jit(solution)/shard_map/ppermute | solution.py:41
  25.8 13.1 %collective-permute-start.6 = (bf16[512,384]{1,0:T(8,128)(2,1)S(1)}, bf16[512,384]{1,0:T(8,128)(2,1)S(1)}, u32[]{:S(2)}, u32[]{:S(2)}) collective-permute-start(bf16[512,384]{1,0:T(8,128)(2,1)S(1)} %collective-permute-done.refs_3_), channel_id=1, source_target_pairs={{0,2},{1,3},{2,0},{3,1},{4,6},{5,7},{6,4},{7,5},{8,10},{9,11},{10,... | collective-permute-start | bytes 1179656 | tf_op jit(solution)/shard_map/ppermute | solution.py:41
  27.9 25.8 %collective-permute-start.11 = (bf16[48,3584]{1,0:T(8,128)(2,1)S(1)}, bf16[48,3584]{1,0:T(8,128)(2,1)S(1)}, u32[]{:S(2)}, u32[]{:S(2)}) collective-permute-start(bf16[48,3584]{1,0:T(8,128)(2,1)S(1)} %get-tuple-element.122.refs_0_), channel_id=1, source_target_pairs={{0,8},{8,0},{16,24},{24,16},{1,9},{9,1},{17,25},{25,17},{2,10},{10... | collective-permute-start | bytes 1032200 | tf_op jit(solution)/shard_map/ppermute | solution.py:41
  27.9 25.2 %collective-permute-start.9 = (bf16[48,3584]{1,0:T(8,128)(2,1)S(1)}, bf16[48,3584]{1,0:T(8,128)(2,1)S(1)}, u32[]{:S(2)}, u32[]{:S(2)}) collective-permute-start(bf16[48,3584]{1,0:T(8,128)(2,1)S(1)} %get-tuple-element.122.refs_0_), channel_id=1, source_target_pairs={{0,2},{1,3},{2,0},{3,1},{4,6},{5,7},{6,4},{7,5},{8,10},{9,11},{10,... | collective-permute-start | bytes 1032200 | tf_op jit(solution)/shard_map/ppermute | solution.py:41
  28.1 25.6 %collective-permute-start.12 = (bf16[48,3584]{1,0:T(8,128)(2,1)S(1)}, bf16[48,3584]{1,0:T(8,128)(2,1)S(1)}, u32[]{:S(2)}, u32[]{:S(2)}) collective-permute-start(bf16[48,3584]{1,0:T(8,128)(2,1)S(1)} %collective-permute-done.4.refs_1_), channel_id=1, source_target_pairs={{0,8},{8,0},{16,24},{24,16},{1,9},{9,1},{17,25},{25,17},{2,10},{10... | collective-permute-start | bytes 1032200 | tf_op jit(solution)/shard_map/ppermute | solution.py:41
  36.0 17.1 %collective-permute-start.10 = (bf16[48,3584]{1,0:T(8,128)(2,1)S(1)}, bf16[48,3584]{1,0:T(8,128)(2,1)S(1)}, u32[]{:S(2)}, u32[]{:S(2)}) collective-permute-start(bf16[48,3584]{1,0:T(8,128)(2,1)S(1)} %collective-permute-done.4.refs_1_), channel_id=1, source_target_pairs={{0,2},{1,3},{2,0},{3,1},{4,6},{5,7},{6,4},{7,5},{8,10},{9,11},{10,... | collective-permute-start | bytes 1032200 | tf_op jit(solution)/shard_map/ppermute | solution.py:41
  38.9 10.5 %collective-permute-start.7 = (bf16[512,384]{1,0:T(8,128)(2,1)S(1)}, bf16[512,384]{1,0:T(8,128)(2,1)S(1)}, u32[]{:S(2)}, u32[]{:S(2)}) collective-permute-start(bf16[512,384]{1,0:T(8,128)(2,1)S(1)} %collective-permute-done.6.refs_3_), channel_id=1, source_target_pairs={{0,1},{1,0},{2,3},{3,2},{4,5},{5,4},{6,7},{7,6},{8,9},{9,8},{10,11... | collective-permute-start | bytes 1179656 | tf_op jit(solution)/shard_map/ppermute | solution.py:41
  59.1 9.3 %collective-permute-start.15 = (bf16[512,128]{1,0:T(8,128)(2,1)S(1)}, bf16[512,128]{1,0:T(8,128)(2,1)S(1)}, u32[]{:S(2)}, u32[]{:S(2)}) collective-permute-start(bf16[512,128]{1,0:T(8,128)(2,1)S(1)} %get-tuple-element.129.own), channel_id=1, source_target_pairs={{0,4},{1,5},{2,6},{3,7},{4,0},{5,1},{6,2},{7,3},{8,12},{9,13},{10,... | collective-permute-start | bytes 393224 | tf_op jit(solution)/shard_map/ppermute | solution.py:41
  80.5 4.7 %collective-permute-start.19 = (bf16[4,48,3584]{2,1,0:T(8,128)(2,1)S(1)}, bf16[4,48,3584]{2,1,0:T(8,128)(2,1)S(1)}, u32[]{:S(2)}, u32[]{:S(2)}) collective-permute-start(bf16[4,48,3584]{2,1,0:T(8,128)(2,1)S(1)} %get-tuple-element.162), channel_id=1, source_target_pairs={{0,8},{8,0},{16,24},{24,16},{1,9},{9,1},{17,25},{25,17},{2,10},{10... | collective-permute-start | bytes 4128776 | tf_op jit(solution)/shard_map/ppermute | solution.py:41
  85.7 17.9 %collective-permute-start.20 = (bf16[48,3584]{1,0:T(8,128)(2,1)S(1)}, bf16[48,3584]{1,0:T(8,128)(2,1)S(1)}, u32[]{:S(2)}, u32[]{:S(2)}) collective-permute-start(bf16[48,3584]{1,0:T(8,128)(2,1)S(1)} %get-tuple-element.198), channel_id=1, source_target_pairs={{0,1},{1,0},{2,3},{3,2},{4,5},{5,4},{6,7},{7,6},{8,9},{9,8},{10,11... | collective-permute-start | bytes 1032200 | tf_op jit(solution)/shard_map/ppermute | solution.py:41
  87.3 16.3 %collective-permute-start.22 = (bf16[48,3584]{1,0:T(8,128)(2,1)S(1)}, bf16[48,3584]{1,0:T(8,128)(2,1)S(1)}, u32[]{:S(2)}, u32[]{:S(2)}) collective-permute-start(bf16[48,3584]{1,0:T(8,128)(2,1)S(1)} %get-tuple-element.199), channel_id=1, source_target_pairs={{0,3},{1,2},{2,1},{3,0},{4,7},{5,6},{6,5},{7,4},{8,11},{9,10},{10,... | collective-permute-start | bytes 1032200 | tf_op jit(solution)/shard_map/ppermute | solution.py:41
  87.3 17.5 %collective-permute-start.21 = (bf16[48,3584]{1,0:T(8,128)(2,1)S(1)}, bf16[48,3584]{1,0:T(8,128)(2,1)S(1)}, u32[]{:S(2)}, u32[]{:S(2)}) collective-permute-start(bf16[48,3584]{1,0:T(8,128)(2,1)S(1)} %get-tuple-element.200), channel_id=1, source_target_pairs={{0,2},{1,3},{2,0},{3,1},{4,6},{5,7},{6,4},{7,5},{8,10},{9,11},{10,... | collective-permute-start | bytes 1032200 | tf_op jit(solution)/shard_map/ppermute | solution.py:41
  108.2 10.5 %collective-permute-start.29 = (bf16[48,3584]{1,0:T(8,128)(2,1)S(1)}, bf16[48,3584]{1,0:T(8,128)(2,1)S(1)}, u32[]{:S(2)}, u32[]{:S(2)}) collective-permute-start(bf16[48,3584]{1,0:T(8,128)(2,1)S(1)} %fusion.2), channel_id=1, source_target_pairs={{0,16},{8,24},{16,0},{24,8},{1,17},{9,25},{17,1},{25,9},{2,18},{10... | collective-permute-start | bytes 1032200 | tf_op jit(solution)/shard_map/ppermute | solution.py:41
  110.4 8.4 %collective-permute-start.24 = (bf16[48,1280]{1,0:T(8,128)(2,1)S(1)}, bf16[48,1280]{1,0:T(8,128)(2,1)S(1)}, u32[]{:S(2)}, u32[]{:S(2)}) collective-permute-start(bf16[48,1280]{1,0:T(8,128)(2,1)S(1)} %get-tuple-element.201), channel_id=1, source_target_pairs={{0,1},{1,0},{2,3},{3,2},{4,5},{5,4},{6,7},{7,6},{8,9},{9,8},{10,11... | collective-permute-start | bytes 368648 | tf_op jit(solution)/shard_map/ppermute | solution.py:41
  112.0 7.1 %collective-permute-start.26 = (bf16[48,1280]{1,0:T(8,128)(2,1)S(1)}, bf16[48,1280]{1,0:T(8,128)(2,1)S(1)}, u32[]{:S(2)}, u32[]{:S(2)}) collective-permute-start(bf16[48,1280]{1,0:T(8,128)(2,1)S(1)} %get-tuple-element.202), channel_id=1, source_target_pairs={{0,3},{1,2},{2,1},{3,0},{4,7},{5,6},{6,5},{7,4},{8,11},{9,10},{10,... | collective-permute-start | bytes 368648 | tf_op jit(solution)/shard_map/ppermute | solution.py:41
  112.3 7.7 %collective-permute-start.25 = (bf16[48,1280]{1,0:T(8,128)(2,1)S(1)}, bf16[48,1280]{1,0:T(8,128)(2,1)S(1)}, u32[]{:S(2)}, u32[]{:S(2)}) collective-permute-start(bf16[48,1280]{1,0:T(8,128)(2,1)S(1)} %get-tuple-element.203), channel_id=1, source_target_pairs={{0,2},{1,3},{2,0},{3,1},{4,6},{5,7},{6,4},{7,5},{8,10},{9,11},{10,... | collective-permute-start | bytes 368648 | tf_op jit(solution)/shard_map/ppermute | solution.py:41
  114.0 4.8 %collective-permute-start.28 = (f32[8,128]{1,0:T(8,128)S(1)}, f32[8,128]{1,0:T(8,128)S(1)}, u32[]{:S(2)}, u32[]{:S(2)}) collective-permute-start(f32[8,128]{1,0:T(8,128)S(1)} %add.56), channel_id=1, source_target_pairs={{0,16},{8,24},{16,0},{24,8},{1,17},{9,25},{17,1},{25,9},{2,18},{10... | collective-permute-start | bytes 12296 | tf_op jit(solution)/shard_map/ppermute | solution.py:41
  120.0 4.9 %collective-permute-start.31 = (bf16[48,1280]{1,0:T(8,128)(2,1)S(1)}, bf16[48,1280]{1,0:T(8,128)(2,1)S(1)}, u32[]{:S(2)}, u32[]{:S(2)}) collective-permute-start(bf16[48,1280]{1,0:T(8,128)(2,1)S(1)} %fusion.5), channel_id=1, source_target_pairs={{0,16},{8,24},{16,0},{24,8},{1,17},{9,25},{17,1},{25,9},{2,18},{10... | collective-permute-start | bytes 368648 | tf_op jit(solution)/shard_map/ppermute | solution.py:41
  121.5 4.9 %collective-permute-start.30 = (bf16[48,3584]{1,0:T(8,128)(2,1)S(1)}, bf16[48,3584]{1,0:T(8,128)(2,1)S(1)}, u32[]{:S(2)}, u32[]{:S(2)}) collective-permute-start(bf16[48,3584]{1,0:T(8,128)(2,1)S(1)} %add_convert_fusion.2.refs_0_.early), channel_id=1, source_target_pairs={{0,8},{8,0},{16,24},{24,16},{1,9},{9,1},{17,25},{25,17},{2,10},{10... | collective-permute-start | bytes 1032200 | tf_op jit(solution)/shard_map/ppermute | solution.py:41
  (28 other events, 335.7 us)

commit v4 on v3

--- a/solution.py
+++ b/solution.py
@@ -34,7 +34,7 @@
 F32 = jnp.float32
 SCALE = 1.0 / math.sqrt(HEAD)
 LOG_TWO = math.log(2.0)
-VMEM_LIMIT = 14 * 2**20
+VMEM_LIMIT = 16 * 2**20
 
 
 def swap(x, axis, mask):
@@ -57,15 +57,17 @@
     return centred * inverse, inverse
 
 
-def call(kernel, operands, out_shape, flops, moved, place=(), scratch=()):
+def call(kernel, operands, out_shape, flops, moved, place=(), scratch=(), in_specs=None,
+         out_specs=None, aliases=None):
     here = pl.BlockSpec(memory_space=pltpu.VMEM)
     small = pl.BlockSpec(memory_space=pltpu.SMEM)
     return pl.pallas_call(
         kernel,
         out_shape=out_shape,
-        in_specs=[small] * len(place) + [here] * len(operands),
-        out_specs=jax.tree.map(lambda _: here, out_shape),
+        in_specs=[small] * len(place) + (in_specs or [here] * len(operands)),
+        out_specs=out_specs or jax.tree.map(lambda _: here, out_shape),
         scratch_shapes=scratch,
+        input_output_aliases=aliases or {},
         compiler_params=pltpu.CompilerParams(vmem_limit_bytes=VMEM_LIMIT),
         cost_estimate=pl.CostEstimate(flops=flops, bytes_accessed=moved, transcendentals=0),
     )(*place, *operands)
@@ -245,14 +247,15 @@
 
 
 def unpack_kernel(size, place, *refs):
-    pieces, (rest, down) = refs[: 2 * size], refs[2 * size : 2 * size + 2]
-    joined = refs[2 * size + 2]
+    high = size // 2
+    rest, down, joined = refs[2 * high + 2 :]
     core, position = place[0], place[1]
     half = joined.shape[1]
     for side in range(2):
+        pieces = refs[side * (high + 1) : (side + 1) * (high + 1)]
         for other in range(size):
             slot = 2 * (other ^ position) + (side ^ core)
-            joined[slot] = pieces[side * size + other][...]
+            joined[slot] = pieces[other][...] if other < high else pieces[high][other - high]
     for owner in range(size):
         for side in range(2):
             slot = 2 * owner + side
@@ -277,41 +280,49 @@
     )
 
 
-def dense_kernel(inputs, accum, rest, down, gains, estimate, attended_t, inverse_total,
-                 branch_out, third, third_inverse, normed_two, slope, hidden, ffn_out,
-                 out_rows):
+def row_part(part, rows):
+    split = 3 * rows // 4
+    return slice(split, rows) if part else slice(0, split)
+
+
+def dense_kernel(part, inputs, accum, rest, down, gains, *refs):
+    (attended_t, inverse_total, branch_out, third, third_inverse, normed_two, slope, hidden,
+     ffn_out, out_rows, estimate) = refs[-11:]
+    rows = row_part(part, inputs.shape[0])
     for h in range(HEADS):
-        inverse = 1.0 / accum[64 * h + HEAD : 64 * h + HEAD + 1]
-        inverse_total[h : h + 1] = inverse
-        attended_t[HEAD * h : HEAD * (h + 1)] = accum[64 * h : 64 * h + HEAD] * inverse
-    branch = dot(attended_t[...].astype(BF), rest[:, :D], 0, 0)
-    branch_out[...] = branch
-    mid = inputs[...].astype(F32) + gains[6:7] * branch
+        inverse = 1.0 / accum[64 * h + HEAD : 64 * h + HEAD + 1, rows]
+        inverse_total[h : h + 1, rows] = inverse
+        attended_t[HEAD * h : HEAD * (h + 1), rows] = (
+            accum[64 * h : 64 * h + HEAD, rows] * inverse
+        )
+    branch = dot(attended_t[:, rows].astype(BF), rest[:, :D], 0, 0)
+    branch_out[rows] = branch
+    mid = inputs[rows].astype(F32) + gains[6:7] * branch
     hat, inverse = unit_rows(mid)
-    third[...] = hat
-    third_inverse[...] = inverse
+    third[rows] = hat
+    third_inverse[rows] = inverse
     normed = (hat * gains[4:5] + gains[5:6]).astype(BF)
-    normed_two[...] = normed
+    normed_two[rows] = normed
     pre = dot(normed, rest[:, D : D + FF])
     gate = 0.5 * (1.0 + lax.erf(pre * math.sqrt(0.5)))
     hid = (pre * gate).astype(BF)
-    hidden[...] = hid
+    hidden[rows] = hid
     bell = jnp.exp(-0.5 * pre * pre) * (1.0 / math.sqrt(2.0 * math.pi))
-    slope[...] = gate + pre * bell
+    slope[rows] = gate + pre * bell
     ffn = dot(hid, down[...])
-    ffn_out[...] = ffn
+    ffn_out[rows] = ffn
     out = (mid + gains[7:8] * ffn).astype(BF)
-    out_rows[...] = out
+    out_rows[rows] = out
     estimate[...] = dot(out, rest[:, D + FF :]).astype(BF)
 
 
-def dense_forward(inputs, accum, rest, down, gains):
+def dense_forward(part, inputs, accum, rest, down, gains, started):
     rows = inputs.shape[0]
-    return call(
-        dense_kernel,
-        (inputs, accum, rest, down, gains),
+    taken = row_part(part, rows)
+    return call(
+        functools.partial(dense_kernel, part),
+        (inputs, accum, rest, down, gains, *started),
         (
-            sds((rows, OUT), BF),
             sds((D, rows), F32),
             sds((HEADS, rows), F32),
             sds((rows, D), F32),
@@ -322,28 +333,36 @@
             sds((rows, FF), BF),
             sds((rows, D), F32),
             sds((rows, D), BF),
+            sds((taken.stop - taken.start, OUT), BF),
         ),
-        2 * rows * D * (D + 2 * FF + OUT),
-        rows * FF * 8,
-    )
-
-
-def error_kernel(place, own, far, targets, errors, energy):
-    rows = own.shape[0]
-    wanted = targets[pl.ds(pl.multiple_of(place[1] * rows, 8), rows)]
-    error = wanted - (own[...].astype(F32) + far[...].astype(F32))
-    errors[...] = error
+        rows * D * (D + 2 * FF + OUT),
+        rows * FF * 4,
+        aliases={5 + k: k for k in range(len(started))},
+    )
+
+
+def error_kernel(place, *refs):
+    own, far, (targets, errors, energy) = refs[:2], refs[2:4], refs[4:]
+    rows = errors.shape[0]
     row = lax.broadcasted_iota(jnp.int32, (8, OUT), 0)
-    found = jnp.sum(error * error, axis=0, keepdims=True)
-    clean = jnp.sum(wanted * wanted, axis=0, keepdims=True)
-    energy[...] = jnp.where(row == 0, found, jnp.where(row == 1, clean, 0.0))
+    total = jnp.zeros((8, OUT), F32)
+    for part in range(2):
+        taken = row_part(part, rows)
+        first = pl.multiple_of(place[1] * rows + taken.start, 8)
+        wanted = targets[pl.ds(first, taken.stop - taken.start)]
+        error = wanted - (own[part][...].astype(F32) + far[part][...].astype(F32))
+        errors[taken] = error
+        found = jnp.sum(error * error, axis=0, keepdims=True)
+        clean = jnp.sum(wanted * wanted, axis=0, keepdims=True)
+        total = total + jnp.where(row == 0, found, jnp.where(row == 1, clean, 0.0))
+    energy[...] = total
 
 
 def error_energy(place, own, far, targets):
-    rows = own.shape[0]
+    rows = own[0].shape[0] + own[1].shape[0]
     return call(
         error_kernel,
-        (own, far, targets),
+        (*own, *far, targets),
         (sds((rows, OUT), F32), sds((8, OUT), F32)),
         rows * OUT * 8,
         rows * OUT * 12,
@@ -604,19 +623,28 @@
     return call(square_kernel, parts, sds((8, LANES), F32), 2 * size, 2 * size)
 
 
-def group_sum_kernel(place, values, total, joined):
-    total[...] = ordered_sum(place, values, joined)
-
-
-def group_sum(place, values):
-    return call(
-        group_sum_kernel,
-        (values,),
-        sds(values.shape[1:], F32),
-        values.size,
-        4 * values.size,
+def branch_sum_kernel(place, own, *refs):
+    parts, total, joined = refs[:-2], refs[-2], refs[-1]
+    for slot, part in enumerate(parts):
+        value = part[...]
+        if slot == 0:
+            value = jnp.where(place[0] == 0, own[...], value)
+        joined[slot ^ place[1]] = value
+    found = joined[0]
+    for slot in range(1, len(parts)):
+        found = found + joined[slot]
+    total[...] = found
+
+
+def branch_sum(place, own, parts):
+    return call(
+        branch_sum_kernel,
+        (own, *parts),
+        sds(own.shape, F32),
+        own.size,
+        4 * own.size,
         place=(place,),
-        scratch=[pltpu.VMEM(values.shape, F32)],
+        scratch=[pltpu.VMEM((len(parts),) + own.shape, F32)],
     )
 
 
@@ -640,9 +668,25 @@
     return add_low(keep, swap(send, "seg", 1))
 
 
-def scatter_step(total, size):
-    received = [swap(total[mask], "wide", mask) for mask in range(1, size)]
-    return functools.reduce(jnp.add, [x.astype(F32) for x in [total[0]] + received]).astype(BF)
+def branch_parts(values, size):
+    segments, wide = lax.axis_size("seg"), 2 * size
+    found = []
+    for slot in range(size):
+        pairs = []
+        for seg in range(segments):
+            mask = size + slot if seg % 2 else slot
+            if mask:
+                pairs += [(seg * wide + w, seg * wide + (w ^ mask)) for w in range(wide)]
+        found.append(lax.ppermute(values, ("seg", "wide"), pairs))
+    return found
+
+
+def send_members(total, size):
+    return [total[0]] + [swap(total[mask], "wide", mask) for mask in range(1, size)]
+
+
+def sum_low(parts):
+    return functools.reduce(jnp.add, [x.astype(F32) for x in parts]).astype(BF)
 
 
 def exchange(values, size):
@@ -657,50 +701,83 @@
 
 def adam_update(weight, grad, moment, second, rate):
     moment = BETA_ONE * moment + (1 - BETA_ONE) * grad
-    second = BETA_TWO * second + (1 - BETA_TWO) * grad * grad
-    fixed_one = moment / (1 - BETA_ONE**ADAM_STEP)
-    fixed_two = second / (1 - BETA_TWO**ADAM_STEP)
-    weight = weight - rate * (fixed_one / (jnp.sqrt(fixed_two) + ADAM_EPS) + WEIGHT_DECAY * weight)
+    second = BETA_TWO * second + (1 - BETA_TWO) * (grad * grad)
+    fixed_one = moment * (rate / (1 - BETA_ONE**ADAM_STEP))
+    fixed_two = second * (1 / (1 - BETA_TWO**ADAM_STEP))
+    weight = weight * (1 - rate * WEIGHT_DECAY) - fixed_one / (jnp.sqrt(fixed_two) + ADAM_EPS)
     return (weight, moment, second)
 
 
-def adam_kernel(size, place, squares, early, early_other, late, late_other, *refs):
-    masters, firsts, seconds = refs[0:3], refs[3:6], refs[6:9]
-    news, new_firsts, new_seconds = refs[9:12], refs[12:15], refs[15:18]
-    copies, norm = refs[18:21], refs[21]
-    half = early.shape[0]
+def adam_chunks(size, half):
+    tall, across = gain_shape(size)
+    chunks = []
+    for side in range(2):
+        rows, ends = slice(4 * side * half, 4 * (side + 1) * half), slice(0, D)
+        parts = [
+            (slice((4 * side + k) * half, (4 * side + k + 1) * half), ends, 0,
+             slice(REST + D * k, REST + D * (k + 1)))
+            for k in range(4)
+        ]
+        chunks.append((1, side, rows, ends, parts))
+        rows = slice(side * half, (side + 1) * half)
+        parts = [
+            (rows, slice(0, QKV), 1, slice(0, QKV)),
+            (rows, slice(QKV, QKV + REST), 0, slice(0, REST)),
+        ]
+        chunks.append((0, side, rows, slice(0, QKV + REST), parts))
+    rows, lanes = slice(0, tall), slice(0, across)
+    chunks.append((2, 0, rows, lanes, [(rows, lanes, 1, slice(QKV, QKV + across))]))
+    return chunks
+
+
+def tiles(rows, lanes, source):
+    high, across = rows.stop - rows.start, lanes.stop - lanes.start
+    for row in range(0, high, 16):
+        tall = min(16, high - row)
+        for lane in range(0, across, D):
+            part = min(D, across - lane)
+            yield (
+                (slice(rows.start + row, rows.start + row + tall),
+                 slice(lanes.start + lane, lanes.start + lane + part)),
+                (slice(row, row + tall),
+                 slice(source.start + lane, source.start + lane + part)),
+            )
+
+
+def adam_kernel(size, place, squares, squares_other, early, early_other, late, late_other,
+                *refs):
+    states, outs, norm = [refs[k : k + 3] for k in (0, 3, 6)], refs[9:21], refs[21]
+    held, sems = refs[22:34], refs[34]
     same = place[0] == 0
-    grad_norm = jnp.sqrt(squares[0:1, 0:1])
-    norm[...] = jnp.broadcast_to(grad_norm, norm.shape)
+    grad_norm = jnp.sqrt(squares[0:1, 0:1] + squares_other[0:1, 0:1])
+    norm[...] = grad_norm
     factor = jnp.minimum(1.0, CLIP_LIMIT / (grad_norm + 1e-06))
-
-    def update(index, rows, lanes, grad, rate):
-        at = (rows, lanes)
-        found = adam_update(
-            masters[index][at], grad * factor, firsts[index][at], seconds[index][at], rate
-        )
-        news[index][at], new_firsts[index][at], new_seconds[index][at] = found
-        copies[index][at] = found[0].astype(BF)
-
-    for side in range(2):
-        use_own = same if side == 0 else jnp.logical_not(same)
-
-        def pick(own, other, lanes):
-            return jnp.where(use_own, own[:, lanes], other[:, lanes]).astype(F32)
-
-        rows = slice(side * half, (side + 1) * half)
-        update(0, rows, slice(0, QKV), pick(late, late_other, slice(0, QKV)), LEARN_RATE)
-        update(0, rows, slice(QKV, QKV + REST), pick(early, early_other, slice(0, REST)),
-               LEARN_RATE)
-        for part in range(4):
-            first = (4 * side + part) * half
-            lanes = slice(REST + D * part, REST + D * (part + 1))
-            update(1, slice(first, first + half), slice(0, D),
-                   pick(early, early_other, lanes), LEARN_RATE)
-    tall, across = gain_shape(size)
-    lanes = slice(QKV, QKV + across)
-    grad = jnp.where(same, late[:tall, lanes], late_other[:tall, lanes]).astype(F32)
-    update(2, slice(0, tall), slice(0, across), grad, GAIN_RATE)
+    copies, aligned = [], early.shape[0] % 16 == 0
+
+    def send(source, target):
+        copies.append(pltpu.make_async_copy(source, target, sems.at[len(copies)]))
+        copies[-1].start()
+
+    for index, side, rows, lanes, parts in adam_chunks(size, early.shape[0]):
+        rate = GAIN_RATE if index == 2 else LEARN_RATE
+        for part_rows, part_lanes, which, source in parts:
+            own, other = (late, late_other) if which else (early, early_other)
+            if side:
+                own, other = other, own
+            for here, there in tiles(part_rows, part_lanes, source):
+                grad = jnp.where(same, own[there].astype(F32), other[there].astype(F32))
+                weight, moment, second = (x[index][here] for x in states)
+                found = adam_update(weight, grad * factor, moment, second, rate)
+                for kind, value in enumerate((*found, found[0].astype(BF))):
+                    held[3 * kind + index][here] = value
+        if aligned:
+            for slot in range(index, 12, 3):
+                send(held[slot].at[rows, lanes], outs[slot].at[rows, lanes])
+    if not aligned:
+        for slot in range(12):
+            send(held[slot], outs[slot])
+    for copy in copies:
+        copy.wait()
 
 
 def adam(place, squares, grads, states, size):
@@ -708,25 +785,19 @@
     states = [x.reshape(flat) if x.ndim == 1 else x for x in states]
     shapes = [x.shape for x in states[:3]]
     count = sum(x.size for x in states[:3])
+    kinds = [(shape, F32) for shape in shapes] * 3 + [(shape, BF) for shape in shapes]
+    outside = pl.BlockSpec(memory_space=pl.ANY)
     return call(
         functools.partial(adam_kernel, size),
-        (squares, *grads, *states),
-        tuple(sds(x, F32) for x in shapes) * 3
-        + tuple(sds(x, BF) for x in shapes)
-        + (sds((8, LANES), F32),),
+        (*squares, *grads, *states),
+        tuple(sds(*kind) for kind in kinds) + (sds((1, 1), F32),),
         20 * count,
         28 * count,
         place=(place,),
-    )
-
-
-def adam_update(weight, grad, moment, second, rate):
-    moment = BETA_ONE * moment + (1 - BETA_ONE) * grad
-    second = BETA_TWO * second + (1 - BETA_TWO) * grad * grad
-    fixed_one = moment / (1 - BETA_ONE**ADAM_STEP)
-    fixed_two = second / (1 - BETA_TWO**ADAM_STEP)
-    weight = weight - rate * (fixed_one / (jnp.sqrt(fixed_two) + ADAM_EPS) + WEIGHT_DECAY * weight)
-    return (weight, moment, second)
+        out_specs=(outside,) * 12 + (pl.BlockSpec(memory_space=pltpu.VMEM),),
+        scratch=[pltpu.VMEM(*kind) for kind in kinds]
+        + [pltpu.SemaphoreType.DMA((4 * len(adam_chunks(size, grads[0].shape[0])),))],
+    )
 
 
 def body(
@@ -756,35 +827,48 @@
     low_mine = [rest] + [swap(rest, "wide", mask) for mask in range(1, high)]
     far[0], first_mine, *low_mine = tie(far[0], first_mine, *low_mine)
     first_other = swap(first_mine, "seg", 1)
+    far[high] = swap(far[0], "wide", high)
+    near, first_other = tie(far[0], first_other)
+    for mask in range(1, high):
+        far[mask] = swap(near, "wide", mask)
     queries_t, own_unit, weights_t, gains = start(place, own, first_mine, first_other, size)
 
-    for mask in [high, *range(1, high)]:
-        far[mask] = swap(far[0], "wide", mask)
-    high_mine = [swap(x, "wide", high) for x in low_mine]
-    low_other = [swap(x, "seg", 1) for x in low_mine]
-    for mask in range(1, high):
-        far[high + mask] = swap(far[high], "wide", mask)
+    high_mine = swap(jnp.stack(low_mine), "wide", high)
     order = [high, *range(1, high), *range(high + 1, size)]
     groups = [[0]] + [order[k : k + 2] for k in range(0, size - 1, 2)]
 
     carry = None
     saved, units = [], []
     for group in groups:
+        if len(saved) == 1:
+            carry[0], far[high], *low_mine = tie(carry[0], far[high], *low_mine)
+            low_other = [swap(x, "seg", 1) for x in low_mine]
+            for mask in range(1, high):
+                far[high + mask] = swap(far[high], "wide", mask)
         probs, keys_t, values_t, unit, tops, *carry = attend(
             [far[mask] for mask in group], queries_t, weights_t, gains, carry
         )
         saved.append((probs, keys_t, values_t, tops))
+        if len(saved) == 2:
+            carry[0], *low_other = tie(carry[0], *low_other)
         units.append(unit)
     accum, top = carry
-    accum, *high_mine = tie(accum, *high_mine)
-    high_other = [swap(x, "seg", 1) for x in high_mine]
-    rest_mine, rest_other = low_mine + high_mine, low_other + high_other
-
-    rest_all, down_all = unpack(place, rest_mine + rest_other, size)
-    (est_own, attended_t, inverse_total, branch_out, third, third_inverse, normed_two, slope,
-     hidden, ffn_out, out_rows) = dense_forward(own, accum, rest_all, down_all, gains)
-
-    errors, energy = error_energy(place, est_own, swap(est_own, "wide", size), targets[0])
+    accum, high_mine = tie(accum, high_mine)
+    high_other = swap(high_mine, "seg", 1)
+    pieces = (*low_mine, high_mine, *low_other, high_other)
+
+    rest_all, down_all = unpack(place, pieces, size)
+    started, own_parts, far_parts = (), [], []
+    for part in range(2):
+        *started, estimate = dense_forward(
+            part, own, accum, rest_all, down_all, gains, started
+        )
+        own_parts.append(estimate)
+        far_parts.append(swap(estimate, "wide", size))
+    (attended_t, inverse_total, branch_out, third, third_inverse, normed_two, slope, hidden,
+     ffn_out, out_rows) = started
+
+    errors, energy = error_energy(place, own_parts, far_parts, targets[0])
     energy = exchange(energy, size)
     seg_count = lax.axis_size("seg")
     (grad_est, grad_ffn, grad_pre, grad_branch, grad_attended_t, delta, late_gains,
@@ -807,28 +891,28 @@
         grads.append(grad_kv)
         if k == 0:
             grad_queries, early = tie(grad_queries, early)
-            early = scatter_step(early, size)
-    grad_queries, early = tie(grad_queries, early)
-    early = segment_step(early)
+            early = send_members(early, size)
     keep, send = finish(
         place, grad_queries, own_unit, weights_t, gains, late_gains, grads, units, size
     )
+    keep, send, *early = tie(keep, send, *early)
     late = core_step(keep, send)
+    early = segment_step(sum_low(early))
     late, loss = tie(late, loss)
     for mask in bits(seg_count):
         loss = loss + swap(loss, "seg", mask)
-    late = scatter_step(late, size)
+    late = sum_low(send_members(late, size))
     late, loss, early = tie(late, loss, early)
     early_other = swap(early, "seg", 1)
     late = segment_step(late)
     late_other = swap(late, "seg", 1)
 
     squares = square_sum(early, early_other, late, late_other)
-    squares = group_sum(place, exchange(squares, size))
-    squares = squares + swap(squares, "wide", size)
+    squares = branch_sum(place, squares, branch_parts(squares, size))
+    squares_other = swap(squares, "seg", 1)
     *updated, grad_norm = adam(
         place,
-        squares,
+        (squares, squares_other),
         (early, early_other, late, late_other),
         (wide_master, down_master, gain_master, wide_first, down_first, gain_first,
          wide_second, down_second, gain_second),
@@ -836,7 +920,7 @@
     )
     return (
         loss[0, 0],
-        grad_norm[0, 0],
+        grad_norm.reshape(()),
         *(x.reshape(-1) if k % 3 == 2 else x for k, x in enumerate(updated)),
     )
 

time: 144 us -> 139 us (0.965)
  waiting for transfers between devices: 47.3 us -> 37.2 us
  starting transfers between devices: 36.4 us -> 41.6 us
    ppermute x37 -> x33, waiting for transfers between devices: 47.3 us -> 34.7 us  [swap(): lax.ppermute(x, axis, [(i, i ^ mask) for i in range(lax.axis_size(axis))])]
    ppermute x0 -> x4, starting transfers between devices: none -> 4.14 us  [branch_parts(): found.append(lax.ppermute(values, ('seg', 'wide'), pairs))]
    ppermute x0 -> x4, waiting for transfers between devices: none -> 2.44 us  [branch_parts(): found.append(lax.ppermute(values, ('seg', 'wide'), pairs))]
    ppermute x37 -> x33, starting transfers between devices: 36.4 us -> 37.5 us  [swap(): lax.ppermute(x, axis, [(i, i ^ mask) for i in range(lax.axis_size(axis))])]
    pallas_call x17 -> x18, Pallas kernels: 53.5 us -> 54.1 us  [call(): pl.pallas_call(kernel, out_shape=out_shape, in_specs=[small] * len(place)...]
  transfers between devices with their start and end apart: 37 -> 37, of which waited for: 22 -> 19; matrix products, arithmetic and copies ran while one was open for 1% -> 1% of each run, Pallas kernels for 24% -> 28%
where the time goes in v4:
time: 139 us
  Pallas kernels  54.1 us (39%)
  starting transfers between devices  41.6 us (30%)
  waiting for transfers between devices  37.2 us (27%)
  local copies, waits for them, and re-layouts  3.73 us (3%)
    pallas_call x18, Pallas kernels, call(): pl.pallas_call(kernel, out_shape=out_shape, in_specs=[small] * len(place)...  54.1 us
    ppermute x33, starting transfers between devices, swap(): lax.ppermute(x, axis, [(i, i ^ mask) for i in range(lax.axis_size(axis))])  37.5 us
    ppermute x33, waiting for transfers between devices, swap(): lax.ppermute(x, axis, [(i, i ^ mask) for i in range(lax.axis_size(axis))])  34.7 us
    ppermute x4, starting transfers between devices, branch_parts(): found.append(lax.ppermute(values, ('seg', 'wide'), pairs))  4.14 us
    unnamed x30, local copies, waits for them, and re-layouts  3.1 us
  transfers between devices with their start and end apart: 37, of which 19 were waited for; matrix products, arithmetic and copies ran while one was open for 1% of the time, Pallas kernels for 28%

profile of v4, /device:TPU:0, one launch (start us, length us, event | category | flops | bytes accessed | tf_op | source)
XLA Modules:
  0.0 138.9 jit_solution(685420652813224426)
XLA Ops:
  0.6 4.1 %collective-permute-start = (bf16[512,384]{1,0:T(8,128)(2,1)}, bf16[512,384]{1,0:T(8,128)(2,1)S(1)}, u32[]{:S(2)}, u32[]{:S(2)}) collective-permute-start(bf16[512,384]{1,0:T(8,128)(2,1)} %bitcast.40), channel_id=1, source_target_pairs={{0,4},{1,5},{2,6},{3,7},{4,0},{5,1},{6,2},{7,3},{8,12},{9,13},{10,... | collective-permute-start | bytes 1179656 | tf_op jit(solution)/shard_map/ppermute | solution.py:41
  8.5 2.6 %collective-permute-start.3 = (bf16[48,1280]{1,0:T(8,128)(2,1)S(1)}, bf16[48,1280]{1,0:T(8,128)(2,1)S(1)}, u32[]{:S(2)}, u32[]{:S(2)}) collective-permute-start(bf16[48,1280]{1,0:T(8,128)(2,1)S(1)} %get-tuple-element.129), channel_id=1, source_target_pairs={{0,3},{1,2},{2,1},{3,0},{4,7},{5,6},{6,5},{7,4},{8,11},{9,10},{10,... | collective-permute-start | bytes 368648 | tf_op jit(solution)/shard_map/ppermute | solution.py:41
  13.6 3.6 %collective-permute-done.3 = bf16[48,1280]{1,0:T(8,128)(2,1)S(1)} collective-permute-done((bf16[48,1280]{1,0:T(8,128)(2,1)S(1)}, bf16[48,1280]{1,0:T(8,128)(2,1)S(1)}, u32[]{:S(2)}, u32[]{:S(2)}) %collective-permute-start.3) | collective-permute-done | bytes 122912 | tf_op jit(solution)/shard_map/ppermute | solution.py:41
  17.2 7.0 %collective-permute-done.2 = bf16[48,1280]{1,0:T(8,128)(2,1)S(1)} collective-permute-done((bf16[48,1280]{1,0:T(8,128)(2,1)S(1)}, bf16[48,1280]{1,0:T(8,128)(2,1)S(1)}, u32[]{:S(2)}, u32[]{:S(2)}) %collective-permute-start.2) | collective-permute-done | bytes 122912 | tf_op jit(solution)/shard_map/ppermute | solution.py:41
  24.4 2.9 %collective-permute-start.6 = (bf16[512,384]{1,0:T(8,128)(2,1)S(1)}, bf16[512,384]{1,0:T(8,128)(2,1)S(1)}, u32[]{:S(2)}, u32[]{:S(2)}) collective-permute-start(bf16[512,384]{1,0:T(8,128)(2,1)S(1)} %collective-permute-done.refs_3_), channel_id=1, source_target_pairs={{0,2},{1,3},{2,0},{3,1},{4,6},{5,7},{6,4},{7,5},{8,10},{9,11},{10,... | collective-permute-start | bytes 1179656 | tf_op jit(solution)/shard_map/ppermute | solution.py:41
  31.1 3.6 %shard_map.229 = (bf16[1,8,512,512]{3,2,1,0:T(8,128)(2,1)S(1)}, bf16[1,384,512]{2,1,0:T(8,128)(2,1)S(1)}, bf16[1,384,512]{2,1,0:T(8,128)(2,1)S(1)}, bf16[1,512,3...) custom-call(bf16[384,512]{1,0:T(8,128)(2,1)S(1)} %get-tuple-element.134.refs_0_., ...), custom_call_target="tpu_custom_call" | custom-call | flops 2315255808 | bytes 4194304 | tf_op jit(solution)/shard_map/pallas_call | solution.py:64
  34.7 2.6 %collective-permute-done.6.refs_3_ = bf16[512,384]{1,0:T(8,128)(2,1)S(1)} collective-permute-done((bf16[512,384]{1,0:T(8,128)(2,1)S(1)}, bf16[512,384]{1,0:T(8,128)(2,1)S(1)}, u32[]{:S(2)}, u32[]{:S(2)}) %collective-permute-start.6) | collective-permute-done | bytes 393248 | tf_op jit(solution)/shard_map/ppermute | solution.py:41
  38.6 7.6 %shard_map.230 = (bf16[2,8,512,512]{3,2,1,0:T(8,128)(2,1)S(1)}, bf16[2,384,512]{2,1,0:T(8,128)(2,1)S(1)}, bf16[2,384,512]{2,1,0:T(8,128)(2,1)S(1)}, bf16[2,512,3...) custom-call(bf16[384,512]{1,0:T(8,128)(2,1)S(1)} %get-tuple-element.134.refs_0_., ...), custom_call_target="tpu_custom_call" | custom-call | flops 4630511616 | bytes 8388608 | tf_op jit(solution)/shard_map/pallas_call | solution.py:64
  46.3 2.6 %collective-permute-done.7.refs_3_ = bf16[512,384]{1,0:T(8,128)(2,1)S(1)} collective-permute-done((bf16[512,384]{1,0:T(8,128)(2,1)S(1)}, bf16[512,384]{1,0:T(8,128)(2,1)S(1)}, u32[]{:S(2)}, u32[]{:S(2)}) %collective-permute-start.7) | collective-permute-done | bytes 393248 | tf_op jit(solution)/shard_map/ppermute | solution.py:41
  48.9 3.7 %shard_map.231 = (bf16[1,8,512,512]{3,2,1,0:T(8,128)(2,1)S(1)}, bf16[1,384,512]{2,1,0:T(8,128)(2,1)S(1)}, bf16[1,384,512]{2,1,0:T(8,128)(2,1)S(1)}, bf16[1,512,3...) custom-call(bf16[384,512]{1,0:T(8,128)(2,1)S(1)} %get-tuple-element.134.refs_0_., ...), custom_call_target="tpu_custom_call" | custom-call | flops 2315255808 | bytes 4194304 | tf_op jit(solution)/shard_map/pallas_call | solution.py:64
  52.7 2.1 %collective-permute-done.12.refs_5_ = bf16[2,48,3584]{2,1,0:T(8,128)(2,1)S(1)} collective-permute-done((bf16[2,48,3584]{2,1,0:T(8,128)(2,1)S(1)}, bf16[2,48,3584]{2,1,0:T(8,128)(2,1)S(1)}, u32[]{:S(2)}, u32[]{:S(2)}) %collective-permute-start.12) | collective-permute-done | bytes 688160 | tf_op jit(solution)/shard_map/ppermute | solution.py:41
  55.7 2.4 %shard_map.233 = (f32[384,512]{1,0:T(8,128)S(1)}, f32[8,512]{1,0:T(8,128)S(1)}, f32[512,384]{1,0:T(8,128)S(1)}, f32[512,384]{1,0:T(8,128)S(1)}, f32[512,1]{1,0:T...) custom-call(bf16[512,384]{1,0:T(8,128)(2,1)S(1)} %bitcast.42, ...), custom_call_target="tpu_custom_call" | custom-call | flops 704643072 | bytes 3145728 | tf_op jit(solution)/shard_map/pallas_call | solution.py:64
  60.2 2.3 %collective-permute-start.14 = (bf16[128,128]{1,0:T(8,128)(2,1)S(1)}, bf16[128,128]{1,0:T(8,128)(2,1)S(1)}, u32[]{:S(2)}, u32[]{:S(2)}) collective-permute-start(bf16[128,128]{1,0:T(8,128)(2,1)S(1)} %get-tuple-element.171.refs_1_), channel_id=1, source_target_pairs={{0,4},{1,5},{2,6},{3,7},{4,0},{5,1},{6,2},{7,3},{8,12},{9,13},{10,... | collective-permute-start | bytes 98312 | tf_op jit(solution)/shard_map/ppermute | solution.py:41
  62.5 4.9 %collective-permute-done.14.refs_3_ = bf16[128,128]{1,0:T(8,128)(2,1)S(1)} collective-permute-done((bf16[128,128]{1,0:T(8,128)(2,1)S(1)}, bf16[128,128]{1,0:T(8,128)(2,1)S(1)}, u32[]{:S(2)}, u32[]{:S(2)}) %collective-permute-start.14) | collective-permute-done | bytes 32800 | tf_op jit(solution)/shard_map/ppermute | solution.py:41
  73.7 3.3 %shard_map.236 = (bf16[512,128]{1,0:T(8,128)(2,1)S(1)}, bf16[512,384]{1,0:T(8,128)(2,1)S(1)}, bf16[512,1536]{1,0:T(8,128)(2,1)S(1)}, bf16[512,384]{1,0:T(8,128)(...) custom-call(s32[2]{0:T(128)S(1)} %pad_add_fusion.place, ...), custom_call_target="tpu_custom_call" | custom-call | flops 1409286144 | bytes 6291456 | tf_op jit(solution)/shard_map/pallas_call | solution.py:64
  77.0 2.5 %shard_map.237 = (bf16[4,48,3584]{2,1,0:T(8,128)(2,1)S(1)}, bf16[4,48,3584]{2,1,0:T(8,128)(2,1)S(1)}) custom-call(s32[2]{0:T(128)S(1)} %pad_add_fusion.place, bf16[512,128]{1,0:T(8,128)(2,1)S(1)} %get-tuple-element.184.grad_est, bf16[512,384]{1,0:T(8,128)(2,1)S(1)} %get-tuple-element.185.grad_ffn, bf16[512,1536]{1,0:T(8,128)(2,1)S(1)} %get-tuple-element.186.grad_pre, ...), custom_call_target="tpu_custom_call" | custom-call | flops 1409286144 | bytes 6291456 | tf_op jit(solution)/shard_map/pallas_call | solution.py:64
  79.6 4.6 %shard_map.238 = (f32[384,512]{1,0:T(8,128)S(1)}, bf16[1,768,512]{2,1,0:T(8,128)(2,1)S(1)}) custom-call(bf16[1,8,512,512]{3,2,1,0:T(8,128)(2,1)S(1)} %get-tuple-element.198.probs, bf16[1,384,512]{2,1,0:T(8,128)(2,1)S(1)} %get-tuple-element.199.keys_t, bf16[1,384,512]{2,1,0:T(8,128)(2,1)S(1)} %get-tuple-element.200.values_t, ...), custom_call_target="tpu_custom_call" | custom-call | flops 4026531840 | bytes 4194304 | tf_op jit(solution)/shard_map/pallas_call | solution.py:64
  88.2 8.9 %shard_map.239 = (f32[384,512]{1,0:T(8,128)S(1)}, bf16[2,768,512]{2,1,0:T(8,128)(2,1)S(1)}) custom-call(bf16[2,8,512,512]{3,2,1,0:T(8,128)(2,1)S(1)} %get-tuple-element.194.probs, bf16[2,384,512]{2,1,0:T(8,128)(2,1)S(1)} %get-tuple-element.195.keys_t, bf16[2,384,512]{2,1,0:T(8,128)(2,1)S(1)} %get-tuple-element.196.values_t, ...), custom_call_target="tpu_custom_call" | custom-call | flops 8053063680 | bytes 8388608 | tf_op jit(solution)/shard_map/pallas_call | solution.py:64
  97.1 4.4 %shard_map.240 = (f32[384,512]{1,0:T(8,128)S(1)}, bf16[1,768,512]{2,1,0:T(8,128)(2,1)S(1)}) custom-call(bf16[1,8,512,512]{3,2,1,0:T(8,128)(2,1)S(1)} %get-tuple-element.149.probs, bf16[1,384,512]{2,1,0:T(8,128)(2,1)S(1)} %get-tuple-element.150.keys_t, bf16[1,384,512]{2,1,0:T(8,128)(2,1)S(1)} %get-tuple-element.151.values_t, ...), custom_call_target="tpu_custom_call" | custom-call | flops 4026531840 | bytes 4194304 | tf_op jit(solution)/shard_map/pallas_call | solution.py:64
  101.5 3.1 %shard_map.241 = (bf16[4,48,1280]{2,1,0:T(8,128)(2,1)S(1)}, bf16[4,48,1280]{2,1,0:T(8,128)(2,1)S(1)}) custom-call(s32[2]{0:T(128)S(1)} %pad_add_fusion.place, f32[384,512]{1,0:T(8,128)S(1)} %get-tuple-element.207.grad_queries, bf16[512,384]{1,0:T(8,128)(2,1)S(1)} %get-tuple-element.208.own_unit, bf16[1152,384]{1,0:T(8,128)(2,1)S(1)} %get-tuple-element.135.refs_1_.weights_t, ...), custom_call_target="tpu_custom_call" | custom-call | flops 1811939328 | bytes 1572864 | tf_op jit(solution)/shard_map/pallas_call | solution.py:64
  112.1 3.4 %collective-permute-done.28 = bf16[48,3584]{1,0:T(8,128)(2,1)S(1)} collective-permute-done((bf16[48,3584]{1,0:T(8,128)(2,1)S(1)}, bf16[48,3584]{1,0:T(8,128)(2,1)S(1)}, u32[]{:S(2)}, u32[]{:S(2)}) %collective-permute-start.28) | collective-permute-done | bytes 344096 | tf_op jit(solution)/shard_map/ppermute | solution.py:41
  118.1 3.4 %collective-permute-done.30 = bf16[48,1280]{1,0:T(8,128)(2,1)S(1)} collective-permute-done((bf16[48,1280]{1,0:T(8,128)(2,1)S(1)}, bf16[48,1280]{1,0:T(8,128)(2,1)S(1)}, u32[]{:S(2)}, u32[]{:S(2)}) %collective-permute-start.30) | collective-permute-done | bytes 122912 | tf_op jit(solution)/shard_map/ppermute | solution.py:41
  130.3 3.1 %collective-permute-start.36 = (f32[8,128]{1,0:T(8,128)S(1)}, f32[8,128]{1,0:T(8,128)S(1)}, u32[]{:S(2)}, u32[]{:S(2)}) collective-permute-start(f32[8,128]{1,0:T(8,128)S(1)} %shard_map.243.squares), channel_id=1, source_target_pairs={{0,8},{8,0},{16,24},{24,16},{1,9},{9,1},{17,25},{25,17},{2,10},{10... | collective-permute-start | bytes 12296 | tf_op jit(solution)/shard_map/ppermute | solution.py:41
  134.3 4.4 %shard_map.244 = (f32[96,3200]{1,0:T(8,128)}, f32[384,384]{1,0:T(8,128)}, f32[6,128]{1,0:T(8,128)}, f32[96,3200]{1,0:T(8,128)}, f32[384,384]{1,0:T(8,128)}, /*in...) custom-call(s32[2]{0:T(128)S(1)} %pad_add_fusion.place, ...), custom_call_target="tpu_custom_call" | custom-call | flops 9108480 | bytes 12751872 | tf_op jit(solution)/shard_map/pallas_call | solution.py:64
  (113 shorter events, 44.5 us)
Async XLA Ops:
  0.6 23.8 %collective-permute-start = (bf16[512,384]{1,0:T(8,128)(2,1)}, bf16[512,384]{1,0:T(8,128)(2,1)S(1)}, u32[]{:S(2)}, u32[]{:S(2)}) collective-permute-start(bf16[512,384]{1,0:T(8,128)(2,1)} %bitcast.40), channel_id=1, source_target_pairs={{0,4},{1,5},{2,6},{3,7},{4,0},{5,1},{6,2},{7,3},{8,12},{9,13},{10,... | collective-permute-start | bytes 1179656 | tf_op jit(solution)/shard_map/ppermute | solution.py:41
  8.5 8.7 %collective-permute-start.3 = (bf16[48,1280]{1,0:T(8,128)(2,1)S(1)}, bf16[48,1280]{1,0:T(8,128)(2,1)S(1)}, u32[]{:S(2)}, u32[]{:S(2)}) collective-permute-start(bf16[48,1280]{1,0:T(8,128)(2,1)S(1)} %get-tuple-element.129), channel_id=1, source_target_pairs={{0,3},{1,2},{2,1},{3,0},{4,7},{5,6},{6,5},{7,4},{8,11},{9,10},{10,... | collective-permute-start | bytes 368648 | tf_op jit(solution)/shard_map/ppermute | solution.py:41
  11.1 13.1 %collective-permute-start.2 = (bf16[48,1280]{1,0:T(8,128)(2,1)S(1)}, bf16[48,1280]{1,0:T(8,128)(2,1)S(1)}, u32[]{:S(2)}, u32[]{:S(2)}) collective-permute-start(bf16[48,1280]{1,0:T(8,128)(2,1)S(1)} %get-tuple-element.129), channel_id=1, source_target_pairs={{0,2},{1,3},{2,0},{3,1},{4,6},{5,7},{6,4},{7,5},{8,10},{9,11},{10,... | collective-permute-start | bytes 368648 | tf_op jit(solution)/shard_map/ppermute | solution.py:41
  11.6 12.7 %collective-permute-start.1 = (bf16[48,1280]{1,0:T(8,128)(2,1)S(1)}, bf16[48,1280]{1,0:T(8,128)(2,1)S(1)}, u32[]{:S(2)}, u32[]{:S(2)}) collective-permute-start(bf16[48,1280]{1,0:T(8,128)(2,1)S(1)} %get-tuple-element.129), channel_id=1, source_target_pairs={{0,1},{1,0},{2,3},{3,2},{4,5},{5,4},{6,7},{7,6},{8,9},{9,8},{10,11... | collective-permute-start | bytes 368648 | tf_op jit(solution)/shard_map/ppermute | solution.py:41
  12.1 12.4 %collective-permute-start.4 = (bf16[48,3584]{1,0:T(8,128)(2,1)S(1)}, bf16[48,3584]{1,0:T(8,128)(2,1)S(1)}, u32[]{:S(2)}, u32[]{:S(2)}) collective-permute-start(bf16[48,3584]{1,0:T(8,128)(2,1)S(1)} %get-tuple-element.145.refs_0_), channel_id=1, source_target_pairs={{0,1},{1,0},{2,3},{3,2},{4,5},{5,4},{6,7},{7,6},{8,9},{9,8},{10,11... | collective-permute-start | bytes 1032200 | tf_op jit(solution)/shard_map/ppermute | solution.py:41
  24.4 12.9 %collective-permute-start.6 = (bf16[512,384]{1,0:T(8,128)(2,1)S(1)}, bf16[512,384]{1,0:T(8,128)(2,1)S(1)}, u32[]{:S(2)}, u32[]{:S(2)}) collective-permute-start(bf16[512,384]{1,0:T(8,128)(2,1)S(1)} %collective-permute-done.refs_3_), channel_id=1, source_target_pairs={{0,2},{1,3},{2,0},{3,1},{4,6},{5,7},{6,4},{7,5},{8,10},{9,11},{10,... | collective-permute-start | bytes 1179656 | tf_op jit(solution)/shard_map/ppermute | solution.py:41
  27.4 11.2 %collective-permute-start.8 = (bf16[512,384]{1,0:T(8,128)(2,1)S(1)}, bf16[512,384]{1,0:T(8,128)(2,1)S(1)}, u32[]{:S(2)}, u32[]{:S(2)}) collective-permute-start(bf16[512,384]{1,0:T(8,128)(2,1)S(1)} %collective-permute-done.refs_3_), channel_id=1, source_target_pairs={{0,1},{1,0},{2,3},{3,2},{4,5},{5,4},{6,7},{7,6},{8,9},{9,8},{10,11... | collective-permute-start | bytes 1179656 | tf_op jit(solution)/shard_map/ppermute | solution.py:41
  27.9 24.6 %collective-permute-start.11 = (bf16[2,48,3584]{2,1,0:T(8,128)(2,1)S(1)}, bf16[2,48,3584]{2,1,0:T(8,128)(2,1)S(1)}, u32[]{:S(2)}, u32[]{:S(2)}) collective-permute-start(bf16[2,48,3584]{2,1,0:T(8,128)(2,1)S(1)} %pad_maximum_fusion), channel_id=1, source_target_pairs={{0,2},{1,3},{2,0},{3,1},{4,6},{5,7},{6,4},{7,5},{8,10},{9,11},{10,... | collective-permute-start | bytes 2064392 | tf_op jit(solution)/shard_map/ppermute | solution.py:41
  37.3 8.9 %collective-permute-start.9 = (bf16[48,3584]{1,0:T(8,128)(2,1)S(1)}, bf16[48,3584]{1,0:T(8,128)(2,1)S(1)}, u32[]{:S(2)}, u32[]{:S(2)}) collective-permute-start(bf16[48,3584]{1,0:T(8,128)(2,1)S(1)} %get-tuple-element.145.refs_0_), channel_id=1, source_target_pairs={{0,8},{8,0},{16,24},{24,16},{1,9},{9,1},{17,25},{25,17},{2,10},{10... | collective-permute-start | bytes 1032200 | tf_op jit(solution)/shard_map/ppermute | solution.py:41
  37.3 9.0 %collective-permute-start.10 = (bf16[48,3584]{1,0:T(8,128)(2,1)S(1)}, bf16[48,3584]{1,0:T(8,128)(2,1)S(1)}, u32[]{:S(2)}, u32[]{:S(2)}) collective-permute-start(bf16[48,3584]{1,0:T(8,128)(2,1)S(1)} %collective-permute-done.4.refs_1_), channel_id=1, source_target_pairs={{0,8},{8,0},{16,24},{24,16},{1,9},{9,1},{17,25},{25,17},{2,10},{10... | collective-permute-start | bytes 1032200 | tf_op jit(solution)/shard_map/ppermute | solution.py:41
  37.8 11.0 %collective-permute-start.7 = (bf16[512,384]{1,0:T(8,128)(2,1)S(1)}, bf16[512,384]{1,0:T(8,128)(2,1)S(1)}, u32[]{:S(2)}, u32[]{:S(2)}) collective-permute-start(bf16[512,384]{1,0:T(8,128)(2,1)S(1)} %collective-permute-done.6.refs_3_), channel_id=1, source_target_pairs={{0,1},{1,0},{2,3},{3,2},{4,5},{5,4},{6,7},{7,6},{8,9},{9,8},{10,11... | collective-permute-start | bytes 1179656 | tf_op jit(solution)/shard_map/ppermute | solution.py:41
  58.1 9.3 %collective-permute-start.13 = (bf16[384,128]{1,0:T(8,128)(2,1)S(1)}, bf16[384,128]{1,0:T(8,128)(2,1)S(1)}, u32[]{:S(2)}, u32[]{:S(2)}) collective-permute-start(bf16[384,128]{1,0:T(8,128)(2,1)S(1)} %get-tuple-element.160.refs_0_), channel_id=1, source_target_pairs={{0,4},{1,5},{2,6},{3,7},{4,0},{5,1},{6,2},{7,3},{8,12},{9,13},{10,... | collective-permute-start | bytes 294920 | tf_op jit(solution)/shard_map/ppermute | solution.py:41
  60.2 7.2 %collective-permute-start.14 = (bf16[128,128]{1,0:T(8,128)(2,1)S(1)}, bf16[128,128]{1,0:T(8,128)(2,1)S(1)}, u32[]{:S(2)}, u32[]{:S(2)}) collective-permute-start(bf16[128,128]{1,0:T(8,128)(2,1)S(1)} %get-tuple-element.171.refs_1_), channel_id=1, source_target_pairs={{0,4},{1,5},{2,6},{3,7},{4,0},{5,1},{6,2},{7,3},{8,12},{9,13},{10,... | collective-permute-start | bytes 98312 | tf_op jit(solution)/shard_map/ppermute | solution.py:41
  79.5 4.7 %collective-permute-start.18 = (bf16[4,48,3584]{2,1,0:T(8,128)(2,1)S(1)}, bf16[4,48,3584]{2,1,0:T(8,128)(2,1)S(1)}, u32[]{:S(2)}, u32[]{:S(2)}) collective-permute-start(bf16[4,48,3584]{2,1,0:T(8,128)(2,1)S(1)} %get-tuple-element.204), channel_id=1, source_target_pairs={{0,8},{8,0},{16,24},{24,16},{1,9},{9,1},{17,25},{25,17},{2,10},{10... | collective-permute-start | bytes 4128776 | tf_op jit(solution)/shard_map/ppermute | solution.py:41
  84.7 19.9 %collective-permute-start.21 = (bf16[48,3584]{1,0:T(8,128)(2,1)S(1)}, bf16[48,3584]{1,0:T(8,128)(2,1)S(1)}, u32[]{:S(2)}, u32[]{:S(2)}) collective-permute-start(bf16[48,3584]{1,0:T(8,128)(2,1)S(1)} %get-tuple-element.244), channel_id=1, source_target_pairs={{0,3},{1,2},{2,1},{3,0},{4,7},{5,6},{6,5},{7,4},{8,11},{9,10},{10,... | collective-permute-start | bytes 1032200 | tf_op jit(solution)/shard_map/ppermute | solution.py:41
  85.7 18.9 %collective-permute-start.20 = (bf16[48,3584]{1,0:T(8,128)(2,1)S(1)}, bf16[48,3584]{1,0:T(8,128)(2,1)S(1)}, u32[]{:S(2)}, u32[]{:S(2)}) collective-permute-start(bf16[48,3584]{1,0:T(8,128)(2,1)S(1)} %get-tuple-element.245), channel_id=1, source_target_pairs={{0,2},{1,3},{2,0},{3,1},{4,6},{5,7},{6,4},{7,5},{8,10},{9,11},{10,... | collective-permute-start | bytes 1032200 | tf_op jit(solution)/shard_map/ppermute | solution.py:41
  87.7 16.9 %collective-permute-start.19 = (bf16[48,3584]{1,0:T(8,128)(2,1)S(1)}, bf16[48,3584]{1,0:T(8,128)(2,1)S(1)}, u32[]{:S(2)}, u32[]{:S(2)}) collective-permute-start(bf16[48,3584]{1,0:T(8,128)(2,1)S(1)} %get-tuple-element.246), channel_id=1, source_target_pairs={{0,1},{1,0},{2,3},{3,2},{4,5},{5,4},{6,7},{7,6},{8,9},{9,8},{10,11... | collective-permute-start | bytes 1032200 | tf_op jit(solution)/shard_map/ppermute | solution.py:41
  104.9 10.6 %collective-permute-start.28 = (bf16[48,3584]{1,0:T(8,128)(2,1)S(1)}, bf16[48,3584]{1,0:T(8,128)(2,1)S(1)}, u32[]{:S(2)}, u32[]{:S(2)}) collective-permute-start(bf16[48,3584]{1,0:T(8,128)(2,1)S(1)} %add_convert_fusion.3), channel_id=1, source_target_pairs={{0,16},{8,24},{16,0},{24,8},{1,17},{9,25},{17,1},{25,9},{2,18},{10... | collective-permute-start | bytes 1032200 | tf_op jit(solution)/shard_map/ppermute | solution.py:41
  106.9 8.7 %collective-permute-start.23 = (bf16[48,1280]{1,0:T(8,128)(2,1)S(1)}, bf16[48,1280]{1,0:T(8,128)(2,1)S(1)}, u32[]{:S(2)}, u32[]{:S(2)}) collective-permute-start(bf16[48,1280]{1,0:T(8,128)(2,1)S(1)} %get-tuple-element.248), channel_id=1, source_target_pairs={{0,1},{1,0},{2,3},{3,2},{4,5},{5,4},{6,7},{7,6},{8,9},{9,8},{10,11... | collective-permute-start | bytes 368648 | tf_op jit(solution)/shard_map/ppermute | solution.py:41
  108.5 7.1 %collective-permute-start.25 = (bf16[48,1280]{1,0:T(8,128)(2,1)S(1)}, bf16[48,1280]{1,0:T(8,128)(2,1)S(1)}, u32[]{:S(2)}, u32[]{:S(2)}) collective-permute-start(bf16[48,1280]{1,0:T(8,128)(2,1)S(1)} %get-tuple-element.249), channel_id=1, source_target_pairs={{0,3},{1,2},{2,1},{3,0},{4,7},{5,6},{6,5},{7,4},{8,11},{9,10},{10,... | collective-permute-start | bytes 368648 | tf_op jit(solution)/shard_map/ppermute | solution.py:41
  108.6 7.8 %collective-permute-start.24 = (bf16[48,1280]{1,0:T(8,128)(2,1)S(1)}, bf16[48,1280]{1,0:T(8,128)(2,1)S(1)}, u32[]{:S(2)}, u32[]{:S(2)}) collective-permute-start(bf16[48,1280]{1,0:T(8,128)(2,1)S(1)} %get-tuple-element.250), channel_id=1, source_target_pairs={{0,2},{1,3},{2,0},{3,1},{4,6},{5,7},{6,4},{7,5},{8,10},{9,11},{10,... | collective-permute-start | bytes 368648 | tf_op jit(solution)/shard_map/ppermute | solution.py:41
  110.6 5.0 %collective-permute-start.27 = (f32[8,128]{1,0:T(8,128)S(1)}, f32[8,128]{1,0:T(8,128)S(1)}, u32[]{:S(2)}, u32[]{:S(2)}) collective-permute-start(f32[8,128]{1,0:T(8,128)S(1)} %add.50), channel_id=1, source_target_pairs={{0,16},{8,24},{16,0},{24,8},{1,17},{9,25},{17,1},{25,9},{2,18},{10... | collective-permute-start | bytes 12296 | tf_op jit(solution)/shard_map/ppermute | solution.py:41
  116.5 4.9 %collective-permute-start.30 = (bf16[48,1280]{1,0:T(8,128)(2,1)S(1)}, bf16[48,1280]{1,0:T(8,128)(2,1)S(1)}, u32[]{:S(2)}, u32[]{:S(2)}) collective-permute-start(bf16[48,1280]{1,0:T(8,128)(2,1)S(1)} %fusion.2), channel_id=1, source_target_pairs={{0,16},{8,24},{16,0},{24,8},{1,17},{9,25},{17,1},{25,9},{2,18},{10... | collective-permute-start | bytes 368648 | tf_op jit(solution)/shard_map/ppermute | solution.py:41
  118.1 4.8 %collective-permute-start.29 = (bf16[48,3584]{1,0:T(8,128)(2,1)S(1)}, bf16[48,3584]{1,0:T(8,128)(2,1)S(1)}, u32[]{:S(2)}, u32[]{:S(2)}) collective-permute-start(bf16[48,3584]{1,0:T(8,128)(2,1)S(1)} %add_convert_fusion.2.refs_0_.early), channel_id=1, source_target_pairs={{0,8},{8,0},{16,24},{24,16},{1,9},{9,1},{17,25},{25,17},{2,10},{10... | collective-permute-start | bytes 1032200 | tf_op jit(solution)/shard_map/ppermute | solution.py:41
  (28 other events, 318.0 us)

commit v5 on v4

--- a/solution.py
+++ b/solution.py
@@ -240,8 +240,8 @@
             sds((64 * HEADS, tokens), F32),
             sds((HEADS, tokens), F32),
         ),
-        count * (4 * rows * tokens * D * 5 + 4 * rows * D * D),
-        count * (HEADS * rows * tokens * 2),
+        count * rows * tokens * D,
+        count * rows * tokens,
         scratch=[pltpu.VMEM((count, rows, D), BF)],
     )
 
@@ -828,9 +828,8 @@
     far[0], first_mine, *low_mine = tie(far[0], first_mine, *low_mine)
     first_other = swap(first_mine, "seg", 1)
     far[high] = swap(far[0], "wide", high)
-    near, first_other = tie(far[0], first_other)
     for mask in range(1, high):
-        far[mask] = swap(near, "wide", mask)
+        far[mask] = swap(far[0], "wide", mask)
     queries_t, own_unit, weights_t, gains = start(place, own, first_mine, first_other, size)
 
     high_mine = swap(jnp.stack(low_mine), "wide", high)
@@ -841,7 +840,9 @@
     saved, units = [], []
     for group in groups:
         if len(saved) == 1:
-            carry[0], far[high], *low_mine = tie(carry[0], far[high], *low_mine)
+            near = [far[mask] for mask in range(1, high)]
+            carry[0], far[high], near, *low_mine = tie(carry[0], far[high], near, *low_mine)
+            far.update(zip(range(1, high), near))
             low_other = [swap(x, "seg", 1) for x in low_mine]
             for mask in range(1, high):
                 far[high + mask] = swap(far[high], "wide", mask)

time: 139 us -> 138 us (level)
  transfers between devices with their start and end apart: 37 -> 37, of which waited for: 19 -> 18; matrix products, arithmetic and copies ran while one was open for 1% -> 1% of each run, Pallas kernels for 28% -> 28%
where the time goes in v5:
time: 138 us
  Pallas kernels  54.2 us (39%)
  starting transfers between devices  40.8 us (30%)
  waiting for transfers between devices  36.7 us (27%)
  local copies, waits for them, and re-layouts  3.73 us (3%)
    pallas_call x18, Pallas kernels, call(): pl.pallas_call(kernel, out_shape=out_shape, in_specs=[small] * len(place)...  54.2 us
    ppermute x33, starting transfers between devices, swap(): lax.ppermute(x, axis, [(i, i ^ mask) for i in range(lax.axis_size(axis))])  36.7 us
    ppermute x33, waiting for transfers between devices, swap(): lax.ppermute(x, axis, [(i, i ^ mask) for i in range(lax.axis_size(axis))])  34.3 us
    ppermute x4, starting transfers between devices, branch_parts(): found.append(lax.ppermute(values, ('seg', 'wide'), pairs))  4.14 us
    unnamed x30, local copies, waits for them, and re-layouts  3.1 us
  transfers between devices with their start and end apart: 37, of which 18 were waited for; matrix products, arithmetic and copies ran while one was open for 1% of the time, Pallas kernels for 28%

profile of v5, /device:TPU:0, one launch (start us, length us, event | category | flops | bytes accessed | tf_op | source)
XLA Modules:
  0.0 137.8 jit_solution(803390632994644207)
XLA Ops:
  0.6 4.1 %collective-permute-start = (bf16[512,384]{1,0:T(8,128)(2,1)}, bf16[512,384]{1,0:T(8,128)(2,1)S(1)}, u32[]{:S(2)}, u32[]{:S(2)}) collective-permute-start(bf16[512,384]{1,0:T(8,128)(2,1)} %bitcast.40), channel_id=1, source_target_pairs={{0,4},{1,5},{2,6},{3,7},{4,0},{5,1},{6,2},{7,3},{8,12},{9,13},{10,... | collective-permute-start | bytes 1179656 | tf_op jit(solution)/shard_map/ppermute | solution.py:41
  8.5 2.6 %collective-permute-start.3 = (bf16[48,1280]{1,0:T(8,128)(2,1)S(1)}, bf16[48,1280]{1,0:T(8,128)(2,1)S(1)}, u32[]{:S(2)}, u32[]{:S(2)}) collective-permute-start(bf16[48,1280]{1,0:T(8,128)(2,1)S(1)} %get-tuple-element.128), channel_id=1, source_target_pairs={{0,3},{1,2},{2,1},{3,0},{4,7},{5,6},{6,5},{7,4},{8,11},{9,10},{10,... | collective-permute-start | bytes 368648 | tf_op jit(solution)/shard_map/ppermute | solution.py:41
  13.6 3.6 %collective-permute-done.3 = bf16[48,1280]{1,0:T(8,128)(2,1)S(1)} collective-permute-done((bf16[48,1280]{1,0:T(8,128)(2,1)S(1)}, bf16[48,1280]{1,0:T(8,128)(2,1)S(1)}, u32[]{:S(2)}, u32[]{:S(2)}) %collective-permute-start.3) | collective-permute-done | bytes 122912 | tf_op jit(solution)/shard_map/ppermute | solution.py:41
  17.2 7.0 %collective-permute-done.2 = bf16[48,1280]{1,0:T(8,128)(2,1)S(1)} collective-permute-done((bf16[48,1280]{1,0:T(8,128)(2,1)S(1)}, bf16[48,1280]{1,0:T(8,128)(2,1)S(1)}, u32[]{:S(2)}, u32[]{:S(2)}) %collective-permute-start.2) | collective-permute-done | bytes 122912 | tf_op jit(solution)/shard_map/ppermute | solution.py:41
  25.8 2.1 %collective-permute-start.6 = (bf16[512,384]{1,0:T(8,128)(2,1)S(1)}, bf16[512,384]{1,0:T(8,128)(2,1)S(1)}, u32[]{:S(2)}, u32[]{:S(2)}) collective-permute-start(bf16[512,384]{1,0:T(8,128)(2,1)S(1)} %collective-permute-done.refs_3_), channel_id=1, source_target_pairs={{0,2},{1,3},{2,0},{3,1},{4,6},{5,7},{6,4},{7,5},{8,10},{9,11},{10,... | collective-permute-start | bytes 1179656 | tf_op jit(solution)/shard_map/ppermute | solution.py:41
  31.0 3.6 %shard_map.229 = (bf16[1,8,512,512]{3,2,1,0:T(8,128)(2,1)S(1)}, bf16[1,384,512]{2,1,0:T(8,128)(2,1)S(1)}, bf16[1,384,512]{2,1,0:T(8,128)(2,1)S(1)}, bf16[1,512,3...) custom-call(bf16[384,512]{1,0:T(8,128)(2,1)S(1)} %get-tuple-element.131.refs_0_., ...), custom_call_target="tpu_custom_call" | custom-call | flops 100663296 | bytes 262144 | tf_op jit(solution)/shard_map/pallas_call | solution.py:64
  34.6 3.3 %collective-permute-done.6.refs_3_ = bf16[512,384]{1,0:T(8,128)(2,1)S(1)} collective-permute-done((bf16[512,384]{1,0:T(8,128)(2,1)S(1)}, bf16[512,384]{1,0:T(8,128)(2,1)S(1)}, u32[]{:S(2)}, u32[]{:S(2)}) %collective-permute-start.6) | collective-permute-done | bytes 393248 | tf_op jit(solution)/shard_map/ppermute | solution.py:41
  39.9 7.7 %shard_map.230 = (bf16[2,8,512,512]{3,2,1,0:T(8,128)(2,1)S(1)}, bf16[2,384,512]{2,1,0:T(8,128)(2,1)S(1)}, bf16[2,384,512]{2,1,0:T(8,128)(2,1)S(1)}, bf16[2,512,3...) custom-call(bf16[384,512]{1,0:T(8,128)(2,1)S(1)} %get-tuple-element.131.refs_0_., ...), custom_call_target="tpu_custom_call" | custom-call | flops 201326592 | bytes 524288 | tf_op jit(solution)/shard_map/pallas_call | solution.py:64
  47.7 3.7 %shard_map.231 = (bf16[1,8,512,512]{3,2,1,0:T(8,128)(2,1)S(1)}, bf16[1,384,512]{2,1,0:T(8,128)(2,1)S(1)}, bf16[1,384,512]{2,1,0:T(8,128)(2,1)S(1)}, bf16[1,512,3...) custom-call(bf16[384,512]{1,0:T(8,128)(2,1)S(1)} %get-tuple-element.131.refs_0_., ...), custom_call_target="tpu_custom_call" | custom-call | flops 100663296 | bytes 262144 | tf_op jit(solution)/shard_map/pallas_call | solution.py:64
  51.5 2.1 %collective-permute-done.12.refs_5_ = bf16[2,48,3584]{2,1,0:T(8,128)(2,1)S(1)} collective-permute-done((bf16[2,48,3584]{2,1,0:T(8,128)(2,1)S(1)}, bf16[2,48,3584]{2,1,0:T(8,128)(2,1)S(1)}, u32[]{:S(2)}, u32[]{:S(2)}) %collective-permute-start.12) | collective-permute-done | bytes 688160 | tf_op jit(solution)/shard_map/ppermute | solution.py:41
  54.6 2.4 %shard_map.233 = (f32[384,512]{1,0:T(8,128)S(1)}, f32[8,512]{1,0:T(8,128)S(1)}, f32[512,384]{1,0:T(8,128)S(1)}, f32[512,384]{1,0:T(8,128)S(1)}, f32[512,1]{1,0:T...) custom-call(bf16[512,384]{1,0:T(8,128)(2,1)S(1)} %bitcast.42, ...), custom_call_target="tpu_custom_call" | custom-call | flops 704643072 | bytes 3145728 | tf_op jit(solution)/shard_map/pallas_call | solution.py:64
  59.1 2.2 %collective-permute-start.14 = (bf16[128,128]{1,0:T(8,128)(2,1)S(1)}, bf16[128,128]{1,0:T(8,128)(2,1)S(1)}, u32[]{:S(2)}, u32[]{:S(2)}) collective-permute-start(bf16[128,128]{1,0:T(8,128)(2,1)S(1)} %get-tuple-element.169.refs_1_), channel_id=1, source_target_pairs={{0,4},{1,5},{2,6},{3,7},{4,0},{5,1},{6,2},{7,3},{8,12},{9,13},{10,... | collective-permute-start | bytes 98312 | tf_op jit(solution)/shard_map/ppermute | solution.py:41
  61.4 4.9 %collective-permute-done.14.refs_3_ = bf16[128,128]{1,0:T(8,128)(2,1)S(1)} collective-permute-done((bf16[128,128]{1,0:T(8,128)(2,1)S(1)}, bf16[128,128]{1,0:T(8,128)(2,1)S(1)}, u32[]{:S(2)}, u32[]{:S(2)}) %collective-permute-start.14) | collective-permute-done | bytes 32800 | tf_op jit(solution)/shard_map/ppermute | solution.py:41
  72.6 3.3 %shard_map.236 = (bf16[512,128]{1,0:T(8,128)(2,1)S(1)}, bf16[512,384]{1,0:T(8,128)(2,1)S(1)}, bf16[512,1536]{1,0:T(8,128)(2,1)S(1)}, bf16[512,384]{1,0:T(8,128)(...) custom-call(s32[2]{0:T(128)S(1)} %pad_add_fusion.place, ...), custom_call_target="tpu_custom_call" | custom-call | flops 1409286144 | bytes 6291456 | tf_op jit(solution)/shard_map/pallas_call | solution.py:64
  75.9 2.5 %shard_map.237 = (bf16[4,48,3584]{2,1,0:T(8,128)(2,1)S(1)}, bf16[4,48,3584]{2,1,0:T(8,128)(2,1)S(1)}) custom-call(s32[2]{0:T(128)S(1)} %pad_add_fusion.place, bf16[512,128]{1,0:T(8,128)(2,1)S(1)} %get-tuple-element.182.grad_est, bf16[512,384]{1,0:T(8,128)(2,1)S(1)} %get-tuple-element.183.grad_ffn, bf16[512,1536]{1,0:T(8,128)(2,1)S(1)} %get-tuple-element.184.grad_pre, ...), custom_call_target="tpu_custom_call" | custom-call | flops 1409286144 | bytes 6291456 | tf_op jit(solution)/shard_map/pallas_call | solution.py:64
  78.5 4.6 %shard_map.238 = (f32[384,512]{1,0:T(8,128)S(1)}, bf16[1,768,512]{2,1,0:T(8,128)(2,1)S(1)}) custom-call(bf16[1,8,512,512]{3,2,1,0:T(8,128)(2,1)S(1)} %get-tuple-element.196.probs, bf16[1,384,512]{2,1,0:T(8,128)(2,1)S(1)} %get-tuple-element.197.keys_t, bf16[1,384,512]{2,1,0:T(8,128)(2,1)S(1)} %get-tuple-element.198.values_t, ...), custom_call_target="tpu_custom_call" | custom-call | flops 4026531840 | bytes 4194304 | tf_op jit(solution)/shard_map/pallas_call | solution.py:64
  87.1 8.9 %shard_map.239 = (f32[384,512]{1,0:T(8,128)S(1)}, bf16[2,768,512]{2,1,0:T(8,128)(2,1)S(1)}) custom-call(bf16[2,8,512,512]{3,2,1,0:T(8,128)(2,1)S(1)} %get-tuple-element.192.probs, bf16[2,384,512]{2,1,0:T(8,128)(2,1)S(1)} %get-tuple-element.193.keys_t, bf16[2,384,512]{2,1,0:T(8,128)(2,1)S(1)} %get-tuple-element.194.values_t, ...), custom_call_target="tpu_custom_call" | custom-call | flops 8053063680 | bytes 8388608 | tf_op jit(solution)/shard_map/pallas_call | solution.py:64
  96.0 4.4 %shard_map.240 = (f32[384,512]{1,0:T(8,128)S(1)}, bf16[1,768,512]{2,1,0:T(8,128)(2,1)S(1)}) custom-call(bf16[1,8,512,512]{3,2,1,0:T(8,128)(2,1)S(1)} %get-tuple-element.147.probs, bf16[1,384,512]{2,1,0:T(8,128)(2,1)S(1)} %get-tuple-element.148.keys_t, bf16[1,384,512]{2,1,0:T(8,128)(2,1)S(1)} %get-tuple-element.149.values_t, ...), custom_call_target="tpu_custom_call" | custom-call | flops 4026531840 | bytes 4194304 | tf_op jit(solution)/shard_map/pallas_call | solution.py:64
  100.4 3.1 %shard_map.241 = (bf16[4,48,1280]{2,1,0:T(8,128)(2,1)S(1)}, bf16[4,48,1280]{2,1,0:T(8,128)(2,1)S(1)}) custom-call(s32[2]{0:T(128)S(1)} %pad_add_fusion.place, f32[384,512]{1,0:T(8,128)S(1)} %get-tuple-element.205.grad_queries, bf16[512,384]{1,0:T(8,128)(2,1)S(1)} %get-tuple-element.206.own_unit, bf16[1152,384]{1,0:T(8,128)(2,1)S(1)} %get-tuple-element.132.refs_1_.weights_t, ...), custom_call_target="tpu_custom_call" | custom-call | flops 1811939328 | bytes 1572864 | tf_op jit(solution)/shard_map/pallas_call | solution.py:64
  111.0 3.4 %collective-permute-done.28 = bf16[48,3584]{1,0:T(8,128)(2,1)S(1)} collective-permute-done((bf16[48,3584]{1,0:T(8,128)(2,1)S(1)}, bf16[48,3584]{1,0:T(8,128)(2,1)S(1)}, u32[]{:S(2)}, u32[]{:S(2)}) %collective-permute-start.28) | collective-permute-done | bytes 344096 | tf_op jit(solution)/shard_map/ppermute | solution.py:41
  117.0 3.4 %collective-permute-done.30 = bf16[48,1280]{1,0:T(8,128)(2,1)S(1)} collective-permute-done((bf16[48,1280]{1,0:T(8,128)(2,1)S(1)}, bf16[48,1280]{1,0:T(8,128)(2,1)S(1)}, u32[]{:S(2)}, u32[]{:S(2)}) %collective-permute-start.30) | collective-permute-done | bytes 122912 | tf_op jit(solution)/shard_map/ppermute | solution.py:41
  123.0 2.0 %collective-permute-start.34 = (f32[8,128]{1,0:T(8,128)S(1)}, f32[8,128]{1,0:T(8,128)S(1)}, u32[]{:S(2)}, u32[]{:S(2)}) collective-permute-start(f32[8,128]{1,0:T(8,128)S(1)} %shard_map.242.own), channel_id=1, source_target_pairs={{0,2},{1,3},{2,0},{3,1},{4,6},{5,7},{6,4},{7,5},{8,14},{9,15},{10,... | collective-permute-start | bytes 12296 | tf_op jit(solution)/shard_map/ppermute | solution.py:680
  129.2 3.1 %collective-permute-start.36 = (f32[8,128]{1,0:T(8,128)S(1)}, f32[8,128]{1,0:T(8,128)S(1)}, u32[]{:S(2)}, u32[]{:S(2)}) collective-permute-start(f32[8,128]{1,0:T(8,128)S(1)} %shard_map.243.squares), channel_id=1, source_target_pairs={{0,8},{8,0},{16,24},{24,16},{1,9},{9,1},{17,25},{25,17},{2,10},{10... | collective-permute-start | bytes 12296 | tf_op jit(solution)/shard_map/ppermute | solution.py:41
  133.2 4.4 %shard_map.244 = (f32[96,3200]{1,0:T(8,128)}, f32[384,384]{1,0:T(8,128)}, f32[6,128]{1,0:T(8,128)}, f32[96,3200]{1,0:T(8,128)}, f32[384,384]{1,0:T(8,128)}, /*in...) custom-call(s32[2]{0:T(128)S(1)} %pad_add_fusion.place, ...), custom_call_target="tpu_custom_call" | custom-call | flops 9108480 | bytes 12751872 | tf_op jit(solution)/shard_map/pallas_call | solution.py:64
  (113 shorter events, 44.0 us)
Async XLA Ops:
  0.6 23.8 %collective-permute-start = (bf16[512,384]{1,0:T(8,128)(2,1)}, bf16[512,384]{1,0:T(8,128)(2,1)S(1)}, u32[]{:S(2)}, u32[]{:S(2)}) collective-permute-start(bf16[512,384]{1,0:T(8,128)(2,1)} %bitcast.40), channel_id=1, source_target_pairs={{0,4},{1,5},{2,6},{3,7},{4,0},{5,1},{6,2},{7,3},{8,12},{9,13},{10,... | collective-permute-start | bytes 1179656 | tf_op jit(solution)/shard_map/ppermute | solution.py:41
  8.5 8.7 %collective-permute-start.3 = (bf16[48,1280]{1,0:T(8,128)(2,1)S(1)}, bf16[48,1280]{1,0:T(8,128)(2,1)S(1)}, u32[]{:S(2)}, u32[]{:S(2)}) collective-permute-start(bf16[48,1280]{1,0:T(8,128)(2,1)S(1)} %get-tuple-element.128), channel_id=1, source_target_pairs={{0,3},{1,2},{2,1},{3,0},{4,7},{5,6},{6,5},{7,4},{8,11},{9,10},{10,... | collective-permute-start | bytes 368648 | tf_op jit(solution)/shard_map/ppermute | solution.py:41
  11.1 13.1 %collective-permute-start.2 = (bf16[48,1280]{1,0:T(8,128)(2,1)S(1)}, bf16[48,1280]{1,0:T(8,128)(2,1)S(1)}, u32[]{:S(2)}, u32[]{:S(2)}) collective-permute-start(bf16[48,1280]{1,0:T(8,128)(2,1)S(1)} %get-tuple-element.128), channel_id=1, source_target_pairs={{0,2},{1,3},{2,0},{3,1},{4,6},{5,7},{6,4},{7,5},{8,10},{9,11},{10,... | collective-permute-start | bytes 368648 | tf_op jit(solution)/shard_map/ppermute | solution.py:41
  11.6 12.7 %collective-permute-start.1 = (bf16[48,1280]{1,0:T(8,128)(2,1)S(1)}, bf16[48,1280]{1,0:T(8,128)(2,1)S(1)}, u32[]{:S(2)}, u32[]{:S(2)}) collective-permute-start(bf16[48,1280]{1,0:T(8,128)(2,1)S(1)} %get-tuple-element.128), channel_id=1, source_target_pairs={{0,1},{1,0},{2,3},{3,2},{4,5},{5,4},{6,7},{7,6},{8,9},{9,8},{10,11... | collective-permute-start | bytes 368648 | tf_op jit(solution)/shard_map/ppermute | solution.py:41
  12.1 12.4 %collective-permute-start.4 = (bf16[48,3584]{1,0:T(8,128)(2,1)S(1)}, bf16[48,3584]{1,0:T(8,128)(2,1)S(1)}, u32[]{:S(2)}, u32[]{:S(2)}) collective-permute-start(bf16[48,3584]{1,0:T(8,128)(2,1)S(1)} %get-tuple-element.143.refs_0_), channel_id=1, source_target_pairs={{0,1},{1,0},{2,3},{3,2},{4,5},{5,4},{6,7},{7,6},{8,9},{9,8},{10,11... | collective-permute-start | bytes 1032200 | tf_op jit(solution)/shard_map/ppermute | solution.py:41
  24.4 10.2 %collective-permute-start.7 = (bf16[512,384]{1,0:T(8,128)(2,1)S(1)}, bf16[512,384]{1,0:T(8,128)(2,1)S(1)}, u32[]{:S(2)}, u32[]{:S(2)}) collective-permute-start(bf16[512,384]{1,0:T(8,128)(2,1)S(1)} %collective-permute-done.refs_3_), channel_id=1, source_target_pairs={{0,1},{1,0},{2,3},{3,2},{4,5},{5,4},{6,7},{7,6},{8,9},{9,8},{10,11... | collective-permute-start | bytes 1179656 | tf_op jit(solution)/shard_map/ppermute | solution.py:41
  25.8 12.1 %collective-permute-start.6 = (bf16[512,384]{1,0:T(8,128)(2,1)S(1)}, bf16[512,384]{1,0:T(8,128)(2,1)S(1)}, u32[]{:S(2)}, u32[]{:S(2)}) collective-permute-start(bf16[512,384]{1,0:T(8,128)(2,1)S(1)} %collective-permute-done.refs_3_), channel_id=1, source_target_pairs={{0,2},{1,3},{2,0},{3,1},{4,6},{5,7},{6,4},{7,5},{8,10},{9,11},{10,... | collective-permute-start | bytes 1179656 | tf_op jit(solution)/shard_map/ppermute | solution.py:41
  27.9 23.5 %collective-permute-start.11 = (bf16[2,48,3584]{2,1,0:T(8,128)(2,1)S(1)}, bf16[2,48,3584]{2,1,0:T(8,128)(2,1)S(1)}, u32[]{:S(2)}, u32[]{:S(2)}) collective-permute-start(bf16[2,48,3584]{2,1,0:T(8,128)(2,1)S(1)} %pad_maximum_fusion), channel_id=1, source_target_pairs={{0,2},{1,3},{2,0},{3,1},{4,6},{5,7},{6,4},{7,5},{8,10},{9,11},{10,... | collective-permute-start | bytes 2064392 | tf_op jit(solution)/shard_map/ppermute | solution.py:41
  37.9 9.8 %collective-permute-start.8 = (bf16[512,384]{1,0:T(8,128)(2,1)S(1)}, bf16[512,384]{1,0:T(8,128)(2,1)S(1)}, u32[]{:S(2)}, u32[]{:S(2)}) collective-permute-start(bf16[512,384]{1,0:T(8,128)(2,1)S(1)} %collective-permute-done.6.refs_3_), channel_id=1, source_target_pairs={{0,1},{1,0},{2,3},{3,2},{4,5},{5,4},{6,7},{7,6},{8,9},{9,8},{10,11... | collective-permute-start | bytes 1179656 | tf_op jit(solution)/shard_map/ppermute | solution.py:41
  39.4 8.2 %collective-permute-start.9 = (bf16[48,3584]{1,0:T(8,128)(2,1)S(1)}, bf16[48,3584]{1,0:T(8,128)(2,1)S(1)}, u32[]{:S(2)}, u32[]{:S(2)}) collective-permute-start(bf16[48,3584]{1,0:T(8,128)(2,1)S(1)} %get-tuple-element.143.refs_0_), channel_id=1, source_target_pairs={{0,8},{8,0},{16,24},{24,16},{1,9},{9,1},{17,25},{25,17},{2,10},{10... | collective-permute-start | bytes 1032200 | tf_op jit(solution)/shard_map/ppermute | solution.py:41
  39.4 8.2 %collective-permute-start.10 = (bf16[48,3584]{1,0:T(8,128)(2,1)S(1)}, bf16[48,3584]{1,0:T(8,128)(2,1)S(1)}, u32[]{:S(2)}, u32[]{:S(2)}) collective-permute-start(bf16[48,3584]{1,0:T(8,128)(2,1)S(1)} %collective-permute-done.4.refs_1_), channel_id=1, source_target_pairs={{0,8},{8,0},{16,24},{24,16},{1,9},{9,1},{17,25},{25,17},{2,10},{10... | collective-permute-start | bytes 1032200 | tf_op jit(solution)/shard_map/ppermute | solution.py:41
  57.0 9.3 %collective-permute-start.13 = (bf16[384,128]{1,0:T(8,128)(2,1)S(1)}, bf16[384,128]{1,0:T(8,128)(2,1)S(1)}, u32[]{:S(2)}, u32[]{:S(2)}) collective-permute-start(bf16[384,128]{1,0:T(8,128)(2,1)S(1)} %get-tuple-element.158.refs_0_), channel_id=1, source_target_pairs={{0,4},{1,5},{2,6},{3,7},{4,0},{5,1},{6,2},{7,3},{8,12},{9,13},{10,... | collective-permute-start | bytes 294920 | tf_op jit(solution)/shard_map/ppermute | solution.py:41
  59.1 7.2 %collective-permute-start.14 = (bf16[128,128]{1,0:T(8,128)(2,1)S(1)}, bf16[128,128]{1,0:T(8,128)(2,1)S(1)}, u32[]{:S(2)}, u32[]{:S(2)}) collective-permute-start(bf16[128,128]{1,0:T(8,128)(2,1)S(1)} %get-tuple-element.169.refs_1_), channel_id=1, source_target_pairs={{0,4},{1,5},{2,6},{3,7},{4,0},{5,1},{6,2},{7,3},{8,12},{9,13},{10,... | collective-permute-start | bytes 98312 | tf_op jit(solution)/shard_map/ppermute | solution.py:41
  78.4 4.7 %collective-permute-start.18 = (bf16[4,48,3584]{2,1,0:T(8,128)(2,1)S(1)}, bf16[4,48,3584]{2,1,0:T(8,128)(2,1)S(1)}, u32[]{:S(2)}, u32[]{:S(2)}) collective-permute-start(bf16[4,48,3584]{2,1,0:T(8,128)(2,1)S(1)} %get-tuple-element.202), channel_id=1, source_target_pairs={{0,8},{8,0},{16,24},{24,16},{1,9},{9,1},{17,25},{25,17},{2,10},{10... | collective-permute-start | bytes 4128776 | tf_op jit(solution)/shard_map/ppermute | solution.py:41
  83.5 20.0 %collective-permute-start.21 = (bf16[48,3584]{1,0:T(8,128)(2,1)S(1)}, bf16[48,3584]{1,0:T(8,128)(2,1)S(1)}, u32[]{:S(2)}, u32[]{:S(2)}) collective-permute-start(bf16[48,3584]{1,0:T(8,128)(2,1)S(1)} %get-tuple-element.242), channel_id=1, source_target_pairs={{0,3},{1,2},{2,1},{3,0},{4,7},{5,6},{6,5},{7,4},{8,11},{9,10},{10,... | collective-permute-start | bytes 1032200 | tf_op jit(solution)/shard_map/ppermute | solution.py:41
  84.6 19.0 %collective-permute-start.20 = (bf16[48,3584]{1,0:T(8,128)(2,1)S(1)}, bf16[48,3584]{1,0:T(8,128)(2,1)S(1)}, u32[]{:S(2)}, u32[]{:S(2)}) collective-permute-start(bf16[48,3584]{1,0:T(8,128)(2,1)S(1)} %get-tuple-element.243), channel_id=1, source_target_pairs={{0,2},{1,3},{2,0},{3,1},{4,6},{5,7},{6,4},{7,5},{8,10},{9,11},{10,... | collective-permute-start | bytes 1032200 | tf_op jit(solution)/shard_map/ppermute | solution.py:41
  86.6 17.0 %collective-permute-start.19 = (bf16[48,3584]{1,0:T(8,128)(2,1)S(1)}, bf16[48,3584]{1,0:T(8,128)(2,1)S(1)}, u32[]{:S(2)}, u32[]{:S(2)}) collective-permute-start(bf16[48,3584]{1,0:T(8,128)(2,1)S(1)} %get-tuple-element.244), channel_id=1, source_target_pairs={{0,1},{1,0},{2,3},{3,2},{4,5},{5,4},{6,7},{7,6},{8,9},{9,8},{10,11... | collective-permute-start | bytes 1032200 | tf_op jit(solution)/shard_map/ppermute | solution.py:41
  103.9 10.6 %collective-permute-start.28 = (bf16[48,3584]{1,0:T(8,128)(2,1)S(1)}, bf16[48,3584]{1,0:T(8,128)(2,1)S(1)}, u32[]{:S(2)}, u32[]{:S(2)}) collective-permute-start(bf16[48,3584]{1,0:T(8,128)(2,1)S(1)} %add_convert_fusion.3), channel_id=1, source_target_pairs={{0,16},{8,24},{16,0},{24,8},{1,17},{9,25},{17,1},{25,9},{2,18},{10... | collective-permute-start | bytes 1032200 | tf_op jit(solution)/shard_map/ppermute | solution.py:41
  105.8 8.7 %collective-permute-start.23 = (bf16[48,1280]{1,0:T(8,128)(2,1)S(1)}, bf16[48,1280]{1,0:T(8,128)(2,1)S(1)}, u32[]{:S(2)}, u32[]{:S(2)}) collective-permute-start(bf16[48,1280]{1,0:T(8,128)(2,1)S(1)} %get-tuple-element.246), channel_id=1, source_target_pairs={{0,1},{1,0},{2,3},{3,2},{4,5},{5,4},{6,7},{7,6},{8,9},{9,8},{10,11... | collective-permute-start | bytes 368648 | tf_op jit(solution)/shard_map/ppermute | solution.py:41
  107.5 7.1 %collective-permute-start.25 = (bf16[48,1280]{1,0:T(8,128)(2,1)S(1)}, bf16[48,1280]{1,0:T(8,128)(2,1)S(1)}, u32[]{:S(2)}, u32[]{:S(2)}) collective-permute-start(bf16[48,1280]{1,0:T(8,128)(2,1)S(1)} %get-tuple-element.247), channel_id=1, source_target_pairs={{0,3},{1,2},{2,1},{3,0},{4,7},{5,6},{6,5},{7,4},{8,11},{9,10},{10,... | collective-permute-start | bytes 368648 | tf_op jit(solution)/shard_map/ppermute | solution.py:41
  107.5 7.8 %collective-permute-start.24 = (bf16[48,1280]{1,0:T(8,128)(2,1)S(1)}, bf16[48,1280]{1,0:T(8,128)(2,1)S(1)}, u32[]{:S(2)}, u32[]{:S(2)}) collective-permute-start(bf16[48,1280]{1,0:T(8,128)(2,1)S(1)} %get-tuple-element.248), channel_id=1, source_target_pairs={{0,2},{1,3},{2,0},{3,1},{4,6},{5,7},{6,4},{7,5},{8,10},{9,11},{10,... | collective-permute-start | bytes 368648 | tf_op jit(solution)/shard_map/ppermute | solution.py:41
  109.5 5.0 %collective-permute-start.27 = (f32[8,128]{1,0:T(8,128)S(1)}, f32[8,128]{1,0:T(8,128)S(1)}, u32[]{:S(2)}, u32[]{:S(2)}) collective-permute-start(f32[8,128]{1,0:T(8,128)S(1)} %add.50), channel_id=1, source_target_pairs={{0,16},{8,24},{16,0},{24,8},{1,17},{9,25},{17,1},{25,9},{2,18},{10... | collective-permute-start | bytes 12296 | tf_op jit(solution)/shard_map/ppermute | solution.py:41
  115.4 4.9 %collective-permute-start.30 = (bf16[48,1280]{1,0:T(8,128)(2,1)S(1)}, bf16[48,1280]{1,0:T(8,128)(2,1)S(1)}, u32[]{:S(2)}, u32[]{:S(2)}) collective-permute-start(bf16[48,1280]{1,0:T(8,128)(2,1)S(1)} %fusion.2), channel_id=1, source_target_pairs={{0,16},{8,24},{16,0},{24,8},{1,17},{9,25},{17,1},{25,9},{2,18},{10... | collective-permute-start | bytes 368648 | tf_op jit(solution)/shard_map/ppermute | solution.py:41
  117.0 4.8 %collective-permute-start.29 = (bf16[48,3584]{1,0:T(8,128)(2,1)S(1)}, bf16[48,3584]{1,0:T(8,128)(2,1)S(1)}, u32[]{:S(2)}, u32[]{:S(2)}) collective-permute-start(bf16[48,3584]{1,0:T(8,128)(2,1)S(1)} %add_convert_fusion.2.refs_0_.early), channel_id=1, source_target_pairs={{0,8},{8,0},{16,24},{24,16},{1,9},{9,1},{17,25},{25,17},{2,10},{10... | collective-permute-start | bytes 1032200 | tf_op jit(solution)/shard_map/ppermute | solution.py:41
  (28 other events, 316.8 us)

commit v6 on v5

--- a/solution.py
+++ b/solution.py
@@ -682,7 +682,7 @@
 
 
 def send_members(total, size):
-    return [total[0]] + [swap(total[mask], "wide", mask) for mask in range(1, size)]
+    return [total[0]] + [swap(total[mask], "wide", mask) for mask in [2, 3, 1]]
 
 
 def sum_low(parts):
@@ -841,7 +841,7 @@
     for group in groups:
         if len(saved) == 1:
             near = [far[mask] for mask in range(1, high)]
-            carry[0], far[high], near, *low_mine = tie(carry[0], far[high], near, *low_mine)
+            near, far[high], carry[0], *low_mine = tie(near, far[high], carry[0], *low_mine)
             far.update(zip(range(1, high), near))
             low_other = [swap(x, "seg", 1) for x in low_mine]
             for mask in range(1, high):

time: 138 us -> 137 us (level)
  transfers between devices with their start and end apart: 37 -> 37, of which waited for: 18 -> 19; matrix products, arithmetic and copies ran while one was open for 1% -> 1% of each run, Pallas kernels for 28% -> 29%
where the time goes in v6:
time: 137 us; the launch traced here: 136 us
  Pallas kernels  54.2 us (40%)
  starting transfers between devices  40.1 us (29%)
  waiting for transfers between devices  36 us (26%)
  local copies, waits for them, and re-layouts  3.73 us (3%)
    pallas_call x18, Pallas kernels, call(): pl.pallas_call(kernel, out_shape=out_shape, in_specs=[small] * len(place)...  54.2 us
    ppermute x33, starting transfers between devices, swap(): lax.ppermute(x, axis, [(i, i ^ mask) for i in range(lax.axis_size(axis))])  36 us
    ppermute x33, waiting for transfers between devices, swap(): lax.ppermute(x, axis, [(i, i ^ mask) for i in range(lax.axis_size(axis))])  34.1 us
    ppermute x4, starting transfers between devices, branch_parts(): found.append(lax.ppermute(values, ('seg', 'wide'), pairs))  4.14 us
    unnamed x30, local copies, waits for them, and re-layouts  3.1 us
  transfers between devices with their start and end apart: 37, of which 19 were waited for; matrix products, arithmetic and copies ran while one was open for 1% of the time, Pallas kernels for 29%

profile of v6, /device:TPU:0, one launch (start us, length us, event | category | flops | bytes accessed | tf_op | source)
XLA Modules:
  0.0 136.4 jit_solution(9585055502526033598)
XLA Ops:
  0.6 4.1 %collective-permute-start = (bf16[512,384]{1,0:T(8,128)(2,1)}, bf16[512,384]{1,0:T(8,128)(2,1)S(1)}, u32[]{:S(2)}, u32[]{:S(2)}) collective-permute-start(bf16[512,384]{1,0:T(8,128)(2,1)} %bitcast.40), channel_id=1, source_target_pairs={{0,4},{1,5},{2,6},{3,7},{4,0},{5,1},{6,2},{7,3},{8,12},{9,13},{10,... | collective-permute-start | bytes 1179656 | tf_op jit(solution)/shard_map/ppermute | solution.py:41
  8.5 2.6 %collective-permute-start.3 = (bf16[48,1280]{1,0:T(8,128)(2,1)S(1)}, bf16[48,1280]{1,0:T(8,128)(2,1)S(1)}, u32[]{:S(2)}, u32[]{:S(2)}) collective-permute-start(bf16[48,1280]{1,0:T(8,128)(2,1)S(1)} %get-tuple-element.128), channel_id=1, source_target_pairs={{0,3},{1,2},{2,1},{3,0},{4,7},{5,6},{6,5},{7,4},{8,11},{9,10},{10,... | collective-permute-start | bytes 368648 | tf_op jit(solution)/shard_map/ppermute | solution.py:41
  13.6 3.6 %collective-permute-done.3 = bf16[48,1280]{1,0:T(8,128)(2,1)S(1)} collective-permute-done((bf16[48,1280]{1,0:T(8,128)(2,1)S(1)}, bf16[48,1280]{1,0:T(8,128)(2,1)S(1)}, u32[]{:S(2)}, u32[]{:S(2)}) %collective-permute-start.3) | collective-permute-done | bytes 122912 | tf_op jit(solution)/shard_map/ppermute | solution.py:41
  17.2 7.0 %collective-permute-done.2 = bf16[48,1280]{1,0:T(8,128)(2,1)S(1)} collective-permute-done((bf16[48,1280]{1,0:T(8,128)(2,1)S(1)}, bf16[48,1280]{1,0:T(8,128)(2,1)S(1)}, u32[]{:S(2)}, u32[]{:S(2)}) %collective-permute-start.2) | collective-permute-done | bytes 122912 | tf_op jit(solution)/shard_map/ppermute | solution.py:41
  24.4 2.9 %collective-permute-start.7 = (bf16[512,384]{1,0:T(8,128)(2,1)S(1)}, bf16[512,384]{1,0:T(8,128)(2,1)S(1)}, u32[]{:S(2)}, u32[]{:S(2)}) collective-permute-start(bf16[512,384]{1,0:T(8,128)(2,1)S(1)} %collective-permute-done.refs_3_), channel_id=1, source_target_pairs={{0,2},{1,3},{2,0},{3,1},{4,6},{5,7},{6,4},{7,5},{8,10},{9,11},{10,... | collective-permute-start | bytes 1179656 | tf_op jit(solution)/shard_map/ppermute | solution.py:41
  31.0 3.6 %shard_map.229 = (bf16[1,8,512,512]{3,2,1,0:T(8,128)(2,1)S(1)}, bf16[1,384,512]{2,1,0:T(8,128)(2,1)S(1)}, bf16[1,384,512]{2,1,0:T(8,128)(2,1)S(1)}, bf16[1,512,3...) custom-call(bf16[384,512]{1,0:T(8,128)(2,1)S(1)} %get-tuple-element.131.refs_0_., ...), custom_call_target="tpu_custom_call" | custom-call | flops 100663296 | bytes 262144 | tf_op jit(solution)/shard_map/pallas_call | solution.py:64
  34.6 2.8 %collective-permute-done.7.refs_3_ = bf16[512,384]{1,0:T(8,128)(2,1)S(1)} collective-permute-done((bf16[512,384]{1,0:T(8,128)(2,1)S(1)}, bf16[512,384]{1,0:T(8,128)(2,1)S(1)}, u32[]{:S(2)}, u32[]{:S(2)}) %collective-permute-start.7) | collective-permute-done | bytes 393248 | tf_op jit(solution)/shard_map/ppermute | solution.py:41
  38.4 7.7 %shard_map.230 = (bf16[2,8,512,512]{3,2,1,0:T(8,128)(2,1)S(1)}, bf16[2,384,512]{2,1,0:T(8,128)(2,1)S(1)}, bf16[2,384,512]{2,1,0:T(8,128)(2,1)S(1)}, bf16[2,512,3...) custom-call(bf16[384,512]{1,0:T(8,128)(2,1)S(1)} %get-tuple-element.131.refs_0_., ...), custom_call_target="tpu_custom_call" | custom-call | flops 201326592 | bytes 524288 | tf_op jit(solution)/shard_map/pallas_call | solution.py:64
  46.2 3.7 %shard_map.231 = (bf16[1,8,512,512]{3,2,1,0:T(8,128)(2,1)S(1)}, bf16[1,384,512]{2,1,0:T(8,128)(2,1)S(1)}, bf16[1,384,512]{2,1,0:T(8,128)(2,1)S(1)}, bf16[1,512,3...) custom-call(bf16[384,512]{1,0:T(8,128)(2,1)S(1)} %get-tuple-element.131.refs_0_., ...), custom_call_target="tpu_custom_call" | custom-call | flops 100663296 | bytes 262144 | tf_op jit(solution)/shard_map/pallas_call | solution.py:64
  50.0 2.1 %collective-permute-done.12.refs_5_ = bf16[2,48,3584]{2,1,0:T(8,128)(2,1)S(1)} collective-permute-done((bf16[2,48,3584]{2,1,0:T(8,128)(2,1)S(1)}, bf16[2,48,3584]{2,1,0:T(8,128)(2,1)S(1)}, u32[]{:S(2)}, u32[]{:S(2)}) %collective-permute-start.12) | collective-permute-done | bytes 688160 | tf_op jit(solution)/shard_map/ppermute | solution.py:41
  53.0 2.4 %shard_map.233 = (f32[384,512]{1,0:T(8,128)S(1)}, f32[8,512]{1,0:T(8,128)S(1)}, f32[512,384]{1,0:T(8,128)S(1)}, f32[512,384]{1,0:T(8,128)S(1)}, f32[512,1]{1,0:T...) custom-call(bf16[512,384]{1,0:T(8,128)(2,1)S(1)} %bitcast.42, ...), custom_call_target="tpu_custom_call" | custom-call | flops 704643072 | bytes 3145728 | tf_op jit(solution)/shard_map/pallas_call | solution.py:64
  59.8 4.9 %collective-permute-done.14.refs_3_ = bf16[128,128]{1,0:T(8,128)(2,1)S(1)} collective-permute-done((bf16[128,128]{1,0:T(8,128)(2,1)S(1)}, bf16[128,128]{1,0:T(8,128)(2,1)S(1)}, u32[]{:S(2)}, u32[]{:S(2)}) %collective-permute-start.14) | collective-permute-done | bytes 32800 | tf_op jit(solution)/shard_map/ppermute | solution.py:41
  65.8 2.7 %collective-permute-start.16 = (f32[8,128]{1,0:T(8,128)S(1)}, f32[8,128]{1,0:T(8,128)S(1)}, u32[]{:S(2)}, u32[]{:S(2)}) collective-permute-start(f32[8,128]{1,0:T(8,128)S(1)} %get-tuple-element.170), channel_id=1, source_target_pairs={{0,2},{1,3},{2,0},{3,1},{4,6},{5,7},{6,4},{7,5},{8,10},{9,11},{10,... | collective-permute-start | bytes 12296 | tf_op jit(solution)/shard_map/ppermute | solution.py:41
  72.1 3.3 %shard_map.236 = (bf16[512,128]{1,0:T(8,128)(2,1)S(1)}, bf16[512,384]{1,0:T(8,128)(2,1)S(1)}, bf16[512,1536]{1,0:T(8,128)(2,1)S(1)}, bf16[512,384]{1,0:T(8,128)(...) custom-call(s32[2]{0:T(128)S(1)} %pad_add_fusion.place, ...), custom_call_target="tpu_custom_call" | custom-call | flops 1409286144 | bytes 6291456 | tf_op jit(solution)/shard_map/pallas_call | solution.py:64
  75.4 2.5 %shard_map.237 = (bf16[4,48,3584]{2,1,0:T(8,128)(2,1)S(1)}, bf16[4,48,3584]{2,1,0:T(8,128)(2,1)S(1)}) custom-call(s32[2]{0:T(128)S(1)} %pad_add_fusion.place, bf16[512,128]{1,0:T(8,128)(2,1)S(1)} %get-tuple-element.182.grad_est, bf16[512,384]{1,0:T(8,128)(2,1)S(1)} %get-tuple-element.183.grad_ffn, bf16[512,1536]{1,0:T(8,128)(2,1)S(1)} %get-tuple-element.184.grad_pre, ...), custom_call_target="tpu_custom_call" | custom-call | flops 1409286144 | bytes 6291456 | tf_op jit(solution)/shard_map/pallas_call | solution.py:64
  78.0 4.6 %shard_map.238 = (f32[384,512]{1,0:T(8,128)S(1)}, bf16[1,768,512]{2,1,0:T(8,128)(2,1)S(1)}) custom-call(bf16[1,8,512,512]{3,2,1,0:T(8,128)(2,1)S(1)} %get-tuple-element.196.probs, bf16[1,384,512]{2,1,0:T(8,128)(2,1)S(1)} %get-tuple-element.197.keys_t, bf16[1,384,512]{2,1,0:T(8,128)(2,1)S(1)} %get-tuple-element.198.values_t, ...), custom_call_target="tpu_custom_call" | custom-call | flops 4026531840 | bytes 4194304 | tf_op jit(solution)/shard_map/pallas_call | solution.py:64
  86.6 8.9 %shard_map.239 = (f32[384,512]{1,0:T(8,128)S(1)}, bf16[2,768,512]{2,1,0:T(8,128)(2,1)S(1)}) custom-call(bf16[2,8,512,512]{3,2,1,0:T(8,128)(2,1)S(1)} %get-tuple-element.192.probs, bf16[2,384,512]{2,1,0:T(8,128)(2,1)S(1)} %get-tuple-element.193.keys_t, bf16[2,384,512]{2,1,0:T(8,128)(2,1)S(1)} %get-tuple-element.194.values_t, ...), custom_call_target="tpu_custom_call" | custom-call | flops 8053063680 | bytes 8388608 | tf_op jit(solution)/shard_map/pallas_call | solution.py:64
  95.5 4.4 %shard_map.240 = (f32[384,512]{1,0:T(8,128)S(1)}, bf16[1,768,512]{2,1,0:T(8,128)(2,1)S(1)}) custom-call(bf16[1,8,512,512]{3,2,1,0:T(8,128)(2,1)S(1)} %get-tuple-element.147.probs, bf16[1,384,512]{2,1,0:T(8,128)(2,1)S(1)} %get-tuple-element.148.keys_t, bf16[1,384,512]{2,1,0:T(8,128)(2,1)S(1)} %get-tuple-element.149.values_t, ...), custom_call_target="tpu_custom_call" | custom-call | flops 4026531840 | bytes 4194304 | tf_op jit(solution)/shard_map/pallas_call | solution.py:64
  99.9 3.1 %shard_map.241 = (bf16[4,48,1280]{2,1,0:T(8,128)(2,1)S(1)}, bf16[4,48,1280]{2,1,0:T(8,128)(2,1)S(1)}) custom-call(s32[2]{0:T(128)S(1)} %pad_add_fusion.place, f32[384,512]{1,0:T(8,128)S(1)} %get-tuple-element.205.grad_queries, bf16[512,384]{1,0:T(8,128)(2,1)S(1)} %get-tuple-element.206.own_unit, bf16[1152,384]{1,0:T(8,128)(2,1)S(1)} %get-tuple-element.132.refs_1_.weights_t, ...), custom_call_target="tpu_custom_call" | custom-call | flops 1811939328 | bytes 1572864 | tf_op jit(solution)/shard_map/pallas_call | solution.py:64
  106.1 2.8 %collective-permute-start.24 = (bf16[48,1280]{1,0:T(8,128)(2,1)S(1)}, bf16[48,1280]{1,0:T(8,128)(2,1)S(1)}, u32[]{:S(2)}, u32[]{:S(2)}) collective-permute-start(bf16[48,1280]{1,0:T(8,128)(2,1)S(1)} %get-tuple-element.248), channel_id=1, source_target_pairs={{0,3},{1,2},{2,1},{3,0},{4,7},{5,6},{6,5},{7,4},{8,11},{9,10},{10,... | collective-permute-start | bytes 368648 | tf_op jit(solution)/shard_map/ppermute | solution.py:41
  110.5 3.4 %collective-permute-done.28 = bf16[48,3584]{1,0:T(8,128)(2,1)S(1)} collective-permute-done((bf16[48,3584]{1,0:T(8,128)(2,1)S(1)}, bf16[48,3584]{1,0:T(8,128)(2,1)S(1)}, u32[]{:S(2)}, u32[]{:S(2)}) %collective-permute-start.28) | collective-permute-done | bytes 344096 | tf_op jit(solution)/shard_map/ppermute | solution.py:41
  115.7 3.4 %collective-permute-done.30 = bf16[48,1280]{1,0:T(8,128)(2,1)S(1)} collective-permute-done((bf16[48,1280]{1,0:T(8,128)(2,1)S(1)}, bf16[48,1280]{1,0:T(8,128)(2,1)S(1)}, u32[]{:S(2)}, u32[]{:S(2)}) %collective-permute-start.30) | collective-permute-done | bytes 122912 | tf_op jit(solution)/shard_map/ppermute | solution.py:41
  127.4 3.5 %collective-permute-start.36 = (f32[8,128]{1,0:T(8,128)S(1)}, f32[8,128]{1,0:T(8,128)S(1)}, u32[]{:S(2)}, u32[]{:S(2)}) collective-permute-start(f32[8,128]{1,0:T(8,128)S(1)} %shard_map.243.squares), channel_id=1, source_target_pairs={{0,8},{8,0},{16,24},{24,16},{1,9},{9,1},{17,25},{25,17},{2,10},{10... | collective-permute-start | bytes 12296 | tf_op jit(solution)/shard_map/ppermute | solution.py:41
  131.8 4.4 %shard_map.244 = (f32[96,3200]{1,0:T(8,128)}, f32[384,384]{1,0:T(8,128)}, f32[6,128]{1,0:T(8,128)}, f32[96,3200]{1,0:T(8,128)}, f32[384,384]{1,0:T(8,128)}, /*in...) custom-call(s32[2]{0:T(128)S(1)} %pad_add_fusion.place, ...), custom_call_target="tpu_custom_call" | custom-call | flops 9108480 | bytes 12751872 | tf_op jit(solution)/shard_map/pallas_call | solution.py:64
  (113 shorter events, 40.5 us)
Async XLA Ops:
  0.6 23.8 %collective-permute-start = (bf16[512,384]{1,0:T(8,128)(2,1)}, bf16[512,384]{1,0:T(8,128)(2,1)S(1)}, u32[]{:S(2)}, u32[]{:S(2)}) collective-permute-start(bf16[512,384]{1,0:T(8,128)(2,1)} %bitcast.40), channel_id=1, source_target_pairs={{0,4},{1,5},{2,6},{3,7},{4,0},{5,1},{6,2},{7,3},{8,12},{9,13},{10,... | collective-permute-start | bytes 1179656 | tf_op jit(solution)/shard_map/ppermute | solution.py:41
  8.5 8.7 %collective-permute-start.3 = (bf16[48,1280]{1,0:T(8,128)(2,1)S(1)}, bf16[48,1280]{1,0:T(8,128)(2,1)S(1)}, u32[]{:S(2)}, u32[]{:S(2)}) collective-permute-start(bf16[48,1280]{1,0:T(8,128)(2,1)S(1)} %get-tuple-element.128), channel_id=1, source_target_pairs={{0,3},{1,2},{2,1},{3,0},{4,7},{5,6},{6,5},{7,4},{8,11},{9,10},{10,... | collective-permute-start | bytes 368648 | tf_op jit(solution)/shard_map/ppermute | solution.py:41
  11.1 13.1 %collective-permute-start.2 = (bf16[48,1280]{1,0:T(8,128)(2,1)S(1)}, bf16[48,1280]{1,0:T(8,128)(2,1)S(1)}, u32[]{:S(2)}, u32[]{:S(2)}) collective-permute-start(bf16[48,1280]{1,0:T(8,128)(2,1)S(1)} %get-tuple-element.128), channel_id=1, source_target_pairs={{0,2},{1,3},{2,0},{3,1},{4,6},{5,7},{6,4},{7,5},{8,10},{9,11},{10,... | collective-permute-start | bytes 368648 | tf_op jit(solution)/shard_map/ppermute | solution.py:41
  11.6 12.7 %collective-permute-start.1 = (bf16[48,1280]{1,0:T(8,128)(2,1)S(1)}, bf16[48,1280]{1,0:T(8,128)(2,1)S(1)}, u32[]{:S(2)}, u32[]{:S(2)}) collective-permute-start(bf16[48,1280]{1,0:T(8,128)(2,1)S(1)} %get-tuple-element.128), channel_id=1, source_target_pairs={{0,1},{1,0},{2,3},{3,2},{4,5},{5,4},{6,7},{7,6},{8,9},{9,8},{10,11... | collective-permute-start | bytes 368648 | tf_op jit(solution)/shard_map/ppermute | solution.py:41
  12.1 12.4 %collective-permute-start.4 = (bf16[48,3584]{1,0:T(8,128)(2,1)S(1)}, bf16[48,3584]{1,0:T(8,128)(2,1)S(1)}, u32[]{:S(2)}, u32[]{:S(2)}) collective-permute-start(bf16[48,3584]{1,0:T(8,128)(2,1)S(1)} %get-tuple-element.143.refs_0_), channel_id=1, source_target_pairs={{0,1},{1,0},{2,3},{3,2},{4,5},{5,4},{6,7},{7,6},{8,9},{9,8},{10,11... | collective-permute-start | bytes 1032200 | tf_op jit(solution)/shard_map/ppermute | solution.py:41
  24.4 13.0 %collective-permute-start.7 = (bf16[512,384]{1,0:T(8,128)(2,1)S(1)}, bf16[512,384]{1,0:T(8,128)(2,1)S(1)}, u32[]{:S(2)}, u32[]{:S(2)}) collective-permute-start(bf16[512,384]{1,0:T(8,128)(2,1)S(1)} %collective-permute-done.refs_3_), channel_id=1, source_target_pairs={{0,2},{1,3},{2,0},{3,1},{4,6},{5,7},{6,4},{7,5},{8,10},{9,11},{10,... | collective-permute-start | bytes 1179656 | tf_op jit(solution)/shard_map/ppermute | solution.py:41
  27.4 10.0 %collective-permute-start.6 = (bf16[512,384]{1,0:T(8,128)(2,1)S(1)}, bf16[512,384]{1,0:T(8,128)(2,1)S(1)}, u32[]{:S(2)}, u32[]{:S(2)}) collective-permute-start(bf16[512,384]{1,0:T(8,128)(2,1)S(1)} %collective-permute-done.refs_3_), channel_id=1, source_target_pairs={{0,1},{1,0},{2,3},{3,2},{4,5},{5,4},{6,7},{7,6},{8,9},{9,8},{10,11... | collective-permute-start | bytes 1179656 | tf_op jit(solution)/shard_map/ppermute | solution.py:41
  27.9 22.0 %collective-permute-start.11 = (bf16[2,48,3584]{2,1,0:T(8,128)(2,1)S(1)}, bf16[2,48,3584]{2,1,0:T(8,128)(2,1)S(1)}, u32[]{:S(2)}, u32[]{:S(2)}) collective-permute-start(bf16[2,48,3584]{2,1,0:T(8,128)(2,1)S(1)} %pad_maximum_fusion), channel_id=1, source_target_pairs={{0,2},{1,3},{2,0},{3,1},{4,6},{5,7},{6,4},{7,5},{8,10},{9,11},{10,... | collective-permute-start | bytes 2064392 | tf_op jit(solution)/shard_map/ppermute | solution.py:41
  37.4 8.8 %collective-permute-start.8 = (bf16[512,384]{1,0:T(8,128)(2,1)S(1)}, bf16[512,384]{1,0:T(8,128)(2,1)S(1)}, u32[]{:S(2)}, u32[]{:S(2)}) collective-permute-start(bf16[512,384]{1,0:T(8,128)(2,1)S(1)} %collective-permute-done.7.refs_3_), channel_id=1, source_target_pairs={{0,1},{1,0},{2,3},{3,2},{4,5},{5,4},{6,7},{7,6},{8,9},{9,8},{10,11... | collective-permute-start | bytes 1179656 | tf_op jit(solution)/shard_map/ppermute | solution.py:41
  37.9 8.2 %collective-permute-start.9 = (bf16[48,3584]{1,0:T(8,128)(2,1)S(1)}, bf16[48,3584]{1,0:T(8,128)(2,1)S(1)}, u32[]{:S(2)}, u32[]{:S(2)}) collective-permute-start(bf16[48,3584]{1,0:T(8,128)(2,1)S(1)} %get-tuple-element.143.refs_0_), channel_id=1, source_target_pairs={{0,8},{8,0},{16,24},{24,16},{1,9},{9,1},{17,25},{25,17},{2,10},{10... | collective-permute-start | bytes 1032200 | tf_op jit(solution)/shard_map/ppermute | solution.py:41
  37.9 8.2 %collective-permute-start.10 = (bf16[48,3584]{1,0:T(8,128)(2,1)S(1)}, bf16[48,3584]{1,0:T(8,128)(2,1)S(1)}, u32[]{:S(2)}, u32[]{:S(2)}) collective-permute-start(bf16[48,3584]{1,0:T(8,128)(2,1)S(1)} %collective-permute-done.4.refs_1_), channel_id=1, source_target_pairs={{0,8},{8,0},{16,24},{24,16},{1,9},{9,1},{17,25},{25,17},{2,10},{10... | collective-permute-start | bytes 1032200 | tf_op jit(solution)/shard_map/ppermute | solution.py:41
  55.5 9.3 %collective-permute-start.13 = (bf16[384,128]{1,0:T(8,128)(2,1)S(1)}, bf16[384,128]{1,0:T(8,128)(2,1)S(1)}, u32[]{:S(2)}, u32[]{:S(2)}) collective-permute-start(bf16[384,128]{1,0:T(8,128)(2,1)S(1)} %get-tuple-element.158.refs_0_), channel_id=1, source_target_pairs={{0,4},{1,5},{2,6},{3,7},{4,0},{5,1},{6,2},{7,3},{8,12},{9,13},{10,... | collective-permute-start | bytes 294920 | tf_op jit(solution)/shard_map/ppermute | solution.py:41
  57.8 7.0 %collective-permute-start.14 = (bf16[128,128]{1,0:T(8,128)(2,1)S(1)}, bf16[128,128]{1,0:T(8,128)(2,1)S(1)}, u32[]{:S(2)}, u32[]{:S(2)}) collective-permute-start(bf16[128,128]{1,0:T(8,128)(2,1)S(1)} %get-tuple-element.169.refs_1_), channel_id=1, source_target_pairs={{0,4},{1,5},{2,6},{3,7},{4,0},{5,1},{6,2},{7,3},{8,12},{9,13},{10,... | collective-permute-start | bytes 98312 | tf_op jit(solution)/shard_map/ppermute | solution.py:41
  77.9 4.7 %collective-permute-start.18 = (bf16[4,48,3584]{2,1,0:T(8,128)(2,1)S(1)}, bf16[4,48,3584]{2,1,0:T(8,128)(2,1)S(1)}, u32[]{:S(2)}, u32[]{:S(2)}) collective-permute-start(bf16[4,48,3584]{2,1,0:T(8,128)(2,1)S(1)} %get-tuple-element.202), channel_id=1, source_target_pairs={{0,8},{8,0},{16,24},{24,16},{1,9},{9,1},{17,25},{25,17},{2,10},{10... | collective-permute-start | bytes 4128776 | tf_op jit(solution)/shard_map/ppermute | solution.py:41
  83.0 20.0 %collective-permute-start.21 = (bf16[48,3584]{1,0:T(8,128)(2,1)S(1)}, bf16[48,3584]{1,0:T(8,128)(2,1)S(1)}, u32[]{:S(2)}, u32[]{:S(2)}) collective-permute-start(bf16[48,3584]{1,0:T(8,128)(2,1)S(1)} %get-tuple-element.242), channel_id=1, source_target_pairs={{0,1},{1,0},{2,3},{3,2},{4,5},{5,4},{6,7},{7,6},{8,9},{9,8},{10,11... | collective-permute-start | bytes 1032200 | tf_op jit(solution)/shard_map/ppermute | solution.py:41
  83.6 19.4 %collective-permute-start.20 = (bf16[48,3584]{1,0:T(8,128)(2,1)S(1)}, bf16[48,3584]{1,0:T(8,128)(2,1)S(1)}, u32[]{:S(2)}, u32[]{:S(2)}) collective-permute-start(bf16[48,3584]{1,0:T(8,128)(2,1)S(1)} %get-tuple-element.243), channel_id=1, source_target_pairs={{0,3},{1,2},{2,1},{3,0},{4,7},{5,6},{6,5},{7,4},{8,11},{9,10},{10,... | collective-permute-start | bytes 1032200 | tf_op jit(solution)/shard_map/ppermute | solution.py:41
  84.6 18.5 %collective-permute-start.19 = (bf16[48,3584]{1,0:T(8,128)(2,1)S(1)}, bf16[48,3584]{1,0:T(8,128)(2,1)S(1)}, u32[]{:S(2)}, u32[]{:S(2)}) collective-permute-start(bf16[48,3584]{1,0:T(8,128)(2,1)S(1)} %get-tuple-element.244), channel_id=1, source_target_pairs={{0,2},{1,3},{2,0},{3,1},{4,6},{5,7},{6,4},{7,5},{8,10},{9,11},{10,... | collective-permute-start | bytes 1032200 | tf_op jit(solution)/shard_map/ppermute | solution.py:41
  103.4 10.6 %collective-permute-start.28 = (bf16[48,3584]{1,0:T(8,128)(2,1)S(1)}, bf16[48,3584]{1,0:T(8,128)(2,1)S(1)}, u32[]{:S(2)}, u32[]{:S(2)}) collective-permute-start(bf16[48,3584]{1,0:T(8,128)(2,1)S(1)} %add_convert_fusion.3), channel_id=1, source_target_pairs={{0,16},{8,24},{16,0},{24,8},{1,17},{9,25},{17,1},{25,9},{2,18},{10... | collective-permute-start | bytes 1032200 | tf_op jit(solution)/shard_map/ppermute | solution.py:41
  105.3 8.7 %collective-permute-start.23 = (bf16[48,1280]{1,0:T(8,128)(2,1)S(1)}, bf16[48,1280]{1,0:T(8,128)(2,1)S(1)}, u32[]{:S(2)}, u32[]{:S(2)}) collective-permute-start(bf16[48,1280]{1,0:T(8,128)(2,1)S(1)} %get-tuple-element.246), channel_id=1, source_target_pairs={{0,2},{1,3},{2,0},{3,1},{4,6},{5,7},{6,4},{7,5},{8,10},{9,11},{10,... | collective-permute-start | bytes 368648 | tf_op jit(solution)/shard_map/ppermute | solution.py:41
  105.4 8.6 %collective-permute-start.25 = (bf16[48,1280]{1,0:T(8,128)(2,1)S(1)}, bf16[48,1280]{1,0:T(8,128)(2,1)S(1)}, u32[]{:S(2)}, u32[]{:S(2)}) collective-permute-start(bf16[48,1280]{1,0:T(8,128)(2,1)S(1)} %get-tuple-element.247), channel_id=1, source_target_pairs={{0,1},{1,0},{2,3},{3,2},{4,5},{5,4},{6,7},{7,6},{8,9},{9,8},{10,11... | collective-permute-start | bytes 368648 | tf_op jit(solution)/shard_map/ppermute | solution.py:41
  106.1 8.0 %collective-permute-start.24 = (bf16[48,1280]{1,0:T(8,128)(2,1)S(1)}, bf16[48,1280]{1,0:T(8,128)(2,1)S(1)}, u32[]{:S(2)}, u32[]{:S(2)}) collective-permute-start(bf16[48,1280]{1,0:T(8,128)(2,1)S(1)} %get-tuple-element.248), channel_id=1, source_target_pairs={{0,3},{1,2},{2,1},{3,0},{4,7},{5,6},{6,5},{7,4},{8,11},{9,10},{10,... | collective-permute-start | bytes 368648 | tf_op jit(solution)/shard_map/ppermute | solution.py:41
  109.0 5.0 %collective-permute-start.27 = (f32[8,128]{1,0:T(8,128)S(1)}, f32[8,128]{1,0:T(8,128)S(1)}, u32[]{:S(2)}, u32[]{:S(2)}) collective-permute-start(f32[8,128]{1,0:T(8,128)S(1)} %add.50), channel_id=1, source_target_pairs={{0,16},{8,24},{16,0},{24,8},{1,17},{9,25},{17,1},{25,9},{2,18},{10... | collective-permute-start | bytes 12296 | tf_op jit(solution)/shard_map/ppermute | solution.py:41
  114.1 5.0 %collective-permute-start.30 = (bf16[48,1280]{1,0:T(8,128)(2,1)S(1)}, bf16[48,1280]{1,0:T(8,128)(2,1)S(1)}, u32[]{:S(2)}, u32[]{:S(2)}) collective-permute-start(bf16[48,1280]{1,0:T(8,128)(2,1)S(1)} %fusion.2), channel_id=1, source_target_pairs={{0,16},{8,24},{16,0},{24,8},{1,17},{9,25},{17,1},{25,9},{2,18},{10... | collective-permute-start | bytes 368648 | tf_op jit(solution)/shard_map/ppermute | solution.py:41
  115.7 4.8 %collective-permute-start.29 = (bf16[48,3584]{1,0:T(8,128)(2,1)S(1)}, bf16[48,3584]{1,0:T(8,128)(2,1)S(1)}, u32[]{:S(2)}, u32[]{:S(2)}) collective-permute-start(bf16[48,3584]{1,0:T(8,128)(2,1)S(1)} %add_convert_fusion.2.refs_0_.early), channel_id=1, source_target_pairs={{0,8},{8,0},{16,24},{24,16},{1,9},{9,1},{17,25},{25,17},{2,10},{10... | collective-permute-start | bytes 1032200 | tf_op jit(solution)/shard_map/ppermute | solution.py:41
  (28 other events, 309.4 us)

commit v7 on v6

--- a/solution.py
+++ b/solution.py
@@ -118,7 +118,8 @@
     )
 
 
-def start_kernel(size, place, own, mine, other, queries_t, own_unit, weights_t, gains, joined):
+def start_kernel(size, place, own, mine, other, queries_t, own_unit_t, weights_t, gains,
+                 joined):
     core, position = place[0], place[1]
     half = mine.shape[1]
     for owner in range(size):
@@ -134,7 +135,7 @@
         ].astype(F32)
     weights_t[...] = joined[:, :QKV].T
     hat, _ = unit_rows(own[...].astype(F32))
-    own_unit[...] = hat.astype(BF)
+    own_unit_t[...] = hat.astype(BF).T
     normed = (hat * gains[0:1] + gains[1:2]).astype(BF)
     found = dot(weights_t[:D], normed, 1, 1)
     queries_t[...] = (found * (SCALE / LOG_TWO)).astype(BF)
@@ -145,11 +146,16 @@
     return call(
         functools.partial(start_kernel, size),
         (own, mine, other),
-        (sds((D, rows), BF), sds((rows, D), BF), sds((QKV, D), BF), sds((8, D), F32)),
+        (
+            sds((D, rows), BF),
+            sds((D, rows), BF),
+            sds((QKV, D), BF),
+            sds((8, D), F32),
+            sds((D, QKV + LANES), BF),
+        ),
         2 * rows * D * D,
         rows * D * 8,
         place=(place,),
-        scratch=[pltpu.VMEM((D, QKV + LANES), BF)],
     )
 
 
@@ -184,7 +190,7 @@
     if carried:
         accum_in, top_in = refs[:2]
         refs = refs[2:]
-    probs, keys_t, values_t, unit, tops, accum, top, joined = refs
+    probs, keys_t, values_t, unit_t, tops, accum, top, joined = refs
     if carried:
         accum[...] = accum_in[...]
         top[...] = top_in[...]
@@ -196,7 +202,7 @@
 
     def visit(block):
         hat, _ = unit_rows(joined[block].astype(F32))
-        unit[block] = hat.astype(BF)
+        unit_t[block] = hat.astype(BF).T
         crossed = (hat * gains[2:3] + gains[3:4]).astype(BF)
         keys_t[block] = dot(weights_t[D : 2 * D], crossed, 1, 1).astype(BF)
         values_t[block] = dot(weights_t[2 * D :], crossed, 1, 1).astype(BF)
@@ -235,7 +241,7 @@
             sds((count, HEADS, rows, tokens), BF),
             sds((count, D, rows), BF),
             sds((count, D, rows), BF),
-            sds((count, rows, D), BF),
+            sds((count, D, rows), BF),
             sds((count, HEADS, tokens), F32),
             sds((64 * HEADS, tokens), F32),
             sds((HEADS, tokens), F32),
@@ -548,29 +554,37 @@
     )
 
 
-def finish_kernel(size, groups, place, grad_queries, own_unit, weights_t, gains, late,
-                  *refs):
+def unit_products(units, grads):
+    total = None
+    for k in range(0, len(units), 4):
+        left = jnp.concatenate(units[k : k + 4], axis=1)
+        left = jnp.concatenate([left, jnp.ones((16, left.shape[1]), BF)], axis=0)
+        term = dot(left, jnp.concatenate(grads[k : k + 4], axis=1), 1, 1)
+        total = term if total is None else total + term
+    return total
+
+
+def finish_kernel(size, groups, place, grad_queries, own_unit_t, weights, gains, late, *refs):
     grads, units = refs[:groups], refs[groups : 2 * groups]
-    keep, send, moments, full, grad_gains = refs[2 * groups :]
-    rows = own_unit.shape[0]
-    ones = jnp.ones((rows, LANES), BF)
+    keep, send, full, grad_gains = refs[2 * groups :]
     query = (grad_queries[...] * SCALE).astype(BF)
-    moments[:D] = dot(query, jnp.concatenate([own_unit[...], ones], axis=1))
-    total = None
-    for grad, unit in zip(grads, units):
-        for block in range(grad.shape[0]):
-            term = dot(grad[block], jnp.concatenate([unit[block], ones], axis=1))
-            total = term if total is None else total + term
-    moments[D:] = total
-    for first, size_out, row in ((0, D, 0), (D, 2 * D, 2)):
-        at = slice(first, first + size_out)
-        moment = moments[at, :D]
-        column = moments[at, D : D + 1]
-        weight = weights_t[at].astype(F32)
-        grad_gains[row : row + 1] = jnp.sum(weight * moment, axis=0, keepdims=True)
-        grad_gains[row + 1 : row + 2] = jnp.sum(weight * column, axis=0, keepdims=True)
-        product = moment * gains[row : row + 1] + column * gains[row + 1 : row + 2]
-        full[:, at] = product.T
+    blocks = [(g, block) for g, grad in enumerate(grads) for block in range(grad.shape[0])]
+    found = (
+        unit_products([own_unit_t[...]], [query]),
+        unit_products([units[g][b] for g, b in blocks], [grads[g][b] for g, b in blocks]),
+    )
+    columns = gains[...].T
+    lane = lax.broadcasted_iota(jnp.int32, (D, LANES), 1)
+    small = jnp.zeros((D, LANES), F32)
+    for product, first, row in zip(found, (0, D), (0, 2)):
+        at = slice(first, first + product.shape[1])
+        moment, total = product[:D], product[D : D + 1]
+        weight = weights[:, at].astype(F32)
+        for k, terms in enumerate((weight * moment, weight * total)):
+            small = jnp.where(lane == row + k, jnp.sum(terms, axis=1, keepdims=True), small)
+        value = moment * columns[:, row : row + 1] + total * columns[:, row + 1 : row + 2]
+        full[:, at] = value.astype(BF)
+    grad_gains[:4] = small.T[:4]
     grad_gains[4:8] = late[...]
     half = keep.shape[1]
     for owner in range(size):
@@ -579,31 +593,34 @@
             size, place, full[row : row + half], full[row + half : row + 2 * half],
             keep, send, owner, slice(0, QKV),
         )
+    same = place[0] == 0
+    tall, across = gain_shape(size)
+    for owner in range(size):
+        rows = [
+            grad_gains[vector : vector + 1, lane : lane + across]
+            for where, _, vector, lane, _ in gain_places(size)
+            if where == owner
+        ]
+        block = jnp.concatenate(rows + [jnp.zeros((half - tall, across), F32)], axis=0)
+        if across < LANES:
+            block = jnp.concatenate([block, jnp.zeros((half, LANES - across), F32)], axis=1)
         slot = owner ^ place[1]
-        keep[slot, :, QKV:] = jnp.zeros((half, LANES), BF)
-        send[slot, :, QKV:] = jnp.zeros((half, LANES), BF)
-    same = place[0] == 0
-    for owner, row, vector, lane, across in gain_places(size):
-        slot = owner ^ place[1]
-        value = grad_gains[vector : vector + 1, lane : lane + across]
-        at = slice(QKV, QKV + across)
-        keep[slot, row : row + 1, at] = jnp.where(same, value, 0.0).astype(BF)
-        send[slot, row : row + 1, at] = jnp.where(same, 0.0, value).astype(BF)
-
-
-def finish(place, grad_queries, own_unit, weights_t, gains, late, grads, units, size):
-    rows = own_unit.shape[0]
+        keep[slot, :, QKV:] = jnp.where(same, block, 0.0).astype(BF)
+        send[slot, :, QKV:] = jnp.where(same, 0.0, block).astype(BF)
+
+
+def finish(place, grad_queries, own_unit_t, weights, gains, late, grads, units, size):
+    rows = own_unit_t.shape[1]
     piece = (size, D // size // 2, QKV + LANES)
     return call(
         functools.partial(finish_kernel, size, len(grads)),
-        (grad_queries, own_unit, weights_t, gains, late, *grads, *units),
+        (grad_queries, own_unit_t, weights, gains, late, *grads, *units),
         (sds(piece, BF), sds(piece, BF)),
         2 * rows * D * QKV * size,
         rows * D * 2 * size,
         place=(place,),
         scratch=[
-            pltpu.VMEM((QKV, D + LANES), F32),
-            pltpu.VMEM((D, QKV), F32),
+            pltpu.VMEM((D, QKV), BF),
             pltpu.VMEM((8, D), F32),
         ],
     )
@@ -830,7 +847,7 @@
     far[high] = swap(far[0], "wide", high)
     for mask in range(1, high):
         far[mask] = swap(far[0], "wide", mask)
-    queries_t, own_unit, weights_t, gains = start(place, own, first_mine, first_other, size)
+    queries_t, own_unit_t, weights_t, gains, first_all = start(place, own, first_mine, first_other, size)
 
     high_mine = swap(jnp.stack(low_mine), "wide", high)
     order = [high, *range(1, high), *range(high + 1, size)]
@@ -894,7 +911,7 @@
             grad_queries, early = tie(grad_queries, early)
             early = send_members(early, size)
     keep, send = finish(
-        place, grad_queries, own_unit, weights_t, gains, late_gains, grads, units, size
+        place, grad_queries, own_unit_t, first_all, gains, late_gains, grads, units, size
     )
     keep, send, *early = tie(keep, send, *early)
     late = core_step(keep, send)

time: 137 us -> 136 us (level)
  transfers between devices with their start and end apart: 37 -> 37, of which waited for: 19 -> 19; matrix products, arithmetic and copies ran while one was open for 1% -> 1% of each run, Pallas kernels for 29% -> 28%
where the time goes in v7:
time: 136 us
  Pallas kernels  53.5 us (39%)
  starting transfers between devices  40.3 us (30%)
  waiting for transfers between devices  36.2 us (27%)
  local copies, waits for them, and re-layouts  3.73 us (3%)
    pallas_call x18, Pallas kernels, call(): pl.pallas_call(kernel, out_shape=out_shape, in_specs=[small] * len(place)...  53.5 us
    ppermute x33, starting transfers between devices, swap(): lax.ppermute(x, axis, [(i, i ^ mask) for i in range(lax.axis_size(axis))])  36.1 us
    ppermute x33, waiting for transfers between devices, swap(): lax.ppermute(x, axis, [(i, i ^ mask) for i in range(lax.axis_size(axis))])  34.3 us
    ppermute x4, starting transfers between devices, branch_parts(): found.append(lax.ppermute(values, ('seg', 'wide'), pairs))  4.14 us
    unnamed x30, local copies, waits for them, and re-layouts  3.1 us
  transfers between devices with their start and end apart: 37, of which 19 were waited for; matrix products, arithmetic and copies ran while one was open for 1% of the time, Pallas kernels for 28%

profile of v7, /device:TPU:0, one launch (start us, length us, event | category | flops | bytes accessed | tf_op | source)
XLA Modules:
  0.0 136.0 jit_solution(3977675165871836296)
XLA Ops:
  0.6 4.1 %collective-permute-start = (bf16[512,384]{1,0:T(8,128)(2,1)}, bf16[512,384]{1,0:T(8,128)(2,1)S(1)}, u32[]{:S(2)}, u32[]{:S(2)}) collective-permute-start(bf16[512,384]{1,0:T(8,128)(2,1)} %bitcast.40), channel_id=1, source_target_pairs={{0,4},{1,5},{2,6},{3,7},{4,0},{5,1},{6,2},{7,3},{8,12},{9,13},{10,... | collective-permute-start | bytes 1179656 | tf_op jit(solution)/shard_map/ppermute | solution.py:41
  8.5 2.6 %collective-permute-start.3 = (bf16[48,1280]{1,0:T(8,128)(2,1)S(1)}, bf16[48,1280]{1,0:T(8,128)(2,1)S(1)}, u32[]{:S(2)}, u32[]{:S(2)}) collective-permute-start(bf16[48,1280]{1,0:T(8,128)(2,1)S(1)} %get-tuple-element.129), channel_id=1, source_target_pairs={{0,3},{1,2},{2,1},{3,0},{4,7},{5,6},{6,5},{7,4},{8,11},{9,10},{10,... | collective-permute-start | bytes 368648 | tf_op jit(solution)/shard_map/ppermute | solution.py:41
  13.6 3.6 %collective-permute-done.3 = bf16[48,1280]{1,0:T(8,128)(2,1)S(1)} collective-permute-done((bf16[48,1280]{1,0:T(8,128)(2,1)S(1)}, bf16[48,1280]{1,0:T(8,128)(2,1)S(1)}, u32[]{:S(2)}, u32[]{:S(2)}) %collective-permute-start.3) | collective-permute-done | bytes 122912 | tf_op jit(solution)/shard_map/ppermute | solution.py:41
  17.2 7.0 %collective-permute-done.2 = bf16[48,1280]{1,0:T(8,128)(2,1)S(1)} collective-permute-done((bf16[48,1280]{1,0:T(8,128)(2,1)S(1)}, bf16[48,1280]{1,0:T(8,128)(2,1)S(1)}, u32[]{:S(2)}, u32[]{:S(2)}) %collective-permute-start.2) | collective-permute-done | bytes 122912 | tf_op jit(solution)/shard_map/ppermute | solution.py:41
  24.4 2.9 %collective-permute-start.7 = (bf16[512,384]{1,0:T(8,128)(2,1)S(1)}, bf16[512,384]{1,0:T(8,128)(2,1)S(1)}, u32[]{:S(2)}, u32[]{:S(2)}) collective-permute-start(bf16[512,384]{1,0:T(8,128)(2,1)S(1)} %collective-permute-done.refs_3_), channel_id=1, source_target_pairs={{0,2},{1,3},{2,0},{3,1},{4,6},{5,7},{6,4},{7,5},{8,10},{9,11},{10,... | collective-permute-start | bytes 1179656 | tf_op jit(solution)/shard_map/ppermute | solution.py:41
  31.0 3.5 %shard_map.229 = (bf16[1,8,512,512]{3,2,1,0:T(8,128)(2,1)S(1)}, bf16[1,384,512]{2,1,0:T(8,128)(2,1)S(1)}, bf16[1,384,512]{2,1,0:T(8,128)(2,1)S(1)}, bf16[1,384,5...) custom-call(bf16[384,512]{1,0:T(8,128)(2,1)S(1)} %get-tuple-element.132.refs_0_., ...), custom_call_target="tpu_custom_call" | custom-call | flops 100663296 | bytes 262144 | tf_op jit(solution)/shard_map/pallas_call | solution.py:64
  34.5 2.9 %collective-permute-done.7.refs_3_ = bf16[512,384]{1,0:T(8,128)(2,1)S(1)} collective-permute-done((bf16[512,384]{1,0:T(8,128)(2,1)S(1)}, bf16[512,384]{1,0:T(8,128)(2,1)S(1)}, u32[]{:S(2)}, u32[]{:S(2)}) %collective-permute-start.7) | collective-permute-done | bytes 393248 | tf_op jit(solution)/shard_map/ppermute | solution.py:41
  38.4 7.3 %shard_map.230 = (bf16[2,8,512,512]{3,2,1,0:T(8,128)(2,1)S(1)}, bf16[2,384,512]{2,1,0:T(8,128)(2,1)S(1)}, bf16[2,384,512]{2,1,0:T(8,128)(2,1)S(1)}, bf16[2,384,5...) custom-call(bf16[384,512]{1,0:T(8,128)(2,1)S(1)} %get-tuple-element.132.refs_0_., ...), custom_call_target="tpu_custom_call" | custom-call | flops 201326592 | bytes 524288 | tf_op jit(solution)/shard_map/pallas_call | solution.py:64
  45.8 3.6 %shard_map.231 = (bf16[1,8,512,512]{3,2,1,0:T(8,128)(2,1)S(1)}, bf16[1,384,512]{2,1,0:T(8,128)(2,1)S(1)}, bf16[1,384,512]{2,1,0:T(8,128)(2,1)S(1)}, bf16[1,384,5...) custom-call(bf16[384,512]{1,0:T(8,128)(2,1)S(1)} %get-tuple-element.132.refs_0_., ...), custom_call_target="tpu_custom_call" | custom-call | flops 100663296 | bytes 262144 | tf_op jit(solution)/shard_map/pallas_call | solution.py:64
  50.0 2.1 %collective-permute-done.12.refs_5_ = bf16[2,48,3584]{2,1,0:T(8,128)(2,1)S(1)} collective-permute-done((bf16[2,48,3584]{2,1,0:T(8,128)(2,1)S(1)}, bf16[2,48,3584]{2,1,0:T(8,128)(2,1)S(1)}, u32[]{:S(2)}, u32[]{:S(2)}) %collective-permute-start.12) | collective-permute-done | bytes 688160 | tf_op jit(solution)/shard_map/ppermute | solution.py:41
  53.0 2.4 %shard_map.233 = (f32[384,512]{1,0:T(8,128)S(1)}, f32[8,512]{1,0:T(8,128)S(1)}, f32[512,384]{1,0:T(8,128)S(1)}, f32[512,384]{1,0:T(8,128)S(1)}, f32[512,1]{1,0:T...) custom-call(bf16[512,384]{1,0:T(8,128)(2,1)S(1)} %bitcast.42, ...), custom_call_target="tpu_custom_call" | custom-call | flops 704643072 | bytes 3145728 | tf_op jit(solution)/shard_map/pallas_call | solution.py:64
  57.6 2.3 %collective-permute-start.14 = (bf16[128,128]{1,0:T(8,128)(2,1)S(1)}, bf16[128,128]{1,0:T(8,128)(2,1)S(1)}, u32[]{:S(2)}, u32[]{:S(2)}) collective-permute-start(bf16[128,128]{1,0:T(8,128)(2,1)S(1)} %get-tuple-element.170.refs_1_), channel_id=1, source_target_pairs={{0,4},{1,5},{2,6},{3,7},{4,0},{5,1},{6,2},{7,3},{8,12},{9,13},{10,... | collective-permute-start | bytes 98312 | tf_op jit(solution)/shard_map/ppermute | solution.py:41
  59.8 4.9 %collective-permute-done.14.refs_3_ = bf16[128,128]{1,0:T(8,128)(2,1)S(1)} collective-permute-done((bf16[128,128]{1,0:T(8,128)(2,1)S(1)}, bf16[128,128]{1,0:T(8,128)(2,1)S(1)}, u32[]{:S(2)}, u32[]{:S(2)}) %collective-permute-start.14) | collective-permute-done | bytes 32800 | tf_op jit(solution)/shard_map/ppermute | solution.py:41
  71.5 3.3 %shard_map.236 = (bf16[512,128]{1,0:T(8,128)(2,1)S(1)}, bf16[512,384]{1,0:T(8,128)(2,1)S(1)}, bf16[512,1536]{1,0:T(8,128)(2,1)S(1)}, bf16[512,384]{1,0:T(8,128)(...) custom-call(s32[2]{0:T(128)S(1)} %pad_add_fusion.place, ...), custom_call_target="tpu_custom_call" | custom-call | flops 1409286144 | bytes 6291456 | tf_op jit(solution)/shard_map/pallas_call | solution.py:64
  74.8 2.5 %shard_map.237 = (bf16[4,48,3584]{2,1,0:T(8,128)(2,1)S(1)}, bf16[4,48,3584]{2,1,0:T(8,128)(2,1)S(1)}) custom-call(s32[2]{0:T(128)S(1)} %pad_add_fusion.place, bf16[512,128]{1,0:T(8,128)(2,1)S(1)} %get-tuple-element.183.grad_est, bf16[512,384]{1,0:T(8,128)(2,1)S(1)} %get-tuple-element.184.grad_ffn, bf16[512,1536]{1,0:T(8,128)(2,1)S(1)} %get-tuple-element.185.grad_pre, ...), custom_call_target="tpu_custom_call" | custom-call | flops 1409286144 | bytes 6291456 | tf_op jit(solution)/shard_map/pallas_call | solution.py:64
  77.4 4.7 %shard_map.238 = (f32[384,512]{1,0:T(8,128)S(1)}, bf16[1,768,512]{2,1,0:T(8,128)(2,1)S(1)}) custom-call(bf16[1,8,512,512]{3,2,1,0:T(8,128)(2,1)S(1)} %get-tuple-element.197.probs, bf16[1,384,512]{2,1,0:T(8,128)(2,1)S(1)} %get-tuple-element.198.keys_t, bf16[1,384,512]{2,1,0:T(8,128)(2,1)S(1)} %get-tuple-element.199.values_t, ...), custom_call_target="tpu_custom_call" | custom-call | flops 4026531840 | bytes 4194304 | tf_op jit(solution)/shard_map/pallas_call | solution.py:64
  86.1 8.9 %shard_map.239 = (f32[384,512]{1,0:T(8,128)S(1)}, bf16[2,768,512]{2,1,0:T(8,128)(2,1)S(1)}) custom-call(bf16[2,8,512,512]{3,2,1,0:T(8,128)(2,1)S(1)} %get-tuple-element.193.probs, bf16[2,384,512]{2,1,0:T(8,128)(2,1)S(1)} %get-tuple-element.194.keys_t, bf16[2,384,512]{2,1,0:T(8,128)(2,1)S(1)} %get-tuple-element.195.values_t, ...), custom_call_target="tpu_custom_call" | custom-call | flops 8053063680 | bytes 8388608 | tf_op jit(solution)/shard_map/pallas_call | solution.py:64
  95.0 4.4 %shard_map.240 = (f32[384,512]{1,0:T(8,128)S(1)}, bf16[1,768,512]{2,1,0:T(8,128)(2,1)S(1)}) custom-call(bf16[1,8,512,512]{3,2,1,0:T(8,128)(2,1)S(1)} %get-tuple-element.148.probs, bf16[1,384,512]{2,1,0:T(8,128)(2,1)S(1)} %get-tuple-element.149.keys_t, bf16[1,384,512]{2,1,0:T(8,128)(2,1)S(1)} %get-tuple-element.150.values_t, ...), custom_call_target="tpu_custom_call" | custom-call | flops 4026531840 | bytes 4194304 | tf_op jit(solution)/shard_map/pallas_call | solution.py:64
  99.4 3.0 %shard_map.241 = (bf16[4,48,1280]{2,1,0:T(8,128)(2,1)S(1)}, bf16[4,48,1280]{2,1,0:T(8,128)(2,1)S(1)}) custom-call(s32[2]{0:T(128)S(1)} %pad_add_fusion.place, f32[384,512]{1,0:T(8,128)S(1)} %get-tuple-element.206.grad_queries, bf16[384,512]{1,0:T(8,128)(2,1)S(1)} %get-tuple-element.207.own_unit_t, bf16[384,1280]{1,0:T(8,128)(2,1)S(1)} %get-tuple-element.208.weights, ...), custom_call_target="tpu_custom_call" | custom-call | flops 1811939328 | bytes 1572864 | tf_op jit(solution)/shard_map/pallas_call | solution.py:64
  106.0 2.4 %collective-permute-start.24 = (bf16[48,1280]{1,0:T(8,128)(2,1)S(1)}, bf16[48,1280]{1,0:T(8,128)(2,1)S(1)}, u32[]{:S(2)}, u32[]{:S(2)}) collective-permute-start(bf16[48,1280]{1,0:T(8,128)(2,1)S(1)} %get-tuple-element.250), channel_id=1, source_target_pairs={{0,3},{1,2},{2,1},{3,0},{4,7},{5,6},{6,5},{7,4},{8,11},{9,10},{10,... | collective-permute-start | bytes 368648 | tf_op jit(solution)/shard_map/ppermute | solution.py:41
  110.0 3.3 %collective-permute-done.28 = bf16[48,3584]{1,0:T(8,128)(2,1)S(1)} collective-permute-done((bf16[48,3584]{1,0:T(8,128)(2,1)S(1)}, bf16[48,3584]{1,0:T(8,128)(2,1)S(1)}, u32[]{:S(2)}, u32[]{:S(2)}) %collective-permute-start.28) | collective-permute-done | bytes 344096 | tf_op jit(solution)/shard_map/ppermute | solution.py:41
  115.2 3.4 %collective-permute-done.30 = bf16[48,1280]{1,0:T(8,128)(2,1)S(1)} collective-permute-done((bf16[48,1280]{1,0:T(8,128)(2,1)S(1)}, bf16[48,1280]{1,0:T(8,128)(2,1)S(1)}, u32[]{:S(2)}, u32[]{:S(2)}) %collective-permute-start.30) | collective-permute-done | bytes 122912 | tf_op jit(solution)/shard_map/ppermute | solution.py:41
  126.8 3.6 %collective-permute-start.36 = (f32[8,128]{1,0:T(8,128)S(1)}, f32[8,128]{1,0:T(8,128)S(1)}, u32[]{:S(2)}, u32[]{:S(2)}) collective-permute-start(f32[8,128]{1,0:T(8,128)S(1)} %shard_map.243.squares), channel_id=1, source_target_pairs={{0,8},{8,0},{16,24},{24,16},{1,9},{9,1},{17,25},{25,17},{2,10},{10... | collective-permute-start | bytes 12296 | tf_op jit(solution)/shard_map/ppermute | solution.py:41
  131.4 4.4 %shard_map.244 = (f32[96,3200]{1,0:T(8,128)}, f32[384,384]{1,0:T(8,128)}, f32[6,128]{1,0:T(8,128)}, f32[96,3200]{1,0:T(8,128)}, f32[384,384]{1,0:T(8,128)}, /*in...) custom-call(s32[2]{0:T(128)S(1)} %pad_add_fusion.place, ...), custom_call_target="tpu_custom_call" | custom-call | flops 9108480 | bytes 12751872 | tf_op jit(solution)/shard_map/pallas_call | solution.py:64
  (113 shorter events, 41.5 us)
Async XLA Ops:
  0.6 23.8 %collective-permute-start = (bf16[512,384]{1,0:T(8,128)(2,1)}, bf16[512,384]{1,0:T(8,128)(2,1)S(1)}, u32[]{:S(2)}, u32[]{:S(2)}) collective-permute-start(bf16[512,384]{1,0:T(8,128)(2,1)} %bitcast.40), channel_id=1, source_target_pairs={{0,4},{1,5},{2,6},{3,7},{4,0},{5,1},{6,2},{7,3},{8,12},{9,13},{10,... | collective-permute-start | bytes 1179656 | tf_op jit(solution)/shard_map/ppermute | solution.py:41
  8.5 8.7 %collective-permute-start.3 = (bf16[48,1280]{1,0:T(8,128)(2,1)S(1)}, bf16[48,1280]{1,0:T(8,128)(2,1)S(1)}, u32[]{:S(2)}, u32[]{:S(2)}) collective-permute-start(bf16[48,1280]{1,0:T(8,128)(2,1)S(1)} %get-tuple-element.129), channel_id=1, source_target_pairs={{0,3},{1,2},{2,1},{3,0},{4,7},{5,6},{6,5},{7,4},{8,11},{9,10},{10,... | collective-permute-start | bytes 368648 | tf_op jit(solution)/shard_map/ppermute | solution.py:41
  11.1 13.1 %collective-permute-start.2 = (bf16[48,1280]{1,0:T(8,128)(2,1)S(1)}, bf16[48,1280]{1,0:T(8,128)(2,1)S(1)}, u32[]{:S(2)}, u32[]{:S(2)}) collective-permute-start(bf16[48,1280]{1,0:T(8,128)(2,1)S(1)} %get-tuple-element.129), channel_id=1, source_target_pairs={{0,2},{1,3},{2,0},{3,1},{4,6},{5,7},{6,4},{7,5},{8,10},{9,11},{10,... | collective-permute-start | bytes 368648 | tf_op jit(solution)/shard_map/ppermute | solution.py:41
  11.6 12.7 %collective-permute-start.1 = (bf16[48,1280]{1,0:T(8,128)(2,1)S(1)}, bf16[48,1280]{1,0:T(8,128)(2,1)S(1)}, u32[]{:S(2)}, u32[]{:S(2)}) collective-permute-start(bf16[48,1280]{1,0:T(8,128)(2,1)S(1)} %get-tuple-element.129), channel_id=1, source_target_pairs={{0,1},{1,0},{2,3},{3,2},{4,5},{5,4},{6,7},{7,6},{8,9},{9,8},{10,11... | collective-permute-start | bytes 368648 | tf_op jit(solution)/shard_map/ppermute | solution.py:41
  12.1 12.4 %collective-permute-start.4 = (bf16[48,3584]{1,0:T(8,128)(2,1)S(1)}, bf16[48,3584]{1,0:T(8,128)(2,1)S(1)}, u32[]{:S(2)}, u32[]{:S(2)}) collective-permute-start(bf16[48,3584]{1,0:T(8,128)(2,1)S(1)} %get-tuple-element.144.refs_0_), channel_id=1, source_target_pairs={{0,1},{1,0},{2,3},{3,2},{4,5},{5,4},{6,7},{7,6},{8,9},{9,8},{10,11... | collective-permute-start | bytes 1032200 | tf_op jit(solution)/shard_map/ppermute | solution.py:41
  24.4 13.0 %collective-permute-start.7 = (bf16[512,384]{1,0:T(8,128)(2,1)S(1)}, bf16[512,384]{1,0:T(8,128)(2,1)S(1)}, u32[]{:S(2)}, u32[]{:S(2)}) collective-permute-start(bf16[512,384]{1,0:T(8,128)(2,1)S(1)} %collective-permute-done.refs_3_), channel_id=1, source_target_pairs={{0,2},{1,3},{2,0},{3,1},{4,6},{5,7},{6,4},{7,5},{8,10},{9,11},{10,... | collective-permute-start | bytes 1179656 | tf_op jit(solution)/shard_map/ppermute | solution.py:41
  27.4 10.0 %collective-permute-start.6 = (bf16[512,384]{1,0:T(8,128)(2,1)S(1)}, bf16[512,384]{1,0:T(8,128)(2,1)S(1)}, u32[]{:S(2)}, u32[]{:S(2)}) collective-permute-start(bf16[512,384]{1,0:T(8,128)(2,1)S(1)} %collective-permute-done.refs_3_), channel_id=1, source_target_pairs={{0,1},{1,0},{2,3},{3,2},{4,5},{5,4},{6,7},{7,6},{8,9},{9,8},{10,11... | collective-permute-start | bytes 1179656 | tf_op jit(solution)/shard_map/ppermute | solution.py:41
  27.9 22.0 %collective-permute-start.11 = (bf16[2,48,3584]{2,1,0:T(8,128)(2,1)S(1)}, bf16[2,48,3584]{2,1,0:T(8,128)(2,1)S(1)}, u32[]{:S(2)}, u32[]{:S(2)}) collective-permute-start(bf16[2,48,3584]{2,1,0:T(8,128)(2,1)S(1)} %pad_maximum_fusion), channel_id=1, source_target_pairs={{0,2},{1,3},{2,0},{3,1},{4,6},{5,7},{6,4},{7,5},{8,10},{9,11},{10,... | collective-permute-start | bytes 2064392 | tf_op jit(solution)/shard_map/ppermute | solution.py:41
  37.4 8.4 %collective-permute-start.8 = (bf16[512,384]{1,0:T(8,128)(2,1)S(1)}, bf16[512,384]{1,0:T(8,128)(2,1)S(1)}, u32[]{:S(2)}, u32[]{:S(2)}) collective-permute-start(bf16[512,384]{1,0:T(8,128)(2,1)S(1)} %collective-permute-done.7.refs_3_), channel_id=1, source_target_pairs={{0,1},{1,0},{2,3},{3,2},{4,5},{5,4},{6,7},{7,6},{8,9},{9,8},{10,11... | collective-permute-start | bytes 1179656 | tf_op jit(solution)/shard_map/ppermute | solution.py:41
  37.9 7.9 %collective-permute-start.9 = (bf16[48,3584]{1,0:T(8,128)(2,1)S(1)}, bf16[48,3584]{1,0:T(8,128)(2,1)S(1)}, u32[]{:S(2)}, u32[]{:S(2)}) collective-permute-start(bf16[48,3584]{1,0:T(8,128)(2,1)S(1)} %get-tuple-element.144.refs_0_), channel_id=1, source_target_pairs={{0,8},{8,0},{16,24},{24,16},{1,9},{9,1},{17,25},{25,17},{2,10},{10... | collective-permute-start | bytes 1032200 | tf_op jit(solution)/shard_map/ppermute | solution.py:41
  37.9 7.9 %collective-permute-start.10 = (bf16[48,3584]{1,0:T(8,128)(2,1)S(1)}, bf16[48,3584]{1,0:T(8,128)(2,1)S(1)}, u32[]{:S(2)}, u32[]{:S(2)}) collective-permute-start(bf16[48,3584]{1,0:T(8,128)(2,1)S(1)} %collective-permute-done.4.refs_1_), channel_id=1, source_target_pairs={{0,8},{8,0},{16,24},{24,16},{1,9},{9,1},{17,25},{25,17},{2,10},{10... | collective-permute-start | bytes 1032200 | tf_op jit(solution)/shard_map/ppermute | solution.py:41
  55.5 9.3 %collective-permute-start.13 = (bf16[384,128]{1,0:T(8,128)(2,1)S(1)}, bf16[384,128]{1,0:T(8,128)(2,1)S(1)}, u32[]{:S(2)}, u32[]{:S(2)}) collective-permute-start(bf16[384,128]{1,0:T(8,128)(2,1)S(1)} %get-tuple-element.159.refs_0_), channel_id=1, source_target_pairs={{0,4},{1,5},{2,6},{3,7},{4,0},{5,1},{6,2},{7,3},{8,12},{9,13},{10,... | collective-permute-start | bytes 294920 | tf_op jit(solution)/shard_map/ppermute | solution.py:41
  57.6 7.2 %collective-permute-start.14 = (bf16[128,128]{1,0:T(8,128)(2,1)S(1)}, bf16[128,128]{1,0:T(8,128)(2,1)S(1)}, u32[]{:S(2)}, u32[]{:S(2)}) collective-permute-start(bf16[128,128]{1,0:T(8,128)(2,1)S(1)} %get-tuple-element.170.refs_1_), channel_id=1, source_target_pairs={{0,4},{1,5},{2,6},{3,7},{4,0},{5,1},{6,2},{7,3},{8,12},{9,13},{10,... | collective-permute-start | bytes 98312 | tf_op jit(solution)/shard_map/ppermute | solution.py:41
  77.3 4.7 %collective-permute-start.18 = (bf16[4,48,3584]{2,1,0:T(8,128)(2,1)S(1)}, bf16[4,48,3584]{2,1,0:T(8,128)(2,1)S(1)}, u32[]{:S(2)}, u32[]{:S(2)}) collective-permute-start(bf16[4,48,3584]{2,1,0:T(8,128)(2,1)S(1)} %get-tuple-element.203), channel_id=1, source_target_pairs={{0,8},{8,0},{16,24},{24,16},{1,9},{9,1},{17,25},{25,17},{2,10},{10... | collective-permute-start | bytes 4128776 | tf_op jit(solution)/shard_map/ppermute | solution.py:41
  82.5 19.9 %collective-permute-start.21 = (bf16[48,3584]{1,0:T(8,128)(2,1)S(1)}, bf16[48,3584]{1,0:T(8,128)(2,1)S(1)}, u32[]{:S(2)}, u32[]{:S(2)}) collective-permute-start(bf16[48,3584]{1,0:T(8,128)(2,1)S(1)} %get-tuple-element.244), channel_id=1, source_target_pairs={{0,1},{1,0},{2,3},{3,2},{4,5},{5,4},{6,7},{7,6},{8,9},{9,8},{10,11... | collective-permute-start | bytes 1032200 | tf_op jit(solution)/shard_map/ppermute | solution.py:41
  83.6 18.8 %collective-permute-start.20 = (bf16[48,3584]{1,0:T(8,128)(2,1)S(1)}, bf16[48,3584]{1,0:T(8,128)(2,1)S(1)}, u32[]{:S(2)}, u32[]{:S(2)}) collective-permute-start(bf16[48,3584]{1,0:T(8,128)(2,1)S(1)} %get-tuple-element.245), channel_id=1, source_target_pairs={{0,3},{1,2},{2,1},{3,0},{4,7},{5,6},{6,5},{7,4},{8,11},{9,10},{10,... | collective-permute-start | bytes 1032200 | tf_op jit(solution)/shard_map/ppermute | solution.py:41
  84.1 18.4 %collective-permute-start.19 = (bf16[48,3584]{1,0:T(8,128)(2,1)S(1)}, bf16[48,3584]{1,0:T(8,128)(2,1)S(1)}, u32[]{:S(2)}, u32[]{:S(2)}) collective-permute-start(bf16[48,3584]{1,0:T(8,128)(2,1)S(1)} %get-tuple-element.246), channel_id=1, source_target_pairs={{0,2},{1,3},{2,0},{3,1},{4,6},{5,7},{6,4},{7,5},{8,10},{9,11},{10,... | collective-permute-start | bytes 1032200 | tf_op jit(solution)/shard_map/ppermute | solution.py:41
  102.7 10.6 %collective-permute-start.28 = (bf16[48,3584]{1,0:T(8,128)(2,1)S(1)}, bf16[48,3584]{1,0:T(8,128)(2,1)S(1)}, u32[]{:S(2)}, u32[]{:S(2)}) collective-permute-start(bf16[48,3584]{1,0:T(8,128)(2,1)S(1)} %add_convert_fusion.3), channel_id=1, source_target_pairs={{0,16},{8,24},{16,0},{24,8},{1,17},{9,25},{17,1},{25,9},{2,18},{10... | collective-permute-start | bytes 1032200 | tf_op jit(solution)/shard_map/ppermute | solution.py:41
  104.8 8.7 %collective-permute-start.23 = (bf16[48,1280]{1,0:T(8,128)(2,1)S(1)}, bf16[48,1280]{1,0:T(8,128)(2,1)S(1)}, u32[]{:S(2)}, u32[]{:S(2)}) collective-permute-start(bf16[48,1280]{1,0:T(8,128)(2,1)S(1)} %get-tuple-element.248), channel_id=1, source_target_pairs={{0,2},{1,3},{2,0},{3,1},{4,6},{5,7},{6,4},{7,5},{8,10},{9,11},{10,... | collective-permute-start | bytes 368648 | tf_op jit(solution)/shard_map/ppermute | solution.py:41
  104.9 8.6 %collective-permute-start.25 = (bf16[48,1280]{1,0:T(8,128)(2,1)S(1)}, bf16[48,1280]{1,0:T(8,128)(2,1)S(1)}, u32[]{:S(2)}, u32[]{:S(2)}) collective-permute-start(bf16[48,1280]{1,0:T(8,128)(2,1)S(1)} %get-tuple-element.249), channel_id=1, source_target_pairs={{0,1},{1,0},{2,3},{3,2},{4,5},{5,4},{6,7},{7,6},{8,9},{9,8},{10,11... | collective-permute-start | bytes 368648 | tf_op jit(solution)/shard_map/ppermute | solution.py:41
  106.0 7.6 %collective-permute-start.24 = (bf16[48,1280]{1,0:T(8,128)(2,1)S(1)}, bf16[48,1280]{1,0:T(8,128)(2,1)S(1)}, u32[]{:S(2)}, u32[]{:S(2)}) collective-permute-start(bf16[48,1280]{1,0:T(8,128)(2,1)S(1)} %get-tuple-element.250), channel_id=1, source_target_pairs={{0,3},{1,2},{2,1},{3,0},{4,7},{5,6},{6,5},{7,4},{8,11},{9,10},{10,... | collective-permute-start | bytes 368648 | tf_op jit(solution)/shard_map/ppermute | solution.py:41
  108.4 5.0 %collective-permute-start.27 = (f32[8,128]{1,0:T(8,128)S(1)}, f32[8,128]{1,0:T(8,128)S(1)}, u32[]{:S(2)}, u32[]{:S(2)}) collective-permute-start(f32[8,128]{1,0:T(8,128)S(1)} %add.50), channel_id=1, source_target_pairs={{0,16},{8,24},{16,0},{24,8},{1,17},{9,25},{17,1},{25,9},{2,18},{10... | collective-permute-start | bytes 12296 | tf_op jit(solution)/shard_map/ppermute | solution.py:41
  113.6 4.9 %collective-permute-start.30 = (bf16[48,1280]{1,0:T(8,128)(2,1)S(1)}, bf16[48,1280]{1,0:T(8,128)(2,1)S(1)}, u32[]{:S(2)}, u32[]{:S(2)}) collective-permute-start(bf16[48,1280]{1,0:T(8,128)(2,1)S(1)} %fusion.2), channel_id=1, source_target_pairs={{0,16},{8,24},{16,0},{24,8},{1,17},{9,25},{17,1},{25,9},{2,18},{10... | collective-permute-start | bytes 368648 | tf_op jit(solution)/shard_map/ppermute | solution.py:41
  115.2 4.8 %collective-permute-start.29 = (bf16[48,3584]{1,0:T(8,128)(2,1)S(1)}, bf16[48,3584]{1,0:T(8,128)(2,1)S(1)}, u32[]{:S(2)}, u32[]{:S(2)}) collective-permute-start(bf16[48,3584]{1,0:T(8,128)(2,1)S(1)} %add_convert_fusion.2.refs_0_.early), channel_id=1, source_target_pairs={{0,8},{8,0},{16,24},{24,16},{1,9},{9,1},{17,25},{25,17},{2,10},{10... | collective-permute-start | bytes 1032200 | tf_op jit(solution)/shard_map/ppermute | solution.py:41
  (28 other events, 310.2 us)

commit v8 on v7

--- a/solution.py
+++ b/solution.py
@@ -57,20 +57,28 @@
     return centred * inverse, inverse
 
 
-def call(kernel, operands, out_shape, flops, moved, place=(), scratch=(), in_specs=None,
-         out_specs=None, aliases=None):
+def call(kernel, operands, out_shape, flops, moved, placed=False, scratch=(), out_specs=None,
+         aliases=None):
     here = pl.BlockSpec(memory_space=pltpu.VMEM)
-    small = pl.BlockSpec(memory_space=pltpu.SMEM)
+    size = lax.axis_size("wide") // 2
+
+    def body_of(*refs):
+        if placed:
+            place = lax.axis_index("seg") % 2, lax.axis_index("wide") % size
+            kernel(place, *refs)
+        else:
+            kernel(*refs)
+
     return pl.pallas_call(
-        kernel,
+        body_of,
         out_shape=out_shape,
-        in_specs=[small] * len(place) + (in_specs or [here] * len(operands)),
+        in_specs=[here] * len(operands),
         out_specs=out_specs or jax.tree.map(lambda _: here, out_shape),
         scratch_shapes=scratch,
         input_output_aliases=aliases or {},
         compiler_params=pltpu.CompilerParams(vmem_limit_bytes=VMEM_LIMIT),
         cost_estimate=pl.CostEstimate(flops=flops, bytes_accessed=moved, transcendentals=0),
-    )(*place, *operands)
+    )(*operands)
 
 
 def sds(shape, dtype):
@@ -106,7 +114,7 @@
     first[:tall, QKV : QKV + across] = jnp.where(same, gains[...], 0.0).astype(BF)
 
 
-def pack(place, wide, down, gains, size):
+def pack(wide, down, gains, size):
     half = wide.shape[0] // 2
     return call(
         functools.partial(pack_kernel, size),
@@ -114,7 +122,7 @@
         (sds((half, QKV + LANES), BF), sds((half, REST + 4 * D), BF)),
         1000,
         4 * (wide.size + down.size),
-        place=(place,),
+        placed=True,
     )
 
 
@@ -141,7 +149,7 @@
     queries_t[...] = (found * (SCALE / LOG_TWO)).astype(BF)
 
 
-def start(place, own, mine, other, size):
+def start(own, mine, other, size):
     rows = own.shape[0]
     return call(
         functools.partial(start_kernel, size),
@@ -155,7 +163,7 @@
         ),
         2 * rows * D * D,
         rows * D * 8,
-        place=(place,),
+        placed=True,
     )
 
 
@@ -273,7 +281,7 @@
                 ]
 
 
-def unpack(place, pieces, size):
+def unpack(pieces, size):
     half, across = pieces[0].shape
     return call(
         functools.partial(unpack_kernel, size),
@@ -281,7 +289,7 @@
         (sds((D, REST), BF), sds((FF, D), BF)),
         1000,
         4 * D * across,
-        place=(place,),
+        placed=True,
         scratch=[pltpu.VMEM((2 * size, half, across), BF)],
     )
 
@@ -364,7 +372,7 @@
     energy[...] = total
 
 
-def error_energy(place, own, far, targets):
+def error_energy(own, far, targets):
     rows = own[0].shape[0] + own[1].shape[0]
     return call(
         error_kernel,
@@ -372,18 +380,14 @@
         (sds((rows, OUT), F32), sds((8, OUT), F32)),
         rows * OUT * 8,
         rows * OUT * 12,
-        place=(place,),
-    )
-
-
-def ordered_sum(place, values, joined):
-    size = joined.shape[0]
-    for slot in range(size):
-        joined[slot ^ place[1]] = values[slot]
-    total = joined[0]
-    for slot in range(1, size):
-        total = total + joined[slot]
-    return total
+        placed=True,
+    )
+
+
+def even_sum(parts):
+    while len(parts) > 1:
+        parts = [first + second for first, second in zip(parts[0::2], parts[1::2])]
+    return parts[0]
 
 
 def stem_sums(values):
@@ -395,14 +399,14 @@
     return total
 
 
-def dense_back_kernel(segments, place, present, energies, errors, rest, down, gains, attended_t, branch_out,
+def dense_back_kernel(segments, present, energies, errors, rest, down, gains, attended_t, branch_out,
                       third, third_inverse, slope, ffn_out, grad_est, grad_ffn, grad_pre,
-                      grad_branch, grad_attended_t, delta, grad_gains, loss, joined):
-    energy = ordered_sum(place, energies, joined)
+                      grad_branch, grad_attended_t, delta, grad_gains, loss):
+    energy = even_sum([energies[slot] for slot in range(energies.shape[0])])
     lane = lax.broadcasted_iota(jnp.int32, (1, OUT), 1)
     counted = jnp.zeros((1, OUT), F32)
     for k in range(STEMS):
-        counted = jnp.where(lane // SAMPLES == k, present[0, k].astype(F32), counted)
+        counted = jnp.where(lane // SAMPLES == k, present[:, k : k + 1].astype(F32), counted)
     counted = counted * (10.0 / math.log(10.0) / (segments * STEMS))
     found = stem_sums(energy[0:1]) + ENERGY_EPS
     clean = stem_sums(energy[1:2]) + ENERGY_EPS
@@ -438,12 +442,12 @@
         delta[h : h + 1] = jnp.sum(product[head_rows(h)], axis=0, keepdims=True)
 
 
-def dense_back(segments, place, present, energies, errors, rest, down, gains, attended_t, branch_out, third,
+def dense_back(segments, present, energies, errors, rest, down, gains, attended_t, branch_out, third,
                third_inverse, slope, ffn_out):
     rows = errors.shape[0]
     return call(
         functools.partial(dense_back_kernel, segments),
-        (energies, errors, rest, down, gains, attended_t, branch_out, third,
+        (present, energies, errors, rest, down, gains, attended_t, branch_out, third,
          third_inverse, slope, ffn_out),
         (
             sds((rows, OUT), BF),
@@ -457,8 +461,6 @@
         ),
         2 * rows * D * (D + 2 * FF + OUT),
         rows * FF * 8,
-        place=(place, present),
-        scratch=[pltpu.VMEM(energies.shape, F32)],
     )
 
 
@@ -491,7 +493,7 @@
             )
 
 
-def dense_weights(place, grad_est, grad_ffn, grad_pre, grad_branch, attended_t, normed_two,
+def dense_weights(grad_est, grad_ffn, grad_pre, grad_branch, attended_t, normed_two,
                   hidden, out_rows, size):
     rows = grad_est.shape[0]
     piece = (size, D // size // 2, REST + 4 * D)
@@ -501,7 +503,7 @@
         (sds(piece, BF), sds(piece, BF)),
         2 * rows * D * (D + 2 * FF + OUT),
         rows * FF * 8,
-        place=(place,),
+        placed=True,
         scratch=[pltpu.VMEM((D, REST), F32), pltpu.VMEM((FF, D), F32)],
     )
 
@@ -609,7 +611,7 @@
         send[slot, :, QKV:] = jnp.where(same, 0.0, block).astype(BF)
 
 
-def finish(place, grad_queries, own_unit_t, weights, gains, late, grads, units, size):
+def finish(grad_queries, own_unit_t, weights, gains, late, grads, units, size):
     rows = own_unit_t.shape[1]
     piece = (size, D // size // 2, QKV + LANES)
     return call(
@@ -618,7 +620,7 @@
         (sds(piece, BF), sds(piece, BF)),
         2 * rows * D * QKV * size,
         rows * D * 2 * size,
-        place=(place,),
+        placed=True,
         scratch=[
             pltpu.VMEM((D, QKV), BF),
             pltpu.VMEM((8, D), F32),
@@ -626,43 +628,21 @@
     )
 
 
-def square_kernel(*refs):
-    total = jnp.zeros((1, 1), F32)
-    for ref in refs[:-1]:
+def square_kernel(place, *refs):
+    found = []
+    for ref in refs[:4]:
         values = ref[...].astype(F32)
         rows = jnp.sum(values * values, axis=0, keepdims=True)
-        total = total + jnp.sum(rows, axis=1, keepdims=True)
-    refs[-1][...] = jnp.broadcast_to(total, refs[-1].shape)
+        found.append(jnp.sum(rows, axis=1, keepdims=True))
+    total = jnp.broadcast_to(even_sum(found), refs[4].shape)
+    refs[4][...] = total
+    refs[5][...] = jnp.where(place[0] == 0, total, 0.0)
 
 
 def square_sum(*parts):
     size = sum(x.size for x in parts)
-    return call(square_kernel, parts, sds((8, LANES), F32), 2 * size, 2 * size)
-
-
-def branch_sum_kernel(place, own, *refs):
-    parts, total, joined = refs[:-2], refs[-2], refs[-1]
-    for slot, part in enumerate(parts):
-        value = part[...]
-        if slot == 0:
-            value = jnp.where(place[0] == 0, own[...], value)
-        joined[slot ^ place[1]] = value
-    found = joined[0]
-    for slot in range(1, len(parts)):
-        found = found + joined[slot]
-    total[...] = found
-
-
-def branch_sum(place, own, parts):
-    return call(
-        branch_sum_kernel,
-        (own, *parts),
-        sds(own.shape, F32),
-        own.size,
-        4 * own.size,
-        place=(place,),
-        scratch=[pltpu.VMEM((len(parts),) + own.shape, F32)],
-    )
+    shape = sds((8, LANES), F32)
+    return call(square_kernel, parts, (shape, shape), 2 * size, 2 * size, placed=True)
 
 
 def bits(size):
@@ -797,7 +777,7 @@
         copy.wait()
 
 
-def adam(place, squares, grads, states, size):
+def adam(squares, grads, states, size):
     flat = gain_shape(size)
     states = [x.reshape(flat) if x.ndim == 1 else x for x in states]
     shapes = [x.shape for x in states[:3]]
@@ -810,7 +790,7 @@
         tuple(sds(*kind) for kind in kinds) + (sds((1, 1), F32),),
         20 * count,
         28 * count,
-        place=(place,),
+        placed=True,
         out_specs=(outside,) * 12 + (pl.BlockSpec(memory_space=pltpu.VMEM),),
         scratch=[pltpu.VMEM(*kind) for kind in kinds]
         + [pltpu.SemaphoreType.DMA((4 * len(adam_chunks(size, grads[0].shape[0])),))],
@@ -834,10 +814,9 @@
     size = lax.axis_size("wide") // 2
     position = lax.axis_index("wide") % size
     core = lax.axis_index("seg") % 2
-    place = jnp.stack([core, position]).astype(jnp.int32)
     own = encoded[0]
     far = {0: swap(own, "wide", size)}
-    first, rest = pack(place, wide_master, down_master, gain_master, size)
+    first, rest = pack(wide_master, down_master, gain_master, size)
 
     high = size // 2
     first_mine = jnp.stack([first] + [swap(first, "wide", mask) for mask in range(1, size)])
@@ -847,7 +826,7 @@
     far[high] = swap(far[0], "wide", high)
     for mask in range(1, high):
         far[mask] = swap(far[0], "wide", mask)
-    queries_t, own_unit_t, weights_t, gains, first_all = start(place, own, first_mine, first_other, size)
+    queries_t, own_unit_t, weights_t, gains, first_all = start(own, first_mine, first_other, size)
 
     high_mine = swap(jnp.stack(low_mine), "wide", high)
     order = [high, *range(1, high), *range(high + 1, size)]
@@ -875,7 +854,7 @@
     high_other = swap(high_mine, "seg", 1)
     pieces = (*low_mine, high_mine, *low_other, high_other)
 
-    rest_all, down_all = unpack(place, pieces, size)
+    rest_all, down_all = unpack(pieces, size)
     started, own_parts, far_parts = (), [], []
     for part in range(2):
         *started, estimate = dense_forward(
@@ -886,16 +865,16 @@
     (attended_t, inverse_total, branch_out, third, third_inverse, normed_two, slope, hidden,
      ffn_out, out_rows) = started
 
-    errors, energy = error_energy(place, own_parts, far_parts, targets[0])
+    errors, energy = error_energy(own_parts, far_parts, targets[0])
     energy = exchange(energy, size)
     seg_count = lax.axis_size("seg")
     (grad_est, grad_ffn, grad_pre, grad_branch, grad_attended_t, delta, late_gains,
      loss) = dense_back(
-        seg_count, place, present, energy, errors, rest_all, down_all, gains, attended_t, branch_out,
+        seg_count, present, energy, errors, rest_all, down_all, gains, attended_t, branch_out,
         third, third_inverse, slope, ffn_out,
     )
     keep, send = dense_weights(
-        place, grad_est, grad_ffn, grad_pre, grad_branch, attended_t, normed_two, hidden,
+        grad_est, grad_ffn, grad_pre, grad_branch, attended_t, normed_two, hidden,
         out_rows, size,
     )
     grad_attended_t, keep, send = tie(grad_attended_t, keep, send)
@@ -911,7 +890,7 @@
             grad_queries, early = tie(grad_queries, early)
             early = send_members(early, size)
     keep, send = finish(
-        place, grad_queries, own_unit_t, first_all, gains, late_gains, grads, units, size
+        grad_queries, own_unit_t, first_all, gains, late_gains, grads, units, size
     )
     keep, send, *early = tie(keep, send, *early)
     late = core_step(keep, send)
@@ -925,11 +904,11 @@
     late = segment_step(late)
     late_other = swap(late, "seg", 1)
 
-    squares = square_sum(early, early_other, late, late_other)
-    squares = branch_sum(place, squares, branch_parts(squares, size))
+    squares, kept = square_sum(early, early_other, late, late_other)
+    parts = branch_parts(squares, size)
+    squares = even_sum([kept + parts[0]] + parts[1:])
     squares_other = swap(squares, "seg", 1)
     *updated, grad_norm = adam(
-        place,
         (squares, squares_other),
         (early, early_other, late, late_other),
         (wide_master, down_master, gain_master, wide_first, down_first, gain_first,

time: 136 us -> 132 us (0.971)
  Pallas kernels: 53.5 us -> 48.8 us
    pallas_call x18 -> x17, Pallas kernels: 53.5 us -> 48.8 us  [call(): pl.pallas_call(body_of, out_shape=out_shape, in_specs=[here] * len(operan...]
where the time goes in v8:
time: 132 us
  Pallas kernels  48.8 us (37%)
  starting transfers between devices  40.8 us (31%)
  waiting for transfers between devices  36.7 us (28%)
  local copies, waits for them, and re-layouts  3.73 us (3%)
    pallas_call x17, Pallas kernels, call(): pl.pallas_call(body_of, out_shape=out_shape, in_specs=[here] * len(operan...  48.8 us
    ppermute x33, starting transfers between devices, swap(): lax.ppermute(x, axis, [(i, i ^ mask) for i in range(lax.axis_size(axis))])  36.6 us
    ppermute x33, waiting for transfers between devices, swap(): lax.ppermute(x, axis, [(i, i ^ mask) for i in range(lax.axis_size(axis))])  34.7 us
    ppermute x4, starting transfers between devices, branch_parts(): found.append(lax.ppermute(values, ('seg', 'wide'), pairs))  4.15 us
    unnamed x30, local copies, waits for them, and re-layouts  3.1 us
  transfers between devices with their start and end apart: 37, of which 19 were waited for; matrix products, arithmetic and copies ran while one was open for 1% of the time, Pallas kernels for 28%

profile of v8, /device:TPU:0, one launch (start us, length us, event | category | flops | bytes accessed | tf_op | source)
XLA Modules:
  0.0 132.2 jit_solution(439695817232349095)
XLA Ops:
  0.6 4.1 %collective-permute-start = (bf16[512,384]{1,0:T(8,128)(2,1)}, bf16[512,384]{1,0:T(8,128)(2,1)S(1)}, u32[]{:S(2)}, u32[]{:S(2)}) collective-permute-start(bf16[512,384]{1,0:T(8,128)(2,1)} %bitcast.38), channel_id=1, source_target_pairs={{0,4},{1,5},{2,6},{3,7},{4,0},{5,1},{6,2},{7,3},{8,12},{9,13},{10,... | collective-permute-start | bytes 1179656 | tf_op jit(solution)/shard_map/ppermute | solution.py:41
  7.9 2.6 %collective-permute-start.3 = (bf16[48,1280]{1,0:T(8,128)(2,1)S(1)}, bf16[48,1280]{1,0:T(8,128)(2,1)S(1)}, u32[]{:S(2)}, u32[]{:S(2)}) collective-permute-start(bf16[48,1280]{1,0:T(8,128)(2,1)S(1)} %get-tuple-element.131), channel_id=1, source_target_pairs={{0,3},{1,2},{2,1},{3,0},{4,7},{5,6},{6,5},{7,4},{8,11},{9,10},{10,... | collective-permute-start | bytes 368648 | tf_op jit(solution)/shard_map/ppermute | solution.py:41
  13.0 4.2 %collective-permute-done.3 = bf16[48,1280]{1,0:T(8,128)(2,1)S(1)} collective-permute-done((bf16[48,1280]{1,0:T(8,128)(2,1)S(1)}, bf16[48,1280]{1,0:T(8,128)(2,1)S(1)}, u32[]{:S(2)}, u32[]{:S(2)}) %collective-permute-start.3) | collective-permute-done | bytes 122912 | tf_op jit(solution)/shard_map/ppermute | solution.py:41
  17.2 6.4 %collective-permute-done.2 = bf16[48,1280]{1,0:T(8,128)(2,1)S(1)} collective-permute-done((bf16[48,1280]{1,0:T(8,128)(2,1)S(1)}, bf16[48,1280]{1,0:T(8,128)(2,1)S(1)}, u32[]{:S(2)}, u32[]{:S(2)}) %collective-permute-start.2) | collective-permute-done | bytes 122912 | tf_op jit(solution)/shard_map/ppermute | solution.py:41
  23.8 2.9 %collective-permute-start.7 = (bf16[512,384]{1,0:T(8,128)(2,1)S(1)}, bf16[512,384]{1,0:T(8,128)(2,1)S(1)}, u32[]{:S(2)}, u32[]{:S(2)}) collective-permute-start(bf16[512,384]{1,0:T(8,128)(2,1)S(1)} %collective-permute-done.refs_3_), channel_id=1, source_target_pairs={{0,2},{1,3},{2,0},{3,1},{4,6},{5,7},{6,4},{7,5},{8,10},{9,11},{10,... | collective-permute-start | bytes 1179656 | tf_op jit(solution)/shard_map/ppermute | solution.py:41
  29.9 3.5 %shard_map.229 = (bf16[1,8,512,512]{3,2,1,0:T(8,128)(2,1)S(1)}, bf16[1,384,512]{2,1,0:T(8,128)(2,1)S(1)}, bf16[1,384,512]{2,1,0:T(8,128)(2,1)S(1)}, bf16[1,384,5...) custom-call(bf16[384,512]{1,0:T(8,128)(2,1)S(1)} %get-tuple-element.134.refs_0_., ...), custom_call_target="tpu_custom_call" | custom-call | flops 100663296 | bytes 262144 | tf_op jit(solution)/shard_map/pallas_call | solution.py:72
  33.4 3.4 %collective-permute-done.7.refs_3_ = bf16[512,384]{1,0:T(8,128)(2,1)S(1)} collective-permute-done((bf16[512,384]{1,0:T(8,128)(2,1)S(1)}, bf16[512,384]{1,0:T(8,128)(2,1)S(1)}, u32[]{:S(2)}, u32[]{:S(2)}) %collective-permute-start.7) | collective-permute-done | bytes 393248 | tf_op jit(solution)/shard_map/ppermute | solution.py:41
  37.8 7.4 %shard_map.230 = (bf16[2,8,512,512]{3,2,1,0:T(8,128)(2,1)S(1)}, bf16[2,384,512]{2,1,0:T(8,128)(2,1)S(1)}, bf16[2,384,512]{2,1,0:T(8,128)(2,1)S(1)}, bf16[2,384,5...) custom-call(bf16[384,512]{1,0:T(8,128)(2,1)S(1)} %get-tuple-element.134.refs_0_., ...), custom_call_target="tpu_custom_call" | custom-call | flops 201326592 | bytes 524288 | tf_op jit(solution)/shard_map/pallas_call | solution.py:72
  45.2 3.6 %shard_map.231 = (bf16[1,8,512,512]{3,2,1,0:T(8,128)(2,1)S(1)}, bf16[1,384,512]{2,1,0:T(8,128)(2,1)S(1)}, bf16[1,384,512]{2,1,0:T(8,128)(2,1)S(1)}, bf16[1,384,5...) custom-call(bf16[384,512]{1,0:T(8,128)(2,1)S(1)} %get-tuple-element.134.refs_0_., ...), custom_call_target="tpu_custom_call" | custom-call | flops 100663296 | bytes 262144 | tf_op jit(solution)/shard_map/pallas_call | solution.py:72
  49.1 2.1 %collective-permute-done.12.refs_5_ = bf16[2,48,3584]{2,1,0:T(8,128)(2,1)S(1)} collective-permute-done((bf16[2,48,3584]{2,1,0:T(8,128)(2,1)S(1)}, bf16[2,48,3584]{2,1,0:T(8,128)(2,1)S(1)}, u32[]{:S(2)}, u32[]{:S(2)}) %collective-permute-start.12) | collective-permute-done | bytes 688160 | tf_op jit(solution)/shard_map/ppermute | solution.py:41
  51.6 2.4 %shard_map.233 = (f32[384,512]{1,0:T(8,128)S(1)}, f32[8,512]{1,0:T(8,128)S(1)}, f32[512,384]{1,0:T(8,128)S(1)}, f32[512,384]{1,0:T(8,128)S(1)}, f32[512,1]{1,0:T...) custom-call(bf16[512,384]{1,0:T(8,128)(2,1)S(1)} %bitcast.40, ...), custom_call_target="tpu_custom_call" | custom-call | flops 704643072 | bytes 3145728 | tf_op jit(solution)/shard_map/pallas_call | solution.py:72
  54.0 1.9 %collective-permute-start.13 = (bf16[384,128]{1,0:T(8,128)(2,1)S(1)}, bf16[384,128]{1,0:T(8,128)(2,1)S(1)}, u32[]{:S(2)}, u32[]{:S(2)}) collective-permute-start(bf16[384,128]{1,0:T(8,128)(2,1)S(1)} %get-tuple-element.161.refs_0_), channel_id=1, source_target_pairs={{0,4},{1,5},{2,6},{3,7},{4,0},{5,1},{6,2},{7,3},{8,12},{9,13},{10,... | collective-permute-start | bytes 294920 | tf_op jit(solution)/shard_map/ppermute | solution.py:41
  58.4 4.9 %collective-permute-done.14.refs_3_ = bf16[128,128]{1,0:T(8,128)(2,1)S(1)} collective-permute-done((bf16[128,128]{1,0:T(8,128)(2,1)S(1)}, bf16[128,128]{1,0:T(8,128)(2,1)S(1)}, u32[]{:S(2)}, u32[]{:S(2)}) %collective-permute-start.14) | collective-permute-done | bytes 32800 | tf_op jit(solution)/shard_map/ppermute | solution.py:41
  69.9 2.8 %shard_map.236 = (bf16[512,128]{1,0:T(8,128)(2,1)S(1)}, bf16[512,384]{1,0:T(8,128)(2,1)S(1)}, bf16[512,1536]{1,0:T(8,128)(2,1)S(1)}, bf16[512,384]{1,0:T(8,128)(...) custom-call(s32[1,4]{1,0:T(1,128)S(1)} %copy-done.14, ...), custom_call_target="tpu_custom_call" | custom-call | flops 1409286144 | bytes 6291456 | tf_op jit(solution)/shard_map/pallas_call | solution.py:72
  72.7 2.0 %shard_map.237 = (bf16[4,48,3584]{2,1,0:T(8,128)(2,1)S(1)}, bf16[4,48,3584]{2,1,0:T(8,128)(2,1)S(1)}) custom-call(bf16[512,128]{1,0:T(8,128)(2,1)S(1)} %get-tuple-element.185.refs_0_, bf16[512,384]{1,0:T(8,128)(2,1)S(1)} %get-tuple-element.186.refs_1_, bf16[512,1536]{1,0:T(8,128)(2,1)S(1)} %get-tuple-element.187.refs_2_, ...), custom_call_target="tpu_custom_call" | custom-call | flops 1409286144 | bytes 6291456 | tf_op jit(solution)/shard_map/pallas_call | solution.py:72
  74.8 4.6 %shard_map.238 = (f32[384,512]{1,0:T(8,128)S(1)}, bf16[1,768,512]{2,1,0:T(8,128)(2,1)S(1)}) custom-call(bf16[1,8,512,512]{3,2,1,0:T(8,128)(2,1)S(1)} %get-tuple-element.199.refs_0_, bf16[1,384,512]{2,1,0:T(8,128)(2,1)S(1)} %get-tuple-element.200.refs_1_, bf16[1,384,512]{2,1,0:T(8,128)(2,1)S(1)} %get-tuple-element.201.refs_2_, ...), custom_call_target="tpu_custom_call" | custom-call | flops 4026531840 | bytes 4194304 | tf_op jit(solution)/shard_map/pallas_call | solution.py:72
  83.4 8.9 %shard_map.239 = (f32[384,512]{1,0:T(8,128)S(1)}, bf16[2,768,512]{2,1,0:T(8,128)(2,1)S(1)}) custom-call(bf16[2,8,512,512]{3,2,1,0:T(8,128)(2,1)S(1)} %get-tuple-element.195.refs_0_, bf16[2,384,512]{2,1,0:T(8,128)(2,1)S(1)} %get-tuple-element.196.refs_1_, bf16[2,384,512]{2,1,0:T(8,128)(2,1)S(1)} %get-tuple-element.197.refs_2_, ...), custom_call_target="tpu_custom_call" | custom-call | flops 8053063680 | bytes 8388608 | tf_op jit(solution)/shard_map/pallas_call | solution.py:72
  92.3 4.4 %shard_map.240 = (f32[384,512]{1,0:T(8,128)S(1)}, bf16[1,768,512]{2,1,0:T(8,128)(2,1)S(1)}) custom-call(bf16[1,8,512,512]{3,2,1,0:T(8,128)(2,1)S(1)} %get-tuple-element.150.refs_0_, bf16[1,384,512]{2,1,0:T(8,128)(2,1)S(1)} %get-tuple-element.151.refs_1_, bf16[1,384,512]{2,1,0:T(8,128)(2,1)S(1)} %get-tuple-element.152.refs_2_, ...), custom_call_target="tpu_custom_call" | custom-call | flops 4026531840 | bytes 4194304 | tf_op jit(solution)/shard_map/pallas_call | solution.py:72
  96.8 2.5 %shard_map.241 = (bf16[4,48,1280]{2,1,0:T(8,128)(2,1)S(1)}, bf16[4,48,1280]{2,1,0:T(8,128)(2,1)S(1)}) custom-call(f32[384,512]{1,0:T(8,128)S(1)} %get-tuple-element.208.refs_0_, bf16[384,512]{1,0:T(8,128)(2,1)S(1)} %get-tuple-element.209.refs_1_, bf16[384,1280]{1,0:T(8,128)(2,1)S(1)} %get-tuple-element.210.refs_2_, ...), custom_call_target="tpu_custom_call" | custom-call | flops 1811939328 | bytes 1572864 | tf_op jit(solution)/shard_map/pallas_call | solution.py:72
  102.7 2.4 %collective-permute-start.24 = (bf16[48,1280]{1,0:T(8,128)(2,1)S(1)}, bf16[48,1280]{1,0:T(8,128)(2,1)S(1)}, u32[]{:S(2)}, u32[]{:S(2)}) collective-permute-start(bf16[48,1280]{1,0:T(8,128)(2,1)S(1)} %get-tuple-element.254), channel_id=1, source_target_pairs={{0,3},{1,2},{2,1},{3,0},{4,7},{5,6},{6,5},{7,4},{8,11},{9,10},{10,... | collective-permute-start | bytes 368648 | tf_op jit(solution)/shard_map/ppermute | solution.py:41
  106.7 3.3 %collective-permute-done.28 = bf16[48,3584]{1,0:T(8,128)(2,1)S(1)} collective-permute-done((bf16[48,3584]{1,0:T(8,128)(2,1)S(1)}, bf16[48,3584]{1,0:T(8,128)(2,1)S(1)}, u32[]{:S(2)}, u32[]{:S(2)}) %collective-permute-start.28) | collective-permute-done | bytes 344096 | tf_op jit(solution)/shard_map/ppermute | solution.py:41
  111.9 3.4 %collective-permute-done.30 = bf16[48,1280]{1,0:T(8,128)(2,1)S(1)} collective-permute-done((bf16[48,1280]{1,0:T(8,128)(2,1)S(1)}, bf16[48,1280]{1,0:T(8,128)(2,1)S(1)}, u32[]{:S(2)}, u32[]{:S(2)}) %collective-permute-start.30) | collective-permute-done | bytes 122912 | tf_op jit(solution)/shard_map/ppermute | solution.py:41
  123.1 4.1 %collective-permute-start.36 = (f32[8,128]{1,0:T(8,128)S(1)}, f32[8,128]{1,0:T(8,128)S(1)}, u32[]{:S(2)}, u32[]{:S(2)}) collective-permute-start(f32[8,128]{1,0:T(8,128)S(1)} %add_add_fusion.refs_0_), channel_id=1, source_target_pairs={{0,8},{8,0},{16,24},{24,16},{1,9},{9,1},{17,25},{25,17},{2,10},{10... | collective-permute-start | bytes 12296 | tf_op jit(solution)/shard_map/ppermute | solution.py:41
  128.1 3.9 %shard_map.243 = (f32[96,3200]{1,0:T(8,128)}, f32[384,384]{1,0:T(8,128)}, f32[6,128]{1,0:T(8,128)}, f32[96,3200]{1,0:T(8,128)}, f32[384,384]{1,0:T(8,128)}, /*in...) custom-call(f32[8,128]{1,0:T(8,128)S(1)} %add_add_fusion.refs_0_, ...), custom_call_target="tpu_custom_call" | custom-call | flops 9108480 | bytes 12751872 | tf_op jit(solution)/shard_map/pallas_call | solution.py:72
  (112 shorter events, 39.0 us)
Async XLA Ops:
  0.6 23.2 %collective-permute-start = (bf16[512,384]{1,0:T(8,128)(2,1)}, bf16[512,384]{1,0:T(8,128)(2,1)S(1)}, u32[]{:S(2)}, u32[]{:S(2)}) collective-permute-start(bf16[512,384]{1,0:T(8,128)(2,1)} %bitcast.38), channel_id=1, source_target_pairs={{0,4},{1,5},{2,6},{3,7},{4,0},{5,1},{6,2},{7,3},{8,12},{9,13},{10,... | collective-permute-start | bytes 1179656 | tf_op jit(solution)/shard_map/ppermute | solution.py:41
  7.9 9.3 %collective-permute-start.3 = (bf16[48,1280]{1,0:T(8,128)(2,1)S(1)}, bf16[48,1280]{1,0:T(8,128)(2,1)S(1)}, u32[]{:S(2)}, u32[]{:S(2)}) collective-permute-start(bf16[48,1280]{1,0:T(8,128)(2,1)S(1)} %get-tuple-element.131), channel_id=1, source_target_pairs={{0,3},{1,2},{2,1},{3,0},{4,7},{5,6},{6,5},{7,4},{8,11},{9,10},{10,... | collective-permute-start | bytes 368648 | tf_op jit(solution)/shard_map/ppermute | solution.py:41
  10.5 13.1 %collective-permute-start.2 = (bf16[48,1280]{1,0:T(8,128)(2,1)S(1)}, bf16[48,1280]{1,0:T(8,128)(2,1)S(1)}, u32[]{:S(2)}, u32[]{:S(2)}) collective-permute-start(bf16[48,1280]{1,0:T(8,128)(2,1)S(1)} %get-tuple-element.131), channel_id=1, source_target_pairs={{0,2},{1,3},{2,0},{3,1},{4,6},{5,7},{6,4},{7,5},{8,10},{9,11},{10,... | collective-permute-start | bytes 368648 | tf_op jit(solution)/shard_map/ppermute | solution.py:41
  10.9 12.7 %collective-permute-start.1 = (bf16[48,1280]{1,0:T(8,128)(2,1)S(1)}, bf16[48,1280]{1,0:T(8,128)(2,1)S(1)}, u32[]{:S(2)}, u32[]{:S(2)}) collective-permute-start(bf16[48,1280]{1,0:T(8,128)(2,1)S(1)} %get-tuple-element.131), channel_id=1, source_target_pairs={{0,1},{1,0},{2,3},{3,2},{4,5},{5,4},{6,7},{7,6},{8,9},{9,8},{10,11... | collective-permute-start | bytes 368648 | tf_op jit(solution)/shard_map/ppermute | solution.py:41
  11.4 12.4 %collective-permute-start.4 = (bf16[48,3584]{1,0:T(8,128)(2,1)S(1)}, bf16[48,3584]{1,0:T(8,128)(2,1)S(1)}, u32[]{:S(2)}, u32[]{:S(2)}) collective-permute-start(bf16[48,3584]{1,0:T(8,128)(2,1)S(1)} %get-tuple-element.146.refs_0_), channel_id=1, source_target_pairs={{0,1},{1,0},{2,3},{3,2},{4,5},{5,4},{6,7},{7,6},{8,9},{9,8},{10,11... | collective-permute-start | bytes 1032200 | tf_op jit(solution)/shard_map/ppermute | solution.py:41
  23.8 13.0 %collective-permute-start.7 = (bf16[512,384]{1,0:T(8,128)(2,1)S(1)}, bf16[512,384]{1,0:T(8,128)(2,1)S(1)}, u32[]{:S(2)}, u32[]{:S(2)}) collective-permute-start(bf16[512,384]{1,0:T(8,128)(2,1)S(1)} %collective-permute-done.refs_3_), channel_id=1, source_target_pairs={{0,2},{1,3},{2,0},{3,1},{4,6},{5,7},{6,4},{7,5},{8,10},{9,11},{10,... | collective-permute-start | bytes 1179656 | tf_op jit(solution)/shard_map/ppermute | solution.py:41
  26.7 10.0 %collective-permute-start.6 = (bf16[512,384]{1,0:T(8,128)(2,1)S(1)}, bf16[512,384]{1,0:T(8,128)(2,1)S(1)}, u32[]{:S(2)}, u32[]{:S(2)}) collective-permute-start(bf16[512,384]{1,0:T(8,128)(2,1)S(1)} %collective-permute-done.refs_3_), channel_id=1, source_target_pairs={{0,1},{1,0},{2,3},{3,2},{4,5},{5,4},{6,7},{7,6},{8,9},{9,8},{10,11... | collective-permute-start | bytes 1179656 | tf_op jit(solution)/shard_map/ppermute | solution.py:41
  27.3 21.7 %collective-permute-start.11 = (bf16[2,48,3584]{2,1,0:T(8,128)(2,1)S(1)}, bf16[2,48,3584]{2,1,0:T(8,128)(2,1)S(1)}, u32[]{:S(2)}, u32[]{:S(2)}) collective-permute-start(bf16[2,48,3584]{2,1,0:T(8,128)(2,1)S(1)} %pad_maximum_fusion), channel_id=1, source_target_pairs={{0,2},{1,3},{2,0},{3,1},{4,6},{5,7},{6,4},{7,5},{8,10},{9,11},{10,... | collective-permute-start | bytes 2064392 | tf_op jit(solution)/shard_map/ppermute | solution.py:41
  36.8 8.4 %collective-permute-start.8 = (bf16[512,384]{1,0:T(8,128)(2,1)S(1)}, bf16[512,384]{1,0:T(8,128)(2,1)S(1)}, u32[]{:S(2)}, u32[]{:S(2)}) collective-permute-start(bf16[512,384]{1,0:T(8,128)(2,1)S(1)} %collective-permute-done.7.refs_3_), channel_id=1, source_target_pairs={{0,1},{1,0},{2,3},{3,2},{4,5},{5,4},{6,7},{7,6},{8,9},{9,8},{10,11... | collective-permute-start | bytes 1179656 | tf_op jit(solution)/shard_map/ppermute | solution.py:41
  37.3 7.9 %collective-permute-start.9 = (bf16[48,3584]{1,0:T(8,128)(2,1)S(1)}, bf16[48,3584]{1,0:T(8,128)(2,1)S(1)}, u32[]{:S(2)}, u32[]{:S(2)}) collective-permute-start(bf16[48,3584]{1,0:T(8,128)(2,1)S(1)} %get-tuple-element.146.refs_0_), channel_id=1, source_target_pairs={{0,8},{8,0},{16,24},{24,16},{1,9},{9,1},{17,25},{25,17},{2,10},{10... | collective-permute-start | bytes 1032200 | tf_op jit(solution)/shard_map/ppermute | solution.py:41
  37.3 7.9 %collective-permute-start.10 = (bf16[48,3584]{1,0:T(8,128)(2,1)S(1)}, bf16[48,3584]{1,0:T(8,128)(2,1)S(1)}, u32[]{:S(2)}, u32[]{:S(2)}) collective-permute-start(bf16[48,3584]{1,0:T(8,128)(2,1)S(1)} %collective-permute-done.4.refs_1_), channel_id=1, source_target_pairs={{0,8},{8,0},{16,24},{24,16},{1,9},{9,1},{17,25},{25,17},{2,10},{10... | collective-permute-start | bytes 1032200 | tf_op jit(solution)/shard_map/ppermute | solution.py:41
  54.0 9.3 %collective-permute-start.13 = (bf16[384,128]{1,0:T(8,128)(2,1)S(1)}, bf16[384,128]{1,0:T(8,128)(2,1)S(1)}, u32[]{:S(2)}, u32[]{:S(2)}) collective-permute-start(bf16[384,128]{1,0:T(8,128)(2,1)S(1)} %get-tuple-element.161.refs_0_), channel_id=1, source_target_pairs={{0,4},{1,5},{2,6},{3,7},{4,0},{5,1},{6,2},{7,3},{8,12},{9,13},{10,... | collective-permute-start | bytes 294920 | tf_op jit(solution)/shard_map/ppermute | solution.py:41
  57.2 6.1 %collective-permute-start.14 = (bf16[128,128]{1,0:T(8,128)(2,1)S(1)}, bf16[128,128]{1,0:T(8,128)(2,1)S(1)}, u32[]{:S(2)}, u32[]{:S(2)}) collective-permute-start(bf16[128,128]{1,0:T(8,128)(2,1)S(1)} %get-tuple-element.172.refs_1_), channel_id=1, source_target_pairs={{0,4},{1,5},{2,6},{3,7},{4,0},{5,1},{6,2},{7,3},{8,12},{9,13},{10,... | collective-permute-start | bytes 98312 | tf_op jit(solution)/shard_map/ppermute | solution.py:41
  79.9 19.4 %collective-permute-start.21 = (bf16[48,3584]{1,0:T(8,128)(2,1)S(1)}, bf16[48,3584]{1,0:T(8,128)(2,1)S(1)}, u32[]{:S(2)}, u32[]{:S(2)}) collective-permute-start(bf16[48,3584]{1,0:T(8,128)(2,1)S(1)} %get-tuple-element.248), channel_id=1, source_target_pairs={{0,1},{1,0},{2,3},{3,2},{4,5},{5,4},{6,7},{7,6},{8,9},{9,8},{10,11... | collective-permute-start | bytes 1032200 | tf_op jit(solution)/shard_map/ppermute | solution.py:41
  80.6 18.7 %collective-permute-start.20 = (bf16[48,3584]{1,0:T(8,128)(2,1)S(1)}, bf16[48,3584]{1,0:T(8,128)(2,1)S(1)}, u32[]{:S(2)}, u32[]{:S(2)}) collective-permute-start(bf16[48,3584]{1,0:T(8,128)(2,1)S(1)} %get-tuple-element.249), channel_id=1, source_target_pairs={{0,3},{1,2},{2,1},{3,0},{4,7},{5,6},{6,5},{7,4},{8,11},{9,10},{10,... | collective-permute-start | bytes 1032200 | tf_op jit(solution)/shard_map/ppermute | solution.py:41
  81.9 17.3 %collective-permute-start.19 = (bf16[48,3584]{1,0:T(8,128)(2,1)S(1)}, bf16[48,3584]{1,0:T(8,128)(2,1)S(1)}, u32[]{:S(2)}, u32[]{:S(2)}) collective-permute-start(bf16[48,3584]{1,0:T(8,128)(2,1)S(1)} %get-tuple-element.250), channel_id=1, source_target_pairs={{0,2},{1,3},{2,0},{3,1},{4,6},{5,7},{6,4},{7,5},{8,10},{9,11},{10,... | collective-permute-start | bytes 1032200 | tf_op jit(solution)/shard_map/ppermute | solution.py:41
  99.5 10.6 %collective-permute-start.28 = (bf16[48,3584]{1,0:T(8,128)(2,1)S(1)}, bf16[48,3584]{1,0:T(8,128)(2,1)S(1)}, u32[]{:S(2)}, u32[]{:S(2)}) collective-permute-start(bf16[48,3584]{1,0:T(8,128)(2,1)S(1)} %add_convert_fusion.3), channel_id=1, source_target_pairs={{0,16},{8,24},{16,0},{24,8},{1,17},{9,25},{17,1},{25,9},{2,18},{10... | collective-permute-start | bytes 1032200 | tf_op jit(solution)/shard_map/ppermute | solution.py:41
  101.6 8.7 %collective-permute-start.23 = (bf16[48,1280]{1,0:T(8,128)(2,1)S(1)}, bf16[48,1280]{1,0:T(8,128)(2,1)S(1)}, u32[]{:S(2)}, u32[]{:S(2)}) collective-permute-start(bf16[48,1280]{1,0:T(8,128)(2,1)S(1)} %get-tuple-element.252), channel_id=1, source_target_pairs={{0,2},{1,3},{2,0},{3,1},{4,6},{5,7},{6,4},{7,5},{8,10},{9,11},{10,... | collective-permute-start | bytes 368648 | tf_op jit(solution)/shard_map/ppermute | solution.py:41
  102.2 8.0 %collective-permute-start.25 = (bf16[48,1280]{1,0:T(8,128)(2,1)S(1)}, bf16[48,1280]{1,0:T(8,128)(2,1)S(1)}, u32[]{:S(2)}, u32[]{:S(2)}) collective-permute-start(bf16[48,1280]{1,0:T(8,128)(2,1)S(1)} %get-tuple-element.253), channel_id=1, source_target_pairs={{0,1},{1,0},{2,3},{3,2},{4,5},{5,4},{6,7},{7,6},{8,9},{9,8},{10,11... | collective-permute-start | bytes 368648 | tf_op jit(solution)/shard_map/ppermute | solution.py:41
  102.7 7.6 %collective-permute-start.24 = (bf16[48,1280]{1,0:T(8,128)(2,1)S(1)}, bf16[48,1280]{1,0:T(8,128)(2,1)S(1)}, u32[]{:S(2)}, u32[]{:S(2)}) collective-permute-start(bf16[48,1280]{1,0:T(8,128)(2,1)S(1)} %get-tuple-element.254), channel_id=1, source_target_pairs={{0,3},{1,2},{2,1},{3,0},{4,7},{5,6},{6,5},{7,4},{8,11},{9,10},{10,... | collective-permute-start | bytes 368648 | tf_op jit(solution)/shard_map/ppermute | solution.py:41
  105.2 5.0 %collective-permute-start.27 = (f32[8,128]{1,0:T(8,128)S(1)}, f32[8,128]{1,0:T(8,128)S(1)}, u32[]{:S(2)}, u32[]{:S(2)}) collective-permute-start(f32[8,128]{1,0:T(8,128)S(1)} %add.53), channel_id=1, source_target_pairs={{0,16},{8,24},{16,0},{24,8},{1,17},{9,25},{17,1},{25,9},{2,18},{10... | collective-permute-start | bytes 12296 | tf_op jit(solution)/shard_map/ppermute | solution.py:41
  110.3 4.9 %collective-permute-start.30 = (bf16[48,1280]{1,0:T(8,128)(2,1)S(1)}, bf16[48,1280]{1,0:T(8,128)(2,1)S(1)}, u32[]{:S(2)}, u32[]{:S(2)}) collective-permute-start(bf16[48,1280]{1,0:T(8,128)(2,1)S(1)} %fusion.2), channel_id=1, source_target_pairs={{0,16},{8,24},{16,0},{24,8},{1,17},{9,25},{17,1},{25,9},{2,18},{10... | collective-permute-start | bytes 368648 | tf_op jit(solution)/shard_map/ppermute | solution.py:41
  111.9 4.8 %collective-permute-start.29 = (bf16[48,3584]{1,0:T(8,128)(2,1)S(1)}, bf16[48,3584]{1,0:T(8,128)(2,1)S(1)}, u32[]{:S(2)}, u32[]{:S(2)}) collective-permute-start(bf16[48,3584]{1,0:T(8,128)(2,1)S(1)} %add_convert_fusion.2.refs_0_.refs_2_), channel_id=1, source_target_pairs={{0,8},{8,0},{16,24},{24,16},{1,9},{9,1},{17,25},{25,17},{2,10},{10... | collective-permute-start | bytes 1032200 | tf_op jit(solution)/shard_map/ppermute | solution.py:41
  123.1 4.9 %collective-permute-start.36 = (f32[8,128]{1,0:T(8,128)S(1)}, f32[8,128]{1,0:T(8,128)S(1)}, u32[]{:S(2)}, u32[]{:S(2)}) collective-permute-start(f32[8,128]{1,0:T(8,128)S(1)} %add_add_fusion.refs_0_), channel_id=1, source_target_pairs={{0,8},{8,0},{16,24},{24,16},{1,9},{9,1},{17,25},{25,17},{2,10},{10... | collective-permute-start | bytes 12296 | tf_op jit(solution)/shard_map/ppermute | solution.py:41
  (28 other events, 307.1 us)

commit v9 on v8

--- a/solution.py
+++ b/solution.py
@@ -628,21 +628,18 @@
     )
 
 
-def square_kernel(place, *refs):
+def square_kernel(*refs):
     found = []
     for ref in refs[:4]:
         values = ref[...].astype(F32)
         rows = jnp.sum(values * values, axis=0, keepdims=True)
         found.append(jnp.sum(rows, axis=1, keepdims=True))
-    total = jnp.broadcast_to(even_sum(found), refs[4].shape)
-    refs[4][...] = total
-    refs[5][...] = jnp.where(place[0] == 0, total, 0.0)
+    refs[4][...] = jnp.broadcast_to(even_sum(found), refs[4].shape)
 
 
 def square_sum(*parts):
     size = sum(x.size for x in parts)
-    shape = sds((8, LANES), F32)
-    return call(square_kernel, parts, (shape, shape), 2 * size, 2 * size, placed=True)
+    return call(square_kernel, parts, sds((8, LANES), F32), 2 * size, 2 * size)
 
 
 def bits(size):
@@ -663,19 +660,6 @@
 
 def core_step(keep, send):
     return add_low(keep, swap(send, "seg", 1))
-
-
-def branch_parts(values, size):
-    segments, wide = lax.axis_size("seg"), 2 * size
-    found = []
-    for slot in range(size):
-        pairs = []
-        for seg in range(segments):
-            mask = size + slot if seg % 2 else slot
-            if mask:
-                pairs += [(seg * wide + w, seg * wide + (w ^ mask)) for w in range(wide)]
-        found.append(lax.ppermute(values, ("seg", "wide"), pairs))
-    return found
 
 
 def send_members(total, size):
@@ -904,10 +888,9 @@
     late = segment_step(late)
     late_other = swap(late, "seg", 1)
 
-    squares, kept = square_sum(early, early_other, late, late_other)
-    parts = branch_parts(squares, size)
-    squares = even_sum([kept + parts[0]] + parts[1:])
-    squares_other = swap(squares, "seg", 1)
+    squares = square_sum(early, early_other, late, late_other)
+    squares = even_sum([squares] + [swap(squares, "wide", mask) for mask in range(1, size)])
+    squares_other = swap(squares, "wide", size)
     *updated, grad_norm = adam(
         (squares, squares_other),
         (early, early_other, late, late_other),

time: 132 us -> 132 us (level)
  starting transfers between devices: 40.8 us -> 38.2 us
  waiting for transfers between devices: 36.7 us -> 38.8 us
    ppermute x4 -> x0, starting transfers between devices: 4.15 us -> none  [branch_parts(): found.append(lax.ppermute(values, ('seg', 'wide'), pairs))]
    ppermute x33 -> x36, waiting for transfers between devices: 34.7 us -> 38.8 us  [swap(): lax.ppermute(x, axis, [(i, i ^ mask) for i in range(lax.axis_size(axis))])]
    ppermute x4 -> x0, waiting for transfers between devices: 2 us -> none  [branch_parts(): found.append(lax.ppermute(values, ('seg', 'wide'), pairs))]
    ppermute x33 -> x36, starting transfers between devices: 36.6 us -> 38.2 us  [swap(): lax.ppermute(x, axis, [(i, i ^ mask) for i in range(lax.axis_size(axis))])]
  transfers between devices with their start and end apart: 37 -> 36, of which waited for: 19 -> 19; matrix products, arithmetic and copies ran while one was open for 1% -> 1% of each run, Pallas kernels for 28% -> 28%
where the time goes in v9:
time: 132 us
  Pallas kernels  48.8 us (37%)
  waiting for transfers between devices  38.8 us (29%)
  starting transfers between devices  38.2 us (29%)
  local copies, waits for them, and re-layouts  3.73 us (3%)
    pallas_call x17, Pallas kernels, call(): pl.pallas_call(body_of, out_shape=out_shape, in_specs=[here] * len(operan...  48.8 us
    ppermute x36, waiting for transfers between devices, swap(): lax.ppermute(x, axis, [(i, i ^ mask) for i in range(lax.axis_size(axis))])  38.8 us
    ppermute x36, starting transfers between devices, swap(): lax.ppermute(x, axis, [(i, i ^ mask) for i in range(lax.axis_size(axis))])  38.2 us
    unnamed x30, local copies, waits for them, and re-layouts  3.1 us
  transfers between devices with their start and end apart: 36, of which 19 were waited for; matrix products, arithmetic and copies ran while one was open for 1% of the time, Pallas kernels for 28%

profile of v9, /device:TPU:0, one launch (start us, length us, event | category | flops | bytes accessed | tf_op | source)
XLA Modules:
  0.0 131.7 jit_solution(2015293954127507054)
XLA Ops:
  0.6 4.1 %collective-permute-start = (bf16[512,384]{1,0:T(8,128)(2,1)}, bf16[512,384]{1,0:T(8,128)(2,1)S(1)}, u32[]{:S(2)}, u32[]{:S(2)}) collective-permute-start(bf16[512,384]{1,0:T(8,128)(2,1)} %bitcast.38), channel_id=1, source_target_pairs={{0,4},{1,5},{2,6},{3,7},{4,0},{5,1},{6,2},{7,3},{8,12},{9,13},{10,... | collective-permute-start | bytes 1179656 | tf_op jit(solution)/shard_map/ppermute | solution.py:41
  7.9 2.6 %collective-permute-start.3 = (bf16[48,1280]{1,0:T(8,128)(2,1)S(1)}, bf16[48,1280]{1,0:T(8,128)(2,1)S(1)}, u32[]{:S(2)}, u32[]{:S(2)}) collective-permute-start(bf16[48,1280]{1,0:T(8,128)(2,1)S(1)} %get-tuple-element.129), channel_id=1, source_target_pairs={{0,3},{1,2},{2,1},{3,0},{4,7},{5,6},{6,5},{7,4},{8,11},{9,10},{10,... | collective-permute-start | bytes 368648 | tf_op jit(solution)/shard_map/ppermute | solution.py:41
  13.0 4.2 %collective-permute-done.3 = bf16[48,1280]{1,0:T(8,128)(2,1)S(1)} collective-permute-done((bf16[48,1280]{1,0:T(8,128)(2,1)S(1)}, bf16[48,1280]{1,0:T(8,128)(2,1)S(1)}, u32[]{:S(2)}, u32[]{:S(2)}) %collective-permute-start.3) | collective-permute-done | bytes 122912 | tf_op jit(solution)/shard_map/ppermute | solution.py:41
  17.2 6.4 %collective-permute-done.2 = bf16[48,1280]{1,0:T(8,128)(2,1)S(1)} collective-permute-done((bf16[48,1280]{1,0:T(8,128)(2,1)S(1)}, bf16[48,1280]{1,0:T(8,128)(2,1)S(1)}, u32[]{:S(2)}, u32[]{:S(2)}) %collective-permute-start.2) | collective-permute-done | bytes 122912 | tf_op jit(solution)/shard_map/ppermute | solution.py:41
  23.8 2.9 %collective-permute-start.7 = (bf16[512,384]{1,0:T(8,128)(2,1)S(1)}, bf16[512,384]{1,0:T(8,128)(2,1)S(1)}, u32[]{:S(2)}, u32[]{:S(2)}) collective-permute-start(bf16[512,384]{1,0:T(8,128)(2,1)S(1)} %collective-permute-done.refs_3_), channel_id=1, source_target_pairs={{0,2},{1,3},{2,0},{3,1},{4,6},{5,7},{6,4},{7,5},{8,10},{9,11},{10,... | collective-permute-start | bytes 1179656 | tf_op jit(solution)/shard_map/ppermute | solution.py:41
  29.9 3.5 %shard_map.229 = (bf16[1,8,512,512]{3,2,1,0:T(8,128)(2,1)S(1)}, bf16[1,384,512]{2,1,0:T(8,128)(2,1)S(1)}, bf16[1,384,512]{2,1,0:T(8,128)(2,1)S(1)}, bf16[1,384,5...) custom-call(bf16[384,512]{1,0:T(8,128)(2,1)S(1)} %get-tuple-element.132.refs_0_., ...), custom_call_target="tpu_custom_call" | custom-call | flops 100663296 | bytes 262144 | tf_op jit(solution)/shard_map/pallas_call | solution.py:72
  33.4 3.4 %collective-permute-done.7.refs_3_ = bf16[512,384]{1,0:T(8,128)(2,1)S(1)} collective-permute-done((bf16[512,384]{1,0:T(8,128)(2,1)S(1)}, bf16[512,384]{1,0:T(8,128)(2,1)S(1)}, u32[]{:S(2)}, u32[]{:S(2)}) %collective-permute-start.7) | collective-permute-done | bytes 393248 | tf_op jit(solution)/shard_map/ppermute | solution.py:41
  37.8 7.4 %shard_map.230 = (bf16[2,8,512,512]{3,2,1,0:T(8,128)(2,1)S(1)}, bf16[2,384,512]{2,1,0:T(8,128)(2,1)S(1)}, bf16[2,384,512]{2,1,0:T(8,128)(2,1)S(1)}, bf16[2,384,5...) custom-call(bf16[384,512]{1,0:T(8,128)(2,1)S(1)} %get-tuple-element.132.refs_0_., ...), custom_call_target="tpu_custom_call" | custom-call | flops 201326592 | bytes 524288 | tf_op jit(solution)/shard_map/pallas_call | solution.py:72
  45.2 3.6 %shard_map.231 = (bf16[1,8,512,512]{3,2,1,0:T(8,128)(2,1)S(1)}, bf16[1,384,512]{2,1,0:T(8,128)(2,1)S(1)}, bf16[1,384,512]{2,1,0:T(8,128)(2,1)S(1)}, bf16[1,384,5...) custom-call(bf16[384,512]{1,0:T(8,128)(2,1)S(1)} %get-tuple-element.132.refs_0_., ...), custom_call_target="tpu_custom_call" | custom-call | flops 100663296 | bytes 262144 | tf_op jit(solution)/shard_map/pallas_call | solution.py:72
  49.1 2.1 %collective-permute-done.12.refs_5_ = bf16[2,48,3584]{2,1,0:T(8,128)(2,1)S(1)} collective-permute-done((bf16[2,48,3584]{2,1,0:T(8,128)(2,1)S(1)}, bf16[2,48,3584]{2,1,0:T(8,128)(2,1)S(1)}, u32[]{:S(2)}, u32[]{:S(2)}) %collective-permute-start.12) | collective-permute-done | bytes 688160 | tf_op jit(solution)/shard_map/ppermute | solution.py:41
  51.6 2.4 %shard_map.233 = (f32[384,512]{1,0:T(8,128)S(1)}, f32[8,512]{1,0:T(8,128)S(1)}, f32[512,384]{1,0:T(8,128)S(1)}, f32[512,384]{1,0:T(8,128)S(1)}, f32[512,1]{1,0:T...) custom-call(bf16[512,384]{1,0:T(8,128)(2,1)S(1)} %bitcast.40, ...), custom_call_target="tpu_custom_call" | custom-call | flops 704643072 | bytes 3145728 | tf_op jit(solution)/shard_map/pallas_call | solution.py:72
  54.0 1.9 %collective-permute-start.13 = (bf16[384,128]{1,0:T(8,128)(2,1)S(1)}, bf16[384,128]{1,0:T(8,128)(2,1)S(1)}, u32[]{:S(2)}, u32[]{:S(2)}) collective-permute-start(bf16[384,128]{1,0:T(8,128)(2,1)S(1)} %get-tuple-element.159.refs_0_), channel_id=1, source_target_pairs={{0,4},{1,5},{2,6},{3,7},{4,0},{5,1},{6,2},{7,3},{8,12},{9,13},{10,... | collective-permute-start | bytes 294920 | tf_op jit(solution)/shard_map/ppermute | solution.py:41
  58.4 4.9 %collective-permute-done.14.refs_3_ = bf16[128,128]{1,0:T(8,128)(2,1)S(1)} collective-permute-done((bf16[128,128]{1,0:T(8,128)(2,1)S(1)}, bf16[128,128]{1,0:T(8,128)(2,1)S(1)}, u32[]{:S(2)}, u32[]{:S(2)}) %collective-permute-start.14) | collective-permute-done | bytes 32800 | tf_op jit(solution)/shard_map/ppermute | solution.py:41
  69.9 2.8 %shard_map.236 = (bf16[512,128]{1,0:T(8,128)(2,1)S(1)}, bf16[512,384]{1,0:T(8,128)(2,1)S(1)}, bf16[512,1536]{1,0:T(8,128)(2,1)S(1)}, bf16[512,384]{1,0:T(8,128)(...) custom-call(s32[1,4]{1,0:T(1,128)S(1)} %copy-done.14, ...), custom_call_target="tpu_custom_call" | custom-call | flops 1409286144 | bytes 6291456 | tf_op jit(solution)/shard_map/pallas_call | solution.py:72
  72.7 2.0 %shard_map.237 = (bf16[4,48,3584]{2,1,0:T(8,128)(2,1)S(1)}, bf16[4,48,3584]{2,1,0:T(8,128)(2,1)S(1)}) custom-call(bf16[512,128]{1,0:T(8,128)(2,1)S(1)} %get-tuple-element.183.refs_0_, bf16[512,384]{1,0:T(8,128)(2,1)S(1)} %get-tuple-element.184.refs_1_, bf16[512,1536]{1,0:T(8,128)(2,1)S(1)} %get-tuple-element.185.refs_2_, ...), custom_call_target="tpu_custom_call" | custom-call | flops 1409286144 | bytes 6291456 | tf_op jit(solution)/shard_map/pallas_call | solution.py:72
  74.8 4.6 %shard_map.238 = (f32[384,512]{1,0:T(8,128)S(1)}, bf16[1,768,512]{2,1,0:T(8,128)(2,1)S(1)}) custom-call(bf16[1,8,512,512]{3,2,1,0:T(8,128)(2,1)S(1)} %get-tuple-element.197.refs_0_, bf16[1,384,512]{2,1,0:T(8,128)(2,1)S(1)} %get-tuple-element.198.refs_1_, bf16[1,384,512]{2,1,0:T(8,128)(2,1)S(1)} %get-tuple-element.199.refs_2_, ...), custom_call_target="tpu_custom_call" | custom-call | flops 4026531840 | bytes 4194304 | tf_op jit(solution)/shard_map/pallas_call | solution.py:72
  83.4 8.9 %shard_map.239 = (f32[384,512]{1,0:T(8,128)S(1)}, bf16[2,768,512]{2,1,0:T(8,128)(2,1)S(1)}) custom-call(bf16[2,8,512,512]{3,2,1,0:T(8,128)(2,1)S(1)} %get-tuple-element.193.refs_0_, bf16[2,384,512]{2,1,0:T(8,128)(2,1)S(1)} %get-tuple-element.194.refs_1_, bf16[2,384,512]{2,1,0:T(8,128)(2,1)S(1)} %get-tuple-element.195.refs_2_, ...), custom_call_target="tpu_custom_call" | custom-call | flops 8053063680 | bytes 8388608 | tf_op jit(solution)/shard_map/pallas_call | solution.py:72
  92.3 4.4 %shard_map.240 = (f32[384,512]{1,0:T(8,128)S(1)}, bf16[1,768,512]{2,1,0:T(8,128)(2,1)S(1)}) custom-call(bf16[1,8,512,512]{3,2,1,0:T(8,128)(2,1)S(1)} %get-tuple-element.148.refs_0_, bf16[1,384,512]{2,1,0:T(8,128)(2,1)S(1)} %get-tuple-element.149.refs_1_, bf16[1,384,512]{2,1,0:T(8,128)(2,1)S(1)} %get-tuple-element.150.refs_2_, ...), custom_call_target="tpu_custom_call" | custom-call | flops 4026531840 | bytes 4194304 | tf_op jit(solution)/shard_map/pallas_call | solution.py:72
  96.8 2.5 %shard_map.241 = (bf16[4,48,1280]{2,1,0:T(8,128)(2,1)S(1)}, bf16[4,48,1280]{2,1,0:T(8,128)(2,1)S(1)}) custom-call(f32[384,512]{1,0:T(8,128)S(1)} %get-tuple-element.206.refs_0_, bf16[384,512]{1,0:T(8,128)(2,1)S(1)} %get-tuple-element.207.refs_1_, bf16[384,1280]{1,0:T(8,128)(2,1)S(1)} %get-tuple-element.208.refs_2_, ...), custom_call_target="tpu_custom_call" | custom-call | flops 1811939328 | bytes 1572864 | tf_op jit(solution)/shard_map/pallas_call | solution.py:72
  102.7 2.4 %collective-permute-start.24 = (bf16[48,1280]{1,0:T(8,128)(2,1)S(1)}, bf16[48,1280]{1,0:T(8,128)(2,1)S(1)}, u32[]{:S(2)}, u32[]{:S(2)}) collective-permute-start(bf16[48,1280]{1,0:T(8,128)(2,1)S(1)} %get-tuple-element.250), channel_id=1, source_target_pairs={{0,3},{1,2},{2,1},{3,0},{4,7},{5,6},{6,5},{7,4},{8,11},{9,10},{10,... | collective-permute-start | bytes 368648 | tf_op jit(solution)/shard_map/ppermute | solution.py:41
  106.7 3.3 %collective-permute-done.28 = bf16[48,3584]{1,0:T(8,128)(2,1)S(1)} collective-permute-done((bf16[48,3584]{1,0:T(8,128)(2,1)S(1)}, bf16[48,3584]{1,0:T(8,128)(2,1)S(1)}, u32[]{:S(2)}, u32[]{:S(2)}) %collective-permute-start.28) | collective-permute-done | bytes 344096 | tf_op jit(solution)/shard_map/ppermute | solution.py:41
  111.9 3.4 %collective-permute-done.30 = bf16[48,1280]{1,0:T(8,128)(2,1)S(1)} collective-permute-done((bf16[48,1280]{1,0:T(8,128)(2,1)S(1)}, bf16[48,1280]{1,0:T(8,128)(2,1)S(1)}, u32[]{:S(2)}, u32[]{:S(2)}) %collective-permute-start.30) | collective-permute-done | bytes 122912 | tf_op jit(solution)/shard_map/ppermute | solution.py:41
  123.1 2.2 %collective-permute-start.35 = (f32[8,128]{1,0:T(8,128)S(1)}, f32[8,128]{1,0:T(8,128)S(1)}, u32[]{:S(2)}, u32[]{:S(2)}) collective-permute-start(f32[8,128]{1,0:T(8,128)S(1)} %add_add_fusion.refs_0_), channel_id=1, source_target_pairs={{0,4},{1,5},{2,6},{3,7},{4,0},{5,1},{6,2},{7,3},{8,12},{9,13},{10,... | collective-permute-start | bytes 12296 | tf_op jit(solution)/shard_map/ppermute | solution.py:41
  127.6 3.9 %shard_map.243 = (f32[96,3200]{1,0:T(8,128)}, f32[384,384]{1,0:T(8,128)}, f32[6,128]{1,0:T(8,128)}, f32[96,3200]{1,0:T(8,128)}, f32[384,384]{1,0:T(8,128)}, /*in...) custom-call(f32[8,128]{1,0:T(8,128)S(1)} %add_add_fusion.refs_0_, ...), custom_call_target="tpu_custom_call" | custom-call | flops 9108480 | bytes 12751872 | tf_op jit(solution)/shard_map/pallas_call | solution.py:72
  (110 shorter events, 40.5 us)
Async XLA Ops:
  0.6 23.2 %collective-permute-start = (bf16[512,384]{1,0:T(8,128)(2,1)}, bf16[512,384]{1,0:T(8,128)(2,1)S(1)}, u32[]{:S(2)}, u32[]{:S(2)}) collective-permute-start(bf16[512,384]{1,0:T(8,128)(2,1)} %bitcast.38), channel_id=1, source_target_pairs={{0,4},{1,5},{2,6},{3,7},{4,0},{5,1},{6,2},{7,3},{8,12},{9,13},{10,... | collective-permute-start | bytes 1179656 | tf_op jit(solution)/shard_map/ppermute | solution.py:41
  7.9 9.3 %collective-permute-start.3 = (bf16[48,1280]{1,0:T(8,128)(2,1)S(1)}, bf16[48,1280]{1,0:T(8,128)(2,1)S(1)}, u32[]{:S(2)}, u32[]{:S(2)}) collective-permute-start(bf16[48,1280]{1,0:T(8,128)(2,1)S(1)} %get-tuple-element.129), channel_id=1, source_target_pairs={{0,3},{1,2},{2,1},{3,0},{4,7},{5,6},{6,5},{7,4},{8,11},{9,10},{10,... | collective-permute-start | bytes 368648 | tf_op jit(solution)/shard_map/ppermute | solution.py:41
  10.5 13.1 %collective-permute-start.2 = (bf16[48,1280]{1,0:T(8,128)(2,1)S(1)}, bf16[48,1280]{1,0:T(8,128)(2,1)S(1)}, u32[]{:S(2)}, u32[]{:S(2)}) collective-permute-start(bf16[48,1280]{1,0:T(8,128)(2,1)S(1)} %get-tuple-element.129), channel_id=1, source_target_pairs={{0,2},{1,3},{2,0},{3,1},{4,6},{5,7},{6,4},{7,5},{8,10},{9,11},{10,... | collective-permute-start | bytes 368648 | tf_op jit(solution)/shard_map/ppermute | solution.py:41
  10.9 12.7 %collective-permute-start.1 = (bf16[48,1280]{1,0:T(8,128)(2,1)S(1)}, bf16[48,1280]{1,0:T(8,128)(2,1)S(1)}, u32[]{:S(2)}, u32[]{:S(2)}) collective-permute-start(bf16[48,1280]{1,0:T(8,128)(2,1)S(1)} %get-tuple-element.129), channel_id=1, source_target_pairs={{0,1},{1,0},{2,3},{3,2},{4,5},{5,4},{6,7},{7,6},{8,9},{9,8},{10,11... | collective-permute-start | bytes 368648 | tf_op jit(solution)/shard_map/ppermute | solution.py:41
  11.4 12.4 %collective-permute-start.4 = (bf16[48,3584]{1,0:T(8,128)(2,1)S(1)}, bf16[48,3584]{1,0:T(8,128)(2,1)S(1)}, u32[]{:S(2)}, u32[]{:S(2)}) collective-permute-start(bf16[48,3584]{1,0:T(8,128)(2,1)S(1)} %get-tuple-element.144.refs_0_), channel_id=1, source_target_pairs={{0,1},{1,0},{2,3},{3,2},{4,5},{5,4},{6,7},{7,6},{8,9},{9,8},{10,11... | collective-permute-start | bytes 1032200 | tf_op jit(solution)/shard_map/ppermute | solution.py:41
  23.8 13.0 %collective-permute-start.7 = (bf16[512,384]{1,0:T(8,128)(2,1)S(1)}, bf16[512,384]{1,0:T(8,128)(2,1)S(1)}, u32[]{:S(2)}, u32[]{:S(2)}) collective-permute-start(bf16[512,384]{1,0:T(8,128)(2,1)S(1)} %collective-permute-done.refs_3_), channel_id=1, source_target_pairs={{0,2},{1,3},{2,0},{3,1},{4,6},{5,7},{6,4},{7,5},{8,10},{9,11},{10,... | collective-permute-start | bytes 1179656 | tf_op jit(solution)/shard_map/ppermute | solution.py:41
  26.7 10.0 %collective-permute-start.6 = (bf16[512,384]{1,0:T(8,128)(2,1)S(1)}, bf16[512,384]{1,0:T(8,128)(2,1)S(1)}, u32[]{:S(2)}, u32[]{:S(2)}) collective-permute-start(bf16[512,384]{1,0:T(8,128)(2,1)S(1)} %collective-permute-done.refs_3_), channel_id=1, source_target_pairs={{0,1},{1,0},{2,3},{3,2},{4,5},{5,4},{6,7},{7,6},{8,9},{9,8},{10,11... | collective-permute-start | bytes 1179656 | tf_op jit(solution)/shard_map/ppermute | solution.py:41
  27.3 21.7 %collective-permute-start.11 = (bf16[2,48,3584]{2,1,0:T(8,128)(2,1)S(1)}, bf16[2,48,3584]{2,1,0:T(8,128)(2,1)S(1)}, u32[]{:S(2)}, u32[]{:S(2)}) collective-permute-start(bf16[2,48,3584]{2,1,0:T(8,128)(2,1)S(1)} %pad_maximum_fusion), channel_id=1, source_target_pairs={{0,2},{1,3},{2,0},{3,1},{4,6},{5,7},{6,4},{7,5},{8,10},{9,11},{10,... | collective-permute-start | bytes 2064392 | tf_op jit(solution)/shard_map/ppermute | solution.py:41
  36.8 8.4 %collective-permute-start.8 = (bf16[512,384]{1,0:T(8,128)(2,1)S(1)}, bf16[512,384]{1,0:T(8,128)(2,1)S(1)}, u32[]{:S(2)}, u32[]{:S(2)}) collective-permute-start(bf16[512,384]{1,0:T(8,128)(2,1)S(1)} %collective-permute-done.7.refs_3_), channel_id=1, source_target_pairs={{0,1},{1,0},{2,3},{3,2},{4,5},{5,4},{6,7},{7,6},{8,9},{9,8},{10,11... | collective-permute-start | bytes 1179656 | tf_op jit(solution)/shard_map/ppermute | solution.py:41
  37.3 7.9 %collective-permute-start.9 = (bf16[48,3584]{1,0:T(8,128)(2,1)S(1)}, bf16[48,3584]{1,0:T(8,128)(2,1)S(1)}, u32[]{:S(2)}, u32[]{:S(2)}) collective-permute-start(bf16[48,3584]{1,0:T(8,128)(2,1)S(1)} %get-tuple-element.144.refs_0_), channel_id=1, source_target_pairs={{0,8},{8,0},{16,24},{24,16},{1,9},{9,1},{17,25},{25,17},{2,10},{10... | collective-permute-start | bytes 1032200 | tf_op jit(solution)/shard_map/ppermute | solution.py:41
  37.3 7.9 %collective-permute-start.10 = (bf16[48,3584]{1,0:T(8,128)(2,1)S(1)}, bf16[48,3584]{1,0:T(8,128)(2,1)S(1)}, u32[]{:S(2)}, u32[]{:S(2)}) collective-permute-start(bf16[48,3584]{1,0:T(8,128)(2,1)S(1)} %collective-permute-done.4.refs_1_), channel_id=1, source_target_pairs={{0,8},{8,0},{16,24},{24,16},{1,9},{9,1},{17,25},{25,17},{2,10},{10... | collective-permute-start | bytes 1032200 | tf_op jit(solution)/shard_map/ppermute | solution.py:41
  54.0 9.3 %collective-permute-start.13 = (bf16[384,128]{1,0:T(8,128)(2,1)S(1)}, bf16[384,128]{1,0:T(8,128)(2,1)S(1)}, u32[]{:S(2)}, u32[]{:S(2)}) collective-permute-start(bf16[384,128]{1,0:T(8,128)(2,1)S(1)} %get-tuple-element.159.refs_0_), channel_id=1, source_target_pairs={{0,4},{1,5},{2,6},{3,7},{4,0},{5,1},{6,2},{7,3},{8,12},{9,13},{10,... | collective-permute-start | bytes 294920 | tf_op jit(solution)/shard_map/ppermute | solution.py:41
  57.2 6.1 %collective-permute-start.14 = (bf16[128,128]{1,0:T(8,128)(2,1)S(1)}, bf16[128,128]{1,0:T(8,128)(2,1)S(1)}, u32[]{:S(2)}, u32[]{:S(2)}) collective-permute-start(bf16[128,128]{1,0:T(8,128)(2,1)S(1)} %get-tuple-element.170.refs_1_), channel_id=1, source_target_pairs={{0,4},{1,5},{2,6},{3,7},{4,0},{5,1},{6,2},{7,3},{8,12},{9,13},{10,... | collective-permute-start | bytes 98312 | tf_op jit(solution)/shard_map/ppermute | solution.py:41
  74.7 4.7 %collective-permute-start.18 = (bf16[4,48,3584]{2,1,0:T(8,128)(2,1)S(1)}, bf16[4,48,3584]{2,1,0:T(8,128)(2,1)S(1)}, u32[]{:S(2)}, u32[]{:S(2)}) collective-permute-start(bf16[4,48,3584]{2,1,0:T(8,128)(2,1)S(1)} %get-tuple-element.203), channel_id=1, source_target_pairs={{0,8},{8,0},{16,24},{24,16},{1,9},{9,1},{17,25},{25,17},{2,10},{10... | collective-permute-start | bytes 4128776 | tf_op jit(solution)/shard_map/ppermute | solution.py:41
  79.9 19.4 %collective-permute-start.21 = (bf16[48,3584]{1,0:T(8,128)(2,1)S(1)}, bf16[48,3584]{1,0:T(8,128)(2,1)S(1)}, u32[]{:S(2)}, u32[]{:S(2)}) collective-permute-start(bf16[48,3584]{1,0:T(8,128)(2,1)S(1)} %get-tuple-element.244), channel_id=1, source_target_pairs={{0,1},{1,0},{2,3},{3,2},{4,5},{5,4},{6,7},{7,6},{8,9},{9,8},{10,11... | collective-permute-start | bytes 1032200 | tf_op jit(solution)/shard_map/ppermute | solution.py:41
  80.6 18.7 %collective-permute-start.20 = (bf16[48,3584]{1,0:T(8,128)(2,1)S(1)}, bf16[48,3584]{1,0:T(8,128)(2,1)S(1)}, u32[]{:S(2)}, u32[]{:S(2)}) collective-permute-start(bf16[48,3584]{1,0:T(8,128)(2,1)S(1)} %get-tuple-element.245), channel_id=1, source_target_pairs={{0,3},{1,2},{2,1},{3,0},{4,7},{5,6},{6,5},{7,4},{8,11},{9,10},{10,... | collective-permute-start | bytes 1032200 | tf_op jit(solution)/shard_map/ppermute | solution.py:41
  81.9 17.3 %collective-permute-start.19 = (bf16[48,3584]{1,0:T(8,128)(2,1)S(1)}, bf16[48,3584]{1,0:T(8,128)(2,1)S(1)}, u32[]{:S(2)}, u32[]{:S(2)}) collective-permute-start(bf16[48,3584]{1,0:T(8,128)(2,1)S(1)} %get-tuple-element.246), channel_id=1, source_target_pairs={{0,2},{1,3},{2,0},{3,1},{4,6},{5,7},{6,4},{7,5},{8,10},{9,11},{10,... | collective-permute-start | bytes 1032200 | tf_op jit(solution)/shard_map/ppermute | solution.py:41
  99.5 10.6 %collective-permute-start.28 = (bf16[48,3584]{1,0:T(8,128)(2,1)S(1)}, bf16[48,3584]{1,0:T(8,128)(2,1)S(1)}, u32[]{:S(2)}, u32[]{:S(2)}) collective-permute-start(bf16[48,3584]{1,0:T(8,128)(2,1)S(1)} %add_convert_fusion.3), channel_id=1, source_target_pairs={{0,16},{8,24},{16,0},{24,8},{1,17},{9,25},{17,1},{25,9},{2,18},{10... | collective-permute-start | bytes 1032200 | tf_op jit(solution)/shard_map/ppermute | solution.py:41
  101.6 8.7 %collective-permute-start.23 = (bf16[48,1280]{1,0:T(8,128)(2,1)S(1)}, bf16[48,1280]{1,0:T(8,128)(2,1)S(1)}, u32[]{:S(2)}, u32[]{:S(2)}) collective-permute-start(bf16[48,1280]{1,0:T(8,128)(2,1)S(1)} %get-tuple-element.248), channel_id=1, source_target_pairs={{0,2},{1,3},{2,0},{3,1},{4,6},{5,7},{6,4},{7,5},{8,10},{9,11},{10,... | collective-permute-start | bytes 368648 | tf_op jit(solution)/shard_map/ppermute | solution.py:41
  102.2 8.0 %collective-permute-start.25 = (bf16[48,1280]{1,0:T(8,128)(2,1)S(1)}, bf16[48,1280]{1,0:T(8,128)(2,1)S(1)}, u32[]{:S(2)}, u32[]{:S(2)}) collective-permute-start(bf16[48,1280]{1,0:T(8,128)(2,1)S(1)} %get-tuple-element.249), channel_id=1, source_target_pairs={{0,1},{1,0},{2,3},{3,2},{4,5},{5,4},{6,7},{7,6},{8,9},{9,8},{10,11... | collective-permute-start | bytes 368648 | tf_op jit(solution)/shard_map/ppermute | solution.py:41
  102.7 7.6 %collective-permute-start.24 = (bf16[48,1280]{1,0:T(8,128)(2,1)S(1)}, bf16[48,1280]{1,0:T(8,128)(2,1)S(1)}, u32[]{:S(2)}, u32[]{:S(2)}) collective-permute-start(bf16[48,1280]{1,0:T(8,128)(2,1)S(1)} %get-tuple-element.250), channel_id=1, source_target_pairs={{0,3},{1,2},{2,1},{3,0},{4,7},{5,6},{6,5},{7,4},{8,11},{9,10},{10,... | collective-permute-start | bytes 368648 | tf_op jit(solution)/shard_map/ppermute | solution.py:41
  105.2 5.0 %collective-permute-start.27 = (f32[8,128]{1,0:T(8,128)S(1)}, f32[8,128]{1,0:T(8,128)S(1)}, u32[]{:S(2)}, u32[]{:S(2)}) collective-permute-start(f32[8,128]{1,0:T(8,128)S(1)} %add.50), channel_id=1, source_target_pairs={{0,16},{8,24},{16,0},{24,8},{1,17},{9,25},{17,1},{25,9},{2,18},{10... | collective-permute-start | bytes 12296 | tf_op jit(solution)/shard_map/ppermute | solution.py:41
  110.3 4.9 %collective-permute-start.30 = (bf16[48,1280]{1,0:T(8,128)(2,1)S(1)}, bf16[48,1280]{1,0:T(8,128)(2,1)S(1)}, u32[]{:S(2)}, u32[]{:S(2)}) collective-permute-start(bf16[48,1280]{1,0:T(8,128)(2,1)S(1)} %fusion.2), channel_id=1, source_target_pairs={{0,16},{8,24},{16,0},{24,8},{1,17},{9,25},{17,1},{25,9},{2,18},{10... | collective-permute-start | bytes 368648 | tf_op jit(solution)/shard_map/ppermute | solution.py:41
  111.9 4.8 %collective-permute-start.29 = (bf16[48,3584]{1,0:T(8,128)(2,1)S(1)}, bf16[48,3584]{1,0:T(8,128)(2,1)S(1)}, u32[]{:S(2)}, u32[]{:S(2)}) collective-permute-start(bf16[48,3584]{1,0:T(8,128)(2,1)S(1)} %add_convert_fusion.2.refs_0_.refs_2_), channel_id=1, source_target_pairs={{0,8},{8,0},{16,24},{24,16},{1,9},{9,1},{17,25},{25,17},{2,10},{10... | collective-permute-start | bytes 1032200 | tf_op jit(solution)/shard_map/ppermute | solution.py:41
  (27 other events, 300.3 us)

commit v10 on v9

--- a/solution.py
+++ b/solution.py
@@ -663,7 +663,7 @@
 
 
 def send_members(total, size):
-    return [total[0]] + [swap(total[mask], "wide", mask) for mask in [2, 3, 1]]
+    return [total[0]] + [swap(total[mask], "wide", mask) for mask in range(1, size)]
 
 
 def sum_low(parts):

time: 132 us -> 132 us (level)
  no operation moved by 1% of the time
where the time goes in v10:
time: 132 us
  Pallas kernels  48.8 us (37%)
  waiting for transfers between devices  39.8 us (30%)
  starting transfers between devices  37.6 us (28%)
  local copies, waits for them, and re-layouts  3.73 us (3%)
    pallas_call x17, Pallas kernels, call(): pl.pallas_call(body_of, out_shape=out_shape, in_specs=[here] * len(operan...  48.8 us
    ppermute x36, waiting for transfers between devices, swap(): lax.ppermute(x, axis, [(i, i ^ mask) for i in range(lax.axis_size(axis))])  39.8 us
    ppermute x36, starting transfers between devices, swap(): lax.ppermute(x, axis, [(i, i ^ mask) for i in range(lax.axis_size(axis))])  37.6 us
    unnamed x30, local copies, waits for them, and re-layouts  3.1 us
  transfers between devices with their start and end apart: 36, of which 19 were waited for; matrix products, arithmetic and copies ran while one was open for 1% of the time, Pallas kernels for 28%

profile of v10, /device:TPU:0, one launch (start us, length us, event | category | flops | bytes accessed | tf_op | source)
XLA Modules:
  0.0 132.1 jit_solution(18346276293969408639)
XLA Ops:
  0.6 4.1 %collective-permute-start = (bf16[512,384]{1,0:T(8,128)(2,1)}, bf16[512,384]{1,0:T(8,128)(2,1)S(1)}, u32[]{:S(2)}, u32[]{:S(2)}) collective-permute-start(bf16[512,384]{1,0:T(8,128)(2,1)} %bitcast.38), channel_id=1, source_target_pairs={{0,4},{1,5},{2,6},{3,7},{4,0},{5,1},{6,2},{7,3},{8,12},{9,13},{10,... | collective-permute-start | bytes 1179656 | tf_op jit(solution)/shard_map/ppermute | solution.py:41
  7.9 2.6 %collective-permute-start.3 = (bf16[48,1280]{1,0:T(8,128)(2,1)S(1)}, bf16[48,1280]{1,0:T(8,128)(2,1)S(1)}, u32[]{:S(2)}, u32[]{:S(2)}) collective-permute-start(bf16[48,1280]{1,0:T(8,128)(2,1)S(1)} %get-tuple-element.129), channel_id=1, source_target_pairs={{0,3},{1,2},{2,1},{3,0},{4,7},{5,6},{6,5},{7,4},{8,11},{9,10},{10,... | collective-permute-start | bytes 368648 | tf_op jit(solution)/shard_map/ppermute | solution.py:41
  13.0 4.2 %collective-permute-done.3 = bf16[48,1280]{1,0:T(8,128)(2,1)S(1)} collective-permute-done((bf16[48,1280]{1,0:T(8,128)(2,1)S(1)}, bf16[48,1280]{1,0:T(8,128)(2,1)S(1)}, u32[]{:S(2)}, u32[]{:S(2)}) %collective-permute-start.3) | collective-permute-done | bytes 122912 | tf_op jit(solution)/shard_map/ppermute | solution.py:41
  17.2 6.4 %collective-permute-done.2 = bf16[48,1280]{1,0:T(8,128)(2,1)S(1)} collective-permute-done((bf16[48,1280]{1,0:T(8,128)(2,1)S(1)}, bf16[48,1280]{1,0:T(8,128)(2,1)S(1)}, u32[]{:S(2)}, u32[]{:S(2)}) %collective-permute-start.2) | collective-permute-done | bytes 122912 | tf_op jit(solution)/shard_map/ppermute | solution.py:41
  23.8 2.9 %collective-permute-start.7 = (bf16[512,384]{1,0:T(8,128)(2,1)S(1)}, bf16[512,384]{1,0:T(8,128)(2,1)S(1)}, u32[]{:S(2)}, u32[]{:S(2)}) collective-permute-start(bf16[512,384]{1,0:T(8,128)(2,1)S(1)} %collective-permute-done.refs_3_), channel_id=1, source_target_pairs={{0,2},{1,3},{2,0},{3,1},{4,6},{5,7},{6,4},{7,5},{8,10},{9,11},{10,... | collective-permute-start | bytes 1179656 | tf_op jit(solution)/shard_map/ppermute | solution.py:41
  27.4 1.7 %collective-permute-done.5.refs_2_ = bf16[4,48,1280]{2,1,0:T(8,128)(2,1)S(1)} collective-permute-done((bf16[4,48,1280]{2,1,0:T(8,128)(2,1)S(1)}, bf16[4,48,1280]{2,1,0:T(8,128)(2,1)S(1)}, u32[]{:S(2)}, u32[]{:S(2)}) %collective-permute-start.5) | collective-permute-done | bytes 491552 | tf_op jit(solution)/shard_map/ppermute | solution.py:41
  29.9 3.5 %shard_map.229 = (bf16[1,8,512,512]{3,2,1,0:T(8,128)(2,1)S(1)}, bf16[1,384,512]{2,1,0:T(8,128)(2,1)S(1)}, bf16[1,384,512]{2,1,0:T(8,128)(2,1)S(1)}, bf16[1,384,5...) custom-call(bf16[384,512]{1,0:T(8,128)(2,1)S(1)} %get-tuple-element.132.refs_0_., ...), custom_call_target="tpu_custom_call" | custom-call | flops 100663296 | bytes 262144 | tf_op jit(solution)/shard_map/pallas_call | solution.py:72
  33.4 3.4 %collective-permute-done.7.refs_3_ = bf16[512,384]{1,0:T(8,128)(2,1)S(1)} collective-permute-done((bf16[512,384]{1,0:T(8,128)(2,1)S(1)}, bf16[512,384]{1,0:T(8,128)(2,1)S(1)}, u32[]{:S(2)}, u32[]{:S(2)}) %collective-permute-start.7) | collective-permute-done | bytes 393248 | tf_op jit(solution)/shard_map/ppermute | solution.py:41
  37.8 7.4 %shard_map.230 = (bf16[2,8,512,512]{3,2,1,0:T(8,128)(2,1)S(1)}, bf16[2,384,512]{2,1,0:T(8,128)(2,1)S(1)}, bf16[2,384,512]{2,1,0:T(8,128)(2,1)S(1)}, bf16[2,384,5...) custom-call(bf16[384,512]{1,0:T(8,128)(2,1)S(1)} %get-tuple-element.132.refs_0_., ...), custom_call_target="tpu_custom_call" | custom-call | flops 201326592 | bytes 524288 | tf_op jit(solution)/shard_map/pallas_call | solution.py:72
  45.2 3.6 %shard_map.231 = (bf16[1,8,512,512]{3,2,1,0:T(8,128)(2,1)S(1)}, bf16[1,384,512]{2,1,0:T(8,128)(2,1)S(1)}, bf16[1,384,512]{2,1,0:T(8,128)(2,1)S(1)}, bf16[1,384,5...) custom-call(bf16[384,512]{1,0:T(8,128)(2,1)S(1)} %get-tuple-element.132.refs_0_., ...), custom_call_target="tpu_custom_call" | custom-call | flops 100663296 | bytes 262144 | tf_op jit(solution)/shard_map/pallas_call | solution.py:72
  49.1 2.1 %collective-permute-done.12.refs_5_ = bf16[2,48,3584]{2,1,0:T(8,128)(2,1)S(1)} collective-permute-done((bf16[2,48,3584]{2,1,0:T(8,128)(2,1)S(1)}, bf16[2,48,3584]{2,1,0:T(8,128)(2,1)S(1)}, u32[]{:S(2)}, u32[]{:S(2)}) %collective-permute-start.12) | collective-permute-done | bytes 688160 | tf_op jit(solution)/shard_map/ppermute | solution.py:41
  51.6 2.4 %shard_map.233 = (f32[384,512]{1,0:T(8,128)S(1)}, f32[8,512]{1,0:T(8,128)S(1)}, f32[512,384]{1,0:T(8,128)S(1)}, f32[512,384]{1,0:T(8,128)S(1)}, f32[512,1]{1,0:T...) custom-call(bf16[512,384]{1,0:T(8,128)(2,1)S(1)} %bitcast.40, ...), custom_call_target="tpu_custom_call" | custom-call | flops 704643072 | bytes 3145728 | tf_op jit(solution)/shard_map/pallas_call | solution.py:72
  54.0 1.9 %collective-permute-start.13 = (bf16[384,128]{1,0:T(8,128)(2,1)S(1)}, bf16[384,128]{1,0:T(8,128)(2,1)S(1)}, u32[]{:S(2)}, u32[]{:S(2)}) collective-permute-start(bf16[384,128]{1,0:T(8,128)(2,1)S(1)} %get-tuple-element.159.refs_0_), channel_id=1, source_target_pairs={{0,4},{1,5},{2,6},{3,7},{4,0},{5,1},{6,2},{7,3},{8,12},{9,13},{10,... | collective-permute-start | bytes 294920 | tf_op jit(solution)/shard_map/ppermute | solution.py:41
  58.4 4.9 %collective-permute-done.14.refs_3_ = bf16[128,128]{1,0:T(8,128)(2,1)S(1)} collective-permute-done((bf16[128,128]{1,0:T(8,128)(2,1)S(1)}, bf16[128,128]{1,0:T(8,128)(2,1)S(1)}, u32[]{:S(2)}, u32[]{:S(2)}) %collective-permute-start.14) | collective-permute-done | bytes 32800 | tf_op jit(solution)/shard_map/ppermute | solution.py:41
  69.9 2.8 %shard_map.236 = (bf16[512,128]{1,0:T(8,128)(2,1)S(1)}, bf16[512,384]{1,0:T(8,128)(2,1)S(1)}, bf16[512,1536]{1,0:T(8,128)(2,1)S(1)}, bf16[512,384]{1,0:T(8,128)(...) custom-call(s32[1,4]{1,0:T(1,128)S(1)} %copy-done.14, ...), custom_call_target="tpu_custom_call" | custom-call | flops 1409286144 | bytes 6291456 | tf_op jit(solution)/shard_map/pallas_call | solution.py:72
  72.7 2.0 %shard_map.237 = (bf16[4,48,3584]{2,1,0:T(8,128)(2,1)S(1)}, bf16[4,48,3584]{2,1,0:T(8,128)(2,1)S(1)}) custom-call(bf16[512,128]{1,0:T(8,128)(2,1)S(1)} %get-tuple-element.183.refs_0_, bf16[512,384]{1,0:T(8,128)(2,1)S(1)} %get-tuple-element.184.refs_1_, bf16[512,1536]{1,0:T(8,128)(2,1)S(1)} %get-tuple-element.185.refs_2_, ...), custom_call_target="tpu_custom_call" | custom-call | flops 1409286144 | bytes 6291456 | tf_op jit(solution)/shard_map/pallas_call | solution.py:72
  74.8 4.6 %shard_map.238 = (f32[384,512]{1,0:T(8,128)S(1)}, bf16[1,768,512]{2,1,0:T(8,128)(2,1)S(1)}) custom-call(bf16[1,8,512,512]{3,2,1,0:T(8,128)(2,1)S(1)} %get-tuple-element.197.refs_0_, bf16[1,384,512]{2,1,0:T(8,128)(2,1)S(1)} %get-tuple-element.198.refs_1_, bf16[1,384,512]{2,1,0:T(8,128)(2,1)S(1)} %get-tuple-element.199.refs_2_, ...), custom_call_target="tpu_custom_call" | custom-call | flops 4026531840 | bytes 4194304 | tf_op jit(solution)/shard_map/pallas_call | solution.py:72
  83.4 8.9 %shard_map.239 = (f32[384,512]{1,0:T(8,128)S(1)}, bf16[2,768,512]{2,1,0:T(8,128)(2,1)S(1)}) custom-call(bf16[2,8,512,512]{3,2,1,0:T(8,128)(2,1)S(1)} %get-tuple-element.193.refs_0_, bf16[2,384,512]{2,1,0:T(8,128)(2,1)S(1)} %get-tuple-element.194.refs_1_, bf16[2,384,512]{2,1,0:T(8,128)(2,1)S(1)} %get-tuple-element.195.refs_2_, ...), custom_call_target="tpu_custom_call" | custom-call | flops 8053063680 | bytes 8388608 | tf_op jit(solution)/shard_map/pallas_call | solution.py:72
  92.3 4.4 %shard_map.240 = (f32[384,512]{1,0:T(8,128)S(1)}, bf16[1,768,512]{2,1,0:T(8,128)(2,1)S(1)}) custom-call(bf16[1,8,512,512]{3,2,1,0:T(8,128)(2,1)S(1)} %get-tuple-element.148.refs_0_, bf16[1,384,512]{2,1,0:T(8,128)(2,1)S(1)} %get-tuple-element.149.refs_1_, bf16[1,384,512]{2,1,0:T(8,128)(2,1)S(1)} %get-tuple-element.150.refs_2_, ...), custom_call_target="tpu_custom_call" | custom-call | flops 4026531840 | bytes 4194304 | tf_op jit(solution)/shard_map/pallas_call | solution.py:72
  96.8 2.5 %shard_map.241 = (bf16[4,48,1280]{2,1,0:T(8,128)(2,1)S(1)}, bf16[4,48,1280]{2,1,0:T(8,128)(2,1)S(1)}) custom-call(f32[384,512]{1,0:T(8,128)S(1)} %get-tuple-element.206.refs_0_, bf16[384,512]{1,0:T(8,128)(2,1)S(1)} %get-tuple-element.207.refs_1_, bf16[384,1280]{1,0:T(8,128)(2,1)S(1)} %get-tuple-element.208.refs_2_, ...), custom_call_target="tpu_custom_call" | custom-call | flops 1811939328 | bytes 1572864 | tf_op jit(solution)/shard_map/pallas_call | solution.py:72
  106.7 3.3 %collective-permute-done.28 = bf16[48,3584]{1,0:T(8,128)(2,1)S(1)} collective-permute-done((bf16[48,3584]{1,0:T(8,128)(2,1)S(1)}, bf16[48,3584]{1,0:T(8,128)(2,1)S(1)}, u32[]{:S(2)}, u32[]{:S(2)}) %collective-permute-start.28) | collective-permute-done | bytes 344096 | tf_op jit(solution)/shard_map/ppermute | solution.py:41
  112.7 3.4 %collective-permute-done.30 = bf16[48,1280]{1,0:T(8,128)(2,1)S(1)} collective-permute-done((bf16[48,1280]{1,0:T(8,128)(2,1)S(1)}, bf16[48,1280]{1,0:T(8,128)(2,1)S(1)}, u32[]{:S(2)}, u32[]{:S(2)}) %collective-permute-start.30) | collective-permute-done | bytes 122912 | tf_op jit(solution)/shard_map/ppermute | solution.py:41
  125.6 2.4 %collective-permute-done.35.refs_1_ = f32[8,128]{1,0:T(8,128)S(1)} collective-permute-done((f32[8,128]{1,0:T(8,128)S(1)}, f32[8,128]{1,0:T(8,128)S(1)}, u32[]{:S(2)}, u32[]{:S(2)}) %collective-permute-start.35) | collective-permute-done | bytes 4128 | tf_op jit(solution)/shard_map/ppermute | solution.py:41
  128.1 3.9 %shard_map.243 = (f32[96,3200]{1,0:T(8,128)}, f32[384,384]{1,0:T(8,128)}, f32[6,128]{1,0:T(8,128)}, f32[96,3200]{1,0:T(8,128)}, f32[384,384]{1,0:T(8,128)}, /*in...) custom-call(f32[8,128]{1,0:T(8,128)S(1)} %add_add_fusion.refs_0_, ...), custom_call_target="tpu_custom_call" | custom-call | flops 9108480 | bytes 12751872 | tf_op jit(solution)/shard_map/pallas_call | solution.py:72
  (110 shorter events, 41.5 us)
Async XLA Ops:
  0.6 23.2 %collective-permute-start = (bf16[512,384]{1,0:T(8,128)(2,1)}, bf16[512,384]{1,0:T(8,128)(2,1)S(1)}, u32[]{:S(2)}, u32[]{:S(2)}) collective-permute-start(bf16[512,384]{1,0:T(8,128)(2,1)} %bitcast.38), channel_id=1, source_target_pairs={{0,4},{1,5},{2,6},{3,7},{4,0},{5,1},{6,2},{7,3},{8,12},{9,13},{10,... | collective-permute-start | bytes 1179656 | tf_op jit(solution)/shard_map/ppermute | solution.py:41
  7.9 9.3 %collective-permute-start.3 = (bf16[48,1280]{1,0:T(8,128)(2,1)S(1)}, bf16[48,1280]{1,0:T(8,128)(2,1)S(1)}, u32[]{:S(2)}, u32[]{:S(2)}) collective-permute-start(bf16[48,1280]{1,0:T(8,128)(2,1)S(1)} %get-tuple-element.129), channel_id=1, source_target_pairs={{0,3},{1,2},{2,1},{3,0},{4,7},{5,6},{6,5},{7,4},{8,11},{9,10},{10,... | collective-permute-start | bytes 368648 | tf_op jit(solution)/shard_map/ppermute | solution.py:41
  10.5 13.1 %collective-permute-start.2 = (bf16[48,1280]{1,0:T(8,128)(2,1)S(1)}, bf16[48,1280]{1,0:T(8,128)(2,1)S(1)}, u32[]{:S(2)}, u32[]{:S(2)}) collective-permute-start(bf16[48,1280]{1,0:T(8,128)(2,1)S(1)} %get-tuple-element.129), channel_id=1, source_target_pairs={{0,2},{1,3},{2,0},{3,1},{4,6},{5,7},{6,4},{7,5},{8,10},{9,11},{10,... | collective-permute-start | bytes 368648 | tf_op jit(solution)/shard_map/ppermute | solution.py:41
  10.9 12.7 %collective-permute-start.1 = (bf16[48,1280]{1,0:T(8,128)(2,1)S(1)}, bf16[48,1280]{1,0:T(8,128)(2,1)S(1)}, u32[]{:S(2)}, u32[]{:S(2)}) collective-permute-start(bf16[48,1280]{1,0:T(8,128)(2,1)S(1)} %get-tuple-element.129), channel_id=1, source_target_pairs={{0,1},{1,0},{2,3},{3,2},{4,5},{5,4},{6,7},{7,6},{8,9},{9,8},{10,11... | collective-permute-start | bytes 368648 | tf_op jit(solution)/shard_map/ppermute | solution.py:41
  11.4 12.4 %collective-permute-start.4 = (bf16[48,3584]{1,0:T(8,128)(2,1)S(1)}, bf16[48,3584]{1,0:T(8,128)(2,1)S(1)}, u32[]{:S(2)}, u32[]{:S(2)}) collective-permute-start(bf16[48,3584]{1,0:T(8,128)(2,1)S(1)} %get-tuple-element.144.refs_0_), channel_id=1, source_target_pairs={{0,1},{1,0},{2,3},{3,2},{4,5},{5,4},{6,7},{7,6},{8,9},{9,8},{10,11... | collective-permute-start | bytes 1032200 | tf_op jit(solution)/shard_map/ppermute | solution.py:41
  23.8 13.0 %collective-permute-start.7 = (bf16[512,384]{1,0:T(8,128)(2,1)S(1)}, bf16[512,384]{1,0:T(8,128)(2,1)S(1)}, u32[]{:S(2)}, u32[]{:S(2)}) collective-permute-start(bf16[512,384]{1,0:T(8,128)(2,1)S(1)} %collective-permute-done.refs_3_), channel_id=1, source_target_pairs={{0,2},{1,3},{2,0},{3,1},{4,6},{5,7},{6,4},{7,5},{8,10},{9,11},{10,... | collective-permute-start | bytes 1179656 | tf_op jit(solution)/shard_map/ppermute | solution.py:41
  26.7 10.0 %collective-permute-start.6 = (bf16[512,384]{1,0:T(8,128)(2,1)S(1)}, bf16[512,384]{1,0:T(8,128)(2,1)S(1)}, u32[]{:S(2)}, u32[]{:S(2)}) collective-permute-start(bf16[512,384]{1,0:T(8,128)(2,1)S(1)} %collective-permute-done.refs_3_), channel_id=1, source_target_pairs={{0,1},{1,0},{2,3},{3,2},{4,5},{5,4},{6,7},{7,6},{8,9},{9,8},{10,11... | collective-permute-start | bytes 1179656 | tf_op jit(solution)/shard_map/ppermute | solution.py:41
  27.3 21.7 %collective-permute-start.11 = (bf16[2,48,3584]{2,1,0:T(8,128)(2,1)S(1)}, bf16[2,48,3584]{2,1,0:T(8,128)(2,1)S(1)}, u32[]{:S(2)}, u32[]{:S(2)}) collective-permute-start(bf16[2,48,3584]{2,1,0:T(8,128)(2,1)S(1)} %pad_maximum_fusion), channel_id=1, source_target_pairs={{0,2},{1,3},{2,0},{3,1},{4,6},{5,7},{6,4},{7,5},{8,10},{9,11},{10,... | collective-permute-start | bytes 2064392 | tf_op jit(solution)/shard_map/ppermute | solution.py:41
  36.8 8.4 %collective-permute-start.8 = (bf16[512,384]{1,0:T(8,128)(2,1)S(1)}, bf16[512,384]{1,0:T(8,128)(2,1)S(1)}, u32[]{:S(2)}, u32[]{:S(2)}) collective-permute-start(bf16[512,384]{1,0:T(8,128)(2,1)S(1)} %collective-permute-done.7.refs_3_), channel_id=1, source_target_pairs={{0,1},{1,0},{2,3},{3,2},{4,5},{5,4},{6,7},{7,6},{8,9},{9,8},{10,11... | collective-permute-start | bytes 1179656 | tf_op jit(solution)/shard_map/ppermute | solution.py:41
  37.3 7.9 %collective-permute-start.9 = (bf16[48,3584]{1,0:T(8,128)(2,1)S(1)}, bf16[48,3584]{1,0:T(8,128)(2,1)S(1)}, u32[]{:S(2)}, u32[]{:S(2)}) collective-permute-start(bf16[48,3584]{1,0:T(8,128)(2,1)S(1)} %get-tuple-element.144.refs_0_), channel_id=1, source_target_pairs={{0,8},{8,0},{16,24},{24,16},{1,9},{9,1},{17,25},{25,17},{2,10},{10... | collective-permute-start | bytes 1032200 | tf_op jit(solution)/shard_map/ppermute | solution.py:41
  37.3 7.9 %collective-permute-start.10 = (bf16[48,3584]{1,0:T(8,128)(2,1)S(1)}, bf16[48,3584]{1,0:T(8,128)(2,1)S(1)}, u32[]{:S(2)}, u32[]{:S(2)}) collective-permute-start(bf16[48,3584]{1,0:T(8,128)(2,1)S(1)} %collective-permute-done.4.refs_1_), channel_id=1, source_target_pairs={{0,8},{8,0},{16,24},{24,16},{1,9},{9,1},{17,25},{25,17},{2,10},{10... | collective-permute-start | bytes 1032200 | tf_op jit(solution)/shard_map/ppermute | solution.py:41
  54.0 9.3 %collective-permute-start.13 = (bf16[384,128]{1,0:T(8,128)(2,1)S(1)}, bf16[384,128]{1,0:T(8,128)(2,1)S(1)}, u32[]{:S(2)}, u32[]{:S(2)}) collective-permute-start(bf16[384,128]{1,0:T(8,128)(2,1)S(1)} %get-tuple-element.159.refs_0_), channel_id=1, source_target_pairs={{0,4},{1,5},{2,6},{3,7},{4,0},{5,1},{6,2},{7,3},{8,12},{9,13},{10,... | collective-permute-start | bytes 294920 | tf_op jit(solution)/shard_map/ppermute | solution.py:41
  57.2 6.1 %collective-permute-start.14 = (bf16[128,128]{1,0:T(8,128)(2,1)S(1)}, bf16[128,128]{1,0:T(8,128)(2,1)S(1)}, u32[]{:S(2)}, u32[]{:S(2)}) collective-permute-start(bf16[128,128]{1,0:T(8,128)(2,1)S(1)} %get-tuple-element.170.refs_1_), channel_id=1, source_target_pairs={{0,4},{1,5},{2,6},{3,7},{4,0},{5,1},{6,2},{7,3},{8,12},{9,13},{10,... | collective-permute-start | bytes 98312 | tf_op jit(solution)/shard_map/ppermute | solution.py:41
  74.7 4.7 %collective-permute-start.18 = (bf16[4,48,3584]{2,1,0:T(8,128)(2,1)S(1)}, bf16[4,48,3584]{2,1,0:T(8,128)(2,1)S(1)}, u32[]{:S(2)}, u32[]{:S(2)}) collective-permute-start(bf16[4,48,3584]{2,1,0:T(8,128)(2,1)S(1)} %get-tuple-element.203), channel_id=1, source_target_pairs={{0,8},{8,0},{16,24},{24,16},{1,9},{9,1},{17,25},{25,17},{2,10},{10... | collective-permute-start | bytes 4128776 | tf_op jit(solution)/shard_map/ppermute | solution.py:41
  79.9 19.4 %collective-permute-start.21 = (bf16[48,3584]{1,0:T(8,128)(2,1)S(1)}, bf16[48,3584]{1,0:T(8,128)(2,1)S(1)}, u32[]{:S(2)}, u32[]{:S(2)}) collective-permute-start(bf16[48,3584]{1,0:T(8,128)(2,1)S(1)} %get-tuple-element.244), channel_id=1, source_target_pairs={{0,3},{1,2},{2,1},{3,0},{4,7},{5,6},{6,5},{7,4},{8,11},{9,10},{10,... | collective-permute-start | bytes 1032200 | tf_op jit(solution)/shard_map/ppermute | solution.py:41
  80.4 18.8 %collective-permute-start.20 = (bf16[48,3584]{1,0:T(8,128)(2,1)S(1)}, bf16[48,3584]{1,0:T(8,128)(2,1)S(1)}, u32[]{:S(2)}, u32[]{:S(2)}) collective-permute-start(bf16[48,3584]{1,0:T(8,128)(2,1)S(1)} %get-tuple-element.245), channel_id=1, source_target_pairs={{0,2},{1,3},{2,0},{3,1},{4,6},{5,7},{6,4},{7,5},{8,10},{9,11},{10,... | collective-permute-start | bytes 1032200 | tf_op jit(solution)/shard_map/ppermute | solution.py:41
  82.1 17.2 %collective-permute-start.19 = (bf16[48,3584]{1,0:T(8,128)(2,1)S(1)}, bf16[48,3584]{1,0:T(8,128)(2,1)S(1)}, u32[]{:S(2)}, u32[]{:S(2)}) collective-permute-start(bf16[48,3584]{1,0:T(8,128)(2,1)S(1)} %get-tuple-element.246), channel_id=1, source_target_pairs={{0,1},{1,0},{2,3},{3,2},{4,5},{5,4},{6,7},{7,6},{8,9},{9,8},{10,11... | collective-permute-start | bytes 1032200 | tf_op jit(solution)/shard_map/ppermute | solution.py:41
  99.5 10.6 %collective-permute-start.28 = (bf16[48,3584]{1,0:T(8,128)(2,1)S(1)}, bf16[48,3584]{1,0:T(8,128)(2,1)S(1)}, u32[]{:S(2)}, u32[]{:S(2)}) collective-permute-start(bf16[48,3584]{1,0:T(8,128)(2,1)S(1)} %add_convert_fusion.3), channel_id=1, source_target_pairs={{0,16},{8,24},{16,0},{24,8},{1,17},{9,25},{17,1},{25,9},{2,18},{10... | collective-permute-start | bytes 1032200 | tf_op jit(solution)/shard_map/ppermute | solution.py:41
  101.6 8.7 %collective-permute-start.23 = (bf16[48,1280]{1,0:T(8,128)(2,1)S(1)}, bf16[48,1280]{1,0:T(8,128)(2,1)S(1)}, u32[]{:S(2)}, u32[]{:S(2)}) collective-permute-start(bf16[48,1280]{1,0:T(8,128)(2,1)S(1)} %get-tuple-element.248), channel_id=1, source_target_pairs={{0,1},{1,0},{2,3},{3,2},{4,5},{5,4},{6,7},{7,6},{8,9},{9,8},{10,11... | collective-permute-start | bytes 368648 | tf_op jit(solution)/shard_map/ppermute | solution.py:41
  102.3 7.9 %collective-permute-start.25 = (bf16[48,1280]{1,0:T(8,128)(2,1)S(1)}, bf16[48,1280]{1,0:T(8,128)(2,1)S(1)}, u32[]{:S(2)}, u32[]{:S(2)}) collective-permute-start(bf16[48,1280]{1,0:T(8,128)(2,1)S(1)} %get-tuple-element.249), channel_id=1, source_target_pairs={{0,3},{1,2},{2,1},{3,0},{4,7},{5,6},{6,5},{7,4},{8,11},{9,10},{10,... | collective-permute-start | bytes 368648 | tf_op jit(solution)/shard_map/ppermute | solution.py:41
  103.6 7.4 %collective-permute-start.24 = (bf16[48,1280]{1,0:T(8,128)(2,1)S(1)}, bf16[48,1280]{1,0:T(8,128)(2,1)S(1)}, u32[]{:S(2)}, u32[]{:S(2)}) collective-permute-start(bf16[48,1280]{1,0:T(8,128)(2,1)S(1)} %get-tuple-element.250), channel_id=1, source_target_pairs={{0,2},{1,3},{2,0},{3,1},{4,6},{5,7},{6,4},{7,5},{8,10},{9,11},{10,... | collective-permute-start | bytes 368648 | tf_op jit(solution)/shard_map/ppermute | solution.py:41
  105.2 5.0 %collective-permute-start.27 = (f32[8,128]{1,0:T(8,128)S(1)}, f32[8,128]{1,0:T(8,128)S(1)}, u32[]{:S(2)}, u32[]{:S(2)}) collective-permute-start(f32[8,128]{1,0:T(8,128)S(1)} %add.50), channel_id=1, source_target_pairs={{0,16},{8,24},{16,0},{24,8},{1,17},{9,25},{17,1},{25,9},{2,18},{10... | collective-permute-start | bytes 12296 | tf_op jit(solution)/shard_map/ppermute | solution.py:41
  111.1 4.9 %collective-permute-start.30 = (bf16[48,1280]{1,0:T(8,128)(2,1)S(1)}, bf16[48,1280]{1,0:T(8,128)(2,1)S(1)}, u32[]{:S(2)}, u32[]{:S(2)}) collective-permute-start(bf16[48,1280]{1,0:T(8,128)(2,1)S(1)} %fusion.2), channel_id=1, source_target_pairs={{0,16},{8,24},{16,0},{24,8},{1,17},{9,25},{17,1},{25,9},{2,18},{10... | collective-permute-start | bytes 368648 | tf_op jit(solution)/shard_map/ppermute | solution.py:41
  112.7 4.8 %collective-permute-start.29 = (bf16[48,3584]{1,0:T(8,128)(2,1)S(1)}, bf16[48,3584]{1,0:T(8,128)(2,1)S(1)}, u32[]{:S(2)}, u32[]{:S(2)}) collective-permute-start(bf16[48,3584]{1,0:T(8,128)(2,1)S(1)} %add_convert_fusion.2.refs_0_.refs_2_), channel_id=1, source_target_pairs={{0,8},{8,0},{16,24},{24,16},{1,9},{9,1},{17,25},{25,17},{2,10},{10... | collective-permute-start | bytes 1032200 | tf_op jit(solution)/shard_map/ppermute | solution.py:41
  (27 other events, 304.6 us)
